TPU v7x, 32 devices: a whole 2x2x4 slice. The times are simulated.
32 devices in a mesh: feat: 4 (over y, x), label: 8 (over z, core).
Axes of the slice: x: 2, y: 2, z: 4, core: 2. Of those that a mesh axis runs over, the one named last changes fastest.
Arguments:
- documents: bfloat16 [160, 1024], P(None, 'label'), may hold values from -6 to 6
- expand_weight: bfloat16 [1024, 32768], P('label', 'feat'), may hold values from -0.1875 to 0.1875
- sparse_weight: bfloat16 [768, 16, 128, 128], P(('feat', 'label')), may hold values from -0.125 to 0.125
- feature_lists: int32 [768, 16], replicated, may hold values from 0 to 255, as said below
- positives: int32 [160, 8], replicated, may hold values from 0 to 98303
Outputs:
- grad_expand: bfloat16 [1024, 32768], P('label', 'feat')
- grad_sparse: bfloat16 [768, 16, 128, 128], P(('feat', 'label'))
Inputs may be any that keep to these rules, and one draw needn't show every extreme that they name: `feature_lists`: within each aligned group of 24 label blocks (taken in order), the entries name exactly 24 distinct feature blocks from each range of 64 consecutive blocks, each named exactly 4 times in the group; the 16 entries of one label block are distinct.
All inputs are finite; a program needn't handle non-finite values.
Results may differ from a plain program's by a relative error of at most 0.014.
Values may be sent and summed in bfloat16 or wider, within the bound.
No kernel may reach another device: no remote copies, remote signals or barrier semaphores. Data moves between devices by JAX's collectives and lax.ppermute only.
A program may use at most 192 MiB of HBM per device.

v0:
```python
import jax
import jax.numpy as jnp
from jax import lax
from jax.sharding import PartitionSpec as P

BLK = 128
FBLOCKS = 256
SLOTS = 16
LBLK_DEV = 24
CAP = 24


def on_device(documents, expand_weight, sparse_weight, feature_lists, positives):
    feat_count = lax.axis_size("feat")
    label_count = lax.axis_size("label")
    feat_index = lax.axis_index("feat")
    label_index = lax.axis_index("label")
    group = feat_index * label_count + label_index
    doc_count = documents.shape[0]
    width_local = expand_weight.shape[0]
    own_count = expand_weight.shape[1] // BLK
    local_weight = expand_weight.reshape(width_local, own_count, BLK)
    partial_pre = jnp.einsum(
        "dk,kbc->bdc", documents, local_weight, preferred_element_type=jnp.float32
    )
    summed_pre = lax.psum(partial_pre, "label")
    hidden = jnp.maximum(summed_pre, 0.0).astype(jnp.bfloat16)
    mine = lax.dynamic_slice_in_dim(feature_lists, group * LBLK_DEV, LBLK_DEV, 0)

    def sender_list(target):
        rows = lax.dynamic_slice_in_dim(
            feature_lists, (target * label_count + label_index) * LBLK_DEV, LBLK_DEV, 0
        )
        local_ids = feat_index * own_count + jnp.arange(own_count, dtype=jnp.int32)
        used = jnp.any(rows.reshape(-1)[:, None] == local_ids[None, :], axis=0)
        order = jnp.argsort(jnp.where(used, 0, 1).astype(jnp.int32), stable=True)
        return order[:CAP]

    send_index = jax.vmap(sender_list)(jnp.arange(feat_count, dtype=jnp.int32))
    outgoing = jnp.take(hidden, send_index, axis=0)
    incoming = lax.all_to_all(outgoing, "feat", split_axis=0, concat_axis=0, tiled=True)
    present = jnp.any(
        mine.reshape(-1)[:, None] == jnp.arange(FBLOCKS, dtype=jnp.int32)[None, :], axis=0
    )
    ranks = jnp.cumsum(present.reshape(feat_count, own_count).astype(jnp.int32), axis=1) - 1
    position_table = (jnp.arange(feat_count, dtype=jnp.int32)[:, None] * CAP + ranks).reshape(-1)
    slot_position = jnp.take(position_table, mine, axis=0)
    picked = jnp.take(incoming.reshape(feat_count * CAP, doc_count, BLK), slot_position, axis=0)
    logits = jnp.einsum("lsdc,lsce->dle", picked, sparse_weight, preferred_element_type=jnp.float32)
    label_ids = (group * LBLK_DEV + jnp.arange(LBLK_DEV, dtype=jnp.int32))[
        :, None
    ] * BLK + jnp.arange(BLK, dtype=jnp.int32)[None, :]
    targets = jnp.any(positives[:, :, None, None] == label_ids[None, None, :, :], axis=1).astype(
        jnp.float32
    )
    residual = (jax.nn.sigmoid(logits) - targets).astype(jnp.bfloat16)
    grad_sparse = jnp.einsum(
        "lsdc,dle->lsce", picked, residual, preferred_element_type=jnp.float32
    ).astype(jnp.bfloat16)
    back = jnp.einsum("dle,lsce->lsdc", residual, sparse_weight, preferred_element_type=jnp.float32)
    back_rows = back.reshape(LBLK_DEV * SLOTS, doc_count, BLK)
    group_part = jax.ops.segment_sum(
        back_rows, slot_position.reshape(-1), num_segments=feat_count * CAP
    )
    group_part = group_part.astype(jnp.bfloat16).reshape(feat_count, CAP, doc_count, BLK)
    returned = lax.all_to_all(group_part, "feat", split_axis=0, concat_axis=0, tiled=True)
    column_sum = jax.ops.segment_sum(
        returned.astype(jnp.float32).reshape(feat_count * CAP, doc_count, BLK),
        send_index.reshape(-1),
        num_segments=own_count,
    )
    block_grad = lax.psum(column_sum.astype(jnp.bfloat16), "label").astype(jnp.float32)
    grad_hidden = jnp.where(hidden > 0, block_grad, 0.0).astype(jnp.bfloat16)
    grad_expand = jnp.einsum(
        "dk,bdc->kbc", documents, grad_hidden, preferred_element_type=jnp.float32
    )
    grad_expand = grad_expand.reshape(width_local, own_count * BLK).astype(jnp.bfloat16)
    return (grad_expand, grad_sparse)


def solution(mesh):
    return jax.shard_map(
        on_device,
        mesh=mesh,
        in_specs=(
            P(None, "label"),
            P("label", "feat"),
            P(("feat", "label"), None, None, None),
            P(),
            P(),
        ),
        out_specs=(P("label", "feat"), P(("feat", "label"), None, None, None)),
        check_vma=False,
    )
```

profile of v0, /device:TPU:0, one launch (start us, length us, event | category | flops | bytes accessed | tf_op | source)
XLA Modules:
  0.0 502.6 jit_solution(14127657274373574968)
XLA Ops:
  7.2 8.1 %while.1 = (s32[]{:T(128)}, s32[768,16]{0,1:T(8,128)}, s32[4,2]{0,1:T(2,128)S(1)}, s32[4,24,16]{1,2,0:T(8,128)S(1)}, s32[]{:T(128)}) while((s32[]{:T(128)}, s32[768,16]{0,1:T(8,128)}, s32[4,2]{0,1:T(2,128)S(1)}, s32[4,24,16]{1,2,0:T(8,128)S(1)}, s32[]{:T(128)}) %tuple.25), condition=%wide.while_cond, body=%wide.while_body.sunk | while | flops 2 | bytes 9825 | solution.py:31
  7.2 0.1 constant_dynamic-slice_fusion.3
  7.3 0.5 slice.26
  7.8 1.4 bitcast_dynamic-update-slice_fusion.2
  9.3 0.1 constant_dynamic-slice_fusion.3
  9.3 0.5 slice.26
  9.9 1.4 bitcast_dynamic-update-slice_fusion.2
  11.3 0.1 constant_dynamic-slice_fusion.3
  11.4 0.5 slice.26
  11.9 1.4 bitcast_dynamic-update-slice_fusion.2
  13.3 0.1 constant_dynamic-slice_fusion.3
  13.4 0.5 slice.26
  13.9 1.4 bitcast_dynamic-update-slice_fusion.2
  15.4 0.1 copy.20
  15.4 0.1 eq.43
  15.5 0.2 compare_reduce_fusion.1
  15.8 0.1 copy.21
  15.9 1.0 sort.17
  16.9 0.1 copy.25
  17.0 0.1 reshape.170
  17.1 4.0 convolution_bitcast_fusion
  21.1 111.1 %all-reduce.5 = bf16[64,160,128]{2,1,0:T(8,128)(2,1)} all-reduce(f32[64,160,128]{2,1,0:T(8,128)} %convolution_bitcast_fusion), channel_id=1, replica_groups=mesh['feat'=4,'label'=8] {'label'}, use_global_device_ids=true, to_apply=%region_0.0 | all-reduce | flops 1310720 | bytes 7864320 | tf_op jit(solution)/shard_map/psum | solution.py:26
  132.1 3.8 maximum_convert_fusion
  135.9 0.1 copy.24
  136.0 4.8 gather_fusion.1
  140.8 4.5 broadcast_select_fusion.5
  145.3 5.0 all-to-all-start
  150.3 0.8 constant_dynamic-slice_fusion.1
  151.1 0.1 copy.31
  151.2 0.1 eq.47
  151.2 0.1 reshape.162
  151.3 0.1 fusion.16
  151.5 0.1 reshape.157
  151.6 0.2 reduce_window_sum.11
  151.8 0.1 add_add_fusion
  151.9 0.1 add.134
  152.0 2.8 gather_fusion
  154.8 0.1 reshape.161
  154.9 0.1 reshape.186
  155.0 0.1 reshape.178
  155.1 0.1 copy.26
  155.2 0.1 iota_add_fusion
  155.3 3.7 compare_reduce_fusion
  159.0 32.3 %all-to-all-done = bf16[4,24,160,128]{3,2,1,0:T(8,128)(2,1)} async-done(((bf16[4,24,160,128]{3,2,1,0:T(8,128)(2,1)}), bf16[4,24,160,128]{3,2,1,0:T(8,128)(2,1)}, u32[]{:S(2)}, u32[]{:S(2)}) %all-to-all-start) | async-done | bytes 3932192 | tf_op jit(solution)/shard_map/all_to_all | solution.py:41
  191.3 14.8 %gather_fusion.2 = bf16[384,160,128]{2,1,0:T(8,128)(2,1)} fusion(bf16[96,160,128]{2,1,0:T(8,128)(2,1)} %bitcast.3, s32[1024]{0:T(1024)S(1)} %pad_clamp_fusion), kind=kCustom, calls=%fused_computation.2 | custom fusion | bytes 31458816 | tf_op jit(solution)/shard_map/jit(_take)/gather | solution.py:48
  206.0 11.4 %fusion.14 = bf16[160,24,128,1]{2,0,3,1:T(8,128)(2,1)S(1)} fusion(pred[160,24,128]{2,1,0:T(8,128)(4,1)S(1)} %compare_reduce_fusion, bf16[24,16,128,128]{3,2,1,0:T(8,128)(2,1)} %param.7, bf16[24,16,160,128]{3,2,1,0:T(8,128)(2,1)} %bitcast.62, pred[24,16]{1,0:T(8,128)(4,1)S(1)} %get-tuple-element.26), kind=kOutput, calls=%fused_computation.30 | convolution fusion | flops 2024079360 | bytes 29786496 | tf_op jit(solution)/shard_map/lsdc,lsce->dle/dot_general | solution.py:49
  217.5 15.2 %fusion.23 = f32[24,160,16,128]{3,1,2,0:T(8,128)} fusion(bf16[160,24,128,1]{2,0,3,1:T(8,128)(2,1)S(1)} %fusion.14, bf16[24,16,128,128]{3,2,1,0:T(8,128)(2,1)} %param.7), kind=kOutput, calls=%fused_computation.58 | convolution fusion | flops 2013265920 | bytes 45023232 | tf_op jit(solution)/shard_map/dle,lsce->lsdc/dot_general | solution.py:60
  232.7 4.2 broadcast_in_dim.58
  236.9 87.4 %scatter_fusion = f32[96,160,128]{2,1,0:T(8,128)} fusion(f32[96,160,128]{2,1,0:T(8,128)} %broadcast_in_dim.58, s32[384]{0:T(512)S(1)} %reshape.186, f32[384,160,128]{2,1,0:T(8,128)} %bitcast.61), kind=kCustom, calls=%fused_computation.3 | custom fusion | flops 7864320 | bytes 94373376 | tf_op jit(solution)/shard_map/scatter-add | solution.py:62
  324.3 5.8 %convert_element_type.45 = bf16[96,160,128]{2,1,0:T(8,128)(2,1)} convert(f32[96,160,128]{2,1,0:T(8,128)} %scatter_fusion) | non-fusion elementwise | flops 1966080 | bytes 11796480 | tf_op jit(solution)/shard_map/convert_element_type | solution.py:65
  330.2 4.8 all-to-all-start.1
  335.0 0.3 all-reduce.4.cloned.1.call-start
  335.2 0.1 copy.22
  335.3 0.1 reshape.194
  335.4 43.7 %all-to-all-done.1 = bf16[4,24,160,128]{3,2,1,0:T(8,128)(2,1)} async-done(((bf16[4,24,160,128]{3,2,1,0:T(8,128)(2,1)}), bf16[4,24,160,128]{3,2,1,0:T(8,128)(2,1)}, u32[]{:S(2)}, u32[]{:S(2)}) %all-to-all-start.1) | async-done | bytes 3932192 | tf_op jit(solution)/shard_map/all_to_all | solution.py:66
  379.1 6.4 %bitcast_convert_fusion = f32[96,160,128]{2,1,0:T(8,128)} fusion(bf16[4,24,160,128]{3,2,1,0:T(8,128)(2,1)} %all-to-all-done.1), kind=kLoop, calls=%fused_computation.16 | loop fusion | flops 1966080 | bytes 11796480 | tf_op jit(solution)/shard_map/reshape | solution.py:68
  385.5 3.0 broadcast.134
  388.4 22.5 %scatter_fusion.1 = f32[64,160,128]{2,1,0:T(8,128)} fusion(f32[64,160,128]{2,1,0:T(8,128)} %broadcast.134, s32[96]{0:T(128)S(1)} %reshape.194, f32[96,160,128]{2,1,0:T(8,128)} %bitcast_convert_fusion), kind=kCustom, calls=%fused_computation.4 | custom fusion | flops 1966080 | bytes 23593344 | tf_op jit(solution)/shard_map/scatter-add | solution.py:67
  410.9 4.4 convert_element_type.46
  415.3 0.0 all-reduce.4.cloned.1.call-update
  415.3 14.3 %fusion.4 = bf16[24,16,128,128]{3,2,1,0:T(8,128)(2,1)} fusion(bf16[160,24,128,1]{2,0,3,1:T(8,128)(2,1)S(1)} %fusion.14, bf16[24,16,160,128]{3,2,1,0:T(8,128)(2,1)} %bitcast.63, pred[24,16]{1,0:T(8,128)(4,1)S(1)} %get-tuple-element.26), kind=kOutput, calls=%fused_computation.13 | convolution fusion | flops 2027421696 | bytes 29294976 | tf_op jit(solution)/shard_map/lsdc,dle->lsce/dot_general | solution.py:57
  429.6 56.9 %all-reduce.4.cloned.1.call-done = bf16[64,160,128]{2,1,0:T(8,128)(2,1)} async-done(((bf16[64,160,128]{2,1,0:T(8,128)(2,1)}), bf16[64,160,128]{2,1,0:T(8,128)(2,1)}) %all-reduce.4.cloned.1.call-update) | async-done | bytes 2621456 | tf_op jit(solution)/shard_map/psum | solution.py:72
  486.5 5.2 %fusion.13 = bf16[64,128,128]{2,1,0:T(8,128)(2,1)} fusion(bf16[64,160,128]{2,1,0:T(8,128)(2,1)} %all-reduce.4.cloned.1.call-done, bf16[160,128]{1,0:T(8,128)(2,1)S(1)} %copy-done.2, bf16[64,160,128]{2,1,0:T(8,128)(2,1)} %all-reduce.5), kind=kOutput, calls=%fused_computation.29 | convolution fusion | flops 345767936 | bytes 7380992 | tf_op jit(solution)/shard_map/dk,bdc->kbc/dot_general | solution.py:74
  491.7 4.1 copy.28
  (25 shorter events, 0.1 us)
Async XLA Ops:
  7.2 9.9 %copy-start = (bf16[128,8192]{1,0:T(8,128)(2,1)S(1)}, bf16[128,8192]{1,0:T(8,128)(2,1)}, u32[]{:S(2)}) copy-start(bf16[128,8192]{1,0:T(8,128)(2,1)} %param.6) | copy-start | bytes 6291460
  145.3 46.0 %all-to-all-start = ((bf16[4,24,160,128]{3,2,1,0:T(8,128)(2,1)}), bf16[4,24,160,128]{3,2,1,0:T(8,128)(2,1)}, u32[]{:S(2)}, u32[]{:S(2)}) async-start(bf16[4,24,160,128]{3,2,1,0:T(8,128)(2,1)} %broadcast_select_fusion.5), calls=%async_computation | async-start | bytes 7864320 | tf_op jit(solution)/shard_map/all_to_all | solution.py:41
  152.0 3.1 copy-start.3
  330.2 48.9 %all-to-all-start.1 = ((bf16[4,24,160,128]{3,2,1,0:T(8,128)(2,1)}), bf16[4,24,160,128]{3,2,1,0:T(8,128)(2,1)}, u32[]{:S(2)}, u32[]{:S(2)}) async-start(bf16[4,24,160,128]{3,2,1,0:T(8,128)(2,1)} %bitcast.64), calls=%async_computation.1 | async-start | bytes 7864320 | tf_op jit(solution)/shard_map/all_to_all | solution.py:66
  335.0 151.5 %all-reduce.4.cloned.1.call-start = ((), (), s32[]{:S(2)}) async-start(), calls=%async_computation.2 | async-start | bytes 5242880 | tf_op jit(solution)/shard_map/psum | solution.py:72
  415.3 71.2 %copy-start.2 = (bf16[160,128]{1,0:T(8,128)(2,1)S(1)}, bf16[160,128]{1,0:T(8,128)(2,1)}, u32[]{:S(2)}) copy-start(bf16[160,128]{1,0:T(8,128)(2,1)} %param.5) | copy-start | bytes 122884
  415.3 80.4 %copy-start.1 = (bf16[128,8192]{1,0:T(8,128)(2,1)S(1)}, bf16[128,8192]{1,0:T(8,128)(2,1)}, u32[]{:S(2)}) copy-start(bf16[128,8192]{1,0:T(8,128)(2,1)} %param.6) | copy-start | bytes 6291460
Sparse Core Ops, SparseCore 0:
  415.4 71.0 all-reduce.3
where the time goes:
time: 505 us; the launch traced here: 503 us
  other arithmetic  140 us (28%)
  waiting for transfers between devices  133 us (26%)
  blocking collectives  111 us (22%)
  matrix products  50.1 us (10%)
  local copies, waits for them, and re-layouts  44 us (9%)
  between operations  14.2 us (3%)
  starting transfers between devices  10 us (2%)
    psum x1, blocking collectives, on_device(): summed_pre = lax.psum(partial_pre, 'label')  111 us
    scatter-add x1, other arithmetic, on_device(): jax.ops.segment_sum(back_rows, slot_position.reshape(-1), num_segments=fe...  87.4 us
    psum x1, waiting for transfers between devices, on_device(): lax.psum(column_sum.astype(jnp.bfloat16), 'label').astype(jnp.float32)  56.9 us
    all_to_all x1, waiting for transfers between devices, on_device(): lax.all_to_all(group_part, 'feat', split_axis=0, concat_axis=0, tiled=True)  43.7 us
    all_to_all x1, waiting for transfers between devices, on_device(): lax.all_to_all(outgoing, 'feat', split_axis=0, concat_axis=0, tiled=True)  32.3 us
    scatter-add x1, other arithmetic, on_device(): jax.ops.segment_sum(returned.astype(jnp.float32).reshape(feat_count * CAP...  22.5 us
    dot_general x1, matrix products, on_device(): jnp.einsum('dle,lsce->lsdc', residual, sparse_weight, preferred_element_t...  15.2 us
    gather x1, local copies, waits for them, and re-layouts, on_device(): jnp.take(incoming.reshape(feat_count * CAP, doc_count, BLK), slot_positio...  14.8 us
  transfers between devices with their start and end apart: 3, of which 3 were waited for; matrix products, arithmetic and copies ran while one was open for 5% of the time, Pallas kernels for 0%

commit v1 on v0

v1 whole, which is shorter than its diff:
```python
import jax
import jax.numpy as jnp
from jax import lax
from jax.experimental import pallas as pl
from jax.experimental.pallas import tpu as pltpu
from jax.sharding import PartitionSpec as P

BLK = 128
CORES = 2
CHUNKS = 2
UNROLL = 4

BF16 = jnp.bfloat16
F32 = jnp.float32
VMEM = pl.BlockSpec(memory_space=pltpu.VMEM)
SMEM = pl.BlockSpec(memory_space=pltpu.SMEM)
ANY = pl.BlockSpec(memory_space=pl.ANY)


def ring_shift(x, offset):
    count = lax.axis_size("label")
    ring = count // CORES
    pairs = [
        (r * CORES + c, ((r + offset) % ring) * CORES + c)
        for r in range(ring)
        for c in range(CORES)
    ]
    return lax.ppermute(x, "label", pairs)


def swap_cores(x):
    count = lax.axis_size("label")
    return lax.ppermute(x, "label", [(i, i ^ 1) for i in range(count)])


def feat_exchange(x, flip):
    return lax.ppermute(x, "feat", [(i, i ^ flip) for i in range(lax.axis_size("feat"))])


def ring_gather(own):
    ring = lax.axis_size("label") // CORES
    far = ring // 2
    half = own.shape[0] // 2
    pieces = [None] * ring
    pieces[0] = own
    up = down = own
    for step in range(1, far):
        up = ring_shift(up, 1)
        down = ring_shift(down, -1)
        pieces[(-step) % ring] = up
        pieces[step] = down
    first = ring_shift(up[:half], 1)
    second = ring_shift(down[half:], -1)
    pieces[far] = jnp.concatenate([first, second], axis=0)
    return pieces


def ring_reduce(pieces):
    ring = len(pieces)
    far = ring // 2
    half = pieces[0].shape[0] // 2
    up = ring_shift(pieces[far][:half], 1)
    down = ring_shift(pieces[far][half:], -1)
    for step in range(far - 1, 0, -1):
        ahead = pieces[step].astype(F32)
        behind = pieces[(-step) % ring].astype(F32)
        if step == far - 1:
            ahead = jnp.concatenate([ahead[:half] + up.astype(F32), ahead[half:]], axis=0)
            behind = jnp.concatenate([behind[:half], behind[half:] + down.astype(F32)], axis=0)
        else:
            ahead = ahead + up.astype(F32)
            behind = behind + down.astype(F32)
        up = ring_shift(ahead.astype(BF16), 1)
        down = ring_shift(behind.astype(BF16), -1)
    return [pieces[0].astype(F32), up.astype(F32), down.astype(F32)]


def select_blocks(pools, index, cap):
    size, docs, blk = pools[0].shape
    outs = index.shape[0] // cap

    def kernel(index_ref, *refs):
        ins = refs[: len(pools)]
        out_refs = refs[len(pools) : len(pools) + outs]
        pool, sem = refs[len(pools) + outs :]
        copies = [
            pltpu.make_async_copy(ref, pool.at[pl.ds(i * size, size)], sem.at[i])
            for i, ref in enumerate(ins)
        ]
        for copy in copies:
            copy.start()
        for copy in copies:
            copy.wait()
        for m in range(outs):

            def step(k, carry):
                out_refs[m][k] = pool[index_ref[m * cap + k]]
                return carry

            lax.fori_loop(0, cap, step, 0, unroll=UNROLL)

    return pl.pallas_call(
        kernel,
        out_shape=[jax.ShapeDtypeStruct((cap, docs, blk), BF16)] * outs,
        in_specs=[SMEM] + [ANY] * len(pools),
        out_specs=[VMEM] * outs,
        scratch_shapes=[
            pltpu.VMEM((len(pools) * size, docs, blk), BF16),
            pltpu.SemaphoreType.DMA((len(pools),)),
        ],
        name="select_blocks",
    )(index, *pools)


def add_blocks(parts, index, blocks, outs):
    cap, docs, blk = parts[0].shape
    size = blocks // outs

    def kernel(index_ref, *refs):
        ins = refs[: len(parts)]
        out_refs = refs[len(parts) : len(parts) + outs]
        total = refs[-1]
        total[...] = jnp.zeros_like(total)
        for m, ref in enumerate(ins):

            def step(k, carry):
                total[index_ref[m * cap + k]] += ref[k].astype(F32)
                return carry

            lax.fori_loop(0, cap, step, 0, unroll=UNROLL)
        for i, ref in enumerate(out_refs):
            ref[...] = total[pl.ds(i * size, size)].astype(BF16)

    return pl.pallas_call(
        kernel,
        out_shape=[jax.ShapeDtypeStruct((size, docs, blk), BF16)] * outs,
        in_specs=[SMEM] + [VMEM] * len(parts),
        out_specs=[VMEM] * outs,
        scratch_shapes=[pltpu.VMEM((blocks, docs, blk), F32)],
        name="add_blocks",
    )(index, *parts)


def residual_and_back(parts, weight, slot_position, order, positives, first_label):
    count = len(parts)
    cap, docs, blk = parts[0].shape
    label_blocks, slots = weight.shape[:2]
    uses = label_blocks * slots // (count * cap)
    pos_count = positives.shape[1]

    def kernel(position_ref, order_ref, first_ref, positives_ref, weight_hbm, *refs):
        ins = refs[:count]
        residual_ref = refs[count]
        outs = refs[count + 1 : 2 * count + 1]
        pool, weight_ref, pool_sem, weight_sem = refs[2 * count + 1 :]
        copies = [
            pltpu.make_async_copy(ins[q], pool.at[pl.ds(q * cap, cap)], pool_sem.at[q])
            for q in range(count)
        ]
        loads = [
            pltpu.make_async_copy(
                weight_hbm.at[g], weight_ref.at[pl.ds(g * slots, slots)], weight_sem.at[g]
            )
            for g in range(label_blocks)
        ]
        for copy in copies + loads:
            copy.start()
        for copy in copies:
            copy.wait()

        def forward(g, carry):
            pltpu.make_async_copy(
                weight_hbm.at[g], weight_ref.at[pl.ds(g * slots, slots)], weight_sem.at[g]
            ).wait()
            lhs = jnp.concatenate(
                [pool[position_ref[g * slots + s]] for s in range(slots)], axis=1
            )
            rhs = weight_ref[pl.ds(g * slots, slots)].reshape(slots * blk, blk)
            logits = jnp.dot(lhs, rhs, preferred_element_type=F32)
            ids = first_ref[0] + g * blk + lax.broadcasted_iota(jnp.int32, (docs, blk), 1)
            hit = positives_ref[:, 0:1] == ids
            for p in range(1, pos_count):
                hit = hit | (positives_ref[:, p : p + 1] == ids)
            residual_ref[g] = (jax.nn.sigmoid(logits) - jnp.where(hit, 1.0, 0.0)).astype(BF16)
            return carry

        lax.fori_loop(0, label_blocks, forward, 0, unroll=UNROLL)
        for q in range(count):

            def backward(k, carry):
                where = [order_ref[(q * cap + k) * uses + u] for u in range(uses)]
                lhs = jnp.concatenate([residual_ref[w // slots] for w in where], axis=1)
                rhs = jnp.concatenate([weight_ref[w] for w in where], axis=1)
                outs[q][k] = lax.dot_general(
                    lhs, rhs, (((1,), (1,)), ((), ())), preferred_element_type=F32
                ).astype(BF16)
                return carry

            lax.fori_loop(0, cap, backward, 0, unroll=2 * UNROLL)

    out = pl.pallas_call(
        kernel,
        out_shape=[jax.ShapeDtypeStruct((label_blocks, docs, blk), BF16)]
        + [jax.ShapeDtypeStruct((cap, docs, blk), BF16)] * count,
        in_specs=[SMEM] * 3 + [VMEM] + [ANY] * (count + 1),
        out_specs=[VMEM] * (count + 1),
        scratch_shapes=[
            pltpu.VMEM((count * cap, docs, blk), BF16),
            pltpu.VMEM((label_blocks * slots, blk, blk), BF16),
            pltpu.SemaphoreType.DMA((count,)),
            pltpu.SemaphoreType.DMA((label_blocks,)),
        ],
        name="residual_and_back",
    )(slot_position, order, first_label, positives, weight, *parts)
    return out[0], list(out[1:])


def block_weight_grad(chunks, residuals, order, label_blocks, slots):
    pieces = len(chunks)
    count = len(chunks[0])
    cap, _, blk = chunks[0][0].shape
    docs = [chunk[0].shape[1] for chunk in chunks]
    uses = label_blocks * slots // (count * cap)

    def kernel(order_ref, *refs):
        residual_refs = refs[:pieces]
        ins = refs[pieces : pieces + pieces * count]
        out_ref = refs[pieces + pieces * count]
        pools = refs[pieces + pieces * count + 1 :][:pieces]
        buffer, sem, out_sem = refs[-3:]
        copies = [
            pltpu.make_async_copy(
                ins[i * count + q], pools[i].at[pl.ds(q * cap, cap)], sem.at[i * count + q]
            )
            for i in range(pieces)
            for q in range(count)
        ]
        for copy in copies:
            copy.start()
        for copy in copies:
            copy.wait()

        def step(k, carry):
            where = [order_ref[k * uses + u] for u in range(uses)]
            rhs = jnp.concatenate(
                [
                    jnp.concatenate([ref[w // slots] for w in where], axis=1)
                    for ref in residual_refs
                ],
                axis=0,
            )
            lhs = jnp.concatenate([pool[k] for pool in pools], axis=0)
            out = lax.dot_general(
                lhs, rhs, (((0,), (0,)), ((), ())), preferred_element_type=F32
            ).astype(BF16)
            for u in range(uses):
                buffer[k * uses + u] = out[:, u * blk : (u + 1) * blk]
                pltpu.make_async_copy(
                    buffer.at[k * uses + u], out_ref.at[where[u]], out_sem
                ).start()
            return carry

        lax.fori_loop(0, count * cap, step, 0, unroll=UNROLL)
        pltpu.make_async_copy(buffer, out_ref, out_sem).wait()

    out = pl.pallas_call(
        kernel,
        out_shape=jax.ShapeDtypeStruct((label_blocks * slots, blk, blk), BF16),
        in_specs=[SMEM] + [VMEM] * pieces + [ANY] * (pieces * count),
        out_specs=ANY,
        scratch_shapes=[pltpu.VMEM((count * cap, d, blk), BF16) for d in docs]
        + [
            pltpu.VMEM((label_blocks * slots, blk, blk), BF16),
            pltpu.SemaphoreType.DMA((pieces * count,)),
            pltpu.SemaphoreType.DMA(()),
        ],
        name="block_weight_grad",
    )(order, *residuals, *[part for chunk in chunks for part in chunk])
    return out.reshape(label_blocks, slots, blk, blk)


def expand_weight_grad(documents, groups, columns, width):
    pieces = len(groups)
    chunks = len(groups[0])
    size, _, blk = groups[0][0].shape
    docs_all, rows = documents.shape

    def kernel(columns_ref, documents_ref, *refs):
        out_ref = refs[-1]
        lhs = documents_ref[...]
        for i in range(pieces):
            ins = refs[i * chunks : (i + 1) * chunks]
            rhs = jnp.concatenate(
                [jnp.concatenate([ref[j] for ref in ins], axis=0) for j in range(size)], axis=1
            )
            out = lax.dot_general(
                lhs, rhs, (((0,), (0,)), ((), ())), preferred_element_type=F32
            )
            start = pl.multiple_of(columns_ref[i], blk)
            out_ref[:, pl.ds(start, size * blk)] = out.astype(BF16)

    return pl.pallas_call(
        kernel,
        out_shape=jax.ShapeDtypeStruct((rows, width), BF16),
        in_specs=[SMEM, VMEM] + [VMEM] * (pieces * chunks),
        out_specs=VMEM,
        name="expand_weight_grad",
    )(columns, documents, *[part for group in groups for part in group])


def list_tables(feature_lists, feat_index, label_index, label_count, own_count, label_blocks, cap):
    feat_count = lax.axis_size("feat")
    slots = feature_lists.shape[1]
    entries = label_blocks * slots
    ring = label_count // CORES
    own_blocks = own_count // label_count
    flips = jnp.arange(feat_count, dtype=jnp.int32)
    by_device = feature_lists.reshape(feat_count, label_count, entries)
    column = lax.dynamic_index_in_dim(by_device, label_index, 1, keepdims=False)
    mine = lax.dynamic_index_in_dim(column, feat_index, 0, keepdims=False)

    local = jnp.arange(own_count, dtype=jnp.int32)
    wanted = jnp.any(
        column[:, :, None] == (feat_index * own_count + local)[None, None, :], axis=1
    )
    rank = jnp.sum(wanted[:, None, :] & (local[None, :] < local[:, None])[None], axis=2)
    chosen = wanted[:, None, :] & (rank[:, None, :] == jnp.arange(cap)[None, :, None])
    ring_index, core = label_index // CORES, label_index % CORES
    owner_ring = local // (CORES * own_blocks)
    owner_core = local // own_blocks % CORES
    place = (
        jnp.where(owner_core == core, 0, ring) + (owner_ring - ring_index) % ring
    ) * own_blocks + local % own_blocks
    send = jnp.sum(jnp.where(chosen, place[None, None, :], 0), axis=2).astype(jnp.int32)
    send = jnp.stack(
        [lax.dynamic_index_in_dim(send, feat_index ^ m, 0, keepdims=False) for m in range(feat_count)]
    ).reshape(-1)

    block = jnp.arange(feat_count * own_count, dtype=jnp.int32)
    present = jnp.any(mine[:, None] == block[None, :], axis=0)
    before = jnp.sum(
        present[None, :]
        & (block[None, :] // own_count == block[:, None] // own_count)
        & (block[None, :] < block[:, None]),
        axis=1,
    )
    table = ((block // own_count) ^ feat_index) * cap + before
    position = jnp.sum(
        jnp.where(mine[:, None] == block[None, :], table[None, :], 0), axis=1
    ).astype(jnp.int32)
    entry = jnp.arange(entries, dtype=jnp.int32)
    earlier = jnp.sum((mine[None, :] == mine[:, None]) & (entry[None, :] < entry[:, None]), axis=1)
    uses = entries // (feat_count * cap)
    key = position * uses + earlier
    order = jnp.sum(jnp.where(key[None, :] == entry[:, None], entry[None, :], 0), axis=1)
    return send, position, order.astype(jnp.int32)


def on_device(documents, expand_weight, sparse_weight, feature_lists, positives):
    feat_count = lax.axis_size("feat")
    label_count = lax.axis_size("label")
    feat_index = lax.axis_index("feat")
    label_index = lax.axis_index("label")
    group = feat_index * label_count + label_index
    ring = label_count // CORES
    far = ring // 2
    ring_index, core = label_index // CORES, label_index % CORES
    docs = documents.shape[0]
    rows, width = expand_weight.shape
    own_count = width // BLK
    own_blocks = own_count // label_count
    label_blocks, slots = sparse_weight.shape[:2]
    cap = CAP
    chunk = docs // CHUNKS
    cuts = [slice(i * chunk, (i + 1) * chunk) for i in range(CHUNKS)]

    ring_width = width // ring

    def columns_of(offset):
        start = (ring_index + offset) % ring * ring_width
        return lax.dynamic_slice_in_dim(expand_weight, start, ring_width, 1)

    far_columns = columns_of(far)
    half = rows // 2
    up, down = far_columns[:half], far_columns[half:]
    up = ring_shift(up, 1)
    down = ring_shift(down, -1)
    arrived = {}
    for offset in range(1, ring):
        if offset != far:
            arrived[offset] = ring_shift(columns_of(offset), offset)
    for _ in range(far - 1):
        up = ring_shift(up, 1)
        down = ring_shift(down, -1)
    others = {offset: ring_shift(documents, offset) for offset in range(1, ring)}

    def product(left, right):
        right = right.reshape(right.shape[0], ring_width // BLK, BLK)
        return jnp.einsum("dk,kbc->bdc", left, right, preferred_element_type=F32)

    expanded = product(documents, columns_of(0))
    for offset in range(1, ring):
        if offset != far:
            expanded = expanded + product(others[offset], arrived[offset])
    expanded = expanded + product(others[far], jnp.concatenate([up, down], axis=0))
    kept = lax.dynamic_slice_in_dim(expanded, core * own_blocks, own_blocks, 0)
    given = lax.dynamic_slice_in_dim(expanded, (1 - core) * own_blocks, own_blocks, 0)
    hidden = jnp.maximum(kept + swap_cores(given), 0.0).astype(BF16)

    send, position, order = list_tables(
        feature_lists, feat_index, label_index, label_count, own_count, label_blocks, cap
    )
    first_label = (group * label_blocks * BLK).reshape(1)

    picked, residuals, gradients = [], [], []
    for cut in cuts:
        pool = jnp.concatenate(ring_gather(hidden[:, cut]), axis=0)
        outgoing = select_blocks([pool, swap_cores(pool)], send, cap)
        parts = [outgoing[0]] + [feat_exchange(outgoing[m], m) for m in range(1, feat_count)]
        residual, back = residual_and_back(
            parts, sparse_weight, position, order, positives[cut], first_label
        )
        picked.append(parts)
        residuals.append(residual)
        returned = [back[0]] + [feat_exchange(back[m], m) for m in range(1, feat_count)]
        kept, given = add_blocks(returned, send, own_count, CORES)
        both = (kept.astype(F32) + swap_cores(given).astype(F32)).astype(BF16)
        terms = ring_reduce([both[k * own_blocks : (k + 1) * own_blocks] for k in range(ring)])
        gradient = jnp.where(hidden[:, cut] > 0, sum(terms), 0.0).astype(BF16)
        gathered = jnp.concatenate(ring_gather(gradient), axis=0)
        gradients.append((gathered, swap_cores(gathered)))

    grad_sparse = block_weight_grad(picked, residuals, order, label_blocks, slots)

    groups, starts = [], []
    for side in range(CORES):
        for k in range(ring):
            groups.append(
                [g[side][k * own_blocks : (k + 1) * own_blocks] for g in gradients]
            )
            starts.append(
                (((ring_index + k) % ring) * CORES + (core ^ side)) * own_blocks * BLK
            )
    grad_expand = expand_weight_grad(documents, groups, jnp.stack(starts), width)
    return (grad_expand, grad_sparse)


CAP = 24


def solution(mesh):
    return jax.shard_map(
        on_device,
        mesh=mesh,
        in_specs=(
            P(None, "label"),
            P("label", "feat"),
            P(("feat", "label"), None, None, None),
            P(),
            P(),
        ),
        out_specs=(P("label", "feat"), P(("feat", "label"), None, None, None)),
        check_vma=False,
    )
```

time: 505 us -> 333 us (0.66)
  other arithmetic: 140 us -> 5.21 us
  blocking collectives: 111 us -> 0 us
  Pallas kernels: 0 us -> 69.7 us
  starting transfers between devices: 10 us -> 76.7 us
  matrix products: 50.1 us -> 2.37 us
  waiting for transfers between devices: 133 us -> 157 us
  local copies, waits for them, and re-layouts: 44 us -> 20.2 us
  between operations: 14.2 us -> 1.36 us
    ppermute x0 -> x52, waiting for transfers between devices: none -> 157 us  [the longest x33 92.5 us: ring_shift(): return lax.ppermute(x, 'label', pairs)]
    psum x1 -> x0, blocking collectives: 111 us -> none  [on_device(): summed_pre = lax.psum(partial_pre, 'label')]
    scatter-add x2 -> x0, other arithmetic: 110 us -> none  [the longest x1 87.4 us: on_device(): jax.ops.segment_sum(back_rows, slot_position.reshape(-1), num_segments=fe...]
    ppermute x0 -> x52, starting transfers between devices: none -> 76.7 us  [the longest x33 61.7 us: ring_shift(): return lax.ppermute(x, 'label', pairs)]
    all_to_all x2 -> x0, waiting for transfers between devices: 75.9 us -> none  [the longest x1 43.7 us: on_device(): lax.all_to_all(group_part, 'feat', split_axis=0, concat_axis=0, tiled=True)]
    pallas_call x0 -> x8, Pallas kernels: none -> 69.7 us  [the longest x2 39.4 us: residual_and_back(): pl.pallas_call(kernel, out_shape=[jax.ShapeDtypeStruct((label_blocks, doc...]
    psum x1 -> x0, waiting for transfers between devices: 56.9 us -> none  [on_device(): lax.psum(column_sum.astype(jnp.bfloat16), 'label').astype(jnp.float32)]
    dot_general x5 -> x4, matrix products: 50.1 us -> 2.37 us  [product(): return jnp.einsum('dk,kbc->bdc', left, right, preferred_element_type=F32)]
  transfers between devices with their start and end apart: 3 -> 52, of which waited for: 3 -> 31; matrix products, arithmetic and copies ran while one was open for 5% -> 6% of each run, Pallas kernels for 0% -> 20%
where the time goes in v1:
time: 333 us; the launch traced here: 332 us
  waiting for transfers between devices  157 us (47%)
  starting transfers between devices  76.7 us (23%)
  Pallas kernels  69.7 us (21%)
  local copies, waits for them, and re-layouts  20.2 us (6%)
  other arithmetic  5.21 us (2%)
    ppermute x33, waiting for transfers between devices, ring_shift(): return lax.ppermute(x, 'label', pairs)  92.5 us
    ppermute x12, waiting for transfers between devices, feat_exchange(): lax.ppermute(x, 'feat', [(i, i ^ flip) for i in range(lax.axis_size('feat...  62.6 us
    ppermute x33, starting transfers between devices, ring_shift(): return lax.ppermute(x, 'label', pairs)  61.7 us
    pallas_call x2, Pallas kernels, residual_and_back(): pl.pallas_call(kernel, out_shape=[jax.ShapeDtypeStruct((label_blocks, doc...  39.4 us
    ppermute x12, starting transfers between devices, feat_exchange(): lax.ppermute(x, 'feat', [(i, i ^ flip) for i in range(lax.axis_size('feat...  14.2 us
    unnamed x75, local copies, waits for them, and re-layouts  13.7 us
    pallas_call x1, Pallas kernels, block_weight_grad(): pl.pallas_call(kernel, out_shape=jax.ShapeDtypeStruct((label_blocks * slo...  12.7 us
    pallas_call x2, Pallas kernels, select_blocks(): pl.pallas_call(kernel, out_shape=[jax.ShapeDtypeStruct((cap, docs, blk),...  7.09 us
  transfers between devices with their start and end apart: 52, of which 31 were waited for; matrix products, arithmetic and copies ran while one was open for 6% of the time, Pallas kernels for 20%

profile of v1, /device:TPU:0, one launch (start us, length us, event | category | flops | bytes accessed | tf_op | source)
XLA Modules:
  0.0 332.2 jit_solution(3664963144533918307)
XLA Ops:
  0.6 5.1 %collective-permute-start.3 = (bf16[160,128]{1,0:T(8,128)(2,1)}, bf16[160,128]{1,0:T(8,128)(2,1)S(1)}, u32[]{:S(2)}, u32[]{:S(2)}) collective-permute-start(bf16[160,128]{1,0:T(8,128)(2,1)} %documents_ref.1), channel_id=1, source_target_pairs={{0,6},{1,7},{2,0},{3,1},{4,2},{5,3},{6,4},{7,5},{8,14},{9,15},{10,... | collective-permute-start | bytes 122888 | tf_op jit(solution)/shard_map/ppermute | solution.py:28
  5.8 1.2 constant_dynamic-slice_fusion
  8.0 3.8 %collective-permute-start.6 = (bf16[64,2048]{0,1:T(8,128)(2,1)}, bf16[64,2048]{0,1:T(8,128)(2,1)}, u32[]{:S(2)}, u32[]{:S(2)}) collective-permute-start(bf16[64,2048]{0,1:T(8,128)(2,1)} %copy.41), channel_id=1, source_target_pairs={{0,6},{1,7},{2,0},{3,1},{4,2},{5,3},{6,4},{7,5},{8,14},{9,15},{10,... | collective-permute-start | bytes 786440 | tf_op jit(solution)/shard_map/ppermute | solution.py:28
  13.8 2.1 copy.37
  17.6 4.4 %collective-permute-start.8 = (bf16[160,128]{1,0:T(8,128)(2,1)S(1)}, bf16[160,128]{1,0:T(8,128)(2,1)S(1)}, u32[]{:S(2)}, u32[]{:S(2)}) collective-permute-start(bf16[160,128]{1,0:T(8,128)(2,1)S(1)} %copy-done.23), channel_id=1, source_target_pairs={{0,4},{1,5},{2,6},{3,7},{4,0},{5,1},{6,2},{7,3},{8,12},{9,13},{10,... | collective-permute-start | bytes 122888 | tf_op jit(solution)/shard_map/ppermute | solution.py:28
  22.1 2.4 collective-permute-done.6
  24.4 4.3 %collective-permute-start.2 = (bf16[128,2048]{0,1:T(8,128)(2,1)S(1)}, bf16[128,2048]{0,1:T(8,128)(2,1)S(1)}, u32[]{:S(2)}, u32[]{:S(2)}) collective-permute-start(bf16[128,2048]{0,1:T(8,128)(2,1)S(1)} %copy.38), channel_id=1, source_target_pairs={{0,6},{1,7},{2,0},{3,1},{4,2},{5,3},{6,4},{7,5},{8,14},{9,15},{10,... | collective-permute-start | bytes 1572872 | tf_op jit(solution)/shard_map/ppermute | solution.py:28
  28.7 7.5 %collective-permute-done.4 = bf16[64,2048]{0,1:T(8,128)(2,1)} collective-permute-done((bf16[64,2048]{0,1:T(8,128)(2,1)}, bf16[64,2048]{0,1:T(8,128)(2,1)}, u32[]{:S(2)}, u32[]{:S(2)}) %collective-permute-start.4) | collective-permute-done | bytes 262176 | tf_op jit(solution)/shard_map/ppermute | solution.py:28
  36.2 2.1 collective-permute-start.7
  38.4 9.0 %collective-permute-done = bf16[128,2048]{0,1:T(8,128)(2,1)} collective-permute-done((bf16[128,2048]{0,1:T(8,128)(2,1)}, bf16[128,2048]{0,1:T(8,128)(2,1)}, u32[]{:S(2)}, u32[]{:S(2)}) %collective-permute-start) | collective-permute-done | bytes 524320 | tf_op jit(solution)/shard_map/ppermute | solution.py:28
  47.4 2.0 collective-permute-start.5
  49.4 1.4 convolution_add_fusion.1
  50.8 19.5 %collective-permute-done.7 = bf16[64,2048]{0,1:T(8,128)(2,1)S(1)} collective-permute-done((bf16[64,2048]{0,1:T(8,128)(2,1)}, bf16[64,2048]{0,1:T(8,128)(2,1)S(1)}, u32[]{:S(2)}, u32[]{:S(2)}) %collective-permute-start.7) | collective-permute-done | bytes 262176 | tf_op jit(solution)/shard_map/ppermute | solution.py:28
  70.3 10.2 %collective-permute-done.5 = bf16[64,2048]{0,1:T(8,128)(2,1)S(1)} collective-permute-done((bf16[64,2048]{0,1:T(8,128)(2,1)}, bf16[64,2048]{0,1:T(8,128)(2,1)S(1)}, u32[]{:S(2)}, u32[]{:S(2)}) %collective-permute-start.5) | collective-permute-done | bytes 262176 | tf_op jit(solution)/shard_map/ppermute | solution.py:28
  82.1 1.6 collective-permute-done.9
  83.9 3.4 %collective-permute-start.26 = (bf16[8,80,128]{2,1,0:T(8,128)(2,1)S(1)}, bf16[8,80,128]{2,1,0:T(8,128)(2,1)S(1)}, u32[]{:S(2)}, u32[]{:S(2)}) collective-permute-start(bf16[8,80,128]{2,1,0:T(8,128)(2,1)S(1)} %get-tuple-element.77), channel_id=1, source_target_pairs={{0,6},{1,7},{2,0},{3,1},{4,2},{5,3},{6,4},{7,5},{8,14},{9,15},{10,... | collective-permute-start | bytes 491528 | tf_op jit(solution)/shard_map/ppermute | solution.py:28
  87.5 4.4 %collective-permute-done.26 = bf16[8,80,128]{2,1,0:T(8,128)(2,1)S(1)} collective-permute-done((bf16[8,80,128]{2,1,0:T(8,128)(2,1)S(1)}, bf16[8,80,128]{2,1,0:T(8,128)(2,1)S(1)}, u32[]{:S(2)}, u32[]{:S(2)}) %collective-permute-start.26) | collective-permute-done | bytes 163872 | tf_op jit(solution)/shard_map/ppermute | solution.py:28
  91.9 4.3 %collective-permute-start.29 = (bf16[4,80,128]{2,1,0:T(8,128)(2,1)S(1)}, bf16[4,80,128]{2,1,0:T(8,128)(2,1)S(1)}, u32[]{:S(2)}, u32[]{:S(2)}) collective-permute-start(bf16[4,80,128]{2,1,0:T(8,128)(2,1)S(1)} %slice.196), channel_id=1, source_target_pairs={{0,6},{1,7},{2,0},{3,1},{4,2},{5,3},{6,4},{7,5},{8,14},{9,15},{10,... | collective-permute-start | bytes 245768 | tf_op jit(solution)/shard_map/ppermute | solution.py:28
  97.1 5.4 %collective-permute-done.28 = bf16[4,80,128]{2,1,0:T(8,128)(2,1)S(1)} collective-permute-done((bf16[4,80,128]{2,1,0:T(8,128)(2,1)S(1)}, bf16[4,80,128]{2,1,0:T(8,128)(2,1)S(1)}, u32[]{:S(2)}, u32[]{:S(2)}) %collective-permute-start.28) | collective-permute-done | bytes 81952 | tf_op jit(solution)/shard_map/ppermute | solution.py:28
  102.8 2.0 collective-permute-start.11
  105.7 7.2 %collective-permute-done.10 = bf16[8,80,128]{2,1,0:T(8,128)(2,1)S(1)} collective-permute-done((bf16[8,80,128]{2,1,0:T(8,128)(2,1)S(1)}, bf16[8,80,128]{2,1,0:T(8,128)(2,1)S(1)}, u32[]{:S(2)}, u32[]{:S(2)}) %collective-permute-start.10) | collective-permute-done | bytes 163872 | tf_op jit(solution)/shard_map/ppermute | solution.py:28
  112.9 2.2 collective-permute-start.12
  115.1 4.2 %collective-permute-done.12 = bf16[4,80,128]{2,1,0:T(8,128)(2,1)S(1)} collective-permute-done((bf16[4,80,128]{2,1,0:T(8,128)(2,1)S(1)}, bf16[4,80,128]{2,1,0:T(8,128)(2,1)S(1)}, u32[]{:S(2)}, u32[]{:S(2)}) %collective-permute-start.12) | collective-permute-done | bytes 81952 | tf_op jit(solution)/shard_map/ppermute | solution.py:28
  120.2 3.5 %select_blocks.3 = (bf16[24,80,128]{2,1,0:T(8,128)(2,1)}, bf16[24,80,128]{2,1,0:T(8,128)(2,1)}, bf16[24,80,128]{2,1,0:T(8,128)(2,1)}, bf16[24,80,128]{2,1,0:T(8,128)(2,1)}) custom-call(s32[96]{0:T(128)} %reshape.202.index_ref, bf16[32,80,128]{2,1,0:T(8,128)(2,1)} %copy-done.12, bf16[32,80,128]{2,1,0:T(8,128)(2,1)} %copy-done.15), custom_call_target="tpu_custom_call" | custom-call | tf_op jit(solution)/shard_map/select_blocks/pallas_call | solution.py:102
  123.8 1.6 collective-permute-start.31
  125.3 1.5 collective-permute-start.32
  129.0 9.2 %collective-permute-done.31.refs_1_.refs_7_ = bf16[24,80,128]{2,1,0:T(8,128)(2,1)S(1)} collective-permute-done((bf16[24,80,128]{2,1,0:T(8,128)(2,1)}, bf16[24,80,128]{2,1,0:T(8,128)(2,1)S(1)}, u32[]{:S(2)}, u32[]{:S(2)}) %collective-permute-start.31) | collective-permute-done | bytes 491552 | tf_op jit(solution)/shard_map/ppermute | solution.py:37
  138.2 9.4 %collective-permute-done.32.refs_2_.refs_8_ = bf16[24,80,128]{2,1,0:T(8,128)(2,1)S(1)} collective-permute-done((bf16[24,80,128]{2,1,0:T(8,128)(2,1)}, bf16[24,80,128]{2,1,0:T(8,128)(2,1)S(1)}, u32[]{:S(2)}, u32[]{:S(2)}) %collective-permute-start.32) | collective-permute-done | bytes 491552 | tf_op jit(solution)/shard_map/ppermute | solution.py:37
  148.5 19.7 %residual_and_back.3 = (bf16[24,80,128]{2,1,0:T(8,128)(2,1)}, bf16[24,80,128]{2,1,0:T(8,128)(2,1)}, bf16[24,80,128]{2,1,0:T(8,128)(2,1)}, bf16[24,80,128]{2,1,0:T(8,128)(2,1)}, bf16[24,80,128]{2,1,0:T(8,128)(2,1)}) custom-call(s32[384]{0:T(512)} %copy-done.25, s32[384]{0:T(512)} %select_reduce_fusion.order_ref, s32[1]{0:T(128)} %bitcast.18.first_ref, ...), custom_call_target="tpu_custom_call" | custom-call | tf_op jit(solution)/shard_map/residual_and_back/pallas_call | solution.py:201
  168.2 1.1 collective-permute-start.34
  170.3 1.5 collective-permute-start.36
  172.6 3.5 %select_blocks.2 = (bf16[24,80,128]{2,1,0:T(8,128)(2,1)}, bf16[24,80,128]{2,1,0:T(8,128)(2,1)}, bf16[24,80,128]{2,1,0:T(8,128)(2,1)}, bf16[24,80,128]{2,1,0:T(8,128)(2,1)}) custom-call(s32[96]{0:T(128)} %reshape.202.index_ref, bf16[32,80,128]{2,1,0:T(8,128)(2,1)} %copy-done.11, bf16[32,80,128]{2,1,0:T(8,128)(2,1)} %copy-done.16), custom_call_target="tpu_custom_call" | custom-call | tf_op jit(solution)/shard_map/select_blocks/pallas_call | solution.py:102
  176.1 1.1 collective-permute-start.15
  178.2 4.3 %collective-permute-done.34.refs_1_ = bf16[24,80,128]{2,1,0:T(8,128)(2,1)S(1)} collective-permute-done((bf16[24,80,128]{2,1,0:T(8,128)(2,1)}, bf16[24,80,128]{2,1,0:T(8,128)(2,1)S(1)}, u32[]{:S(2)}, u32[]{:S(2)}) %collective-permute-start.34) | collective-permute-done | bytes 491552 | tf_op jit(solution)/shard_map/ppermute | solution.py:37
  183.3 1.5 collective-permute-start.17
  184.8 9.4 %collective-permute-done.35.refs_2_ = bf16[24,80,128]{2,1,0:T(8,128)(2,1)} collective-permute-done((bf16[24,80,128]{2,1,0:T(8,128)(2,1)}, bf16[24,80,128]{2,1,0:T(8,128)(2,1)}, u32[]{:S(2)}, u32[]{:S(2)}) %collective-permute-start.35) | collective-permute-done | bytes 491552 | tf_op jit(solution)/shard_map/ppermute | solution.py:37
  194.2 3.3 add_blocks.3
  198.2 5.4 %collective-permute-done.15.refs_1_.refs_3_ = bf16[24,80,128]{2,1,0:T(8,128)(2,1)S(1)} collective-permute-done((bf16[24,80,128]{2,1,0:T(8,128)(2,1)}, bf16[24,80,128]{2,1,0:T(8,128)(2,1)S(1)}, u32[]{:S(2)}, u32[]{:S(2)}) %collective-permute-start.15) | collective-permute-done | bytes 491552 | tf_op jit(solution)/shard_map/ppermute | solution.py:37
  203.7 8.0 %collective-permute-done.16.refs_2_.refs_4_ = bf16[24,80,128]{2,1,0:T(8,128)(2,1)S(1)} collective-permute-done((bf16[24,80,128]{2,1,0:T(8,128)(2,1)}, bf16[24,80,128]{2,1,0:T(8,128)(2,1)S(1)}, u32[]{:S(2)}, u32[]{:S(2)}) %collective-permute-start.16) | collective-permute-done | bytes 491552 | tf_op jit(solution)/shard_map/ppermute | solution.py:37
  212.7 19.8 %residual_and_back.2 = (bf16[24,80,128]{2,1,0:T(8,128)(2,1)}, bf16[24,80,128]{2,1,0:T(8,128)(2,1)}, bf16[24,80,128]{2,1,0:T(8,128)(2,1)}, bf16[24,80,128]{2,1,0:T(8,128)(2,1)}, bf16[24,80,128]{2,1,0:T(8,128)(2,1)}) custom-call(s32[384]{0:T(512)} %copy-done.25, s32[384]{0:T(512)} %select_reduce_fusion.order_ref, s32[1]{0:T(128)} %bitcast.18.first_ref, ...), custom_call_target="tpu_custom_call" | custom-call | tf_op jit(solution)/shard_map/residual_and_back/pallas_call | solution.py:201
  234.1 1.9 collective-permute-start.20
  236.0 10.0 %collective-permute-done.18.refs_1_ = bf16[24,80,128]{2,1,0:T(8,128)(2,1)S(1)} collective-permute-done((bf16[24,80,128]{2,1,0:T(8,128)(2,1)}, bf16[24,80,128]{2,1,0:T(8,128)(2,1)S(1)}, u32[]{:S(2)}, u32[]{:S(2)}) %collective-permute-start.18) | collective-permute-done | bytes 491552 | tf_op jit(solution)/shard_map/ppermute | solution.py:37
  245.9 6.8 %collective-permute-done.19.refs_2_ = bf16[24,80,128]{2,1,0:T(8,128)(2,1)S(1)} collective-permute-done((bf16[24,80,128]{2,1,0:T(8,128)(2,1)}, bf16[24,80,128]{2,1,0:T(8,128)(2,1)S(1)}, u32[]{:S(2)}, u32[]{:S(2)}) %collective-permute-start.19) | collective-permute-done | bytes 491552 | tf_op jit(solution)/shard_map/ppermute | solution.py:37
  253.8 3.3 %add_blocks.2 = (bf16[32,80,128]{2,1,0:T(8,128)(2,1)}, bf16[32,80,128]{2,1,0:T(8,128)(2,1)}) custom-call(s32[96]{0:T(128)} %reshape.202.index_ref, bf16[24,80,128]{2,1,0:T(8,128)(2,1)} %get-tuple-element.28.refs_0_, bf16[24,80,128]{2,1,0:T(8,128)(2,1)} %copy-done.20, bf16[24,80,128]{2,1,0:T(8,128)(2,1)} %copy-done.21, bf16[24,80,128]{2,1,0:T(8,128)(2,1)} %copy-done.22), custom_call_target="tpu_custom_call" | custom-call | tf_op jit(solution)/shard_map/add_blocks/pallas_call | solution.py:134
  257.5 3.8 %collective-permute-start.40 = (bf16[4,80,128]{2,1,0:T(8,128)(2,1)S(1)}, bf16[4,80,128]{2,1,0:T(8,128)(2,1)S(1)}, u32[]{:S(2)}, u32[]{:S(2)}) collective-permute-start(bf16[4,80,128]{2,1,0:T(8,128)(2,1)S(1)} %get-tuple-element.66), channel_id=1, source_target_pairs={{0,6},{1,7},{2,0},{3,1},{4,2},{5,3},{6,4},{7,5},{8,14},{9,15},{10,... | collective-permute-start | bytes 245768 | tf_op jit(solution)/shard_map/ppermute | solution.py:28
  261.5 1.1 collective-permute-start.22
  262.6 2.8 collective-permute-start.24
  266.0 2.4 collective-permute-start.41
  269.6 2.8 collective-permute-start.25
  272.6 1.7 collective-permute-done.41
  274.3 4.4 %collective-permute-done.39 = bf16[8,80,128]{2,1,0:T(8,128)(2,1)S(1)} collective-permute-done((bf16[8,80,128]{2,1,0:T(8,128)(2,1)S(1)}, bf16[8,80,128]{2,1,0:T(8,128)(2,1)S(1)}, u32[]{:S(2)}, u32[]{:S(2)}) %collective-permute-start.39) | collective-permute-done | bytes 163872 | tf_op jit(solution)/shard_map/ppermute | solution.py:28
  278.7 1.5 collective-permute-done.25
  280.2 4.2 %collective-permute-done.23 = bf16[8,80,128]{2,1,0:T(8,128)(2,1)S(1)} collective-permute-done((bf16[8,80,128]{2,1,0:T(8,128)(2,1)S(1)}, bf16[8,80,128]{2,1,0:T(8,128)(2,1)S(1)}, u32[]{:S(2)}, u32[]{:S(2)}) %collective-permute-start.23) | collective-permute-done | bytes 163872 | tf_op jit(solution)/shard_map/ppermute | solution.py:28
  285.3 3.7 %collective-permute-start.43 = (bf16[8,80,128]{2,1,0:T(8,128)(2,1)S(1)}, bf16[8,80,128]{2,1,0:T(8,128)(2,1)S(1)}, u32[]{:S(2)}, u32[]{:S(2)}) collective-permute-start(bf16[8,80,128]{2,1,0:T(8,128)(2,1)S(1)} %get-tuple-element.47.refs_1_), channel_id=1, source_target_pairs={{0,6},{1,7},{2,0},{3,1},{4,2},{5,3},{6,4},{7,5},{8,14},{9,15},{10,... | collective-permute-start | bytes 491528 | tf_op jit(solution)/shard_map/ppermute | solution.py:28
  289.1 3.8 %collective-permute-start.42 = (bf16[8,80,128]{2,1,0:T(8,128)(2,1)S(1)}, bf16[8,80,128]{2,1,0:T(8,128)(2,1)S(1)}, u32[]{:S(2)}, u32[]{:S(2)}) collective-permute-start(bf16[8,80,128]{2,1,0:T(8,128)(2,1)S(1)} %get-tuple-element.76.refs_0_), channel_id=1, source_target_pairs={{0,6},{1,7},{2,0},{3,1},{4,2},{5,3},{6,4},{7,5},{8,14},{9,15},{10,... | collective-permute-start | bytes 491528 | tf_op jit(solution)/shard_map/ppermute | solution.py:28
  292.9 1.2 collective-permute-done.47.refs_7_
  294.1 1.1 collective-permute-start.48
  295.2 2.1 collective-permute-done.43.refs_3_
  298.1 3.2 collective-permute-done.44.refs_6_
  301.2 2.1 collective-permute-start.45
  303.5 2.2 collective-permute-start.46
  306.4 2.3 collective-permute-done.45
  312.5 12.7 %block_weight_grad.1 = bf16[384,128,128]{2,1,0:T(8,128)(2,1)} custom-call(s32[384]{0:T(512)} %select_reduce_fusion.order_ref, bf16[24,80,128]{2,1,0:T(8,128)(2,1)} %get-tuple-element.44.refs_0_, bf16[24,80,128]{2,1,0:T(8,128)(2,1)} %get-tuple-element.45.refs_1_, bf16[24,80,128]{2,1,0:T(8,128)(2,1)} %get-tuple-element.24.refs_0_.refs_2_, ...), custom_call_target="tpu_custom_call" | custom-call | tf_op jit(solution)/shard_map/block_weight_grad/pallas_call | solution.py:266
  328.4 3.9 %expand_weight_grad.1 = bf16[128,8192]{1,0:T(8,128)(2,1)} custom-call(s32[8]{0:T(128)} %stack.42.columns_ref, bf16[160,128]{1,0:T(8,128)(2,1)} %documents_ref.1, bf16[8,80,128]{2,1,0:T(8,128)(2,1)} %copy-done.14, bf16[8,80,128]{2,1,0:T(8,128)(2,1)} %copy-done.13, bf16[8,80,128]{2,1,0:T(8,128)(2,1)} %copy-done.10, bf16[8,80,128]{2,1,0:T(8,128)(2,1)} %copy-done.8, ...), custom_call_target="tpu_custom_call" | custom-call | tf_op jit(solution)/shard_map/expand_weight_grad/pallas_call | solution.py:302
  (182 shorter events, 32.4 us)
Async XLA Ops:
  0.6 80.5 %collective-permute-start.3 = (bf16[160,128]{1,0:T(8,128)(2,1)}, bf16[160,128]{1,0:T(8,128)(2,1)S(1)}, u32[]{:S(2)}, u32[]{:S(2)}) collective-permute-start(bf16[160,128]{1,0:T(8,128)(2,1)} %documents_ref.1), channel_id=1, source_target_pairs={{0,6},{1,7},{2,0},{3,1},{4,2},{5,3},{6,4},{7,5},{8,14},{9,15},{10,... | collective-permute-start | bytes 122888 | tf_op jit(solution)/shard_map/ppermute | solution.py:28
  5.8 11.9 %collective-permute-start.1 = (bf16[160,128]{1,0:T(8,128)(2,1)}, bf16[160,128]{1,0:T(8,128)(2,1)S(1)}, u32[]{:S(2)}, u32[]{:S(2)}) collective-permute-start(bf16[160,128]{1,0:T(8,128)(2,1)} %documents_ref.1), channel_id=1, source_target_pairs={{0,2},{1,3},{2,4},{3,5},{4,6},{5,7},{6,0},{7,1},{8,10},{9,11},{10,... | collective-permute-start | bytes 122888 | tf_op jit(solution)/shard_map/ppermute | solution.py:28
  8.0 16.5 %collective-permute-start.6 = (bf16[64,2048]{0,1:T(8,128)(2,1)}, bf16[64,2048]{0,1:T(8,128)(2,1)}, u32[]{:S(2)}, u32[]{:S(2)}) collective-permute-start(bf16[64,2048]{0,1:T(8,128)(2,1)} %copy.41), channel_id=1, source_target_pairs={{0,6},{1,7},{2,0},{3,1},{4,2},{5,3},{6,4},{7,5},{8,14},{9,15},{10,... | collective-permute-start | bytes 786440 | tf_op jit(solution)/shard_map/ppermute | solution.py:28
  12.8 23.4 %collective-permute-start.4 = (bf16[64,2048]{0,1:T(8,128)(2,1)}, bf16[64,2048]{0,1:T(8,128)(2,1)}, u32[]{:S(2)}, u32[]{:S(2)}) collective-permute-start(bf16[64,2048]{0,1:T(8,128)(2,1)} %copy.40), channel_id=1, source_target_pairs={{0,2},{1,3},{2,4},{3,5},{4,6},{5,7},{6,0},{7,1},{8,10},{9,11},{10,... | collective-permute-start | bytes 786440 | tf_op jit(solution)/shard_map/ppermute | solution.py:28
  15.8 31.6 %collective-permute-start = (bf16[128,2048]{0,1:T(8,128)(2,1)}, bf16[128,2048]{0,1:T(8,128)(2,1)}, u32[]{:S(2)}, u32[]{:S(2)}) collective-permute-start(bf16[128,2048]{0,1:T(8,128)(2,1)} %copy.37), channel_id=1, source_target_pairs={{0,2},{1,3},{2,4},{3,5},{4,6},{5,7},{6,0},{7,1},{8,10},{9,11},{10,... | collective-permute-start | bytes 1572872 | tf_op jit(solution)/shard_map/ppermute | solution.py:28
  17.6 63.1 %collective-permute-start.8 = (bf16[160,128]{1,0:T(8,128)(2,1)S(1)}, bf16[160,128]{1,0:T(8,128)(2,1)S(1)}, u32[]{:S(2)}, u32[]{:S(2)}) collective-permute-start(bf16[160,128]{1,0:T(8,128)(2,1)S(1)} %copy-done.23), channel_id=1, source_target_pairs={{0,4},{1,5},{2,6},{3,7},{4,0},{5,1},{6,2},{7,3},{8,12},{9,13},{10,... | collective-permute-start | bytes 122888 | tf_op jit(solution)/shard_map/ppermute | solution.py:28
  24.4 56.7 %collective-permute-start.2 = (bf16[128,2048]{0,1:T(8,128)(2,1)S(1)}, bf16[128,2048]{0,1:T(8,128)(2,1)S(1)}, u32[]{:S(2)}, u32[]{:S(2)}) collective-permute-start(bf16[128,2048]{0,1:T(8,128)(2,1)S(1)} %copy.38), channel_id=1, source_target_pairs={{0,6},{1,7},{2,0},{3,1},{4,2},{5,3},{6,4},{7,5},{8,14},{9,15},{10,... | collective-permute-start | bytes 1572872 | tf_op jit(solution)/shard_map/ppermute | solution.py:28
  36.2 34.1 %collective-permute-start.7 = (bf16[64,2048]{0,1:T(8,128)(2,1)}, bf16[64,2048]{0,1:T(8,128)(2,1)S(1)}, u32[]{:S(2)}, u32[]{:S(2)}) collective-permute-start(bf16[64,2048]{0,1:T(8,128)(2,1)} %collective-permute-done.6), channel_id=1, source_target_pairs={{0,6},{1,7},{2,0},{3,1},{4,2},{5,3},{6,4},{7,5},{8,14},{9,15},{10,... | collective-permute-start | bytes 786440 | tf_op jit(solution)/shard_map/ppermute | solution.py:28
  47.4 33.1 %collective-permute-start.5 = (bf16[64,2048]{0,1:T(8,128)(2,1)}, bf16[64,2048]{0,1:T(8,128)(2,1)S(1)}, u32[]{:S(2)}, u32[]{:S(2)}) collective-permute-start(bf16[64,2048]{0,1:T(8,128)(2,1)} %collective-permute-done.4), channel_id=1, source_target_pairs={{0,2},{1,3},{2,4},{3,5},{4,6},{5,7},{6,0},{7,1},{8,10},{9,11},{10,... | collective-permute-start | bytes 786440 | tf_op jit(solution)/shard_map/ppermute | solution.py:28
  81.5 2.2 collective-permute-start.9
  83.8 18.9 %copy-start.26 = (s32[160,8]{0,1:T(8,128)S(1)}, s32[160,8]{0,1:T(8,128)}, u32[]{:S(2)}) copy-start(s32[160,8]{0,1:T(8,128)} %param.9) | copy-start | bytes 15364
  83.9 8.0 %collective-permute-start.26 = (bf16[8,80,128]{2,1,0:T(8,128)(2,1)S(1)}, bf16[8,80,128]{2,1,0:T(8,128)(2,1)S(1)}, u32[]{:S(2)}, u32[]{:S(2)}) collective-permute-start(bf16[8,80,128]{2,1,0:T(8,128)(2,1)S(1)} %get-tuple-element.77), channel_id=1, source_target_pairs={{0,6},{1,7},{2,0},{3,1},{4,2},{5,3},{6,4},{7,5},{8,14},{9,15},{10,... | collective-permute-start | bytes 491528 | tf_op jit(solution)/shard_map/ppermute | solution.py:28
  87.2 8.9 %collective-permute-start.27 = (bf16[8,80,128]{2,1,0:T(8,128)(2,1)S(1)}, bf16[8,80,128]{2,1,0:T(8,128)(2,1)S(1)}, u32[]{:S(2)}, u32[]{:S(2)}) collective-permute-start(bf16[8,80,128]{2,1,0:T(8,128)(2,1)S(1)} %get-tuple-element.77), channel_id=1, source_target_pairs={{0,2},{1,3},{2,4},{3,5},{4,6},{5,7},{6,0},{7,1},{8,10},{9,11},{10,... | collective-permute-start | bytes 491528 | tf_op jit(solution)/shard_map/ppermute | solution.py:28
  87.5 40.0 %copy-start.25 = (s32[384]{0:T(512)}, s32[384]{0:T(512)S(1)}, u32[]{:S(2)}) copy-start(s32[384]{0:T(512)S(1)} %select_reduce_fusion.1.position_ref) | copy-start | bytes 4612
  91.9 10.6 %collective-permute-start.29 = (bf16[4,80,128]{2,1,0:T(8,128)(2,1)S(1)}, bf16[4,80,128]{2,1,0:T(8,128)(2,1)S(1)}, u32[]{:S(2)}, u32[]{:S(2)}) collective-permute-start(bf16[4,80,128]{2,1,0:T(8,128)(2,1)S(1)} %slice.196), channel_id=1, source_target_pairs={{0,6},{1,7},{2,0},{3,1},{4,2},{5,3},{6,4},{7,5},{8,14},{9,15},{10,... | collective-permute-start | bytes 245768 | tf_op jit(solution)/shard_map/ppermute | solution.py:28
  96.2 6.3 %collective-permute-start.28 = (bf16[4,80,128]{2,1,0:T(8,128)(2,1)S(1)}, bf16[4,80,128]{2,1,0:T(8,128)(2,1)S(1)}, u32[]{:S(2)}, u32[]{:S(2)}) collective-permute-start(bf16[4,80,128]{2,1,0:T(8,128)(2,1)S(1)} %slice.195), channel_id=1, source_target_pairs={{0,2},{1,3},{2,4},{3,5},{4,6},{5,7},{6,0},{7,1},{8,10},{9,11},{10,... | collective-permute-start | bytes 245768 | tf_op jit(solution)/shard_map/ppermute | solution.py:28
  102.6 16.8 %copy-start.12 = (bf16[32,80,128]{2,1,0:T(8,128)(2,1)}, bf16[32,80,128]{2,1,0:T(8,128)(2,1)S(1)}, u32[]{:S(2)}) copy-start(bf16[32,80,128]{2,1,0:T(8,128)(2,1)S(1)} %constant_dynamic-update-slice_fusion.5.refs_0_) | copy-start | bytes 1966084
  102.6 16.8 %collective-permute-start.30 = (bf16[32,80,128]{2,1,0:T(8,128)(2,1)S(1)}, bf16[32,80,128]{2,1,0:T(8,128)(2,1)S(1)}, u32[]{:S(2)}, u32[]{:S(2)}) collective-permute-start(bf16[32,80,128]{2,1,0:T(8,128)(2,1)S(1)} %constant_dynamic-update-slice_fusion.5.refs_0_), channel_id=1, source_target_pairs={{0,1},{1,0},{2,3},{3,2},{4,5},{5,4},{6,7},{7,6},{8,9},{9,8},{10,11... | collective-permute-start | bytes 1966088 | tf_op jit(solution)/shard_map/ppermute | solution.py:33
  102.7 10.1 %collective-permute-start.10 = (bf16[8,80,128]{2,1,0:T(8,128)(2,1)S(1)}, bf16[8,80,128]{2,1,0:T(8,128)(2,1)S(1)}, u32[]{:S(2)}, u32[]{:S(2)}) collective-permute-start(bf16[8,80,128]{2,1,0:T(8,128)(2,1)S(1)} %get-tuple-element.80), channel_id=1, source_target_pairs={{0,6},{1,7},{2,0},{3,1},{4,2},{5,3},{6,4},{7,5},{8,14},{9,15},{10,... | collective-permute-start | bytes 491528 | tf_op jit(solution)/shard_map/ppermute | solution.py:28
  102.8 10.1 %collective-permute-start.11 = (bf16[8,80,128]{2,1,0:T(8,128)(2,1)S(1)}, bf16[8,80,128]{2,1,0:T(8,128)(2,1)S(1)}, u32[]{:S(2)}, u32[]{:S(2)}) collective-permute-start(bf16[8,80,128]{2,1,0:T(8,128)(2,1)S(1)} %get-tuple-element.80), channel_id=1, source_target_pairs={{0,2},{1,3},{2,4},{3,5},{4,6},{5,7},{6,0},{7,1},{8,10},{9,11},{10,... | collective-permute-start | bytes 491528 | tf_op jit(solution)/shard_map/ppermute | solution.py:28
  112.8 14.5 %collective-permute-start.13 = (bf16[4,80,128]{2,1,0:T(8,128)(2,1)S(1)}, bf16[4,80,128]{2,1,0:T(8,128)(2,1)S(1)}, u32[]{:S(2)}, u32[]{:S(2)}) collective-permute-start(bf16[4,80,128]{2,1,0:T(8,128)(2,1)S(1)} %slice.186), channel_id=1, source_target_pairs={{0,6},{1,7},{2,0},{3,1},{4,2},{5,3},{6,4},{7,5},{8,14},{9,15},{10,... | collective-permute-start | bytes 245768 | tf_op jit(solution)/shard_map/ppermute | solution.py:28
  112.9 6.5 %collective-permute-start.12 = (bf16[4,80,128]{2,1,0:T(8,128)(2,1)S(1)}, bf16[4,80,128]{2,1,0:T(8,128)(2,1)S(1)}, u32[]{:S(2)}, u32[]{:S(2)}) collective-permute-start(bf16[4,80,128]{2,1,0:T(8,128)(2,1)S(1)} %slice.185), channel_id=1, source_target_pairs={{0,2},{1,3},{2,4},{3,5},{4,6},{5,7},{6,0},{7,1},{8,10},{9,11},{10,... | collective-permute-start | bytes 245768 | tf_op jit(solution)/shard_map/ppermute | solution.py:28
  123.8 14.4 %collective-permute-start.31 = (bf16[24,80,128]{2,1,0:T(8,128)(2,1)}, bf16[24,80,128]{2,1,0:T(8,128)(2,1)S(1)}, u32[]{:S(2)}, u32[]{:S(2)}) collective-permute-start(bf16[24,80,128]{2,1,0:T(8,128)(2,1)} %get-tuple-element.35), channel_id=1, source_target_pairs={{0,8},{8,0},{16,24},{24,16},{1,9},{9,1},{17,25},{25,17},{2,10},{10... | collective-permute-start | bytes 1474568 | tf_op jit(solution)/shard_map/ppermute | solution.py:37
  125.3 22.2 %collective-permute-start.32 = (bf16[24,80,128]{2,1,0:T(8,128)(2,1)}, bf16[24,80,128]{2,1,0:T(8,128)(2,1)S(1)}, u32[]{:S(2)}, u32[]{:S(2)}) collective-permute-start(bf16[24,80,128]{2,1,0:T(8,128)(2,1)} %get-tuple-element.36), channel_id=1, source_target_pairs={{0,16},{8,24},{16,0},{24,8},{1,17},{9,25},{17,1},{25,9},{2,18},{10... | collective-permute-start | bytes 1474568 | tf_op jit(solution)/shard_map/ppermute | solution.py:37
  126.9 20.7 %collective-permute-start.33 = (bf16[24,80,128]{2,1,0:T(8,128)(2,1)}, bf16[24,80,128]{2,1,0:T(8,128)(2,1)S(1)}, u32[]{:S(2)}, u32[]{:S(2)}) collective-permute-start(bf16[24,80,128]{2,1,0:T(8,128)(2,1)} %get-tuple-element.37), channel_id=1, source_target_pairs={{0,24},{8,16},{16,8},{24,0},{1,25},{9,17},{17,9},{25,1},{2,26},{10... | collective-permute-start | bytes 1474568 | tf_op jit(solution)/shard_map/ppermute | solution.py:37
  127.4 40.8 %copy-start.11 = (bf16[32,80,128]{2,1,0:T(8,128)(2,1)}, bf16[32,80,128]{2,1,0:T(8,128)(2,1)S(1)}, u32[]{:S(2)}) copy-start(bf16[32,80,128]{2,1,0:T(8,128)(2,1)S(1)} %constant_dynamic-update-slice_fusion.refs_0_) | copy-start | bytes 1966084
  127.4 44.3 %collective-permute-start.14 = (bf16[32,80,128]{2,1,0:T(8,128)(2,1)S(1)}, bf16[32,80,128]{2,1,0:T(8,128)(2,1)S(1)}, u32[]{:S(2)}, u32[]{:S(2)}) collective-permute-start(bf16[32,80,128]{2,1,0:T(8,128)(2,1)S(1)} %constant_dynamic-update-slice_fusion.refs_0_), channel_id=1, source_target_pairs={{0,1},{1,0},{2,3},{3,2},{4,5},{5,4},{6,7},{7,6},{8,9},{9,8},{10,11... | collective-permute-start | bytes 1966088 | tf_op jit(solution)/shard_map/ppermute | solution.py:33
  138.2 9.4 %copy-start.1 = (bf16[24,80,128]{2,1,0:T(8,128)(2,1)}, bf16[24,80,128]{2,1,0:T(8,128)(2,1)S(1)}, u32[]{:S(2)}) copy-start(bf16[24,80,128]{2,1,0:T(8,128)(2,1)S(1)} %collective-permute-done.31.refs_1_.refs_7_) | copy-start | bytes 1474564
  168.2 14.4 %collective-permute-start.34 = (bf16[24,80,128]{2,1,0:T(8,128)(2,1)}, bf16[24,80,128]{2,1,0:T(8,128)(2,1)S(1)}, u32[]{:S(2)}, u32[]{:S(2)}) collective-permute-start(bf16[24,80,128]{2,1,0:T(8,128)(2,1)} %get-tuple-element.39), channel_id=1, source_target_pairs={{0,8},{8,0},{16,24},{24,16},{1,9},{9,1},{17,25},{25,17},{2,10},{10... | collective-permute-start | bytes 1474568 | tf_op jit(solution)/shard_map/ppermute | solution.py:37
  169.3 24.9 %collective-permute-start.35 = (bf16[24,80,128]{2,1,0:T(8,128)(2,1)}, bf16[24,80,128]{2,1,0:T(8,128)(2,1)}, u32[]{:S(2)}, u32[]{:S(2)}) collective-permute-start(bf16[24,80,128]{2,1,0:T(8,128)(2,1)} %get-tuple-element.40), channel_id=1, source_target_pairs={{0,16},{8,24},{16,0},{24,8},{1,17},{9,25},{17,1},{25,9},{2,18},{10... | collective-permute-start | bytes 1474568 | tf_op jit(solution)/shard_map/ppermute | solution.py:37
  170.3 24.0 %collective-permute-start.36 = (bf16[24,80,128]{2,1,0:T(8,128)(2,1)}, bf16[24,80,128]{2,1,0:T(8,128)(2,1)}, u32[]{:S(2)}, u32[]{:S(2)}) collective-permute-start(bf16[24,80,128]{2,1,0:T(8,128)(2,1)} %get-tuple-element.41), channel_id=1, source_target_pairs={{0,24},{8,16},{16,8},{24,0},{1,25},{9,17},{17,9},{25,1},{2,26},{10... | collective-permute-start | bytes 1474568 | tf_op jit(solution)/shard_map/ppermute | solution.py:37
  176.1 27.5 %collective-permute-start.15 = (bf16[24,80,128]{2,1,0:T(8,128)(2,1)}, bf16[24,80,128]{2,1,0:T(8,128)(2,1)S(1)}, u32[]{:S(2)}, u32[]{:S(2)}) collective-permute-start(bf16[24,80,128]{2,1,0:T(8,128)(2,1)} %get-tuple-element.25), channel_id=1, source_target_pairs={{0,8},{8,0},{16,24},{24,16},{1,9},{9,1},{17,25},{25,17},{2,10},{10... | collective-permute-start | bytes 1474568 | tf_op jit(solution)/shard_map/ppermute | solution.py:37
  177.2 34.4 %collective-permute-start.16 = (bf16[24,80,128]{2,1,0:T(8,128)(2,1)}, bf16[24,80,128]{2,1,0:T(8,128)(2,1)S(1)}, u32[]{:S(2)}, u32[]{:S(2)}) collective-permute-start(bf16[24,80,128]{2,1,0:T(8,128)(2,1)} %get-tuple-element.26), channel_id=1, source_target_pairs={{0,16},{8,24},{16,0},{24,8},{1,17},{9,25},{17,1},{25,9},{2,18},{10... | collective-permute-start | bytes 1474568 | tf_op jit(solution)/shard_map/ppermute | solution.py:37
  183.3 28.3 %collective-permute-start.17 = (bf16[24,80,128]{2,1,0:T(8,128)(2,1)}, bf16[24,80,128]{2,1,0:T(8,128)(2,1)S(1)}, u32[]{:S(2)}, u32[]{:S(2)}) collective-permute-start(bf16[24,80,128]{2,1,0:T(8,128)(2,1)} %get-tuple-element.27), channel_id=1, source_target_pairs={{0,24},{8,16},{16,8},{24,0},{1,25},{9,17},{17,9},{25,1},{2,26},{10... | collective-permute-start | bytes 1474568 | tf_op jit(solution)/shard_map/ppermute | solution.py:37
  197.5 59.6 %collective-permute-start.37 = (bf16[32,80,128]{2,1,0:T(8,128)(2,1)}, bf16[32,80,128]{2,1,0:T(8,128)(2,1)S(1)}, u32[]{:S(2)}, u32[]{:S(2)}) collective-permute-start(bf16[32,80,128]{2,1,0:T(8,128)(2,1)} %get-tuple-element.43), channel_id=1, source_target_pairs={{0,1},{1,0},{2,3},{3,2},{4,5},{5,4},{6,7},{7,6},{8,9},{9,8},{10,11... | collective-permute-start | bytes 1966088 | tf_op jit(solution)/shard_map/ppermute | solution.py:33
  232.4 24.7 %copy-start.17 = (bf16[32,80,128]{2,1,0:T(8,128)(2,1)S(1)}, bf16[32,80,128]{2,1,0:T(8,128)(2,1)}, u32[]{:S(2)}) copy-start(bf16[32,80,128]{2,1,0:T(8,128)(2,1)} %get-tuple-element.42) | copy-start | bytes 1966084
  232.4 13.5 %collective-permute-start.18 = (bf16[24,80,128]{2,1,0:T(8,128)(2,1)}, bf16[24,80,128]{2,1,0:T(8,128)(2,1)S(1)}, u32[]{:S(2)}, u32[]{:S(2)}) collective-permute-start(bf16[24,80,128]{2,1,0:T(8,128)(2,1)} %get-tuple-element.29), channel_id=1, source_target_pairs={{0,8},{8,0},{16,24},{24,16},{1,9},{9,1},{17,25},{25,17},{2,10},{10... | collective-permute-start | bytes 1474568 | tf_op jit(solution)/shard_map/ppermute | solution.py:37
  233.1 19.7 %collective-permute-start.19 = (bf16[24,80,128]{2,1,0:T(8,128)(2,1)}, bf16[24,80,128]{2,1,0:T(8,128)(2,1)S(1)}, u32[]{:S(2)}, u32[]{:S(2)}) collective-permute-start(bf16[24,80,128]{2,1,0:T(8,128)(2,1)} %get-tuple-element.30), channel_id=1, source_target_pairs={{0,16},{8,24},{16,0},{24,8},{1,17},{9,25},{17,1},{25,9},{2,18},{10... | collective-permute-start | bytes 1474568 | tf_op jit(solution)/shard_map/ppermute | solution.py:37
  234.1 18.7 %collective-permute-start.20 = (bf16[24,80,128]{2,1,0:T(8,128)(2,1)}, bf16[24,80,128]{2,1,0:T(8,128)(2,1)S(1)}, u32[]{:S(2)}, u32[]{:S(2)}) collective-permute-start(bf16[24,80,128]{2,1,0:T(8,128)(2,1)} %get-tuple-element.31), channel_id=1, source_target_pairs={{0,24},{8,16},{16,8},{24,0},{1,25},{9,17},{17,9},{25,1},{2,26},{10... | collective-permute-start | bytes 1474568 | tf_op jit(solution)/shard_map/ppermute | solution.py:37
  257.1 4.1 %collective-permute-start.21 = (bf16[32,80,128]{2,1,0:T(8,128)(2,1)}, bf16[32,80,128]{2,1,0:T(8,128)(2,1)S(1)}, u32[]{:S(2)}, u32[]{:S(2)}) collective-permute-start(bf16[32,80,128]{2,1,0:T(8,128)(2,1)} %get-tuple-element.33), channel_id=1, source_target_pairs={{0,1},{1,0},{2,3},{3,2},{4,5},{5,4},{6,7},{7,6},{8,9},{9,8},{10,11... | collective-permute-start | bytes 1966088 | tf_op jit(solution)/shard_map/ppermute | solution.py:33
  257.4 8.0 %collective-permute-start.38 = (bf16[4,80,128]{2,1,0:T(8,128)(2,1)S(1)}, bf16[4,80,128]{2,1,0:T(8,128)(2,1)S(1)}, u32[]{:S(2)}, u32[]{:S(2)}) collective-permute-start(bf16[4,80,128]{2,1,0:T(8,128)(2,1)S(1)} %get-tuple-element.65), channel_id=1, source_target_pairs={{0,2},{1,3},{2,4},{3,5},{4,6},{5,7},{6,0},{7,1},{8,10},{9,11},{10,... | collective-permute-start | bytes 245768 | tf_op jit(solution)/shard_map/ppermute | solution.py:28
  257.5 8.4 %collective-permute-start.40 = (bf16[4,80,128]{2,1,0:T(8,128)(2,1)S(1)}, bf16[4,80,128]{2,1,0:T(8,128)(2,1)S(1)}, u32[]{:S(2)}, u32[]{:S(2)}) collective-permute-start(bf16[4,80,128]{2,1,0:T(8,128)(2,1)S(1)} %get-tuple-element.66), channel_id=1, source_target_pairs={{0,6},{1,7},{2,0},{3,1},{4,2},{5,3},{6,4},{7,5},{8,14},{9,15},{10,... | collective-permute-start | bytes 245768 | tf_op jit(solution)/shard_map/ppermute | solution.py:28
  261.5 7.2 %collective-permute-start.22 = (bf16[4,80,128]{2,1,0:T(8,128)(2,1)S(1)}, bf16[4,80,128]{2,1,0:T(8,128)(2,1)S(1)}, u32[]{:S(2)}, u32[]{:S(2)}) collective-permute-start(bf16[4,80,128]{2,1,0:T(8,128)(2,1)S(1)} %get-tuple-element.71), channel_id=1, source_target_pairs={{0,2},{1,3},{2,4},{3,5},{4,6},{5,7},{6,0},{7,1},{8,10},{9,11},{10,... | collective-permute-start | bytes 245768 | tf_op jit(solution)/shard_map/ppermute | solution.py:28
  262.6 6.9 %collective-permute-start.24 = (bf16[4,80,128]{2,1,0:T(8,128)(2,1)S(1)}, bf16[4,80,128]{2,1,0:T(8,128)(2,1)S(1)}, u32[]{:S(2)}, u32[]{:S(2)}) collective-permute-start(bf16[4,80,128]{2,1,0:T(8,128)(2,1)S(1)} %get-tuple-element.72), channel_id=1, source_target_pairs={{0,6},{1,7},{2,0},{3,1},{4,2},{5,3},{6,4},{7,5},{8,14},{9,15},{10,... | collective-permute-start | bytes 245768 | tf_op jit(solution)/shard_map/ppermute | solution.py:28
  266.0 8.3 %collective-permute-start.41 = (bf16[8,80,128]{2,1,0:T(8,128)(2,1)S(1)}, bf16[8,80,128]{2,1,0:T(8,128)(2,1)S(1)}, u32[]{:S(2)}, u32[]{:S(2)}) collective-permute-start(bf16[8,80,128]{2,1,0:T(8,128)(2,1)S(1)} %pad_maximum_fusion.4), channel_id=1, source_target_pairs={{0,6},{1,7},{2,0},{3,1},{4,2},{5,3},{6,4},{7,5},{8,14},{9,15},{10,... | collective-permute-start | bytes 491528 | tf_op jit(solution)/shard_map/ppermute | solution.py:28
  268.4 10.3 %collective-permute-start.39 = (bf16[8,80,128]{2,1,0:T(8,128)(2,1)S(1)}, bf16[8,80,128]{2,1,0:T(8,128)(2,1)S(1)}, u32[]{:S(2)}, u32[]{:S(2)}) collective-permute-start(bf16[8,80,128]{2,1,0:T(8,128)(2,1)S(1)} %pad_maximum_fusion.3), channel_id=1, source_target_pairs={{0,2},{1,3},{2,4},{3,5},{4,6},{5,7},{6,0},{7,1},{8,10},{9,11},{10,... | collective-permute-start | bytes 491528 | tf_op jit(solution)/shard_map/ppermute | solution.py:28
  269.6 10.6 %collective-permute-start.25 = (bf16[8,80,128]{2,1,0:T(8,128)(2,1)S(1)}, bf16[8,80,128]{2,1,0:T(8,128)(2,1)S(1)}, u32[]{:S(2)}, u32[]{:S(2)}) collective-permute-start(bf16[8,80,128]{2,1,0:T(8,128)(2,1)S(1)} %pad_maximum_fusion.2), channel_id=1, source_target_pairs={{0,6},{1,7},{2,0},{3,1},{4,2},{5,3},{6,4},{7,5},{8,14},{9,15},{10,... | collective-permute-start | bytes 491528 | tf_op jit(solution)/shard_map/ppermute | solution.py:28
  272.4 12.0 %collective-permute-start.23 = (bf16[8,80,128]{2,1,0:T(8,128)(2,1)S(1)}, bf16[8,80,128]{2,1,0:T(8,128)(2,1)S(1)}, u32[]{:S(2)}, u32[]{:S(2)}) collective-permute-start(bf16[8,80,128]{2,1,0:T(8,128)(2,1)S(1)} %pad_maximum_fusion.1), channel_id=1, source_target_pairs={{0,2},{1,3},{2,4},{3,5},{4,6},{5,7},{6,0},{7,1},{8,10},{9,11},{10,... | collective-permute-start | bytes 491528 | tf_op jit(solution)/shard_map/ppermute | solution.py:28
  285.2 26.1 %copy-start.13 = (bf16[8,80,128]{2,1,0:T(8,128)(2,1)}, bf16[8,80,128]{2,1,0:T(8,128)(2,1)S(1)}, u32[]{:S(2)}) copy-start(bf16[8,80,128]{2,1,0:T(8,128)(2,1)S(1)} %get-tuple-element.47.refs_1_) | copy-start | bytes 491524
  285.2 26.1 %copy-start.14 = (bf16[8,80,128]{2,1,0:T(8,128)(2,1)}, bf16[8,80,128]{2,1,0:T(8,128)(2,1)S(1)}, u32[]{:S(2)}) copy-start(bf16[8,80,128]{2,1,0:T(8,128)(2,1)S(1)} %get-tuple-element.76.refs_0_) | copy-start | bytes 491524
  285.2 8.9 %collective-permute-start.47 = (bf16[8,80,128]{2,1,0:T(8,128)(2,1)S(1)}, bf16[8,80,128]{2,1,0:T(8,128)(2,1)S(1)}, u32[]{:S(2)}, u32[]{:S(2)}) collective-permute-start(bf16[8,80,128]{2,1,0:T(8,128)(2,1)S(1)} %get-tuple-element.47.refs_1_), channel_id=1, source_target_pairs={{0,2},{1,3},{2,4},{3,5},{4,6},{5,7},{6,0},{7,1},{8,10},{9,11},{10,... | collective-permute-start | bytes 491528 | tf_op jit(solution)/shard_map/ppermute | solution.py:28
  285.3 12.0 %collective-permute-start.43 = (bf16[8,80,128]{2,1,0:T(8,128)(2,1)S(1)}, bf16[8,80,128]{2,1,0:T(8,128)(2,1)S(1)}, u32[]{:S(2)}, u32[]{:S(2)}) collective-permute-start(bf16[8,80,128]{2,1,0:T(8,128)(2,1)S(1)} %get-tuple-element.47.refs_1_), channel_id=1, source_target_pairs={{0,6},{1,7},{2,0},{3,1},{4,2},{5,3},{6,4},{7,5},{8,14},{9,15},{10,... | collective-permute-start | bytes 491528 | tf_op jit(solution)/shard_map/ppermute | solution.py:28
  289.1 12.2 %collective-permute-start.44 = (bf16[8,80,128]{2,1,0:T(8,128)(2,1)S(1)}, bf16[8,80,128]{2,1,0:T(8,128)(2,1)S(1)}, u32[]{:S(2)}, u32[]{:S(2)}) collective-permute-start(bf16[8,80,128]{2,1,0:T(8,128)(2,1)S(1)} %get-tuple-element.76.refs_0_), channel_id=1, source_target_pairs={{0,2},{1,3},{2,4},{3,5},{4,6},{5,7},{6,0},{7,1},{8,10},{9,11},{10,... | collective-permute-start | bytes 491528 | tf_op jit(solution)/shard_map/ppermute | solution.py:28
  289.1 14.4 %collective-permute-start.42 = (bf16[8,80,128]{2,1,0:T(8,128)(2,1)S(1)}, bf16[8,80,128]{2,1,0:T(8,128)(2,1)S(1)}, u32[]{:S(2)}, u32[]{:S(2)}) collective-permute-start(bf16[8,80,128]{2,1,0:T(8,128)(2,1)S(1)} %get-tuple-element.76.refs_0_), channel_id=1, source_target_pairs={{0,6},{1,7},{2,0},{3,1},{4,2},{5,3},{6,4},{7,5},{8,14},{9,15},{10,... | collective-permute-start | bytes 491528 | tf_op jit(solution)/shard_map/ppermute | solution.py:28
  294.1 17.2 %copy-start.7 = (bf16[8,80,128]{2,1,0:T(8,128)(2,1)}, bf16[8,80,128]{2,1,0:T(8,128)(2,1)S(1)}, u32[]{:S(2)}) copy-start(bf16[8,80,128]{2,1,0:T(8,128)(2,1)S(1)} %collective-permute-done.47.refs_7_) | copy-start | bytes 491524
  294.1 15.2 %collective-permute-start.48 = (bf16[4,80,128]{2,1,0:T(8,128)(2,1)S(1)}, bf16[4,80,128]{2,1,0:T(8,128)(2,1)S(1)}, u32[]{:S(2)}, u32[]{:S(2)}) collective-permute-start(bf16[4,80,128]{2,1,0:T(8,128)(2,1)S(1)} %slice.206), channel_id=1, source_target_pairs={{0,2},{1,3},{2,4},{3,5},{4,6},{5,7},{6,0},{7,1},{8,10},{9,11},{10,... | collective-permute-start | bytes 245768 | tf_op jit(solution)/shard_map/ppermute | solution.py:28
  297.3 27.9 %copy-start.8 = (bf16[8,80,128]{2,1,0:T(8,128)(2,1)}, bf16[8,80,128]{2,1,0:T(8,128)(2,1)S(1)}, u32[]{:S(2)}) copy-start(bf16[8,80,128]{2,1,0:T(8,128)(2,1)S(1)} %collective-permute-done.43.refs_3_) | copy-start | bytes 491524
  297.3 12.7 %collective-permute-start.49 = (bf16[4,80,128]{2,1,0:T(8,128)(2,1)S(1)}, bf16[4,80,128]{2,1,0:T(8,128)(2,1)S(1)}, u32[]{:S(2)}, u32[]{:S(2)}) collective-permute-start(bf16[4,80,128]{2,1,0:T(8,128)(2,1)S(1)} %slice.207), channel_id=1, source_target_pairs={{0,6},{1,7},{2,0},{3,1},{4,2},{5,3},{6,4},{7,5},{8,14},{9,15},{10,... | collective-permute-start | bytes 245768 | tf_op jit(solution)/shard_map/ppermute | solution.py:28
  301.2 24.0 %copy-start.9 = (bf16[8,80,128]{2,1,0:T(8,128)(2,1)}, bf16[8,80,128]{2,1,0:T(8,128)(2,1)S(1)}, u32[]{:S(2)}) copy-start(bf16[8,80,128]{2,1,0:T(8,128)(2,1)S(1)} %collective-permute-done.44.refs_6_) | copy-start | bytes 491524
  301.2 7.5 %collective-permute-start.45 = (bf16[4,80,128]{2,1,0:T(8,128)(2,1)S(1)}, bf16[4,80,128]{2,1,0:T(8,128)(2,1)S(1)}, u32[]{:S(2)}, u32[]{:S(2)}) collective-permute-start(bf16[4,80,128]{2,1,0:T(8,128)(2,1)S(1)} %slice.204), channel_id=1, source_target_pairs={{0,2},{1,3},{2,4},{3,5},{4,6},{5,7},{6,0},{7,1},{8,10},{9,11},{10,... | collective-permute-start | bytes 245768 | tf_op jit(solution)/shard_map/ppermute | solution.py:28
  303.4 21.8 %copy-start.10 = (bf16[8,80,128]{2,1,0:T(8,128)(2,1)}, bf16[8,80,128]{2,1,0:T(8,128)(2,1)S(1)}, u32[]{:S(2)}) copy-start(bf16[8,80,128]{2,1,0:T(8,128)(2,1)S(1)} %collective-permute-done.42.refs_2_) | copy-start | bytes 491524
  303.5 5.8 %collective-permute-start.46 = (bf16[4,80,128]{2,1,0:T(8,128)(2,1)S(1)}, bf16[4,80,128]{2,1,0:T(8,128)(2,1)S(1)}, u32[]{:S(2)}, u32[]{:S(2)}) collective-permute-start(bf16[4,80,128]{2,1,0:T(8,128)(2,1)S(1)} %slice.205), channel_id=1, source_target_pairs={{0,6},{1,7},{2,0},{3,1},{4,2},{5,3},{6,4},{7,5},{8,14},{9,15},{10,... | collective-permute-start | bytes 245768 | tf_op jit(solution)/shard_map/ppermute | solution.py:28
  309.3 17.4 %collective-permute-start.50 = (bf16[32,80,128]{2,1,0:T(8,128)(2,1)S(1)}, bf16[32,80,128]{2,1,0:T(8,128)(2,1)S(1)}, u32[]{:S(2)}, u32[]{:S(2)}) collective-permute-start(bf16[32,80,128]{2,1,0:T(8,128)(2,1)S(1)} %constant_dynamic-update-slice_fusion.10), channel_id=1, source_target_pairs={{0,1},{1,0},{2,3},{3,2},{4,5},{5,4},{6,7},{7,6},{8,9},{9,8},{10,11... | collective-permute-start | bytes 1966088 | tf_op jit(solution)/shard_map/ppermute | solution.py:33
  311.3 16.2 %collective-permute-start.51 = (bf16[32,80,128]{2,1,0:T(8,128)(2,1)}, bf16[32,80,128]{2,1,0:T(8,128)(2,1)S(1)}, u32[]{:S(2)}, u32[]{:S(2)}) collective-permute-start(bf16[32,80,128]{2,1,0:T(8,128)(2,1)} %constant_dynamic-update-slice_fusion.15), channel_id=1, source_target_pairs={{0,1},{1,0},{2,3},{3,2},{4,5},{5,4},{6,7},{7,6},{8,9},{9,8},{10,11... | collective-permute-start | bytes 1966088 | tf_op jit(solution)/shard_map/ppermute | solution.py:33
  (15 other events, 39.6 us)

commit v2 on v1

--- a/solution.py
+++ b/solution.py
@@ -5,7 +5,9 @@
 from jax.experimental.pallas import tpu as pltpu
 from jax.sharding import PartitionSpec as P
 
+
 BLK = 128
+CAP = 24
 CORES = 2
 CHUNKS = 2
 UNROLL = 4
@@ -17,15 +19,9 @@
 ANY = pl.BlockSpec(memory_space=pl.ANY)
 
 
-def ring_shift(x, offset):
+def ring_exchange(x, flip):
     count = lax.axis_size("label")
-    ring = count // CORES
-    pairs = [
-        (r * CORES + c, ((r + offset) % ring) * CORES + c)
-        for r in range(ring)
-        for c in range(CORES)
-    ]
-    return lax.ppermute(x, "label", pairs)
+    return lax.ppermute(x, "label", [(i, i ^ (flip * CORES)) for i in range(count)])
 
 
 def swap_cores(x):
@@ -39,62 +35,50 @@
 
 def ring_gather(own):
     ring = lax.axis_size("label") // CORES
-    far = ring // 2
-    half = own.shape[0] // 2
-    pieces = [None] * ring
-    pieces[0] = own
-    up = down = own
-    for step in range(1, far):
-        up = ring_shift(up, 1)
-        down = ring_shift(down, -1)
-        pieces[(-step) % ring] = up
-        pieces[step] = down
-    first = ring_shift(up[:half], 1)
-    second = ring_shift(down[half:], -1)
-    pieces[far] = jnp.concatenate([first, second], axis=0)
-    return pieces
-
-
-def ring_reduce(pieces):
-    ring = len(pieces)
-    far = ring // 2
-    half = pieces[0].shape[0] // 2
-    up = ring_shift(pieces[far][:half], 1)
-    down = ring_shift(pieces[far][half:], -1)
-    for step in range(far - 1, 0, -1):
-        ahead = pieces[step].astype(F32)
-        behind = pieces[(-step) % ring].astype(F32)
-        if step == far - 1:
-            ahead = jnp.concatenate([ahead[:half] + up.astype(F32), ahead[half:]], axis=0)
-            behind = jnp.concatenate([behind[:half], behind[half:] + down.astype(F32)], axis=0)
-        else:
-            ahead = ahead + up.astype(F32)
-            behind = behind + down.astype(F32)
-        up = ring_shift(ahead.astype(BF16), 1)
-        down = ring_shift(behind.astype(BF16), -1)
-    return [pieces[0].astype(F32), up.astype(F32), down.astype(F32)]
-
-
-def select_blocks(pools, index, cap):
-    size, docs, blk = pools[0].shape
-    outs = index.shape[0] // cap
-
-    def kernel(index_ref, *refs):
-        ins = refs[: len(pools)]
-        out_refs = refs[len(pools) : len(pools) + outs]
-        pool, sem = refs[len(pools) + outs :]
+    return [own] + [ring_exchange(own, k) for k in range(1, ring)]
+
+
+def cut_columns(weight, starts, width):
+    count = starts.shape[0]
+
+    def kernel(starts_ref, weight_hbm, *refs):
+        outs, sem = refs[:count], refs[count]
         copies = [
-            pltpu.make_async_copy(ref, pool.at[pl.ds(i * size, size)], sem.at[i])
-            for i, ref in enumerate(ins)
+            pltpu.make_async_copy(
+                weight_hbm.at[:, pl.ds(pl.multiple_of(starts_ref[k], BLK), width)], out, sem.at[k]
+            )
+            for k, out in enumerate(outs)
         ]
         for copy in copies:
             copy.start()
         for copy in copies:
             copy.wait()
+
+    return pl.pallas_call(
+        kernel,
+        out_shape=[jax.ShapeDtypeStruct((weight.shape[0], width), weight.dtype)] * count,
+        in_specs=[SMEM, ANY],
+        out_specs=[ANY] * count,
+        scratch_shapes=[pltpu.SemaphoreType.DMA((count,))],
+        name="cut_columns",
+    )(starts, weight)
+
+
+def select_blocks(pools, index, cap):
+    size, docs, blk = pools[0].shape
+    outs = index.shape[0] // cap
+
+    def kernel(index_ref, *refs):
+        ins = refs[: len(pools)]
+        out_refs = refs[len(pools) :]
         for m in range(outs):
 
             def step(k, carry):
-                out_refs[m][k] = pool[index_ref[m * cap + k]]
+                place = index_ref[m * cap + k]
+                block = ins[0][place % size]
+                for i in range(1, len(ins)):
+                    block = jnp.where(place >= i * size, ins[i][place % size], block)
+                out_refs[m][k] = block
                 return carry
 
             lax.fori_loop(0, cap, step, 0, unroll=UNROLL)
@@ -102,12 +86,8 @@
     return pl.pallas_call(
         kernel,
         out_shape=[jax.ShapeDtypeStruct((cap, docs, blk), BF16)] * outs,
-        in_specs=[SMEM] + [ANY] * len(pools),
+        in_specs=[SMEM] + [VMEM] * len(pools),
         out_specs=[VMEM] * outs,
-        scratch_shapes=[
-            pltpu.VMEM((len(pools) * size, docs, blk), BF16),
-            pltpu.SemaphoreType.DMA((len(pools),)),
-        ],
         name="select_blocks",
     )(index, *pools)
 
@@ -202,7 +182,7 @@
         kernel,
         out_shape=[jax.ShapeDtypeStruct((label_blocks, docs, blk), BF16)]
         + [jax.ShapeDtypeStruct((cap, docs, blk), BF16)] * count,
-        in_specs=[SMEM] * 3 + [VMEM] + [ANY] * (count + 1),
+        in_specs=[SMEM] * 3 + [VMEM, ANY] + [VMEM] * count,
         out_specs=[VMEM] * (count + 1),
         scratch_shapes=[
             pltpu.VMEM((count * cap, docs, blk), BF16),
@@ -219,59 +199,47 @@
     pieces = len(chunks)
     count = len(chunks[0])
     cap, _, blk = chunks[0][0].shape
-    docs = [chunk[0].shape[1] for chunk in chunks]
     uses = label_blocks * slots // (count * cap)
 
     def kernel(order_ref, *refs):
         residual_refs = refs[:pieces]
         ins = refs[pieces : pieces + pieces * count]
         out_ref = refs[pieces + pieces * count]
-        pools = refs[pieces + pieces * count + 1 :][:pieces]
-        buffer, sem, out_sem = refs[-3:]
-        copies = [
-            pltpu.make_async_copy(
-                ins[i * count + q], pools[i].at[pl.ds(q * cap, cap)], sem.at[i * count + q]
-            )
-            for i in range(pieces)
-            for q in range(count)
-        ]
-        for copy in copies:
-            copy.start()
-        for copy in copies:
-            copy.wait()
-
-        def step(k, carry):
-            where = [order_ref[k * uses + u] for u in range(uses)]
-            rhs = jnp.concatenate(
-                [
-                    jnp.concatenate([ref[w // slots] for w in where], axis=1)
-                    for ref in residual_refs
-                ],
-                axis=0,
-            )
-            lhs = jnp.concatenate([pool[k] for pool in pools], axis=0)
-            out = lax.dot_general(
-                lhs, rhs, (((0,), (0,)), ((), ())), preferred_element_type=F32
-            ).astype(BF16)
-            for u in range(uses):
-                buffer[k * uses + u] = out[:, u * blk : (u + 1) * blk]
-                pltpu.make_async_copy(
-                    buffer.at[k * uses + u], out_ref.at[where[u]], out_sem
-                ).start()
-            return carry
-
-        lax.fori_loop(0, count * cap, step, 0, unroll=UNROLL)
+        buffer, out_sem = refs[pieces + pieces * count + 1 :]
+        for q in range(count):
+            pools = [ins[i * count + q] for i in range(pieces)]
+
+            def step(j, carry):
+                k = q * cap + j
+                where = [order_ref[k * uses + u] for u in range(uses)]
+                rhs = jnp.concatenate(
+                    [
+                        jnp.concatenate([ref[w // slots] for w in where], axis=1)
+                        for ref in residual_refs
+                    ],
+                    axis=0,
+                )
+                lhs = jnp.concatenate([pool[j] for pool in pools], axis=0)
+                out = lax.dot_general(
+                    lhs, rhs, (((0,), (0,)), ((), ())), preferred_element_type=F32
+                ).astype(BF16)
+                for u in range(uses):
+                    buffer[k * uses + u] = out[:, u * blk : (u + 1) * blk]
+                    pltpu.make_async_copy(
+                        buffer.at[k * uses + u], out_ref.at[where[u]], out_sem
+                    ).start()
+                return carry
+
+            lax.fori_loop(0, cap, step, 0, unroll=UNROLL)
         pltpu.make_async_copy(buffer, out_ref, out_sem).wait()
 
     out = pl.pallas_call(
         kernel,
         out_shape=jax.ShapeDtypeStruct((label_blocks * slots, blk, blk), BF16),
-        in_specs=[SMEM] + [VMEM] * pieces + [ANY] * (pieces * count),
+        in_specs=[SMEM] + [VMEM] * (pieces + pieces * count),
         out_specs=ANY,
-        scratch_shapes=[pltpu.VMEM((count * cap, d, blk), BF16) for d in docs]
-        + [
+        scratch_shapes=[
             pltpu.VMEM((label_blocks * slots, blk, blk), BF16),
-            pltpu.SemaphoreType.DMA((pieces * count,)),
             pltpu.SemaphoreType.DMA(()),
         ],
         name="block_weight_grad",
@@ -283,7 +251,7 @@
     pieces = len(groups)
     chunks = len(groups[0])
     size, _, blk = groups[0][0].shape
-    docs_all, rows = documents.shape
+    _, rows = documents.shape
 
     def kernel(columns_ref, documents_ref, *refs):
         out_ref = refs[-1]
@@ -329,7 +297,7 @@
     owner_ring = local // (CORES * own_blocks)
     owner_core = local // own_blocks % CORES
     place = (
-        jnp.where(owner_core == core, 0, ring) + (owner_ring - ring_index) % ring
+        jnp.where(owner_core == core, 0, ring) + (owner_ring ^ ring_index)
     ) * own_blocks + local % own_blocks
     send = jnp.sum(jnp.where(chosen, place[None, None, :], 0), axis=2).astype(jnp.int32)
     send = jnp.stack(
@@ -356,17 +324,16 @@
     return send, position, order.astype(jnp.int32)
 
 
-def on_device(documents, expand_weight, sparse_weight, feature_lists, positives):
+def program(documents, expand_weight, sparse_weight, feature_lists, positives):
     feat_count = lax.axis_size("feat")
     label_count = lax.axis_size("label")
     feat_index = lax.axis_index("feat")
     label_index = lax.axis_index("label")
     group = feat_index * label_count + label_index
     ring = label_count // CORES
-    far = ring // 2
     ring_index, core = label_index // CORES, label_index % CORES
     docs = documents.shape[0]
-    rows, width = expand_weight.shape
+    _, width = expand_weight.shape
     own_count = width // BLK
     own_blocks = own_count // label_count
     label_blocks, slots = sparse_weight.shape[:2]
@@ -375,58 +342,59 @@
     cuts = [slice(i * chunk, (i + 1) * chunk) for i in range(CHUNKS)]
 
     ring_width = width // ring
-
-    def columns_of(offset):
-        start = (ring_index + offset) % ring * ring_width
-        return lax.dynamic_slice_in_dim(expand_weight, start, ring_width, 1)
-
-    far_columns = columns_of(far)
-    half = rows // 2
-    up, down = far_columns[:half], far_columns[half:]
-    up = ring_shift(up, 1)
-    down = ring_shift(down, -1)
-    arrived = {}
-    for offset in range(1, ring):
-        if offset != far:
-            arrived[offset] = ring_shift(columns_of(offset), offset)
-    for _ in range(far - 1):
-        up = ring_shift(up, 1)
-        down = ring_shift(down, -1)
-    others = {offset: ring_shift(documents, offset) for offset in range(1, ring)}
+    starts = (jnp.arange(ring, dtype=jnp.int32) ^ ring_index) * ring_width
 
     def product(left, right):
         right = right.reshape(right.shape[0], ring_width // BLK, BLK)
         return jnp.einsum("dk,kbc->bdc", left, right, preferred_element_type=F32)
 
-    expanded = product(documents, columns_of(0))
-    for offset in range(1, ring):
-        if offset != far:
-            expanded = expanded + product(others[offset], arrived[offset])
-    expanded = expanded + product(others[far], jnp.concatenate([up, down], axis=0))
+    columns = cut_columns(expand_weight, starts, ring_width)
+    arrived = [columns[0]] + [None] * (ring - 1)
+    for k in range(ring - 1, 0, -1):
+        arrived[k] = ring_exchange(columns[k], k)
+    documents_late, _ = lax.optimization_barrier((documents, columns[0]))
+    expanded = product(documents, columns[0])
+    for k in range(1, ring):
+        other = ring_exchange(documents_late, k)
+        expanded = expanded + product(other, arrived[k])
     kept = lax.dynamic_slice_in_dim(expanded, core * own_blocks, own_blocks, 0)
     given = lax.dynamic_slice_in_dim(expanded, (1 - core) * own_blocks, own_blocks, 0)
-    hidden = jnp.maximum(kept + swap_cores(given), 0.0).astype(BF16)
 
     send, position, order = list_tables(
         feature_lists, feat_index, label_index, label_count, own_count, label_blocks, cap
     )
     first_label = (group * label_blocks * BLK).reshape(1)
+    known = [positives[cut] for cut in cuts]
+    given, send, position, order, known, first_label = lax.optimization_barrier(
+        (given, send, position, order, known, first_label)
+    )
+    hidden = jnp.maximum(kept + swap_cores(given), 0.0).astype(BF16)
 
     picked, residuals, gradients = [], [], []
-    for cut in cuts:
+    for i, cut in enumerate(cuts):
         pool = jnp.concatenate(ring_gather(hidden[:, cut]), axis=0)
-        outgoing = select_blocks([pool, swap_cores(pool)], send, cap)
-        parts = [outgoing[0]] + [feat_exchange(outgoing[m], m) for m in range(1, feat_count)]
+        pools = [pool, swap_cores(pool)]
+        outgoing = select_blocks(pools, send, cap)
+        parts = [outgoing[0]] + [None] * (feat_count - 1)
+        for m in range(feat_count - 1, 0, -1):
+            parts[m] = feat_exchange(outgoing[m], m)
         residual, back = residual_and_back(
-            parts, sparse_weight, position, order, positives[cut], first_label
+            parts, sparse_weight, position, order, known[i], first_label
         )
         picked.append(parts)
         residuals.append(residual)
-        returned = [back[0]] + [feat_exchange(back[m], m) for m in range(1, feat_count)]
+        returned = [back[0]] + [None] * (feat_count - 1)
+        for m in range(feat_count - 1, 0, -1):
+            returned[m] = feat_exchange(back[m], m)
         kept, given = add_blocks(returned, send, own_count, CORES)
         both = (kept.astype(F32) + swap_cores(given).astype(F32)).astype(BF16)
-        terms = ring_reduce([both[k * own_blocks : (k + 1) * own_blocks] for k in range(ring)])
-        gradient = jnp.where(hidden[:, cut] > 0, sum(terms), 0.0).astype(BF16)
+        pieces = [both[k * own_blocks : (k + 1) * own_blocks] for k in range(ring)]
+        total = pieces[0].astype(F32)
+        for k in range(ring - 1, 0, -1):
+            total = total + ring_exchange(pieces[k], k).astype(F32)
+        if gradients:
+            total, _ = lax.optimization_barrier((total, gradients[-1][0]))
+        gradient = jnp.where(hidden[:, cut] > 0, total, 0.0).astype(BF16)
         gathered = jnp.concatenate(ring_gather(gradient), axis=0)
         gradients.append((gathered, swap_cores(gathered)))
 
@@ -439,18 +407,15 @@
                 [g[side][k * own_blocks : (k + 1) * own_blocks] for g in gradients]
             )
             starts.append(
-                (((ring_index + k) % ring) * CORES + (core ^ side)) * own_blocks * BLK
+                ((ring_index ^ k) * CORES + (core ^ side)) * own_blocks * BLK
             )
     grad_expand = expand_weight_grad(documents, groups, jnp.stack(starts), width)
     return (grad_expand, grad_sparse)
 
 
-CAP = 24
-
-
 def solution(mesh):
     return jax.shard_map(
-        on_device,
+        program,
         mesh=mesh,
         in_specs=(
             P(None, "label"),

time: 333 us -> 362 us (1.087)
  Pallas kernels: 69.7 us -> 130 us
  starting transfers between devices: 76.7 us -> 59.5 us
  local copies, waits for them, and re-layouts: 20.2 us -> 10.7 us
    pallas_call x0 -> x1, Pallas kernels: none -> 65.5 us  [cut_columns(): pl.pallas_call(kernel, out_shape=[jax.ShapeDtypeStruct((weight.shape[0],...]
    ppermute x33 -> x24, starting transfers between devices: 61.7 us -> 45 us  [ring_exchange(): lax.ppermute(x, 'label', [(i, i ^ flip * CORES) for i in range(count)])]
    unnamed x75 -> x60, local copies, waits for them, and re-layouts: 13.7 us -> 4.69 us
    pallas_call x2, Pallas kernels: 39.4 us -> 35.4 us  [residual_and_back(): pl.pallas_call(kernel, out_shape=[jax.ShapeDtypeStruct((label_blocks, doc...]
    ppermute x33 -> x24, waiting for transfers between devices: 92.5 us -> 90 us  [ring_exchange(): lax.ppermute(x, 'label', [(i, i ^ flip * CORES) for i in range(count)])]
  transfers between devices with their start and end apart: 52 -> 43, of which waited for: 31 -> 25; matrix products, arithmetic and copies ran while one was open for 6% -> 2% of each run, Pallas kernels for 20% -> 17%
where the time goes in v2:
time: 362 us; the launch traced here: 361 us
  waiting for transfers between devices  154 us (43%)
  Pallas kernels  130 us (36%)
  starting transfers between devices  59.5 us (16%)
  local copies, waits for them, and re-layouts  10.7 us (3%)
  other arithmetic  4.54 us (1%)
    ppermute x24, waiting for transfers between devices, ring_exchange(): lax.ppermute(x, 'label', [(i, i ^ flip * CORES) for i in range(count)])  90 us
    pallas_call x1, Pallas kernels, cut_columns(): pl.pallas_call(kernel, out_shape=[jax.ShapeDtypeStruct((weight.shape[0],...  65.5 us
    ppermute x12, waiting for transfers between devices, feat_exchange(): lax.ppermute(x, 'feat', [(i, i ^ flip) for i in range(lax.axis_size('feat...  61.1 us
    ppermute x24, starting transfers between devices, ring_exchange(): lax.ppermute(x, 'label', [(i, i ^ flip * CORES) for i in range(count)])  45 us
    pallas_call x2, Pallas kernels, residual_and_back(): pl.pallas_call(kernel, out_shape=[jax.ShapeDtypeStruct((label_blocks, doc...  35.4 us
    ppermute x12, starting transfers between devices, feat_exchange(): lax.ppermute(x, 'feat', [(i, i ^ flip) for i in range(lax.axis_size('feat...  14.2 us
    pallas_call x1, Pallas kernels, block_weight_grad(): pl.pallas_call(kernel, out_shape=jax.ShapeDtypeStruct((label_blocks * slo...  11.6 us
    pallas_call x2, Pallas kernels, select_blocks(): pl.pallas_call(kernel, out_shape=[jax.ShapeDtypeStruct((cap, docs, blk),...  7.31 us
  transfers between devices with their start and end apart: 43, of which 25 were waited for; matrix products, arithmetic and copies ran while one was open for 2% of the time, Pallas kernels for 17%

profile of v2, /device:TPU:0, one launch (start us, length us, event | category | flops | bytes accessed | tf_op | source)
XLA Modules:
  0.0 361.2 jit_solution(16271894353986125139)
XLA Ops:
  1.2 65.5 %cut_columns.1 = (bf16[128,2048]{1,0:T(8,128)(2,1)}, bf16[128,2048]{1,0:T(8,128)(2,1)}, bf16[128,2048]{1,0:T(8,128)(2,1)}, bf16[128,2048]{1,0:T(8,128)(2,1)}) custom-call(s32[4]{0:T(128)} %xor_multiply_fusion.starts_ref, bf16[128,8192]{1,0:T(8,128)(2,1)} %weight_hbm.3), custom_call_target="tpu_custom_call" | custom-call | tf_op jit(solution)/shard_map/cut_columns/pallas_call | solution.py:57
  66.7 5.1 %collective-permute-start.5 = (bf16[160,128]{1,0:T(8,128)(2,1)S(1)}, bf16[160,128]{1,0:T(8,128)(2,1)S(1)}, u32[]{:S(2)}, u32[]{:S(2)}) collective-permute-start(bf16[160,128]{1,0:T(8,128)(2,1)S(1)} %copy-done.25), channel_id=1, source_target_pairs={{0,6},{1,7},{2,4},{3,5},{4,2},{5,3},{6,0},{7,1},{8,14},{9,15},{10,... | collective-permute-start | bytes 122888 | tf_op jit(solution)/shard_map/ppermute | solution.py:24
  72.5 1.4 collective-permute-start
  73.9 2.4 collective-permute-start.4
  81.9 7.8 %collective-permute-done = bf16[128,2048]{1,0:T(8,128)(2,1)S(1)} collective-permute-done((bf16[128,2048]{1,0:T(8,128)(2,1)}, bf16[128,2048]{1,0:T(8,128)(2,1)S(1)}, u32[]{:S(2)}, u32[]{:S(2)}) %collective-permute-start) | collective-permute-done | bytes 524320 | tf_op jit(solution)/shard_map/ppermute | solution.py:24
  90.0 11.3 %collective-permute-done.4 = bf16[128,2048]{1,0:T(8,128)(2,1)S(1)} collective-permute-done((bf16[128,2048]{1,0:T(8,128)(2,1)}, bf16[128,2048]{1,0:T(8,128)(2,1)S(1)}, u32[]{:S(2)}, u32[]{:S(2)}) %collective-permute-start.4) | collective-permute-done | bytes 524320 | tf_op jit(solution)/shard_map/ppermute | solution.py:24
  101.6 20.1 %collective-permute-done.2 = bf16[128,2048]{1,0:T(8,128)(2,1)S(1)} collective-permute-done((bf16[128,2048]{1,0:T(8,128)(2,1)}, bf16[128,2048]{1,0:T(8,128)(2,1)S(1)}, u32[]{:S(2)}, u32[]{:S(2)}) %collective-permute-start.2) | collective-permute-done | bytes 524320 | tf_op jit(solution)/shard_map/ppermute | solution.py:24
  122.2 2.1 collective-permute-done.6
  124.4 2.5 collective-permute-start.9
  126.9 1.9 collective-permute-start.7
  128.8 4.6 %collective-permute-done.9 = bf16[8,80,128]{2,1,0:T(8,128)(2,1)S(1)} collective-permute-done((bf16[8,80,128]{2,1,0:T(8,128)(2,1)S(1)}, bf16[8,80,128]{2,1,0:T(8,128)(2,1)S(1)}, u32[]{:S(2)}, u32[]{:S(2)}) %collective-permute-start.9) | collective-permute-done | bytes 163872 | tf_op jit(solution)/shard_map/ppermute | solution.py:24
  133.5 7.0 %collective-permute-done.8 = bf16[8,80,128]{2,1,0:T(8,128)(2,1)S(1)} collective-permute-done((bf16[8,80,128]{2,1,0:T(8,128)(2,1)S(1)}, bf16[8,80,128]{2,1,0:T(8,128)(2,1)S(1)}, u32[]{:S(2)}, u32[]{:S(2)}) %collective-permute-start.8) | collective-permute-done | bytes 163872 | tf_op jit(solution)/shard_map/ppermute | solution.py:24
  140.6 1.6 collective-permute-start.23
  142.7 0.8 copy-done.17
  143.6 3.8 %select_blocks.2 = (bf16[24,80,128]{2,1,0:T(8,128)(2,1)}, bf16[24,80,128]{2,1,0:T(8,128)(2,1)}, bf16[24,80,128]{2,1,0:T(8,128)(2,1)}, bf16[24,80,128]{2,1,0:T(8,128)(2,1)}) custom-call(s32[96]{0:T(128)} %reshape.191.index_ref, bf16[32,80,128]{2,1,0:T(8,128)(2,1)} %copy-done.1, bf16[32,80,128]{2,1,0:T(8,128)(2,1)} %copy-done.17), custom_call_target="tpu_custom_call" | custom-call | tf_op jit(solution)/shard_map/select_blocks/pallas_call | solution.py:86
  147.3 1.5 collective-permute-start.11
  148.8 1.5 collective-permute-start.12
  150.8 2.4 collective-permute-start.21
  153.2 6.8 %collective-permute-done.22 = bf16[8,80,128]{2,1,0:T(8,128)(2,1)S(1)} collective-permute-done((bf16[8,80,128]{2,1,0:T(8,128)(2,1)S(1)}, bf16[8,80,128]{2,1,0:T(8,128)(2,1)S(1)}, u32[]{:S(2)}, u32[]{:S(2)}) %collective-permute-start.22) | collective-permute-done | bytes 163872 | tf_op jit(solution)/shard_map/ppermute | solution.py:24
  160.3 1.4 collective-permute-done.11.refs_1_.refs_3_
  161.7 10.9 %collective-permute-done.12.refs_2_.refs_4_ = bf16[24,80,128]{2,1,0:T(8,128)(2,1)S(1)} collective-permute-done((bf16[24,80,128]{2,1,0:T(8,128)(2,1)}, bf16[24,80,128]{2,1,0:T(8,128)(2,1)S(1)}, u32[]{:S(2)}, u32[]{:S(2)}) %collective-permute-start.12) | collective-permute-done | bytes 491552 | tf_op jit(solution)/shard_map/ppermute | solution.py:33
  173.5 17.7 %residual_and_back.2 = (bf16[24,80,128]{2,1,0:T(8,128)(2,1)}, bf16[24,80,128]{2,1,0:T(8,128)(2,1)}, bf16[24,80,128]{2,1,0:T(8,128)(2,1)}, bf16[24,80,128]{2,1,0:T(8,128)(2,1)}, bf16[24,80,128]{2,1,0:T(8,128)(2,1)}) custom-call(s32[384]{0:T(512)} %copy-done.27, s32[384]{0:T(512)} %select_reduce_fusion.order_ref, s32[1]{0:T(128)} %bitcast.14.first_ref, ...), custom_call_target="tpu_custom_call" | custom-call | tf_op jit(solution)/shard_map/residual_and_back/pallas_call | solution.py:181
  191.2 1.1 collective-permute-start.14
  192.3 1.0 collective-permute-start.15
  193.4 1.4 collective-permute-start.16
  194.8 0.8 copy-done.16
  195.6 3.5 select_blocks.3
  199.1 1.1 collective-permute-start.25
  200.2 1.0 collective-permute-start.26
  201.2 4.3 %collective-permute-done.14.refs_1_ = bf16[24,80,128]{2,1,0:T(8,128)(2,1)S(1)} collective-permute-done((bf16[24,80,128]{2,1,0:T(8,128)(2,1)}, bf16[24,80,128]{2,1,0:T(8,128)(2,1)S(1)}, u32[]{:S(2)}, u32[]{:S(2)}) %collective-permute-start.14) | collective-permute-done | bytes 491552 | tf_op jit(solution)/shard_map/ppermute | solution.py:33
  205.6 1.5 collective-permute-start.27
  207.1 10.2 %collective-permute-done.15.refs_2_ = bf16[24,80,128]{2,1,0:T(8,128)(2,1)} collective-permute-done((bf16[24,80,128]{2,1,0:T(8,128)(2,1)}, bf16[24,80,128]{2,1,0:T(8,128)(2,1)}, u32[]{:S(2)}, u32[]{:S(2)}) %collective-permute-start.15) | collective-permute-done | bytes 491552 | tf_op jit(solution)/shard_map/ppermute | solution.py:33
  217.3 3.3 add_blocks.2
  220.6 6.1 %collective-permute-done.25.refs_1_.refs_7_ = bf16[24,80,128]{2,1,0:T(8,128)(2,1)S(1)} collective-permute-done((bf16[24,80,128]{2,1,0:T(8,128)(2,1)}, bf16[24,80,128]{2,1,0:T(8,128)(2,1)S(1)}, u32[]{:S(2)}, u32[]{:S(2)}) %collective-permute-start.25) | collective-permute-done | bytes 491552 | tf_op jit(solution)/shard_map/ppermute | solution.py:33
  226.7 1.0 collective-permute-done.26.refs_2_.refs_8_
  227.7 8.6 %collective-permute-done.27.refs_3_.refs_9_ = bf16[24,80,128]{2,1,0:T(8,128)(2,1)S(1)} collective-permute-done((bf16[24,80,128]{2,1,0:T(8,128)(2,1)}, bf16[24,80,128]{2,1,0:T(8,128)(2,1)S(1)}, u32[]{:S(2)}, u32[]{:S(2)}) %collective-permute-start.27) | collective-permute-done | bytes 491552 | tf_op jit(solution)/shard_map/ppermute | solution.py:33
  236.3 0.8 copy-done.7
  237.1 17.7 %residual_and_back.3 = (bf16[24,80,128]{2,1,0:T(8,128)(2,1)}, bf16[24,80,128]{2,1,0:T(8,128)(2,1)}, bf16[24,80,128]{2,1,0:T(8,128)(2,1)}, bf16[24,80,128]{2,1,0:T(8,128)(2,1)}, bf16[24,80,128]{2,1,0:T(8,128)(2,1)}) custom-call(s32[384]{0:T(512)} %copy-done.27, s32[384]{0:T(512)} %select_reduce_fusion.order_ref, s32[1]{0:T(128)} %bitcast.14.first_ref, ...), custom_call_target="tpu_custom_call" | custom-call | tf_op jit(solution)/shard_map/residual_and_back/pallas_call | solution.py:181
  255.6 1.7 collective-permute-start.29
  257.3 1.1 collective-permute-start.30
  258.4 10.8 %collective-permute-done.28.refs_1_ = bf16[24,80,128]{2,1,0:T(8,128)(2,1)S(1)} collective-permute-done((bf16[24,80,128]{2,1,0:T(8,128)(2,1)}, bf16[24,80,128]{2,1,0:T(8,128)(2,1)S(1)}, u32[]{:S(2)}, u32[]{:S(2)}) %collective-permute-start.28) | collective-permute-done | bytes 491552 | tf_op jit(solution)/shard_map/ppermute | solution.py:33
  269.2 7.8 %collective-permute-done.29.refs_2_ = bf16[24,80,128]{2,1,0:T(8,128)(2,1)S(1)} collective-permute-done((bf16[24,80,128]{2,1,0:T(8,128)(2,1)}, bf16[24,80,128]{2,1,0:T(8,128)(2,1)S(1)}, u32[]{:S(2)}, u32[]{:S(2)}) %collective-permute-start.29) | collective-permute-done | bytes 491552 | tf_op jit(solution)/shard_map/ppermute | solution.py:33
  277.1 0.8 copy-done.23
  278.1 3.4 add_blocks.3
  281.7 1.8 collective-permute-start.18
  283.5 2.6 collective-permute-start.19
  286.4 1.8 collective-permute-start.32
  288.2 2.5 collective-permute-done.18
  290.7 1.2 collective-permute-start.33
  291.9 4.6 %collective-permute-done.20 = bf16[8,80,128]{2,1,0:T(8,128)(2,1)S(1)} collective-permute-done((bf16[8,80,128]{2,1,0:T(8,128)(2,1)S(1)}, bf16[8,80,128]{2,1,0:T(8,128)(2,1)S(1)}, u32[]{:S(2)}, u32[]{:S(2)}) %collective-permute-start.20) | collective-permute-done | bytes 163872 | tf_op jit(solution)/shard_map/ppermute | solution.py:24
  296.4 5.7 %collective-permute-done.19 = bf16[8,80,128]{2,1,0:T(8,128)(2,1)S(1)} collective-permute-done((bf16[8,80,128]{2,1,0:T(8,128)(2,1)S(1)}, bf16[8,80,128]{2,1,0:T(8,128)(2,1)S(1)}, u32[]{:S(2)}, u32[]{:S(2)}) %collective-permute-start.19) | collective-permute-done | bytes 163872 | tf_op jit(solution)/shard_map/ppermute | solution.py:24
  302.3 1.3 collective-permute-start.37
  303.6 13.2 %collective-permute-start.35 = (bf16[8,80,128]{2,1,0:T(8,128)(2,1)S(1)}, bf16[8,80,128]{2,1,0:T(8,128)(2,1)S(1)}, u32[]{:S(2)}, u32[]{:S(2)}) collective-permute-start(bf16[8,80,128]{2,1,0:T(8,128)(2,1)S(1)} %select_convert_fusion.1.refs_0_), channel_id=1, source_target_pairs={{0,2},{1,3},{2,0},{3,1},{4,6},{5,7},{6,4},{7,5},{8,10},{9,11},{10,... | collective-permute-start | bytes 491528 | tf_op jit(solution)/shard_map/ppermute | solution.py:24
  316.8 3.0 collective-permute-done.33
  319.9 6.4 %collective-permute-done.36.refs_4_ = bf16[8,80,128]{2,1,0:T(8,128)(2,1)S(1)} collective-permute-done((bf16[8,80,128]{2,1,0:T(8,128)(2,1)S(1)}, bf16[8,80,128]{2,1,0:T(8,128)(2,1)S(1)}, u32[]{:S(2)}, u32[]{:S(2)}) %collective-permute-start.36) | collective-permute-done | bytes 163872 | tf_op jit(solution)/shard_map/ppermute | solution.py:24
  326.5 1.4 collective-permute-start.40
  327.8 3.1 collective-permute-start.38
  330.9 4.6 %collective-permute-done.40.refs_7_ = bf16[8,80,128]{2,1,0:T(8,128)(2,1)S(1)} collective-permute-done((bf16[8,80,128]{2,1,0:T(8,128)(2,1)S(1)}, bf16[8,80,128]{2,1,0:T(8,128)(2,1)S(1)}, u32[]{:S(2)}, u32[]{:S(2)}) %collective-permute-start.40) | collective-permute-done | bytes 163872 | tf_op jit(solution)/shard_map/ppermute | solution.py:24
  335.5 5.6 %collective-permute-done.39.refs_5_ = bf16[8,80,128]{2,1,0:T(8,128)(2,1)S(1)} collective-permute-done((bf16[8,80,128]{2,1,0:T(8,128)(2,1)S(1)}, bf16[8,80,128]{2,1,0:T(8,128)(2,1)S(1)}, u32[]{:S(2)}, u32[]{:S(2)}) %collective-permute-start.39) | collective-permute-done | bytes 163872 | tf_op jit(solution)/shard_map/ppermute | solution.py:24
  341.1 0.9 pad_maximum_fusion.3
  342.8 11.6 %block_weight_grad.1 = bf16[384,128,128]{2,1,0:T(8,128)(2,1)} custom-call(s32[384]{0:T(512)} %select_reduce_fusion.order_ref, bf16[24,80,128]{2,1,0:T(8,128)(2,1)} %get-tuple-element.70.refs_0_, bf16[24,80,128]{2,1,0:T(8,128)(2,1)} %get-tuple-element.71.refs_1_, bf16[24,80,128]{2,1,0:T(8,128)(2,1)} %get-tuple-element.48.refs_0_.refs_2_, ...), custom_call_target="tpu_custom_call" | custom-call | tf_op jit(solution)/shard_map/block_weight_grad/pallas_call | solution.py:236
  354.4 0.9 fusion.28
  355.3 2.0 fusion.27
  357.3 3.9 %expand_weight_grad.1 = bf16[128,8192]{1,0:T(8,128)(2,1)} custom-call(s32[8]{0:T(128)} %stack.42.columns_ref, bf16[160,128]{1,0:T(8,128)(2,1)} %documents_ref.1, bf16[8,80,128]{2,1,0:T(8,128)(2,1)} %copy-done.9, bf16[8,80,128]{2,1,0:T(8,128)(2,1)} %copy-done.8, bf16[8,80,128]{2,1,0:T(8,128)(2,1)} %copy-done.12, bf16[8,80,128]{2,1,0:T(8,128)(2,1)} %copy-done.15, ...), custom_call_target="tpu_custom_call" | custom-call | tf_op jit(solution)/shard_map/expand_weight_grad/pallas_call | solution.py:270
  (136 shorter events, 12.8 us)
Async XLA Ops:
  0.6 66.1 %copy-start.25 = (bf16[160,128]{1,0:T(8,128)(2,1)S(1)}, bf16[160,128]{1,0:T(8,128)(2,1)}, u32[]{:S(2)}) copy-start(bf16[160,128]{1,0:T(8,128)(2,1)} %documents_ref.1) | copy-start | bytes 122884
  0.6 75.7 %copy-start.26 = (s32[768,16]{0,1:T(8,128)S(1)}, s32[768,16]{0,1:T(8,128)}, u32[]{:S(2)}) copy-start(s32[768,16]{0,1:T(8,128)} %param.8) | copy-start | bytes 147460
  1.2 75.9 %copy-start.28 = (s32[160,8]{0,1:T(8,128)S(1)}, s32[160,8]{0,1:T(8,128)}, u32[]{:S(2)}) copy-start(s32[160,8]{0,1:T(8,128)} %param.9) | copy-start | bytes 15364
  66.7 12.2 %copy-start.20 = (bf16[128,2048]{1,0:T(8,128)(2,1)S(1)}, bf16[128,2048]{1,0:T(8,128)(2,1)}, u32[]{:S(2)}) copy-start(bf16[128,2048]{1,0:T(8,128)(2,1)} %get-tuple-element.37) | copy-start | bytes 1572868
  66.7 23.2 %collective-permute-start.5 = (bf16[160,128]{1,0:T(8,128)(2,1)S(1)}, bf16[160,128]{1,0:T(8,128)(2,1)S(1)}, u32[]{:S(2)}, u32[]{:S(2)}) collective-permute-start(bf16[160,128]{1,0:T(8,128)(2,1)S(1)} %copy-done.25), channel_id=1, source_target_pairs={{0,6},{1,7},{2,4},{3,5},{4,2},{5,3},{6,0},{7,1},{8,14},{9,15},{10,... | collective-permute-start | bytes 122888 | tf_op jit(solution)/shard_map/ppermute | solution.py:24
  71.9 29.7 %collective-permute-start.3 = (bf16[160,128]{1,0:T(8,128)(2,1)S(1)}, bf16[160,128]{1,0:T(8,128)(2,1)S(1)}, u32[]{:S(2)}, u32[]{:S(2)}) collective-permute-start(bf16[160,128]{1,0:T(8,128)(2,1)S(1)} %copy-done.25), channel_id=1, source_target_pairs={{0,4},{1,5},{2,6},{3,7},{4,0},{5,1},{6,2},{7,3},{8,12},{9,13},{10,... | collective-permute-start | bytes 122888 | tf_op jit(solution)/shard_map/ppermute | solution.py:24
  71.9 9.4 %collective-permute-start.1 = (bf16[160,128]{1,0:T(8,128)(2,1)S(1)}, bf16[160,128]{1,0:T(8,128)(2,1)S(1)}, u32[]{:S(2)}, u32[]{:S(2)}) collective-permute-start(bf16[160,128]{1,0:T(8,128)(2,1)S(1)} %copy-done.25), channel_id=1, source_target_pairs={{0,2},{1,3},{2,0},{3,1},{4,6},{5,7},{6,4},{7,5},{8,10},{9,11},{10,... | collective-permute-start | bytes 122888 | tf_op jit(solution)/shard_map/ppermute | solution.py:24
  72.5 17.1 %collective-permute-start = (bf16[128,2048]{1,0:T(8,128)(2,1)}, bf16[128,2048]{1,0:T(8,128)(2,1)S(1)}, u32[]{:S(2)}, u32[]{:S(2)}) collective-permute-start(bf16[128,2048]{1,0:T(8,128)(2,1)} %get-tuple-element.38), channel_id=1, source_target_pairs={{0,2},{1,3},{2,0},{3,1},{4,6},{5,7},{6,4},{7,5},{8,10},{9,11},{10,... | collective-permute-start | bytes 1572872 | tf_op jit(solution)/shard_map/ppermute | solution.py:24
  73.9 27.3 %collective-permute-start.4 = (bf16[128,2048]{1,0:T(8,128)(2,1)}, bf16[128,2048]{1,0:T(8,128)(2,1)S(1)}, u32[]{:S(2)}, u32[]{:S(2)}) collective-permute-start(bf16[128,2048]{1,0:T(8,128)(2,1)} %get-tuple-element.41), channel_id=1, source_target_pairs={{0,6},{1,7},{2,4},{3,5},{4,2},{5,3},{6,0},{7,1},{8,14},{9,15},{10,... | collective-permute-start | bytes 1572872 | tf_op jit(solution)/shard_map/ppermute | solution.py:24
  77.6 12.3 %copy-start.27 = (s32[384]{0:T(512)}, s32[384]{0:T(512)S(1)}, u32[]{:S(2)}) copy-start(s32[384]{0:T(512)S(1)} %select_reduce_fusion.1.position_ref) | copy-start | bytes 4612
  81.3 40.4 %collective-permute-start.2 = (bf16[128,2048]{1,0:T(8,128)(2,1)}, bf16[128,2048]{1,0:T(8,128)(2,1)S(1)}, u32[]{:S(2)}, u32[]{:S(2)}) collective-permute-start(bf16[128,2048]{1,0:T(8,128)(2,1)} %get-tuple-element.40), channel_id=1, source_target_pairs={{0,4},{1,5},{2,6},{3,7},{4,0},{5,1},{6,2},{7,3},{8,12},{9,13},{10,... | collective-permute-start | bytes 1572872 | tf_op jit(solution)/shard_map/ppermute | solution.py:24
  122.1 2.2 collective-permute-start.6
  124.4 9.1 %collective-permute-start.9 = (bf16[8,80,128]{2,1,0:T(8,128)(2,1)S(1)}, bf16[8,80,128]{2,1,0:T(8,128)(2,1)S(1)}, u32[]{:S(2)}, u32[]{:S(2)}) collective-permute-start(bf16[8,80,128]{2,1,0:T(8,128)(2,1)S(1)} %get-tuple-element.87), channel_id=1, source_target_pairs={{0,6},{1,7},{2,4},{3,5},{4,2},{5,3},{6,0},{7,1},{8,14},{9,15},{10,... | collective-permute-start | bytes 491528 | tf_op jit(solution)/shard_map/ppermute | solution.py:24
  126.9 13.5 %collective-permute-start.8 = (bf16[8,80,128]{2,1,0:T(8,128)(2,1)S(1)}, bf16[8,80,128]{2,1,0:T(8,128)(2,1)S(1)}, u32[]{:S(2)}, u32[]{:S(2)}) collective-permute-start(bf16[8,80,128]{2,1,0:T(8,128)(2,1)S(1)} %get-tuple-element.87), channel_id=1, source_target_pairs={{0,4},{1,5},{2,6},{3,7},{4,0},{5,1},{6,2},{7,3},{8,12},{9,13},{10,... | collective-permute-start | bytes 491528 | tf_op jit(solution)/shard_map/ppermute | solution.py:24
  126.9 13.5 %collective-permute-start.7 = (bf16[8,80,128]{2,1,0:T(8,128)(2,1)S(1)}, bf16[8,80,128]{2,1,0:T(8,128)(2,1)S(1)}, u32[]{:S(2)}, u32[]{:S(2)}) collective-permute-start(bf16[8,80,128]{2,1,0:T(8,128)(2,1)S(1)} %get-tuple-element.87), channel_id=1, source_target_pairs={{0,2},{1,3},{2,0},{3,1},{4,6},{5,7},{6,4},{7,5},{8,10},{9,11},{10,... | collective-permute-start | bytes 491528 | tf_op jit(solution)/shard_map/ppermute | solution.py:24
  140.6 2.2 collective-permute-start.10
  140.6 10.2 %collective-permute-start.23 = (bf16[8,80,128]{2,1,0:T(8,128)(2,1)S(1)}, bf16[8,80,128]{2,1,0:T(8,128)(2,1)S(1)}, u32[]{:S(2)}, u32[]{:S(2)}) collective-permute-start(bf16[8,80,128]{2,1,0:T(8,128)(2,1)S(1)} %get-tuple-element.86), channel_id=1, source_target_pairs={{0,6},{1,7},{2,4},{3,5},{4,2},{5,3},{6,0},{7,1},{8,14},{9,15},{10,... | collective-permute-start | bytes 491528 | tf_op jit(solution)/shard_map/ppermute | solution.py:24
  147.3 14.3 %collective-permute-start.11 = (bf16[24,80,128]{2,1,0:T(8,128)(2,1)}, bf16[24,80,128]{2,1,0:T(8,128)(2,1)S(1)}, u32[]{:S(2)}, u32[]{:S(2)}) collective-permute-start(bf16[24,80,128]{2,1,0:T(8,128)(2,1)} %get-tuple-element.49), channel_id=1, source_target_pairs={{0,8},{8,0},{16,24},{24,16},{1,9},{9,1},{17,25},{25,17},{2,10},{10... | collective-permute-start | bytes 1474568 | tf_op jit(solution)/shard_map/ppermute | solution.py:33
  148.8 23.7 %collective-permute-start.12 = (bf16[24,80,128]{2,1,0:T(8,128)(2,1)}, bf16[24,80,128]{2,1,0:T(8,128)(2,1)S(1)}, u32[]{:S(2)}, u32[]{:S(2)}) collective-permute-start(bf16[24,80,128]{2,1,0:T(8,128)(2,1)} %get-tuple-element.50), channel_id=1, source_target_pairs={{0,16},{8,24},{16,0},{24,8},{1,17},{9,25},{17,1},{25,9},{2,18},{10... | collective-permute-start | bytes 1474568 | tf_op jit(solution)/shard_map/ppermute | solution.py:33
  150.4 22.2 %collective-permute-start.13 = (bf16[24,80,128]{2,1,0:T(8,128)(2,1)}, bf16[24,80,128]{2,1,0:T(8,128)(2,1)S(1)}, u32[]{:S(2)}, u32[]{:S(2)}) collective-permute-start(bf16[24,80,128]{2,1,0:T(8,128)(2,1)} %get-tuple-element.51), channel_id=1, source_target_pairs={{0,24},{8,16},{16,8},{24,0},{1,25},{9,17},{17,9},{25,1},{2,26},{10... | collective-permute-start | bytes 1474568 | tf_op jit(solution)/shard_map/ppermute | solution.py:33
  150.8 9.1 %collective-permute-start.22 = (bf16[8,80,128]{2,1,0:T(8,128)(2,1)S(1)}, bf16[8,80,128]{2,1,0:T(8,128)(2,1)S(1)}, u32[]{:S(2)}, u32[]{:S(2)}) collective-permute-start(bf16[8,80,128]{2,1,0:T(8,128)(2,1)S(1)} %get-tuple-element.86), channel_id=1, source_target_pairs={{0,4},{1,5},{2,6},{3,7},{4,0},{5,1},{6,2},{7,3},{8,12},{9,13},{10,... | collective-permute-start | bytes 491528 | tf_op jit(solution)/shard_map/ppermute | solution.py:24
  150.8 9.3 %collective-permute-start.21 = (bf16[8,80,128]{2,1,0:T(8,128)(2,1)S(1)}, bf16[8,80,128]{2,1,0:T(8,128)(2,1)S(1)}, u32[]{:S(2)}, u32[]{:S(2)}) collective-permute-start(bf16[8,80,128]{2,1,0:T(8,128)(2,1)S(1)} %get-tuple-element.86), channel_id=1, source_target_pairs={{0,2},{1,3},{2,0},{3,1},{4,6},{5,7},{6,4},{7,5},{8,10},{9,11},{10,... | collective-permute-start | bytes 491528 | tf_op jit(solution)/shard_map/ppermute | solution.py:24
  160.2 31.0 %copy-start = (bf16[32,80,128]{2,1,0:T(8,128)(2,1)}, bf16[32,80,128]{2,1,0:T(8,128)(2,1)S(1)}, u32[]{:S(2)}) copy-start(bf16[32,80,128]{2,1,0:T(8,128)(2,1)S(1)} %pad_maximum_fusion.1.refs_0_) | copy-start | bytes 1966084
  160.2 34.5 %collective-permute-start.24 = (bf16[32,80,128]{2,1,0:T(8,128)(2,1)S(1)}, bf16[32,80,128]{2,1,0:T(8,128)(2,1)S(1)}, u32[]{:S(2)}, u32[]{:S(2)}) collective-permute-start(bf16[32,80,128]{2,1,0:T(8,128)(2,1)S(1)} %pad_maximum_fusion.1.refs_0_), channel_id=1, source_target_pairs={{0,1},{1,0},{2,3},{3,2},{4,5},{5,4},{6,7},{7,6},{8,9},{9,8},{10,11... | collective-permute-start | bytes 1966088 | tf_op jit(solution)/shard_map/ppermute | solution.py:29
  161.7 10.9 %copy-start.2 = (bf16[24,80,128]{2,1,0:T(8,128)(2,1)}, bf16[24,80,128]{2,1,0:T(8,128)(2,1)S(1)}, u32[]{:S(2)}) copy-start(bf16[24,80,128]{2,1,0:T(8,128)(2,1)S(1)} %collective-permute-done.11.refs_1_.refs_3_) | copy-start | bytes 1474564
  191.2 14.4 %collective-permute-start.14 = (bf16[24,80,128]{2,1,0:T(8,128)(2,1)}, bf16[24,80,128]{2,1,0:T(8,128)(2,1)S(1)}, u32[]{:S(2)}, u32[]{:S(2)}) collective-permute-start(bf16[24,80,128]{2,1,0:T(8,128)(2,1)} %get-tuple-element.53), channel_id=1, source_target_pairs={{0,8},{8,0},{16,24},{24,16},{1,9},{9,1},{17,25},{25,17},{2,10},{10... | collective-permute-start | bytes 1474568 | tf_op jit(solution)/shard_map/ppermute | solution.py:33
  192.3 24.9 %collective-permute-start.15 = (bf16[24,80,128]{2,1,0:T(8,128)(2,1)}, bf16[24,80,128]{2,1,0:T(8,128)(2,1)}, u32[]{:S(2)}, u32[]{:S(2)}) collective-permute-start(bf16[24,80,128]{2,1,0:T(8,128)(2,1)} %get-tuple-element.54), channel_id=1, source_target_pairs={{0,16},{8,24},{16,0},{24,8},{1,17},{9,25},{17,1},{25,9},{2,18},{10... | collective-permute-start | bytes 1474568 | tf_op jit(solution)/shard_map/ppermute | solution.py:33
  193.4 23.9 %collective-permute-start.16 = (bf16[24,80,128]{2,1,0:T(8,128)(2,1)}, bf16[24,80,128]{2,1,0:T(8,128)(2,1)}, u32[]{:S(2)}, u32[]{:S(2)}) collective-permute-start(bf16[24,80,128]{2,1,0:T(8,128)(2,1)} %get-tuple-element.55), channel_id=1, source_target_pairs={{0,24},{8,16},{16,8},{24,0},{1,25},{9,17},{17,9},{25,1},{2,26},{10... | collective-permute-start | bytes 1474568 | tf_op jit(solution)/shard_map/ppermute | solution.py:33
  199.1 27.5 %collective-permute-start.25 = (bf16[24,80,128]{2,1,0:T(8,128)(2,1)}, bf16[24,80,128]{2,1,0:T(8,128)(2,1)S(1)}, u32[]{:S(2)}, u32[]{:S(2)}) collective-permute-start(bf16[24,80,128]{2,1,0:T(8,128)(2,1)} %get-tuple-element.60), channel_id=1, source_target_pairs={{0,8},{8,0},{16,24},{24,16},{1,9},{9,1},{17,25},{25,17},{2,10},{10... | collective-permute-start | bytes 1474568 | tf_op jit(solution)/shard_map/ppermute | solution.py:33
  200.2 27.5 %collective-permute-start.26 = (bf16[24,80,128]{2,1,0:T(8,128)(2,1)}, bf16[24,80,128]{2,1,0:T(8,128)(2,1)S(1)}, u32[]{:S(2)}, u32[]{:S(2)}) collective-permute-start(bf16[24,80,128]{2,1,0:T(8,128)(2,1)} %get-tuple-element.61), channel_id=1, source_target_pairs={{0,16},{8,24},{16,0},{24,8},{1,17},{9,25},{17,1},{25,9},{2,18},{10... | collective-permute-start | bytes 1474568 | tf_op jit(solution)/shard_map/ppermute | solution.py:33
  205.6 11.7 %copy-start.21 = (bf16[24,80,128]{2,1,0:T(8,128)(2,1)}, bf16[24,80,128]{2,1,0:T(8,128)(2,1)S(1)}, u32[]{:S(2)}) copy-start(bf16[24,80,128]{2,1,0:T(8,128)(2,1)S(1)} %collective-permute-done.14.refs_1_) | copy-start | bytes 1474564
  205.6 30.7 %collective-permute-start.27 = (bf16[24,80,128]{2,1,0:T(8,128)(2,1)}, bf16[24,80,128]{2,1,0:T(8,128)(2,1)S(1)}, u32[]{:S(2)}, u32[]{:S(2)}) collective-permute-start(bf16[24,80,128]{2,1,0:T(8,128)(2,1)} %get-tuple-element.62), channel_id=1, source_target_pairs={{0,24},{8,16},{16,8},{24,0},{1,25},{9,17},{17,9},{25,1},{2,26},{10... | collective-permute-start | bytes 1474568 | tf_op jit(solution)/shard_map/ppermute | solution.py:33
  220.6 60.8 %collective-permute-start.17 = (bf16[32,80,128]{2,1,0:T(8,128)(2,1)}, bf16[32,80,128]{2,1,0:T(8,128)(2,1)S(1)}, u32[]{:S(2)}, u32[]{:S(2)}) collective-permute-start(bf16[32,80,128]{2,1,0:T(8,128)(2,1)} %get-tuple-element.57), channel_id=1, source_target_pairs={{0,1},{1,0},{2,3},{3,2},{4,5},{5,4},{6,7},{7,6},{8,9},{9,8},{10,11... | collective-permute-start | bytes 1966088 | tf_op jit(solution)/shard_map/ppermute | solution.py:29
  226.7 9.6 %copy-start.5 = (bf16[24,80,128]{2,1,0:T(8,128)(2,1)}, bf16[24,80,128]{2,1,0:T(8,128)(2,1)S(1)}, u32[]{:S(2)}) copy-start(bf16[24,80,128]{2,1,0:T(8,128)(2,1)S(1)} %collective-permute-done.25.refs_1_.refs_7_) | copy-start | bytes 1474564
  227.7 8.6 %copy-start.6 = (bf16[24,80,128]{2,1,0:T(8,128)(2,1)}, bf16[24,80,128]{2,1,0:T(8,128)(2,1)S(1)}, u32[]{:S(2)}) copy-start(bf16[24,80,128]{2,1,0:T(8,128)(2,1)S(1)} %collective-permute-done.26.refs_2_.refs_8_) | copy-start | bytes 1474564
  254.8 26.6 %copy-start.18 = (bf16[32,80,128]{2,1,0:T(8,128)(2,1)S(1)}, bf16[32,80,128]{2,1,0:T(8,128)(2,1)}, u32[]{:S(2)}) copy-start(bf16[32,80,128]{2,1,0:T(8,128)(2,1)} %get-tuple-element.56) | copy-start | bytes 1966084
  254.8 14.4 %collective-permute-start.28 = (bf16[24,80,128]{2,1,0:T(8,128)(2,1)}, bf16[24,80,128]{2,1,0:T(8,128)(2,1)S(1)}, u32[]{:S(2)}, u32[]{:S(2)}) collective-permute-start(bf16[24,80,128]{2,1,0:T(8,128)(2,1)} %get-tuple-element.64), channel_id=1, source_target_pairs={{0,8},{8,0},{16,24},{24,16},{1,9},{9,1},{17,25},{25,17},{2,10},{10... | collective-permute-start | bytes 1474568 | tf_op jit(solution)/shard_map/ppermute | solution.py:33
  255.6 21.4 %collective-permute-start.29 = (bf16[24,80,128]{2,1,0:T(8,128)(2,1)}, bf16[24,80,128]{2,1,0:T(8,128)(2,1)S(1)}, u32[]{:S(2)}, u32[]{:S(2)}) collective-permute-start(bf16[24,80,128]{2,1,0:T(8,128)(2,1)} %get-tuple-element.65), channel_id=1, source_target_pairs={{0,16},{8,24},{16,0},{24,8},{1,17},{9,25},{17,1},{25,9},{2,18},{10... | collective-permute-start | bytes 1474568 | tf_op jit(solution)/shard_map/ppermute | solution.py:33
  257.3 19.7 %collective-permute-start.30 = (bf16[24,80,128]{2,1,0:T(8,128)(2,1)}, bf16[24,80,128]{2,1,0:T(8,128)(2,1)S(1)}, u32[]{:S(2)}, u32[]{:S(2)}) collective-permute-start(bf16[24,80,128]{2,1,0:T(8,128)(2,1)} %get-tuple-element.66), channel_id=1, source_target_pairs={{0,24},{8,16},{16,8},{24,0},{1,25},{9,17},{17,9},{25,1},{2,26},{10... | collective-permute-start | bytes 1474568 | tf_op jit(solution)/shard_map/ppermute | solution.py:33
  269.2 7.9 %copy-start.22 = (bf16[24,80,128]{2,1,0:T(8,128)(2,1)}, bf16[24,80,128]{2,1,0:T(8,128)(2,1)S(1)}, u32[]{:S(2)}) copy-start(bf16[24,80,128]{2,1,0:T(8,128)(2,1)S(1)} %collective-permute-done.28.refs_1_) | copy-start | bytes 1474564
  281.4 4.7 %collective-permute-start.31 = (bf16[32,80,128]{2,1,0:T(8,128)(2,1)}, bf16[32,80,128]{2,1,0:T(8,128)(2,1)S(1)}, u32[]{:S(2)}, u32[]{:S(2)}) collective-permute-start(bf16[32,80,128]{2,1,0:T(8,128)(2,1)} %get-tuple-element.68), channel_id=1, source_target_pairs={{0,1},{1,0},{2,3},{3,2},{4,5},{5,4},{6,7},{7,6},{8,9},{9,8},{10,11... | collective-permute-start | bytes 1966088 | tf_op jit(solution)/shard_map/ppermute | solution.py:29
  281.4 4.7 %copy-start.19 = (bf16[32,80,128]{2,1,0:T(8,128)(2,1)S(1)}, bf16[32,80,128]{2,1,0:T(8,128)(2,1)}, u32[]{:S(2)}) copy-start(bf16[32,80,128]{2,1,0:T(8,128)(2,1)} %get-tuple-element.67) | copy-start | bytes 1966084
  281.7 9.0 %collective-permute-start.18 = (bf16[8,80,128]{2,1,0:T(8,128)(2,1)S(1)}, bf16[8,80,128]{2,1,0:T(8,128)(2,1)S(1)}, u32[]{:S(2)}, u32[]{:S(2)}) collective-permute-start(bf16[8,80,128]{2,1,0:T(8,128)(2,1)S(1)} %get-tuple-element.83), channel_id=1, source_target_pairs={{0,6},{1,7},{2,4},{3,5},{4,2},{5,3},{6,0},{7,1},{8,14},{9,15},{10,... | collective-permute-start | bytes 491528 | tf_op jit(solution)/shard_map/ppermute | solution.py:24
  283.5 12.9 %collective-permute-start.20 = (bf16[8,80,128]{2,1,0:T(8,128)(2,1)S(1)}, bf16[8,80,128]{2,1,0:T(8,128)(2,1)S(1)}, u32[]{:S(2)}, u32[]{:S(2)}) collective-permute-start(bf16[8,80,128]{2,1,0:T(8,128)(2,1)S(1)} %get-tuple-element.84), channel_id=1, source_target_pairs={{0,2},{1,3},{2,0},{3,1},{4,6},{5,7},{6,4},{7,5},{8,10},{9,11},{10,... | collective-permute-start | bytes 491528 | tf_op jit(solution)/shard_map/ppermute | solution.py:24
  283.5 18.6 %collective-permute-start.19 = (bf16[8,80,128]{2,1,0:T(8,128)(2,1)S(1)}, bf16[8,80,128]{2,1,0:T(8,128)(2,1)S(1)}, u32[]{:S(2)}, u32[]{:S(2)}) collective-permute-start(bf16[8,80,128]{2,1,0:T(8,128)(2,1)S(1)} %get-tuple-element.85), channel_id=1, source_target_pairs={{0,4},{1,5},{2,6},{3,7},{4,0},{5,1},{6,2},{7,3},{8,12},{9,13},{10,... | collective-permute-start | bytes 491528 | tf_op jit(solution)/shard_map/ppermute | solution.py:24
  286.4 17.2 %collective-permute-start.32 = (bf16[8,80,128]{2,1,0:T(8,128)(2,1)S(1)}, bf16[8,80,128]{2,1,0:T(8,128)(2,1)S(1)}, u32[]{:S(2)}, u32[]{:S(2)}) collective-permute-start(bf16[8,80,128]{2,1,0:T(8,128)(2,1)S(1)} %get-tuple-element.80), channel_id=1, source_target_pairs={{0,6},{1,7},{2,4},{3,5},{4,2},{5,3},{6,0},{7,1},{8,14},{9,15},{10,... | collective-permute-start | bytes 491528 | tf_op jit(solution)/shard_map/ppermute | solution.py:24
  288.2 28.6 %collective-permute-start.34 = (bf16[8,80,128]{2,1,0:T(8,128)(2,1)S(1)}, bf16[8,80,128]{2,1,0:T(8,128)(2,1)S(1)}, u32[]{:S(2)}, u32[]{:S(2)}) collective-permute-start(bf16[8,80,128]{2,1,0:T(8,128)(2,1)S(1)} %get-tuple-element.81), channel_id=1, source_target_pairs={{0,2},{1,3},{2,0},{3,1},{4,6},{5,7},{6,4},{7,5},{8,10},{9,11},{10,... | collective-permute-start | bytes 491528 | tf_op jit(solution)/shard_map/ppermute | solution.py:24
  290.7 29.1 %collective-permute-start.33 = (bf16[8,80,128]{2,1,0:T(8,128)(2,1)S(1)}, bf16[8,80,128]{2,1,0:T(8,128)(2,1)S(1)}, u32[]{:S(2)}, u32[]{:S(2)}) collective-permute-start(bf16[8,80,128]{2,1,0:T(8,128)(2,1)S(1)} %get-tuple-element.82), channel_id=1, source_target_pairs={{0,4},{1,5},{2,6},{3,7},{4,0},{5,1},{6,2},{7,3},{8,12},{9,13},{10,... | collective-permute-start | bytes 491528 | tf_op jit(solution)/shard_map/ppermute | solution.py:24
  302.3 24.2 %copy-start.9 = (bf16[8,80,128]{2,1,0:T(8,128)(2,1)}, bf16[8,80,128]{2,1,0:T(8,128)(2,1)S(1)}, u32[]{:S(2)}) copy-start(bf16[8,80,128]{2,1,0:T(8,128)(2,1)S(1)} %select_convert_fusion.1.refs_0_) | copy-start | bytes 491524
  302.3 17.6 %collective-permute-start.37 = (bf16[8,80,128]{2,1,0:T(8,128)(2,1)S(1)}, bf16[8,80,128]{2,1,0:T(8,128)(2,1)S(1)}, u32[]{:S(2)}, u32[]{:S(2)}) collective-permute-start(bf16[8,80,128]{2,1,0:T(8,128)(2,1)S(1)} %select_convert_fusion.1.refs_0_), channel_id=1, source_target_pairs={{0,6},{1,7},{2,4},{3,5},{4,2},{5,3},{6,0},{7,1},{8,14},{9,15},{10,... | collective-permute-start | bytes 491528 | tf_op jit(solution)/shard_map/ppermute | solution.py:24
  303.6 22.7 %collective-permute-start.36 = (bf16[8,80,128]{2,1,0:T(8,128)(2,1)S(1)}, bf16[8,80,128]{2,1,0:T(8,128)(2,1)S(1)}, u32[]{:S(2)}, u32[]{:S(2)}) collective-permute-start(bf16[8,80,128]{2,1,0:T(8,128)(2,1)S(1)} %select_convert_fusion.1.refs_0_), channel_id=1, source_target_pairs={{0,4},{1,5},{2,6},{3,7},{4,0},{5,1},{6,2},{7,3},{8,12},{9,13},{10,... | collective-permute-start | bytes 491528 | tf_op jit(solution)/shard_map/ppermute | solution.py:24
  303.6 22.7 %collective-permute-start.35 = (bf16[8,80,128]{2,1,0:T(8,128)(2,1)S(1)}, bf16[8,80,128]{2,1,0:T(8,128)(2,1)S(1)}, u32[]{:S(2)}, u32[]{:S(2)}) collective-permute-start(bf16[8,80,128]{2,1,0:T(8,128)(2,1)S(1)} %select_convert_fusion.1.refs_0_), channel_id=1, source_target_pairs={{0,2},{1,3},{2,0},{3,1},{4,6},{5,7},{6,4},{7,5},{8,10},{9,11},{10,... | collective-permute-start | bytes 491528 | tf_op jit(solution)/shard_map/ppermute | solution.py:24
  319.9 22.2 %copy-start.10 = (bf16[8,80,128]{2,1,0:T(8,128)(2,1)}, bf16[8,80,128]{2,1,0:T(8,128)(2,1)S(1)}, u32[]{:S(2)}) copy-start(bf16[8,80,128]{2,1,0:T(8,128)(2,1)S(1)} %collective-permute-done.37.refs_6_) | copy-start | bytes 491524
  326.3 15.8 %copy-start.11 = (bf16[8,80,128]{2,1,0:T(8,128)(2,1)}, bf16[8,80,128]{2,1,0:T(8,128)(2,1)S(1)}, u32[]{:S(2)}) copy-start(bf16[8,80,128]{2,1,0:T(8,128)(2,1)S(1)} %collective-permute-done.36.refs_4_) | copy-start | bytes 491524
  326.3 15.8 %copy-start.12 = (bf16[8,80,128]{2,1,0:T(8,128)(2,1)}, bf16[8,80,128]{2,1,0:T(8,128)(2,1)S(1)}, u32[]{:S(2)}) copy-start(bf16[8,80,128]{2,1,0:T(8,128)(2,1)S(1)} %collective-permute-done.35.refs_2_) | copy-start | bytes 491524
  326.5 27.9 %copy-start.8 = (bf16[8,80,128]{2,1,0:T(8,128)(2,1)}, bf16[8,80,128]{2,1,0:T(8,128)(2,1)S(1)}, u32[]{:S(2)}) copy-start(bf16[8,80,128]{2,1,0:T(8,128)(2,1)S(1)} %select_convert_fusion.refs_1_) | copy-start | bytes 491524
  326.5 9.1 %collective-permute-start.40 = (bf16[8,80,128]{2,1,0:T(8,128)(2,1)S(1)}, bf16[8,80,128]{2,1,0:T(8,128)(2,1)S(1)}, u32[]{:S(2)}, u32[]{:S(2)}) collective-permute-start(bf16[8,80,128]{2,1,0:T(8,128)(2,1)S(1)} %select_convert_fusion.refs_1_), channel_id=1, source_target_pairs={{0,6},{1,7},{2,4},{3,5},{4,2},{5,3},{6,0},{7,1},{8,14},{9,15},{10,... | collective-permute-start | bytes 491528 | tf_op jit(solution)/shard_map/ppermute | solution.py:24
  327.8 13.3 %collective-permute-start.39 = (bf16[8,80,128]{2,1,0:T(8,128)(2,1)S(1)}, bf16[8,80,128]{2,1,0:T(8,128)(2,1)S(1)}, u32[]{:S(2)}, u32[]{:S(2)}) collective-permute-start(bf16[8,80,128]{2,1,0:T(8,128)(2,1)S(1)} %select_convert_fusion.refs_1_), channel_id=1, source_target_pairs={{0,4},{1,5},{2,6},{3,7},{4,0},{5,1},{6,2},{7,3},{8,12},{9,13},{10,... | collective-permute-start | bytes 491528 | tf_op jit(solution)/shard_map/ppermute | solution.py:24
  327.8 13.3 %collective-permute-start.38 = (bf16[8,80,128]{2,1,0:T(8,128)(2,1)S(1)}, bf16[8,80,128]{2,1,0:T(8,128)(2,1)S(1)}, u32[]{:S(2)}, u32[]{:S(2)}) collective-permute-start(bf16[8,80,128]{2,1,0:T(8,128)(2,1)S(1)} %select_convert_fusion.refs_1_), channel_id=1, source_target_pairs={{0,2},{1,3},{2,0},{3,1},{4,6},{5,7},{6,4},{7,5},{8,10},{9,11},{10,... | collective-permute-start | bytes 491528 | tf_op jit(solution)/shard_map/ppermute | solution.py:24
  330.9 23.5 %collective-permute-start.41 = (bf16[32,80,128]{2,1,0:T(8,128)(2,1)S(1)}, bf16[32,80,128]{2,1,0:T(8,128)(2,1)S(1)}, u32[]{:S(2)}, u32[]{:S(2)}) collective-permute-start(bf16[32,80,128]{2,1,0:T(8,128)(2,1)S(1)} %pad_maximum_fusion.2), channel_id=1, source_target_pairs={{0,1},{1,0},{2,3},{3,2},{4,5},{5,4},{6,7},{7,6},{8,9},{9,8},{10,11... | collective-permute-start | bytes 1966088 | tf_op jit(solution)/shard_map/ppermute | solution.py:29
  335.5 18.9 %copy-start.13 = (bf16[8,80,128]{2,1,0:T(8,128)(2,1)}, bf16[8,80,128]{2,1,0:T(8,128)(2,1)S(1)}, u32[]{:S(2)}) copy-start(bf16[8,80,128]{2,1,0:T(8,128)(2,1)S(1)} %collective-permute-done.40.refs_7_) | copy-start | bytes 491524
  341.1 13.3 %copy-start.14 = (bf16[8,80,128]{2,1,0:T(8,128)(2,1)}, bf16[8,80,128]{2,1,0:T(8,128)(2,1)S(1)}, u32[]{:S(2)}) copy-start(bf16[8,80,128]{2,1,0:T(8,128)(2,1)S(1)} %collective-permute-done.39.refs_5_) | copy-start | bytes 491524
  341.1 13.3 %copy-start.15 = (bf16[8,80,128]{2,1,0:T(8,128)(2,1)}, bf16[8,80,128]{2,1,0:T(8,128)(2,1)S(1)}, u32[]{:S(2)}) copy-start(bf16[8,80,128]{2,1,0:T(8,128)(2,1)S(1)} %collective-permute-done.38.refs_3_) | copy-start | bytes 491524
  342.1 13.2 %collective-permute-start.42 = (bf16[32,80,128]{2,1,0:T(8,128)(2,1)}, bf16[32,80,128]{2,1,0:T(8,128)(2,1)}, u32[]{:S(2)}, u32[]{:S(2)}) collective-permute-start(bf16[32,80,128]{2,1,0:T(8,128)(2,1)} %pad_maximum_fusion.3), channel_id=1, source_target_pairs={{0,1},{1,0},{2,3},{3,2},{4,5},{5,4},{6,7},{7,6},{8,9},{9,8},{10,11... | collective-permute-start | bytes 1966088 | tf_op jit(solution)/shard_map/ppermute | solution.py:29
  (8 other events, 8.2 us)

commit v3 on v2

--- a/solution.py
+++ b/solution.py
@@ -41,25 +41,15 @@
 def cut_columns(weight, starts, width):
     count = starts.shape[0]
 
-    def kernel(starts_ref, weight_hbm, *refs):
-        outs, sem = refs[:count], refs[count]
-        copies = [
-            pltpu.make_async_copy(
-                weight_hbm.at[:, pl.ds(pl.multiple_of(starts_ref[k], BLK), width)], out, sem.at[k]
-            )
-            for k, out in enumerate(outs)
-        ]
-        for copy in copies:
-            copy.start()
-        for copy in copies:
-            copy.wait()
+    def kernel(starts_ref, weight_ref, *outs):
+        for k, out in enumerate(outs):
+            out[...] = weight_ref[:, pl.ds(pl.multiple_of(starts_ref[k], BLK), width)]
 
     return pl.pallas_call(
         kernel,
         out_shape=[jax.ShapeDtypeStruct((weight.shape[0], width), weight.dtype)] * count,
-        in_specs=[SMEM, ANY],
-        out_specs=[ANY] * count,
-        scratch_shapes=[pltpu.SemaphoreType.DMA((count,))],
+        in_specs=[SMEM, VMEM],
+        out_specs=[VMEM] * count,
         name="cut_columns",
     )(starts, weight)
 
@@ -195,71 +185,63 @@
     return out[0], list(out[1:])
 
 
-def block_weight_grad(chunks, residuals, order, label_blocks, slots):
-    pieces = len(chunks)
-    count = len(chunks[0])
-    cap, _, blk = chunks[0][0].shape
-    uses = label_blocks * slots // (count * cap)
+def block_weight_grad(so_far, picked, residuals, order, label_blocks, slots):
+    pieces = len(picked)
+    cap, _, blk = picked[0].shape
+    uses = order.shape[0] // cap
+    earlier = [] if so_far is None else [so_far]
 
     def kernel(order_ref, *refs):
         residual_refs = refs[:pieces]
-        ins = refs[pieces : pieces + pieces * count]
-        out_ref = refs[pieces + pieces * count]
-        buffer, out_sem = refs[pieces + pieces * count + 1 :]
-        for q in range(count):
-            pools = [ins[i * count + q] for i in range(pieces)]
-
-            def step(j, carry):
-                k = q * cap + j
-                where = [order_ref[k * uses + u] for u in range(uses)]
-                rhs = jnp.concatenate(
-                    [
-                        jnp.concatenate([ref[w // slots] for w in where], axis=1)
-                        for ref in residual_refs
-                    ],
-                    axis=0,
-                )
-                lhs = jnp.concatenate([pool[j] for pool in pools], axis=0)
-                out = lax.dot_general(
-                    lhs, rhs, (((0,), (0,)), ((), ())), preferred_element_type=F32
-                ).astype(BF16)
-                for u in range(uses):
-                    buffer[k * uses + u] = out[:, u * blk : (u + 1) * blk]
-                    pltpu.make_async_copy(
-                        buffer.at[k * uses + u], out_ref.at[where[u]], out_sem
-                    ).start()
-                return carry
-
-            lax.fori_loop(0, cap, step, 0, unroll=UNROLL)
-        pltpu.make_async_copy(buffer, out_ref, out_sem).wait()
-
-    out = pl.pallas_call(
+        ins = refs[pieces : 2 * pieces]
+        out_ref, buffer, sem = refs[2 * pieces + len(earlier) :]
+
+        def step(k, carry):
+            where = [order_ref[k * uses + u] for u in range(uses)]
+            rhs = jnp.concatenate(
+                [
+                    jnp.concatenate([ref[w // slots] for w in where], axis=1)
+                    for ref in residual_refs
+                ],
+                axis=0,
+            )
+            lhs = jnp.concatenate([ref[k] for ref in ins], axis=0)
+            out = lax.dot_general(
+                lhs, rhs, (((0,), (0,)), ((), ())), preferred_element_type=F32
+            ).astype(BF16)
+            for u in range(uses):
+                buffer[k * uses + u] = out[:, u * blk : (u + 1) * blk]
+                pltpu.make_async_copy(buffer.at[k * uses + u], out_ref.at[where[u]], sem).start()
+            return carry
+
+        lax.fori_loop(0, cap, step, 0, unroll=UNROLL)
+        pltpu.make_async_copy(buffer, out_ref.at[pl.ds(0, cap * uses)], sem).wait()
+
+    return pl.pallas_call(
         kernel,
         out_shape=jax.ShapeDtypeStruct((label_blocks * slots, blk, blk), BF16),
-        in_specs=[SMEM] + [VMEM] * (pieces + pieces * count),
+        in_specs=[SMEM] + [VMEM] * (2 * pieces) + [ANY] * len(earlier),
         out_specs=ANY,
-        scratch_shapes=[
-            pltpu.VMEM((label_blocks * slots, blk, blk), BF16),
-            pltpu.SemaphoreType.DMA(()),
-        ],
+        input_output_aliases={1 + 2 * pieces: 0} if earlier else {},
+        scratch_shapes=[pltpu.VMEM((cap * uses, blk, blk), BF16), pltpu.SemaphoreType.DMA(())],
         name="block_weight_grad",
-    )(order, *residuals, *[part for chunk in chunks for part in chunk])
-    return out.reshape(label_blocks, slots, blk, blk)
-
-
-def expand_weight_grad(documents, groups, columns, width):
-    pieces = len(groups)
-    chunks = len(groups[0])
-    size, _, blk = groups[0][0].shape
+    )(order, *residuals, *picked, *earlier)
+
+
+def expand_weight_grad(documents, sides, columns, size, width):
+    chunks = len(sides[0])
+    pieces = sides[0][0].shape[0] // size
+    blk = sides[0][0].shape[2]
     _, rows = documents.shape
 
     def kernel(columns_ref, documents_ref, *refs):
         out_ref = refs[-1]
         lhs = documents_ref[...]
-        for i in range(pieces):
-            ins = refs[i * chunks : (i + 1) * chunks]
+        for i in range(len(sides) * pieces):
+            ins = refs[i // pieces * chunks : (i // pieces + 1) * chunks]
+            blocks = range(i % pieces * size, (i % pieces + 1) * size)
             rhs = jnp.concatenate(
-                [jnp.concatenate([ref[j] for ref in ins], axis=0) for j in range(size)], axis=1
+                [jnp.concatenate([ref[j] for ref in ins], axis=0) for j in blocks], axis=1
             )
             out = lax.dot_general(
                 lhs, rhs, (((0,), (0,)), ((), ())), preferred_element_type=F32
@@ -270,10 +252,10 @@
     return pl.pallas_call(
         kernel,
         out_shape=jax.ShapeDtypeStruct((rows, width), BF16),
-        in_specs=[SMEM, VMEM] + [VMEM] * (pieces * chunks),
+        in_specs=[SMEM, VMEM] + [VMEM] * (len(sides) * chunks),
         out_specs=VMEM,
         name="expand_weight_grad",
-    )(columns, documents, *[part for group in groups for part in group])
+    )(columns, documents, *[part for side in sides for part in side])
 
 
 def list_tables(feature_lists, feat_index, label_index, label_count, own_count, label_blocks, cap):
@@ -398,18 +380,25 @@
         gathered = jnp.concatenate(ring_gather(gradient), axis=0)
         gradients.append((gathered, swap_cores(gathered)))
 
-    grad_sparse = block_weight_grad(picked, residuals, order, label_blocks, slots)
-
-    groups, starts = [], []
-    for side in range(CORES):
-        for k in range(ring):
-            groups.append(
-                [g[side][k * own_blocks : (k + 1) * own_blocks] for g in gradients]
-            )
-            starts.append(
-                ((ring_index ^ k) * CORES + (core ^ side)) * own_blocks * BLK
-            )
-    grad_expand = expand_weight_grad(documents, groups, jnp.stack(starts), width)
+    grad_sparse = None
+    share = order.shape[0] // feat_count
+    for m in range(feat_count):
+        grad_sparse = block_weight_grad(
+            grad_sparse,
+            [parts[m] for parts in picked],
+            residuals,
+            order[m * share : (m + 1) * share],
+            label_blocks,
+            slots,
+        )
+    grad_sparse = grad_sparse.reshape(sparse_weight.shape)
+
+    places = jnp.arange(CORES * ring, dtype=jnp.int32)
+    owners = ((places % ring) ^ ring_index) * CORES + (places // ring ^ core)
+    sides = [[gradient[side] for gradient in gradients] for side in range(CORES)]
+    grad_expand = expand_weight_grad(
+        documents, sides, owners * (own_blocks * BLK), own_blocks, width
+    )
     return (grad_expand, grad_sparse)
 
 

time: 362 us -> 303 us (0.84)
  Pallas kernels: 130 us -> 73.6 us
    pallas_call x1, Pallas kernels: 65.5 us -> 3.07 us  [cut_columns(): pl.pallas_call(kernel, out_shape=[jax.ShapeDtypeStruct((weight.shape[0],...]
    pallas_call x1 -> x4, Pallas kernels: 11.6 us -> 17.3 us  [block_weight_grad(): pl.pallas_call(kernel, out_shape=jax.ShapeDtypeStruct((label_blocks * slo...]
  transfers between devices with their start and end apart: 43 -> 43, of which waited for: 25 -> 25; matrix products, arithmetic and copies ran while one was open for 2% -> 3% of each run, Pallas kernels for 17% -> 22%
where the time goes in v3:
time: 303 us
  waiting for transfers between devices  153 us (50%)
  Pallas kernels  73.6 us (24%)
  starting transfers between devices  59.5 us (20%)
  local copies, waits for them, and re-layouts  10.3 us (3%)
  other arithmetic  4.33 us (1%)
    ppermute x24, waiting for transfers between devices, ring_exchange(): lax.ppermute(x, 'label', [(i, i ^ flip * CORES) for i in range(count)])  90 us
    ppermute x12, waiting for transfers between devices, feat_exchange(): lax.ppermute(x, 'feat', [(i, i ^ flip) for i in range(lax.axis_size('feat...  60.2 us
    ppermute x24, starting transfers between devices, ring_exchange(): lax.ppermute(x, 'label', [(i, i ^ flip * CORES) for i in range(count)])  45 us
    pallas_call x2, Pallas kernels, residual_and_back(): pl.pallas_call(kernel, out_shape=[jax.ShapeDtypeStruct((label_blocks, doc...  35.4 us
    pallas_call x4, Pallas kernels, block_weight_grad(): pl.pallas_call(kernel, out_shape=jax.ShapeDtypeStruct((label_blocks * slo...  17.3 us
    ppermute x12, starting transfers between devices, feat_exchange(): lax.ppermute(x, 'feat', [(i, i ^ flip) for i in range(lax.axis_size('feat...  14.2 us
    pallas_call x2, Pallas kernels, select_blocks(): pl.pallas_call(kernel, out_shape=[jax.ShapeDtypeStruct((cap, docs, blk),...  7.44 us
    unnamed x54, local copies, waits for them, and re-layouts  7.15 us
  transfers between devices with their start and end apart: 43, of which 25 were waited for; matrix products, arithmetic and copies ran while one was open for 3% of the time, Pallas kernels for 22%

profile of v3, /device:TPU:0, one launch (start us, length us, event | category | flops | bytes accessed | tf_op | source)
XLA Modules:
  0.0 303.0 jit_solution(3198355901240800595)
XLA Ops:
  1.2 3.1 %cut_columns.1 = (bf16[128,2048]{1,0:T(8,128)(2,1)}, bf16[128,2048]{1,0:T(8,128)(2,1)}, bf16[128,2048]{1,0:T(8,128)(2,1)}, bf16[128,2048]{1,0:T(8,128)(2,1)}) custom-call(s32[4]{0:T(128)} %xor_multiply_fusion.starts_ref, bf16[128,8192]{1,0:T(8,128)(2,1)} %weight_ref.1), custom_call_target="tpu_custom_call" | custom-call | tf_op jit(solution)/shard_map/cut_columns/pallas_call | solution.py:48
  4.3 5.1 %collective-permute-start.5 = (bf16[160,128]{1,0:T(8,128)(2,1)S(1)}, bf16[160,128]{1,0:T(8,128)(2,1)S(1)}, u32[]{:S(2)}, u32[]{:S(2)}) collective-permute-start(bf16[160,128]{1,0:T(8,128)(2,1)S(1)} %copy-done.21), channel_id=1, source_target_pairs={{0,6},{1,7},{2,4},{3,5},{4,2},{5,3},{6,0},{7,1},{8,14},{9,15},{10,... | collective-permute-start | bytes 122888 | tf_op jit(solution)/shard_map/ppermute | solution.py:24
  10.0 1.4 collective-permute-start
  11.4 2.4 collective-permute-start.4
  19.4 7.7 %collective-permute-done = bf16[128,2048]{1,0:T(8,128)(2,1)S(1)} collective-permute-done((bf16[128,2048]{1,0:T(8,128)(2,1)}, bf16[128,2048]{1,0:T(8,128)(2,1)S(1)}, u32[]{:S(2)}, u32[]{:S(2)}) %collective-permute-start) | collective-permute-done | bytes 524320 | tf_op jit(solution)/shard_map/ppermute | solution.py:24
  27.4 11.3 %collective-permute-done.4 = bf16[128,2048]{1,0:T(8,128)(2,1)S(1)} collective-permute-done((bf16[128,2048]{1,0:T(8,128)(2,1)}, bf16[128,2048]{1,0:T(8,128)(2,1)S(1)}, u32[]{:S(2)}, u32[]{:S(2)}) %collective-permute-start.4) | collective-permute-done | bytes 524320 | tf_op jit(solution)/shard_map/ppermute | solution.py:24
  39.1 20.1 %collective-permute-done.2 = bf16[128,2048]{1,0:T(8,128)(2,1)S(1)} collective-permute-done((bf16[128,2048]{1,0:T(8,128)(2,1)}, bf16[128,2048]{1,0:T(8,128)(2,1)S(1)}, u32[]{:S(2)}, u32[]{:S(2)}) %collective-permute-start.2) | collective-permute-done | bytes 524320 | tf_op jit(solution)/shard_map/ppermute | solution.py:24
  59.7 2.1 collective-permute-done.6
  61.9 2.5 collective-permute-start.9
  64.4 1.9 collective-permute-start.7
  66.3 4.6 %collective-permute-done.9 = bf16[8,80,128]{2,1,0:T(8,128)(2,1)S(1)} collective-permute-done((bf16[8,80,128]{2,1,0:T(8,128)(2,1)S(1)}, bf16[8,80,128]{2,1,0:T(8,128)(2,1)S(1)}, u32[]{:S(2)}, u32[]{:S(2)}) %collective-permute-start.9) | collective-permute-done | bytes 163872 | tf_op jit(solution)/shard_map/ppermute | solution.py:24
  70.9 7.0 %collective-permute-done.8 = bf16[8,80,128]{2,1,0:T(8,128)(2,1)S(1)} collective-permute-done((bf16[8,80,128]{2,1,0:T(8,128)(2,1)S(1)}, bf16[8,80,128]{2,1,0:T(8,128)(2,1)S(1)}, u32[]{:S(2)}, u32[]{:S(2)}) %collective-permute-start.8) | collective-permute-done | bytes 163872 | tf_op jit(solution)/shard_map/ppermute | solution.py:24
  78.1 1.6 collective-permute-start.26
  80.2 0.8 copy-done.13
  81.1 3.8 %select_blocks.2 = (bf16[24,80,128]{2,1,0:T(8,128)(2,1)}, bf16[24,80,128]{2,1,0:T(8,128)(2,1)}, bf16[24,80,128]{2,1,0:T(8,128)(2,1)}, bf16[24,80,128]{2,1,0:T(8,128)(2,1)}) custom-call(s32[96]{0:T(128)} %reshape.191.index_ref, bf16[32,80,128]{2,1,0:T(8,128)(2,1)} %copy-done.3, bf16[32,80,128]{2,1,0:T(8,128)(2,1)} %copy-done.13), custom_call_target="tpu_custom_call" | custom-call | tf_op jit(solution)/shard_map/select_blocks/pallas_call | solution.py:76
  84.9 1.5 collective-permute-start.11
  86.4 1.5 collective-permute-start.12
  88.4 2.4 collective-permute-start.24
  90.7 6.8 %collective-permute-done.25 = bf16[8,80,128]{2,1,0:T(8,128)(2,1)S(1)} collective-permute-done((bf16[8,80,128]{2,1,0:T(8,128)(2,1)S(1)}, bf16[8,80,128]{2,1,0:T(8,128)(2,1)S(1)}, u32[]{:S(2)}, u32[]{:S(2)}) %collective-permute-start.25) | collective-permute-done | bytes 163872 | tf_op jit(solution)/shard_map/ppermute | solution.py:24
  97.8 1.4 collective-permute-done.11.refs_1_.refs_2_
  99.2 10.9 %collective-permute-done.12.refs_2_ = bf16[24,80,128]{2,1,0:T(8,128)(2,1)S(1)} collective-permute-done((bf16[24,80,128]{2,1,0:T(8,128)(2,1)}, bf16[24,80,128]{2,1,0:T(8,128)(2,1)S(1)}, u32[]{:S(2)}, u32[]{:S(2)}) %collective-permute-start.12) | collective-permute-done | bytes 491552 | tf_op jit(solution)/shard_map/ppermute | solution.py:33
  111.1 17.7 %residual_and_back.2 = (bf16[24,80,128]{2,1,0:T(8,128)(2,1)}, bf16[24,80,128]{2,1,0:T(8,128)(2,1)}, bf16[24,80,128]{2,1,0:T(8,128)(2,1)}, bf16[24,80,128]{2,1,0:T(8,128)(2,1)}, bf16[24,80,128]{2,1,0:T(8,128)(2,1)}) custom-call(s32[384]{0:T(512)} %copy-done.23, s32[384]{0:T(512)} %select_reduce_fusion.order_ref, s32[1]{0:T(128)} %bitcast.6.first_ref, ...), custom_call_target="tpu_custom_call" | custom-call | tf_op jit(solution)/shard_map/residual_and_back/pallas_call | solution.py:171
  128.8 1.1 collective-permute-start.14
  129.9 1.0 collective-permute-start.15
  130.9 1.4 collective-permute-start.16
  132.3 0.8 copy-done.12
  133.1 3.6 %select_blocks.3 = (bf16[24,80,128]{2,1,0:T(8,128)(2,1)}, bf16[24,80,128]{2,1,0:T(8,128)(2,1)}, bf16[24,80,128]{2,1,0:T(8,128)(2,1)}, bf16[24,80,128]{2,1,0:T(8,128)(2,1)}) custom-call(s32[96]{0:T(128)} %reshape.191.index_ref, bf16[32,80,128]{2,1,0:T(8,128)(2,1)} %copy-done.2, bf16[32,80,128]{2,1,0:T(8,128)(2,1)} %copy-done.12), custom_call_target="tpu_custom_call" | custom-call | tf_op jit(solution)/shard_map/select_blocks/pallas_call | solution.py:76
  136.8 1.1 collective-permute-start.28
  137.8 1.0 collective-permute-start.29
  138.9 4.2 %collective-permute-done.14.refs_1_ = bf16[24,80,128]{2,1,0:T(8,128)(2,1)S(1)} collective-permute-done((bf16[24,80,128]{2,1,0:T(8,128)(2,1)}, bf16[24,80,128]{2,1,0:T(8,128)(2,1)S(1)}, u32[]{:S(2)}, u32[]{:S(2)}) %collective-permute-start.14) | collective-permute-done | bytes 491552 | tf_op jit(solution)/shard_map/ppermute | solution.py:33
  143.9 1.5 collective-permute-start.30
  145.5 9.4 %collective-permute-done.15.refs_2_ = bf16[24,80,128]{2,1,0:T(8,128)(2,1)} collective-permute-done((bf16[24,80,128]{2,1,0:T(8,128)(2,1)}, bf16[24,80,128]{2,1,0:T(8,128)(2,1)}, u32[]{:S(2)}, u32[]{:S(2)}) %collective-permute-start.15) | collective-permute-done | bytes 491552 | tf_op jit(solution)/shard_map/ppermute | solution.py:33
  154.8 3.3 %add_blocks.2 = (bf16[32,80,128]{2,1,0:T(8,128)(2,1)}, bf16[32,80,128]{2,1,0:T(8,128)(2,1)}) custom-call(s32[96]{0:T(128)} %reshape.191.index_ref, bf16[24,80,128]{2,1,0:T(8,128)(2,1)} %get-tuple-element.52.refs_0_, bf16[24,80,128]{2,1,0:T(8,128)(2,1)} %copy-done.17, bf16[24,80,128]{2,1,0:T(8,128)(2,1)} %collective-permute-done.15.refs_2_, ...), custom_call_target="tpu_custom_call" | custom-call | tf_op jit(solution)/shard_map/add_blocks/pallas_call | solution.py:104
  158.1 6.1 %collective-permute-done.28.refs_1_.refs_3_ = bf16[24,80,128]{2,1,0:T(8,128)(2,1)S(1)} collective-permute-done((bf16[24,80,128]{2,1,0:T(8,128)(2,1)}, bf16[24,80,128]{2,1,0:T(8,128)(2,1)S(1)}, u32[]{:S(2)}, u32[]{:S(2)}) %collective-permute-start.28) | collective-permute-done | bytes 491552 | tf_op jit(solution)/shard_map/ppermute | solution.py:33
  164.2 1.0 collective-permute-done.29.refs_2_.refs_3_
  165.3 8.6 %collective-permute-done.30.refs_3_ = bf16[24,80,128]{2,1,0:T(8,128)(2,1)S(1)} collective-permute-done((bf16[24,80,128]{2,1,0:T(8,128)(2,1)}, bf16[24,80,128]{2,1,0:T(8,128)(2,1)S(1)}, u32[]{:S(2)}, u32[]{:S(2)}) %collective-permute-start.30) | collective-permute-done | bytes 491552 | tf_op jit(solution)/shard_map/ppermute | solution.py:33
  174.6 17.7 %residual_and_back.3 = (bf16[24,80,128]{2,1,0:T(8,128)(2,1)}, bf16[24,80,128]{2,1,0:T(8,128)(2,1)}, bf16[24,80,128]{2,1,0:T(8,128)(2,1)}, bf16[24,80,128]{2,1,0:T(8,128)(2,1)}, bf16[24,80,128]{2,1,0:T(8,128)(2,1)}) custom-call(s32[384]{0:T(512)} %copy-done.23, s32[384]{0:T(512)} %select_reduce_fusion.order_ref, s32[1]{0:T(128)} %bitcast.6.first_ref, ...), custom_call_target="tpu_custom_call" | custom-call | tf_op jit(solution)/shard_map/residual_and_back/pallas_call | solution.py:171
  193.1 1.7 collective-permute-start.32
  194.8 1.1 collective-permute-start.33
  195.9 10.8 %collective-permute-done.31.refs_1_ = bf16[24,80,128]{2,1,0:T(8,128)(2,1)S(1)} collective-permute-done((bf16[24,80,128]{2,1,0:T(8,128)(2,1)}, bf16[24,80,128]{2,1,0:T(8,128)(2,1)S(1)}, u32[]{:S(2)}, u32[]{:S(2)}) %collective-permute-start.31) | collective-permute-done | bytes 491552 | tf_op jit(solution)/shard_map/ppermute | solution.py:33
  206.7 7.8 %collective-permute-done.32.refs_2_ = bf16[24,80,128]{2,1,0:T(8,128)(2,1)S(1)} collective-permute-done((bf16[24,80,128]{2,1,0:T(8,128)(2,1)}, bf16[24,80,128]{2,1,0:T(8,128)(2,1)S(1)}, u32[]{:S(2)}, u32[]{:S(2)}) %collective-permute-start.32) | collective-permute-done | bytes 491552 | tf_op jit(solution)/shard_map/ppermute | solution.py:33
  215.6 3.4 %add_blocks.3 = (bf16[32,80,128]{2,1,0:T(8,128)(2,1)}, bf16[32,80,128]{2,1,0:T(8,128)(2,1)}) custom-call(s32[96]{0:T(128)} %reshape.191.index_ref, bf16[24,80,128]{2,1,0:T(8,128)(2,1)} %get-tuple-element.63.refs_0_, bf16[24,80,128]{2,1,0:T(8,128)(2,1)} %copy-done.18, bf16[24,80,128]{2,1,0:T(8,128)(2,1)} %copy-done.19, bf16[24,80,128]{2,1,0:T(8,128)(2,1)} %copy-done.20), custom_call_target="tpu_custom_call" | custom-call | tf_op jit(solution)/shard_map/add_blocks/pallas_call | solution.py:104
  219.2 1.8 collective-permute-start.18
  221.1 2.6 collective-permute-start.19
  223.9 1.8 collective-permute-start.35
  225.7 2.5 collective-permute-done.18
  228.2 1.2 collective-permute-start.36
  229.4 4.5 %collective-permute-done.20 = bf16[8,80,128]{2,1,0:T(8,128)(2,1)S(1)} collective-permute-done((bf16[8,80,128]{2,1,0:T(8,128)(2,1)S(1)}, bf16[8,80,128]{2,1,0:T(8,128)(2,1)S(1)}, u32[]{:S(2)}, u32[]{:S(2)}) %collective-permute-start.20) | collective-permute-done | bytes 163872 | tf_op jit(solution)/shard_map/ppermute | solution.py:24
  233.9 5.8 %collective-permute-done.19 = bf16[8,80,128]{2,1,0:T(8,128)(2,1)S(1)} collective-permute-done((bf16[8,80,128]{2,1,0:T(8,128)(2,1)S(1)}, bf16[8,80,128]{2,1,0:T(8,128)(2,1)S(1)}, u32[]{:S(2)}, u32[]{:S(2)}) %collective-permute-start.19) | collective-permute-done | bytes 163872 | tf_op jit(solution)/shard_map/ppermute | solution.py:24
  239.8 1.3 collective-permute-start.23
  241.1 13.2 %collective-permute-start.21 = (bf16[8,80,128]{2,1,0:T(8,128)(2,1)S(1)}, bf16[8,80,128]{2,1,0:T(8,128)(2,1)S(1)}, u32[]{:S(2)}, u32[]{:S(2)}) collective-permute-start(bf16[8,80,128]{2,1,0:T(8,128)(2,1)S(1)} %select_convert_fusion.1), channel_id=1, source_target_pairs={{0,2},{1,3},{2,0},{3,1},{4,6},{5,7},{6,4},{7,5},{8,10},{9,11},{10,... | collective-permute-start | bytes 491528 | tf_op jit(solution)/shard_map/ppermute | solution.py:24
  254.3 3.0 collective-permute-done.36
  257.4 6.4 %collective-permute-done.22 = bf16[8,80,128]{2,1,0:T(8,128)(2,1)S(1)} collective-permute-done((bf16[8,80,128]{2,1,0:T(8,128)(2,1)S(1)}, bf16[8,80,128]{2,1,0:T(8,128)(2,1)S(1)}, u32[]{:S(2)}, u32[]{:S(2)}) %collective-permute-start.22) | collective-permute-done | bytes 163872 | tf_op jit(solution)/shard_map/ppermute | solution.py:24
  264.0 1.4 collective-permute-start.40
  265.4 3.1 %collective-permute-start.38 = (bf16[8,80,128]{2,1,0:T(8,128)(2,1)S(1)}, bf16[8,80,128]{2,1,0:T(8,128)(2,1)S(1)}, u32[]{:S(2)}, u32[]{:S(2)}) collective-permute-start(bf16[8,80,128]{2,1,0:T(8,128)(2,1)S(1)} %select_convert_fusion), channel_id=1, source_target_pairs={{0,2},{1,3},{2,0},{3,1},{4,6},{5,7},{6,4},{7,5},{8,10},{9,11},{10,... | collective-permute-start | bytes 491528 | tf_op jit(solution)/shard_map/ppermute | solution.py:24
  268.5 4.6 %collective-permute-done.40 = bf16[8,80,128]{2,1,0:T(8,128)(2,1)S(1)} collective-permute-done((bf16[8,80,128]{2,1,0:T(8,128)(2,1)S(1)}, bf16[8,80,128]{2,1,0:T(8,128)(2,1)S(1)}, u32[]{:S(2)}, u32[]{:S(2)}) %collective-permute-start.40) | collective-permute-done | bytes 163872 | tf_op jit(solution)/shard_map/ppermute | solution.py:24
  273.1 5.6 %collective-permute-done.39 = bf16[8,80,128]{2,1,0:T(8,128)(2,1)S(1)} collective-permute-done((bf16[8,80,128]{2,1,0:T(8,128)(2,1)S(1)}, bf16[8,80,128]{2,1,0:T(8,128)(2,1)S(1)}, u32[]{:S(2)}, u32[]{:S(2)}) %collective-permute-start.39) | collective-permute-done | bytes 163872 | tf_op jit(solution)/shard_map/ppermute | solution.py:24
  280.2 4.3 %block_weight_grad.4.refs_4_ = bf16[384,128,128]{2,1,0:T(8,128)(2,1)} custom-call(s32[96]{0:T(128)} %get-tuple-element.82.order_ref, bf16[24,80,128]{2,1,0:T(8,128)(2,1)} %get-tuple-element.70.refs_0_, bf16[24,80,128]{2,1,0:T(8,128)(2,1)} %get-tuple-element.71.refs_1_, bf16[24,80,128]{2,1,0:T(8,128)(2,1)} %get-tuple-element.48.refs_0_.refs_2_, ...), custom_call_target="tpu_custom_call" | custom-call | tf_op jit(solution)/shard_map/block_weight_grad/pallas_call | solution.py:220
  284.6 4.3 %block_weight_grad.5.refs_4_ = bf16[384,128,128]{2,1,0:T(8,128)(2,1)} custom-call(s32[96]{0:T(128)} %get-tuple-element.83.order_ref, bf16[24,80,128]{2,1,0:T(8,128)(2,1)} %get-tuple-element.70.refs_0_, bf16[24,80,128]{2,1,0:T(8,128)(2,1)} %get-tuple-element.71.refs_1_, bf16[24,80,128]{2,1,0:T(8,128)(2,1)} %copy-done.6, ...), custom_call_target="tpu_custom_call", output_to_operand_aliasing={{}: (5, {})} | custom-call | tf_op jit(solution)/shard_map/block_weight_grad/pallas_call | solution.py:220
  288.9 4.3 %block_weight_grad.6.refs_4_ = bf16[384,128,128]{2,1,0:T(8,128)(2,1)} custom-call(s32[96]{0:T(128)} %get-tuple-element.84.order_ref, bf16[24,80,128]{2,1,0:T(8,128)(2,1)} %get-tuple-element.70.refs_0_, bf16[24,80,128]{2,1,0:T(8,128)(2,1)} %get-tuple-element.71.refs_1_, bf16[24,80,128]{2,1,0:T(8,128)(2,1)} %copy-done.5, ...), custom_call_target="tpu_custom_call", output_to_operand_aliasing={{}: (5, {})} | custom-call | tf_op jit(solution)/shard_map/block_weight_grad/pallas_call | solution.py:220
  293.2 4.3 %block_weight_grad.7 = bf16[384,128,128]{2,1,0:T(8,128)(2,1)} custom-call(s32[96]{0:T(128)} %get-tuple-element.85.order_ref, bf16[24,80,128]{2,1,0:T(8,128)(2,1)} %get-tuple-element.70.refs_0_, bf16[24,80,128]{2,1,0:T(8,128)(2,1)} %get-tuple-element.71.refs_1_, bf16[24,80,128]{2,1,0:T(8,128)(2,1)} %copy-done.4, ...), custom_call_target="tpu_custom_call", output_to_operand_aliasing={{}: (5, {})} | custom-call | tf_op jit(solution)/shard_map/block_weight_grad/pallas_call | solution.py:220
  297.6 0.8 copy-done.10
  298.4 0.8 copy-done.11
  299.3 3.8 %expand_weight_grad.1 = bf16[128,8192]{1,0:T(8,128)(2,1)} custom-call(s32[8]{0:T(128)} %fusion.30.columns_ref, bf16[160,128]{1,0:T(8,128)(2,1)} %documents_ref.1, bf16[32,80,128]{2,1,0:T(8,128)(2,1)} %copy-done, bf16[32,80,128]{2,1,0:T(8,128)(2,1)} %copy-done.1, bf16[32,80,128]{2,1,0:T(8,128)(2,1)} %copy-done.10, bf16[32,80,128]{2,1,0:T(8,128)(2,1)} %copy-done.11), custom_call_target="tpu_custom_call" | custom-call | tf_op jit(solution)/shard_map/expand_weight_grad/pallas_call | solution.py:252
  (132 shorter events, 15.9 us)
Async XLA Ops:
  0.6 3.7 %copy-start.21 = (bf16[160,128]{1,0:T(8,128)(2,1)S(1)}, bf16[160,128]{1,0:T(8,128)(2,1)}, u32[]{:S(2)}) copy-start(bf16[160,128]{1,0:T(8,128)(2,1)} %documents_ref.1) | copy-start | bytes 122884
  0.6 13.2 %copy-start.22 = (s32[768,16]{0,1:T(8,128)S(1)}, s32[768,16]{0,1:T(8,128)}, u32[]{:S(2)}) copy-start(s32[768,16]{0,1:T(8,128)} %param.8) | copy-start | bytes 147460
  1.2 13.4 %copy-start.25 = (s32[160,8]{0,1:T(8,128)S(1)}, s32[160,8]{0,1:T(8,128)}, u32[]{:S(2)}) copy-start(s32[160,8]{0,1:T(8,128)} %param.9) | copy-start | bytes 15364
  4.3 12.1 %copy-start.16 = (bf16[128,2048]{1,0:T(8,128)(2,1)S(1)}, bf16[128,2048]{1,0:T(8,128)(2,1)}, u32[]{:S(2)}) copy-start(bf16[128,2048]{1,0:T(8,128)(2,1)} %get-tuple-element.37) | copy-start | bytes 1572868
  4.3 23.2 %collective-permute-start.5 = (bf16[160,128]{1,0:T(8,128)(2,1)S(1)}, bf16[160,128]{1,0:T(8,128)(2,1)S(1)}, u32[]{:S(2)}, u32[]{:S(2)}) collective-permute-start(bf16[160,128]{1,0:T(8,128)(2,1)S(1)} %copy-done.21), channel_id=1, source_target_pairs={{0,6},{1,7},{2,4},{3,5},{4,2},{5,3},{6,0},{7,1},{8,14},{9,15},{10,... | collective-permute-start | bytes 122888 | tf_op jit(solution)/shard_map/ppermute | solution.py:24
  9.4 29.7 %collective-permute-start.3 = (bf16[160,128]{1,0:T(8,128)(2,1)S(1)}, bf16[160,128]{1,0:T(8,128)(2,1)S(1)}, u32[]{:S(2)}, u32[]{:S(2)}) collective-permute-start(bf16[160,128]{1,0:T(8,128)(2,1)S(1)} %copy-done.21), channel_id=1, source_target_pairs={{0,4},{1,5},{2,6},{3,7},{4,0},{5,1},{6,2},{7,3},{8,12},{9,13},{10,... | collective-permute-start | bytes 122888 | tf_op jit(solution)/shard_map/ppermute | solution.py:24
  9.4 9.5 %collective-permute-start.1 = (bf16[160,128]{1,0:T(8,128)(2,1)S(1)}, bf16[160,128]{1,0:T(8,128)(2,1)S(1)}, u32[]{:S(2)}, u32[]{:S(2)}) collective-permute-start(bf16[160,128]{1,0:T(8,128)(2,1)S(1)} %copy-done.21), channel_id=1, source_target_pairs={{0,2},{1,3},{2,0},{3,1},{4,6},{5,7},{6,4},{7,5},{8,10},{9,11},{10,... | collective-permute-start | bytes 122888 | tf_op jit(solution)/shard_map/ppermute | solution.py:24
  10.0 17.1 %collective-permute-start = (bf16[128,2048]{1,0:T(8,128)(2,1)}, bf16[128,2048]{1,0:T(8,128)(2,1)S(1)}, u32[]{:S(2)}, u32[]{:S(2)}) collective-permute-start(bf16[128,2048]{1,0:T(8,128)(2,1)} %get-tuple-element.38), channel_id=1, source_target_pairs={{0,2},{1,3},{2,0},{3,1},{4,6},{5,7},{6,4},{7,5},{8,10},{9,11},{10,... | collective-permute-start | bytes 1572872 | tf_op jit(solution)/shard_map/ppermute | solution.py:24
  11.4 27.3 %collective-permute-start.4 = (bf16[128,2048]{1,0:T(8,128)(2,1)}, bf16[128,2048]{1,0:T(8,128)(2,1)S(1)}, u32[]{:S(2)}, u32[]{:S(2)}) collective-permute-start(bf16[128,2048]{1,0:T(8,128)(2,1)} %get-tuple-element.41), channel_id=1, source_target_pairs={{0,6},{1,7},{2,4},{3,5},{4,2},{5,3},{6,0},{7,1},{8,14},{9,15},{10,... | collective-permute-start | bytes 1572872 | tf_op jit(solution)/shard_map/ppermute | solution.py:24
  15.1 12.3 %copy-start.23 = (s32[384]{0:T(512)}, s32[384]{0:T(512)S(1)}, u32[]{:S(2)}) copy-start(s32[384]{0:T(512)S(1)} %select_reduce_fusion.1.position_ref) | copy-start | bytes 4612
  18.8 40.4 %collective-permute-start.2 = (bf16[128,2048]{1,0:T(8,128)(2,1)}, bf16[128,2048]{1,0:T(8,128)(2,1)S(1)}, u32[]{:S(2)}, u32[]{:S(2)}) collective-permute-start(bf16[128,2048]{1,0:T(8,128)(2,1)} %get-tuple-element.40), channel_id=1, source_target_pairs={{0,4},{1,5},{2,6},{3,7},{4,0},{5,1},{6,2},{7,3},{8,12},{9,13},{10,... | collective-permute-start | bytes 1572872 | tf_op jit(solution)/shard_map/ppermute | solution.py:24
  59.6 2.2 collective-permute-start.6
  61.9 9.1 %collective-permute-start.9 = (bf16[8,80,128]{2,1,0:T(8,128)(2,1)S(1)}, bf16[8,80,128]{2,1,0:T(8,128)(2,1)S(1)}, u32[]{:S(2)}, u32[]{:S(2)}) collective-permute-start(bf16[8,80,128]{2,1,0:T(8,128)(2,1)S(1)} %get-tuple-element.79), channel_id=1, source_target_pairs={{0,6},{1,7},{2,4},{3,5},{4,2},{5,3},{6,0},{7,1},{8,14},{9,15},{10,... | collective-permute-start | bytes 491528 | tf_op jit(solution)/shard_map/ppermute | solution.py:24
  64.4 13.5 %collective-permute-start.8 = (bf16[8,80,128]{2,1,0:T(8,128)(2,1)S(1)}, bf16[8,80,128]{2,1,0:T(8,128)(2,1)S(1)}, u32[]{:S(2)}, u32[]{:S(2)}) collective-permute-start(bf16[8,80,128]{2,1,0:T(8,128)(2,1)S(1)} %get-tuple-element.79), channel_id=1, source_target_pairs={{0,4},{1,5},{2,6},{3,7},{4,0},{5,1},{6,2},{7,3},{8,12},{9,13},{10,... | collective-permute-start | bytes 491528 | tf_op jit(solution)/shard_map/ppermute | solution.py:24
  64.4 13.5 %collective-permute-start.7 = (bf16[8,80,128]{2,1,0:T(8,128)(2,1)S(1)}, bf16[8,80,128]{2,1,0:T(8,128)(2,1)S(1)}, u32[]{:S(2)}, u32[]{:S(2)}) collective-permute-start(bf16[8,80,128]{2,1,0:T(8,128)(2,1)S(1)} %get-tuple-element.79), channel_id=1, source_target_pairs={{0,2},{1,3},{2,0},{3,1},{4,6},{5,7},{6,4},{7,5},{8,10},{9,11},{10,... | collective-permute-start | bytes 491528 | tf_op jit(solution)/shard_map/ppermute | solution.py:24
  78.0 2.2 copy-start.3
  78.1 2.2 collective-permute-start.10
  78.1 10.2 %collective-permute-start.26 = (bf16[8,80,128]{2,1,0:T(8,128)(2,1)S(1)}, bf16[8,80,128]{2,1,0:T(8,128)(2,1)S(1)}, u32[]{:S(2)}, u32[]{:S(2)}) collective-permute-start(bf16[8,80,128]{2,1,0:T(8,128)(2,1)S(1)} %get-tuple-element.78), channel_id=1, source_target_pairs={{0,6},{1,7},{2,4},{3,5},{4,2},{5,3},{6,0},{7,1},{8,14},{9,15},{10,... | collective-permute-start | bytes 491528 | tf_op jit(solution)/shard_map/ppermute | solution.py:24
  80.2 0.8 copy-start.13
  84.9 14.3 %collective-permute-start.11 = (bf16[24,80,128]{2,1,0:T(8,128)(2,1)}, bf16[24,80,128]{2,1,0:T(8,128)(2,1)S(1)}, u32[]{:S(2)}, u32[]{:S(2)}) collective-permute-start(bf16[24,80,128]{2,1,0:T(8,128)(2,1)} %get-tuple-element.49), channel_id=1, source_target_pairs={{0,8},{8,0},{16,24},{24,16},{1,9},{9,1},{17,25},{25,17},{2,10},{10... | collective-permute-start | bytes 1474568 | tf_op jit(solution)/shard_map/ppermute | solution.py:33
  86.4 23.7 %collective-permute-start.12 = (bf16[24,80,128]{2,1,0:T(8,128)(2,1)}, bf16[24,80,128]{2,1,0:T(8,128)(2,1)S(1)}, u32[]{:S(2)}, u32[]{:S(2)}) collective-permute-start(bf16[24,80,128]{2,1,0:T(8,128)(2,1)} %get-tuple-element.50), channel_id=1, source_target_pairs={{0,16},{8,24},{16,0},{24,8},{1,17},{9,25},{17,1},{25,9},{2,18},{10... | collective-permute-start | bytes 1474568 | tf_op jit(solution)/shard_map/ppermute | solution.py:33
  87.9 22.2 %collective-permute-start.13 = (bf16[24,80,128]{2,1,0:T(8,128)(2,1)}, bf16[24,80,128]{2,1,0:T(8,128)(2,1)S(1)}, u32[]{:S(2)}, u32[]{:S(2)}) collective-permute-start(bf16[24,80,128]{2,1,0:T(8,128)(2,1)} %get-tuple-element.51), channel_id=1, source_target_pairs={{0,24},{8,16},{16,8},{24,0},{1,25},{9,17},{17,9},{25,1},{2,26},{10... | collective-permute-start | bytes 1474568 | tf_op jit(solution)/shard_map/ppermute | solution.py:33
  88.4 9.1 %collective-permute-start.25 = (bf16[8,80,128]{2,1,0:T(8,128)(2,1)S(1)}, bf16[8,80,128]{2,1,0:T(8,128)(2,1)S(1)}, u32[]{:S(2)}, u32[]{:S(2)}) collective-permute-start(bf16[8,80,128]{2,1,0:T(8,128)(2,1)S(1)} %get-tuple-element.78), channel_id=1, source_target_pairs={{0,4},{1,5},{2,6},{3,7},{4,0},{5,1},{6,2},{7,3},{8,12},{9,13},{10,... | collective-permute-start | bytes 491528 | tf_op jit(solution)/shard_map/ppermute | solution.py:24
  88.4 9.3 %collective-permute-start.24 = (bf16[8,80,128]{2,1,0:T(8,128)(2,1)S(1)}, bf16[8,80,128]{2,1,0:T(8,128)(2,1)S(1)}, u32[]{:S(2)}, u32[]{:S(2)}) collective-permute-start(bf16[8,80,128]{2,1,0:T(8,128)(2,1)S(1)} %get-tuple-element.78), channel_id=1, source_target_pairs={{0,2},{1,3},{2,0},{3,1},{4,6},{5,7},{6,4},{7,5},{8,10},{9,11},{10,... | collective-permute-start | bytes 491528 | tf_op jit(solution)/shard_map/ppermute | solution.py:24
  97.7 31.0 %copy-start.2 = (bf16[32,80,128]{2,1,0:T(8,128)(2,1)}, bf16[32,80,128]{2,1,0:T(8,128)(2,1)S(1)}, u32[]{:S(2)}) copy-start(bf16[32,80,128]{2,1,0:T(8,128)(2,1)S(1)} %pad_maximum_fusion.2.refs_0_) | copy-start | bytes 1966084
  97.7 34.6 %collective-permute-start.27 = (bf16[32,80,128]{2,1,0:T(8,128)(2,1)S(1)}, bf16[32,80,128]{2,1,0:T(8,128)(2,1)S(1)}, u32[]{:S(2)}, u32[]{:S(2)}) collective-permute-start(bf16[32,80,128]{2,1,0:T(8,128)(2,1)S(1)} %pad_maximum_fusion.2.refs_0_), channel_id=1, source_target_pairs={{0,1},{1,0},{2,3},{3,2},{4,5},{5,4},{6,7},{7,6},{8,9},{9,8},{10,11... | collective-permute-start | bytes 1966088 | tf_op jit(solution)/shard_map/ppermute | solution.py:29
  99.2 10.9 %copy-start.6 = (bf16[24,80,128]{2,1,0:T(8,128)(2,1)}, bf16[24,80,128]{2,1,0:T(8,128)(2,1)S(1)}, u32[]{:S(2)}) copy-start(bf16[24,80,128]{2,1,0:T(8,128)(2,1)S(1)} %collective-permute-done.11.refs_1_.refs_2_) | copy-start | bytes 1474564
  110.1 1.0 copy-start.4
  128.8 14.4 %collective-permute-start.14 = (bf16[24,80,128]{2,1,0:T(8,128)(2,1)}, bf16[24,80,128]{2,1,0:T(8,128)(2,1)S(1)}, u32[]{:S(2)}, u32[]{:S(2)}) collective-permute-start(bf16[24,80,128]{2,1,0:T(8,128)(2,1)} %get-tuple-element.53), channel_id=1, source_target_pairs={{0,8},{8,0},{16,24},{24,16},{1,9},{9,1},{17,25},{25,17},{2,10},{10... | collective-permute-start | bytes 1474568 | tf_op jit(solution)/shard_map/ppermute | solution.py:33
  129.9 24.9 %collective-permute-start.15 = (bf16[24,80,128]{2,1,0:T(8,128)(2,1)}, bf16[24,80,128]{2,1,0:T(8,128)(2,1)}, u32[]{:S(2)}, u32[]{:S(2)}) collective-permute-start(bf16[24,80,128]{2,1,0:T(8,128)(2,1)} %get-tuple-element.54), channel_id=1, source_target_pairs={{0,16},{8,24},{16,0},{24,8},{1,17},{9,25},{17,1},{25,9},{2,18},{10... | collective-permute-start | bytes 1474568 | tf_op jit(solution)/shard_map/ppermute | solution.py:33
  130.9 23.9 %collective-permute-start.16 = (bf16[24,80,128]{2,1,0:T(8,128)(2,1)}, bf16[24,80,128]{2,1,0:T(8,128)(2,1)}, u32[]{:S(2)}, u32[]{:S(2)}) collective-permute-start(bf16[24,80,128]{2,1,0:T(8,128)(2,1)} %get-tuple-element.55), channel_id=1, source_target_pairs={{0,24},{8,16},{16,8},{24,0},{1,25},{9,17},{17,9},{25,1},{2,26},{10... | collective-permute-start | bytes 1474568 | tf_op jit(solution)/shard_map/ppermute | solution.py:33
  136.8 27.5 %collective-permute-start.28 = (bf16[24,80,128]{2,1,0:T(8,128)(2,1)}, bf16[24,80,128]{2,1,0:T(8,128)(2,1)S(1)}, u32[]{:S(2)}, u32[]{:S(2)}) collective-permute-start(bf16[24,80,128]{2,1,0:T(8,128)(2,1)} %get-tuple-element.60), channel_id=1, source_target_pairs={{0,8},{8,0},{16,24},{24,16},{1,9},{9,1},{17,25},{25,17},{2,10},{10... | collective-permute-start | bytes 1474568 | tf_op jit(solution)/shard_map/ppermute | solution.py:33
  137.8 27.4 %collective-permute-start.29 = (bf16[24,80,128]{2,1,0:T(8,128)(2,1)}, bf16[24,80,128]{2,1,0:T(8,128)(2,1)S(1)}, u32[]{:S(2)}, u32[]{:S(2)}) collective-permute-start(bf16[24,80,128]{2,1,0:T(8,128)(2,1)} %get-tuple-element.61), channel_id=1, source_target_pairs={{0,16},{8,24},{16,0},{24,8},{1,17},{9,25},{17,1},{25,9},{2,18},{10... | collective-permute-start | bytes 1474568 | tf_op jit(solution)/shard_map/ppermute | solution.py:33
  143.9 29.9 %collective-permute-start.30 = (bf16[24,80,128]{2,1,0:T(8,128)(2,1)}, bf16[24,80,128]{2,1,0:T(8,128)(2,1)S(1)}, u32[]{:S(2)}, u32[]{:S(2)}) collective-permute-start(bf16[24,80,128]{2,1,0:T(8,128)(2,1)} %get-tuple-element.62), channel_id=1, source_target_pairs={{0,24},{8,16},{16,8},{24,0},{1,25},{9,17},{17,9},{25,1},{2,26},{10... | collective-permute-start | bytes 1474568 | tf_op jit(solution)/shard_map/ppermute | solution.py:33
  158.1 60.8 %collective-permute-start.17 = (bf16[32,80,128]{2,1,0:T(8,128)(2,1)}, bf16[32,80,128]{2,1,0:T(8,128)(2,1)S(1)}, u32[]{:S(2)}, u32[]{:S(2)}) collective-permute-start(bf16[32,80,128]{2,1,0:T(8,128)(2,1)} %get-tuple-element.57), channel_id=1, source_target_pairs={{0,1},{1,0},{2,3},{3,2},{4,5},{5,4},{6,7},{7,6},{8,9},{9,8},{10,11... | collective-permute-start | bytes 1966088 | tf_op jit(solution)/shard_map/ppermute | solution.py:29
  164.2 9.6 %copy-start.8 = (bf16[24,80,128]{2,1,0:T(8,128)(2,1)}, bf16[24,80,128]{2,1,0:T(8,128)(2,1)S(1)}, u32[]{:S(2)}) copy-start(bf16[24,80,128]{2,1,0:T(8,128)(2,1)S(1)} %collective-permute-done.28.refs_1_.refs_3_) | copy-start | bytes 1474564
  165.3 8.6 %copy-start.7 = (bf16[24,80,128]{2,1,0:T(8,128)(2,1)}, bf16[24,80,128]{2,1,0:T(8,128)(2,1)S(1)}, u32[]{:S(2)}) copy-start(bf16[24,80,128]{2,1,0:T(8,128)(2,1)S(1)} %collective-permute-done.29.refs_2_.refs_3_) | copy-start | bytes 1474564
  192.3 26.6 %copy-start.14 = (bf16[32,80,128]{2,1,0:T(8,128)(2,1)S(1)}, bf16[32,80,128]{2,1,0:T(8,128)(2,1)}, u32[]{:S(2)}) copy-start(bf16[32,80,128]{2,1,0:T(8,128)(2,1)} %get-tuple-element.56) | copy-start | bytes 1966084
  192.4 14.4 %collective-permute-start.31 = (bf16[24,80,128]{2,1,0:T(8,128)(2,1)}, bf16[24,80,128]{2,1,0:T(8,128)(2,1)S(1)}, u32[]{:S(2)}, u32[]{:S(2)}) collective-permute-start(bf16[24,80,128]{2,1,0:T(8,128)(2,1)} %get-tuple-element.64), channel_id=1, source_target_pairs={{0,8},{8,0},{16,24},{24,16},{1,9},{9,1},{17,25},{25,17},{2,10},{10... | collective-permute-start | bytes 1474568 | tf_op jit(solution)/shard_map/ppermute | solution.py:33
  193.1 21.4 %collective-permute-start.32 = (bf16[24,80,128]{2,1,0:T(8,128)(2,1)}, bf16[24,80,128]{2,1,0:T(8,128)(2,1)S(1)}, u32[]{:S(2)}, u32[]{:S(2)}) collective-permute-start(bf16[24,80,128]{2,1,0:T(8,128)(2,1)} %get-tuple-element.65), channel_id=1, source_target_pairs={{0,16},{8,24},{16,0},{24,8},{1,17},{9,25},{17,1},{25,9},{2,18},{10... | collective-permute-start | bytes 1474568 | tf_op jit(solution)/shard_map/ppermute | solution.py:33
  194.8 19.7 %collective-permute-start.33 = (bf16[24,80,128]{2,1,0:T(8,128)(2,1)}, bf16[24,80,128]{2,1,0:T(8,128)(2,1)S(1)}, u32[]{:S(2)}, u32[]{:S(2)}) collective-permute-start(bf16[24,80,128]{2,1,0:T(8,128)(2,1)} %get-tuple-element.66), channel_id=1, source_target_pairs={{0,24},{8,16},{16,8},{24,0},{1,25},{9,17},{17,9},{25,1},{2,26},{10... | collective-permute-start | bytes 1474568 | tf_op jit(solution)/shard_map/ppermute | solution.py:33
  206.7 7.8 %copy-start.18 = (bf16[24,80,128]{2,1,0:T(8,128)(2,1)}, bf16[24,80,128]{2,1,0:T(8,128)(2,1)S(1)}, u32[]{:S(2)}) copy-start(bf16[24,80,128]{2,1,0:T(8,128)(2,1)S(1)} %collective-permute-done.31.refs_1_) | copy-start | bytes 1474564
  214.6 1.0 copy-start.20
  219.0 4.7 %collective-permute-start.34 = (bf16[32,80,128]{2,1,0:T(8,128)(2,1)}, bf16[32,80,128]{2,1,0:T(8,128)(2,1)S(1)}, u32[]{:S(2)}, u32[]{:S(2)}) collective-permute-start(bf16[32,80,128]{2,1,0:T(8,128)(2,1)} %get-tuple-element.68), channel_id=1, source_target_pairs={{0,1},{1,0},{2,3},{3,2},{4,5},{5,4},{6,7},{7,6},{8,9},{9,8},{10,11... | collective-permute-start | bytes 1966088 | tf_op jit(solution)/shard_map/ppermute | solution.py:29
  219.0 4.7 %copy-start.15 = (bf16[32,80,128]{2,1,0:T(8,128)(2,1)S(1)}, bf16[32,80,128]{2,1,0:T(8,128)(2,1)}, u32[]{:S(2)}) copy-start(bf16[32,80,128]{2,1,0:T(8,128)(2,1)} %get-tuple-element.67) | copy-start | bytes 1966084
  219.2 9.0 %collective-permute-start.18 = (bf16[8,80,128]{2,1,0:T(8,128)(2,1)S(1)}, bf16[8,80,128]{2,1,0:T(8,128)(2,1)S(1)}, u32[]{:S(2)}, u32[]{:S(2)}) collective-permute-start(bf16[8,80,128]{2,1,0:T(8,128)(2,1)S(1)} %get-tuple-element.75), channel_id=1, source_target_pairs={{0,6},{1,7},{2,4},{3,5},{4,2},{5,3},{6,0},{7,1},{8,14},{9,15},{10,... | collective-permute-start | bytes 491528 | tf_op jit(solution)/shard_map/ppermute | solution.py:24
  221.1 12.9 %collective-permute-start.20 = (bf16[8,80,128]{2,1,0:T(8,128)(2,1)S(1)}, bf16[8,80,128]{2,1,0:T(8,128)(2,1)S(1)}, u32[]{:S(2)}, u32[]{:S(2)}) collective-permute-start(bf16[8,80,128]{2,1,0:T(8,128)(2,1)S(1)} %get-tuple-element.76), channel_id=1, source_target_pairs={{0,2},{1,3},{2,0},{3,1},{4,6},{5,7},{6,4},{7,5},{8,10},{9,11},{10,... | collective-permute-start | bytes 491528 | tf_op jit(solution)/shard_map/ppermute | solution.py:24
  221.1 18.6 %collective-permute-start.19 = (bf16[8,80,128]{2,1,0:T(8,128)(2,1)S(1)}, bf16[8,80,128]{2,1,0:T(8,128)(2,1)S(1)}, u32[]{:S(2)}, u32[]{:S(2)}) collective-permute-start(bf16[8,80,128]{2,1,0:T(8,128)(2,1)S(1)} %get-tuple-element.77), channel_id=1, source_target_pairs={{0,4},{1,5},{2,6},{3,7},{4,0},{5,1},{6,2},{7,3},{8,12},{9,13},{10,... | collective-permute-start | bytes 491528 | tf_op jit(solution)/shard_map/ppermute | solution.py:24
  223.9 17.2 %collective-permute-start.35 = (bf16[8,80,128]{2,1,0:T(8,128)(2,1)S(1)}, bf16[8,80,128]{2,1,0:T(8,128)(2,1)S(1)}, u32[]{:S(2)}, u32[]{:S(2)}) collective-permute-start(bf16[8,80,128]{2,1,0:T(8,128)(2,1)S(1)} %get-tuple-element.72), channel_id=1, source_target_pairs={{0,6},{1,7},{2,4},{3,5},{4,2},{5,3},{6,0},{7,1},{8,14},{9,15},{10,... | collective-permute-start | bytes 491528 | tf_op jit(solution)/shard_map/ppermute | solution.py:24
  225.7 28.6 %collective-permute-start.37 = (bf16[8,80,128]{2,1,0:T(8,128)(2,1)S(1)}, bf16[8,80,128]{2,1,0:T(8,128)(2,1)S(1)}, u32[]{:S(2)}, u32[]{:S(2)}) collective-permute-start(bf16[8,80,128]{2,1,0:T(8,128)(2,1)S(1)} %get-tuple-element.73), channel_id=1, source_target_pairs={{0,2},{1,3},{2,0},{3,1},{4,6},{5,7},{6,4},{7,5},{8,10},{9,11},{10,... | collective-permute-start | bytes 491528 | tf_op jit(solution)/shard_map/ppermute | solution.py:24
  228.2 29.1 %collective-permute-start.36 = (bf16[8,80,128]{2,1,0:T(8,128)(2,1)S(1)}, bf16[8,80,128]{2,1,0:T(8,128)(2,1)S(1)}, u32[]{:S(2)}, u32[]{:S(2)}) collective-permute-start(bf16[8,80,128]{2,1,0:T(8,128)(2,1)S(1)} %get-tuple-element.74), channel_id=1, source_target_pairs={{0,4},{1,5},{2,6},{3,7},{4,0},{5,1},{6,2},{7,3},{8,12},{9,13},{10,... | collective-permute-start | bytes 491528 | tf_op jit(solution)/shard_map/ppermute | solution.py:24
  239.8 17.6 %collective-permute-start.23 = (bf16[8,80,128]{2,1,0:T(8,128)(2,1)S(1)}, bf16[8,80,128]{2,1,0:T(8,128)(2,1)S(1)}, u32[]{:S(2)}, u32[]{:S(2)}) collective-permute-start(bf16[8,80,128]{2,1,0:T(8,128)(2,1)S(1)} %select_convert_fusion.1), channel_id=1, source_target_pairs={{0,6},{1,7},{2,4},{3,5},{4,2},{5,3},{6,0},{7,1},{8,14},{9,15},{10,... | collective-permute-start | bytes 491528 | tf_op jit(solution)/shard_map/ppermute | solution.py:24
  241.1 22.7 %collective-permute-start.22 = (bf16[8,80,128]{2,1,0:T(8,128)(2,1)S(1)}, bf16[8,80,128]{2,1,0:T(8,128)(2,1)S(1)}, u32[]{:S(2)}, u32[]{:S(2)}) collective-permute-start(bf16[8,80,128]{2,1,0:T(8,128)(2,1)S(1)} %select_convert_fusion.1), channel_id=1, source_target_pairs={{0,4},{1,5},{2,6},{3,7},{4,0},{5,1},{6,2},{7,3},{8,12},{9,13},{10,... | collective-permute-start | bytes 491528 | tf_op jit(solution)/shard_map/ppermute | solution.py:24
  241.1 22.7 %collective-permute-start.21 = (bf16[8,80,128]{2,1,0:T(8,128)(2,1)S(1)}, bf16[8,80,128]{2,1,0:T(8,128)(2,1)S(1)}, u32[]{:S(2)}, u32[]{:S(2)}) collective-permute-start(bf16[8,80,128]{2,1,0:T(8,128)(2,1)S(1)} %select_convert_fusion.1), channel_id=1, source_target_pairs={{0,2},{1,3},{2,0},{3,1},{4,6},{5,7},{6,4},{7,5},{8,10},{9,11},{10,... | collective-permute-start | bytes 491528 | tf_op jit(solution)/shard_map/ppermute | solution.py:24
  257.4 22.1 %copy-start.24 = (s32[384]{0:T(512)S(1)}, s32[384]{0:T(512)}, u32[]{:S(2)}) copy-start(s32[384]{0:T(512)} %select_reduce_fusion.order_ref) | copy-start | bytes 4612
  263.9 20.6 %copy-start = (bf16[32,80,128]{2,1,0:T(8,128)(2,1)}, bf16[32,80,128]{2,1,0:T(8,128)(2,1)S(1)}, u32[]{:S(2)}) copy-start(bf16[32,80,128]{2,1,0:T(8,128)(2,1)S(1)} %pad_maximum_fusion.1.refs_0_) | copy-start | bytes 1966084
  264.0 9.1 %collective-permute-start.40 = (bf16[8,80,128]{2,1,0:T(8,128)(2,1)S(1)}, bf16[8,80,128]{2,1,0:T(8,128)(2,1)S(1)}, u32[]{:S(2)}, u32[]{:S(2)}) collective-permute-start(bf16[8,80,128]{2,1,0:T(8,128)(2,1)S(1)} %select_convert_fusion), channel_id=1, source_target_pairs={{0,6},{1,7},{2,4},{3,5},{4,2},{5,3},{6,0},{7,1},{8,14},{9,15},{10,... | collective-permute-start | bytes 491528 | tf_op jit(solution)/shard_map/ppermute | solution.py:24
  265.4 13.3 %collective-permute-start.39 = (bf16[8,80,128]{2,1,0:T(8,128)(2,1)S(1)}, bf16[8,80,128]{2,1,0:T(8,128)(2,1)S(1)}, u32[]{:S(2)}, u32[]{:S(2)}) collective-permute-start(bf16[8,80,128]{2,1,0:T(8,128)(2,1)S(1)} %select_convert_fusion), channel_id=1, source_target_pairs={{0,4},{1,5},{2,6},{3,7},{4,0},{5,1},{6,2},{7,3},{8,12},{9,13},{10,... | collective-permute-start | bytes 491528 | tf_op jit(solution)/shard_map/ppermute | solution.py:24
  265.4 13.3 %collective-permute-start.38 = (bf16[8,80,128]{2,1,0:T(8,128)(2,1)S(1)}, bf16[8,80,128]{2,1,0:T(8,128)(2,1)S(1)}, u32[]{:S(2)}, u32[]{:S(2)}) collective-permute-start(bf16[8,80,128]{2,1,0:T(8,128)(2,1)S(1)} %select_convert_fusion), channel_id=1, source_target_pairs={{0,2},{1,3},{2,0},{3,1},{4,6},{5,7},{6,4},{7,5},{8,10},{9,11},{10,... | collective-permute-start | bytes 491528 | tf_op jit(solution)/shard_map/ppermute | solution.py:24
  268.5 29.1 %collective-permute-start.41 = (bf16[32,80,128]{2,1,0:T(8,128)(2,1)S(1)}, bf16[32,80,128]{2,1,0:T(8,128)(2,1)S(1)}, u32[]{:S(2)}, u32[]{:S(2)}) collective-permute-start(bf16[32,80,128]{2,1,0:T(8,128)(2,1)S(1)} %pad_maximum_fusion.1.refs_0_), channel_id=1, source_target_pairs={{0,1},{1,0},{2,3},{3,2},{4,5},{5,4},{6,7},{7,6},{8,9},{9,8},{10,11... | collective-permute-start | bytes 1966088 | tf_op jit(solution)/shard_map/ppermute | solution.py:29
  278.8 5.8 %copy-start.1 = (bf16[32,80,128]{2,1,0:T(8,128)(2,1)}, bf16[32,80,128]{2,1,0:T(8,128)(2,1)S(1)}, u32[]{:S(2)}) copy-start(bf16[32,80,128]{2,1,0:T(8,128)(2,1)S(1)} %pad_maximum_fusion.3.refs_1_) | copy-start | bytes 1966084
  278.8 18.8 %collective-permute-start.42 = (bf16[32,80,128]{2,1,0:T(8,128)(2,1)S(1)}, bf16[32,80,128]{2,1,0:T(8,128)(2,1)S(1)}, u32[]{:S(2)}, u32[]{:S(2)}) collective-permute-start(bf16[32,80,128]{2,1,0:T(8,128)(2,1)S(1)} %pad_maximum_fusion.3.refs_1_), channel_id=1, source_target_pairs={{0,1},{1,0},{2,3},{3,2},{4,5},{5,4},{6,7},{7,6},{8,9},{9,8},{10,11... | collective-permute-start | bytes 1966088 | tf_op jit(solution)/shard_map/ppermute | solution.py:29
  297.6 0.8 copy-start.10
  298.4 0.8 copy-start.11
  (5 other events, 4.1 us)

commit v4 on v3

--- a/solution.py
+++ b/solution.py
@@ -1,3 +1,5 @@
+import math
+
 import jax
 import jax.numpy as jnp
 from jax import lax
@@ -11,6 +13,7 @@
 CORES = 2
 CHUNKS = 2
 UNROLL = 4
+SPARE_BYTES = 2 << 20
 
 BF16 = jnp.bfloat16
 F32 = jnp.float32
@@ -38,6 +41,17 @@
     return [own] + [ring_exchange(own, k) for k in range(1, ring)]
 
 
+def grant(*blocks):
+    total = 0
+    for shape, dtype in blocks:
+        total += math.prod(shape) * jnp.dtype(dtype).itemsize
+    return pltpu.CompilerParams(vmem_limit_bytes=total + total // 8 + SPARE_BYTES)
+
+
+def blocks_of(arrays):
+    return [(x.shape, x.dtype) for x in arrays]
+
+
 def cut_columns(weight, starts, width):
     count = starts.shape[0]
 
@@ -50,8 +64,26 @@
         out_shape=[jax.ShapeDtypeStruct((weight.shape[0], width), weight.dtype)] * count,
         in_specs=[SMEM, VMEM],
         out_specs=[VMEM] * count,
+        compiler_params=grant((weight.shape, BF16), (weight.shape, BF16)),
         name="cut_columns",
     )(starts, weight)
+
+
+def fetch(array):
+    def kernel(source, target, sem):
+        copy = pltpu.make_async_copy(source, target, sem)
+        copy.start()
+        copy.wait()
+
+    return pl.pallas_call(
+        kernel,
+        out_shape=jax.ShapeDtypeStruct(array.shape, array.dtype),
+        in_specs=[pl.BlockSpec(memory_space=pltpu.HBM)],
+        out_specs=VMEM,
+        scratch_shapes=[pltpu.SemaphoreType.DMA(())],
+        compiler_params=grant((array.shape, array.dtype)),
+        name="fetch",
+    )(pltpu.with_memory_space_constraint(array, pltpu.HBM))
 
 
 def select_blocks(pools, index, cap):
@@ -78,6 +110,7 @@
         out_shape=[jax.ShapeDtypeStruct((cap, docs, blk), BF16)] * outs,
         in_specs=[SMEM] + [VMEM] * len(pools),
         out_specs=[VMEM] * outs,
+        compiler_params=grant(*blocks_of(pools), ((outs * cap, docs, blk), BF16)),
         name="select_blocks",
     )(index, *pools)
 
@@ -107,6 +140,9 @@
         in_specs=[SMEM] + [VMEM] * len(parts),
         out_specs=[VMEM] * outs,
         scratch_shapes=[pltpu.VMEM((blocks, docs, blk), F32)],
+        compiler_params=grant(
+            *blocks_of(parts), ((blocks, docs, blk), F32), ((blocks, docs, blk), BF16)
+        ),
         name="add_blocks",
     )(index, *parts)
 
@@ -118,34 +154,25 @@
     uses = label_blocks * slots // (count * cap)
     pos_count = positives.shape[1]
 
-    def kernel(position_ref, order_ref, first_ref, positives_ref, weight_hbm, *refs):
+    def kernel(position_ref, order_ref, first_ref, positives_ref, weight_ref, *refs):
         ins = refs[:count]
         residual_ref = refs[count]
         outs = refs[count + 1 : 2 * count + 1]
-        pool, weight_ref, pool_sem, weight_sem = refs[2 * count + 1 :]
+        pool, pool_sem = refs[2 * count + 1 :]
         copies = [
             pltpu.make_async_copy(ins[q], pool.at[pl.ds(q * cap, cap)], pool_sem.at[q])
             for q in range(count)
         ]
-        loads = [
-            pltpu.make_async_copy(
-                weight_hbm.at[g], weight_ref.at[pl.ds(g * slots, slots)], weight_sem.at[g]
-            )
-            for g in range(label_blocks)
-        ]
-        for copy in copies + loads:
+        for copy in copies:
             copy.start()
         for copy in copies:
             copy.wait()
 
         def forward(g, carry):
-            pltpu.make_async_copy(
-                weight_hbm.at[g], weight_ref.at[pl.ds(g * slots, slots)], weight_sem.at[g]
-            ).wait()
             lhs = jnp.concatenate(
                 [pool[position_ref[g * slots + s]] for s in range(slots)], axis=1
             )
-            rhs = weight_ref[pl.ds(g * slots, slots)].reshape(slots * blk, blk)
+            rhs = weight_ref[g].reshape(slots * blk, blk)
             logits = jnp.dot(lhs, rhs, preferred_element_type=F32)
             ids = first_ref[0] + g * blk + lax.broadcasted_iota(jnp.int32, (docs, blk), 1)
             hit = positives_ref[:, 0:1] == ids
@@ -160,7 +187,7 @@
             def backward(k, carry):
                 where = [order_ref[(q * cap + k) * uses + u] for u in range(uses)]
                 lhs = jnp.concatenate([residual_ref[w // slots] for w in where], axis=1)
-                rhs = jnp.concatenate([weight_ref[w] for w in where], axis=1)
+                rhs = jnp.concatenate([weight_ref[w // slots, w % slots] for w in where], axis=1)
                 outs[q][k] = lax.dot_general(
                     lhs, rhs, (((1,), (1,)), ((), ())), preferred_element_type=F32
                 ).astype(BF16)
@@ -172,14 +199,17 @@
         kernel,
         out_shape=[jax.ShapeDtypeStruct((label_blocks, docs, blk), BF16)]
         + [jax.ShapeDtypeStruct((cap, docs, blk), BF16)] * count,
-        in_specs=[SMEM] * 3 + [VMEM, ANY] + [VMEM] * count,
+        in_specs=[SMEM] * 3 + [VMEM] * (2 + count),
         out_specs=[VMEM] * (count + 1),
         scratch_shapes=[
             pltpu.VMEM((count * cap, docs, blk), BF16),
-            pltpu.VMEM((label_blocks * slots, blk, blk), BF16),
             pltpu.SemaphoreType.DMA((count,)),
-            pltpu.SemaphoreType.DMA((label_blocks,)),
         ],
+        compiler_params=grant(
+            (weight.shape, BF16),
+            ((3 * count * cap, docs, blk), BF16),
+            ((label_blocks, docs, blk), BF16),
+        ),
         name="residual_and_back",
     )(slot_position, order, first_label, positives, weight, *parts)
     return out[0], list(out[1:])
@@ -224,6 +254,9 @@
         out_specs=ANY,
         input_output_aliases={1 + 2 * pieces: 0} if earlier else {},
         scratch_shapes=[pltpu.VMEM((cap * uses, blk, blk), BF16), pltpu.SemaphoreType.DMA(())],
+        compiler_params=grant(
+            ((cap * uses, blk, blk), BF16), *blocks_of(picked), *blocks_of(residuals)
+        ),
         name="block_weight_grad",
     )(order, *residuals, *picked, *earlier)
 
@@ -254,6 +287,9 @@
         out_shape=jax.ShapeDtypeStruct((rows, width), BF16),
         in_specs=[SMEM, VMEM] + [VMEM] * (len(sides) * chunks),
         out_specs=VMEM,
+        compiler_params=grant(
+            ((rows, width), BF16), ((rows, width), F32), *blocks_of(sum(sides, []))
+        ),
         name="expand_weight_grad",
     )(columns, documents, *[part for side in sides for part in side])
 
@@ -342,6 +378,7 @@
     kept = lax.dynamic_slice_in_dim(expanded, core * own_blocks, own_blocks, 0)
     given = lax.dynamic_slice_in_dim(expanded, (1 - core) * own_blocks, own_blocks, 0)
 
+    block_weight = fetch(sparse_weight)
     send, position, order = list_tables(
         feature_lists, feat_index, label_index, label_count, own_count, label_blocks, cap
     )
@@ -361,7 +398,7 @@
         for m in range(feat_count - 1, 0, -1):
             parts[m] = feat_exchange(outgoing[m], m)
         residual, back = residual_and_back(
-            parts, sparse_weight, position, order, known[i], first_label
+            parts, block_weight, position, order, known[i], first_label
         )
         picked.append(parts)
         residuals.append(residual)

time: 303 us -> 273 us (0.901)
  Pallas kernels: 73.6 us -> 49.6 us
  local copies, waits for them, and re-layouts: 10.3 us -> 2.6 us
    pallas_call x2, Pallas kernels: 35.4 us -> 22.3 us  [residual_and_back(): pl.pallas_call(kernel, out_shape=[jax.ShapeDtypeStruct((label_blocks, doc...]
    unnamed x54 -> x10, local copies, waits for them, and re-layouts: 7.15 us -> 1.84 us
    pallas_call x0 -> x1, Pallas kernels: none -> 4.59 us  [fetch(): pl.pallas_call(kernel, out_shape=jax.ShapeDtypeStruct(array.shape, array....]
    pallas_call x2, Pallas kernels: 7.44 us -> 3.29 us  [select_blocks(): pl.pallas_call(kernel, out_shape=[jax.ShapeDtypeStruct((cap, docs, blk),...]
    pallas_call x2, Pallas kernels: 6.68 us -> 2.75 us  [add_blocks(): pl.pallas_call(kernel, out_shape=[jax.ShapeDtypeStruct((size, docs, blk),...]
    pallas_call x4, Pallas kernels: 17.3 us -> 13.5 us  [block_weight_grad(): pl.pallas_call(kernel, out_shape=jax.ShapeDtypeStruct((label_blocks * slo...]
  transfers between devices with their start and end apart: 43 -> 43, of which waited for: 25 -> 24; matrix products, arithmetic and copies ran while one was open for 3% -> 2% of each run, Pallas kernels for 22% -> 17%
where the time goes in v4:
time: 273 us; the launch traced here: 272 us
  waiting for transfers between devices  154 us (56%)
  starting transfers between devices  59.4 us (22%)
  Pallas kernels  49.6 us (18%)
  matrix products  3.38 us (1%)
    ppermute x24, waiting for transfers between devices, ring_exchange(): lax.ppermute(x, 'label', [(i, i ^ flip * CORES) for i in range(count)])  91.4 us
    ppermute x12, waiting for transfers between devices, feat_exchange(): lax.ppermute(x, 'feat', [(i, i ^ flip) for i in range(lax.axis_size('feat...  59.8 us
    ppermute x24, starting transfers between devices, ring_exchange(): lax.ppermute(x, 'label', [(i, i ^ flip * CORES) for i in range(count)])  44.7 us
    pallas_call x2, Pallas kernels, residual_and_back(): pl.pallas_call(kernel, out_shape=[jax.ShapeDtypeStruct((label_blocks, doc...  22.3 us
    ppermute x12, starting transfers between devices, feat_exchange(): lax.ppermute(x, 'feat', [(i, i ^ flip) for i in range(lax.axis_size('feat...  14.3 us
    pallas_call x4, Pallas kernels, block_weight_grad(): pl.pallas_call(kernel, out_shape=jax.ShapeDtypeStruct((label_blocks * slo...  13.5 us
  transfers between devices with their start and end apart: 43, of which 24 were waited for; matrix products, arithmetic and copies ran while one was open for 2% of the time, Pallas kernels for 17%

profile of v4, /device:TPU:0, one launch (start us, length us, event | category | flops | bytes accessed | tf_op | source)
XLA Modules:
  0.0 272.3 jit_solution(6535777902921221542)
XLA Ops:
  0.7 1.6 copy-done
  2.3 0.7 cut_columns.1
  3.0 5.1 %collective-permute-start.5 = (bf16[160,128]{1,0:T(8,128)(2,1)S(1)}, bf16[160,128]{1,0:T(8,128)(2,1)S(1)}, u32[]{:S(2)}, u32[]{:S(2)}) collective-permute-start(bf16[160,128]{1,0:T(8,128)(2,1)S(1)} %copy-done.1), channel_id=1, source_target_pairs={{0,6},{1,7},{2,4},{3,5},{4,2},{5,3},{6,0},{7,1},{8,14},{9,15},{10,... | collective-permute-start | bytes 122888 | tf_op jit(solution)/shard_map/ppermute | solution.py:27
  8.7 1.4 collective-permute-start
  10.1 2.4 collective-permute-start.4
  15.8 9.3 %collective-permute-done = bf16[128,2048]{1,0:T(8,128)(2,1)} collective-permute-done((bf16[128,2048]{1,0:T(8,128)(2,1)S(1)}, bf16[128,2048]{1,0:T(8,128)(2,1)}, u32[]{:S(2)}, u32[]{:S(2)}) %collective-permute-start) | collective-permute-done | bytes 524320 | tf_op jit(solution)/shard_map/ppermute | solution.py:27
  25.0 1.4 convolution_add_fusion.1
  26.4 11.2 %collective-permute-done.4 = bf16[128,2048]{1,0:T(8,128)(2,1)} collective-permute-done((bf16[128,2048]{1,0:T(8,128)(2,1)S(1)}, bf16[128,2048]{1,0:T(8,128)(2,1)}, u32[]{:S(2)}, u32[]{:S(2)}) %collective-permute-start.4) | collective-permute-done | bytes 524320 | tf_op jit(solution)/shard_map/ppermute | solution.py:27
  37.6 1.4 fusion.4
  39.0 19.0 %collective-permute-done.2 = bf16[128,2048]{1,0:T(8,128)(2,1)S(1)} collective-permute-done((bf16[128,2048]{1,0:T(8,128)(2,1)S(1)}, bf16[128,2048]{1,0:T(8,128)(2,1)S(1)}, u32[]{:S(2)}, u32[]{:S(2)}) %collective-permute-start.2) | collective-permute-done | bytes 524320 | tf_op jit(solution)/shard_map/ppermute | solution.py:27
  58.4 2.1 collective-permute-done.6
  60.6 2.3 collective-permute-start.9
  62.9 2.1 collective-permute-start.7
  65.1 4.6 %collective-permute-done.9 = bf16[8,80,128]{2,1,0:T(8,128)(2,1)S(1)} collective-permute-done((bf16[8,80,128]{2,1,0:T(8,128)(2,1)S(1)}, bf16[8,80,128]{2,1,0:T(8,128)(2,1)S(1)}, u32[]{:S(2)}, u32[]{:S(2)}) %collective-permute-start.9) | collective-permute-done | bytes 163872 | tf_op jit(solution)/shard_map/ppermute | solution.py:27
  69.7 6.7 %collective-permute-done.8 = bf16[8,80,128]{2,1,0:T(8,128)(2,1)S(1)} collective-permute-done((bf16[8,80,128]{2,1,0:T(8,128)(2,1)S(1)}, bf16[8,80,128]{2,1,0:T(8,128)(2,1)S(1)}, u32[]{:S(2)}, u32[]{:S(2)}) %collective-permute-start.8) | collective-permute-done | bytes 163872 | tf_op jit(solution)/shard_map/ppermute | solution.py:27
  76.6 1.7 collective-permute-start.26
  78.6 1.7 select_blocks.2
  80.4 1.6 collective-permute-start.11
  81.9 1.5 collective-permute-start.12
  83.9 1.1 collective-permute-done.26
  85.0 1.5 collective-permute-start.24
  86.6 6.6 %collective-permute-done.25 = bf16[8,80,128]{2,1,0:T(8,128)(2,1)S(1)} collective-permute-done((bf16[8,80,128]{2,1,0:T(8,128)(2,1)S(1)}, bf16[8,80,128]{2,1,0:T(8,128)(2,1)S(1)}, u32[]{:S(2)}, u32[]{:S(2)}) %collective-permute-start.25) | collective-permute-done | bytes 163872 | tf_op jit(solution)/shard_map/ppermute | solution.py:27
  93.2 1.0 collective-permute-done.24
  94.3 4.6 %fetch.1.weight_ref = bf16[24,16,128,128]{3,2,1,0:T(8,128)(2,1)S(1)} custom-call(bf16[24,16,128,128]{3,2,1,0:T(8,128)(2,1)} %source.1), custom_call_target="tpu_custom_call" | custom-call | tf_op jit(solution)/shard_map/fetch/pallas_call | solution.py:78
  98.9 6.5 %collective-permute-done.12.refs_2_ = bf16[24,80,128]{2,1,0:T(8,128)(2,1)S(1)} collective-permute-done((bf16[24,80,128]{2,1,0:T(8,128)(2,1)S(1)}, bf16[24,80,128]{2,1,0:T(8,128)(2,1)S(1)}, u32[]{:S(2)}, u32[]{:S(2)}) %collective-permute-start.12) | collective-permute-done | bytes 491552 | tf_op jit(solution)/shard_map/ppermute | solution.py:36
  105.5 11.2 %residual_and_back.2 = (bf16[24,80,128]{2,1,0:T(8,128)(2,1)S(1)}, bf16[24,80,128]{2,1,0:T(8,128)(2,1)S(1)}, bf16[24,80,128]{2,1,0:T(8,128)(2,1)S(1)}, bf16[24,80...) custom-call(s32[384]{0:T(512)S(1)} %select_reduce_fusion.1.position_ref, s32[384]{0:T(512)S(1)} %select_reduce_fusion.order_ref, ...), custom_call_target="tpu_custom_call" | custom-call | tf_op jit(solution)/shard_map/residual_and_back/pallas_call | solution.py:198
  116.6 1.3 collective-permute-start.14
  117.9 0.8 collective-permute-start.15
  118.7 1.4 collective-permute-start.16
  120.2 1.6 select_blocks.3
  121.7 1.3 collective-permute-start.28
  123.0 0.8 collective-permute-start.29
  123.9 6.9 %collective-permute-done.14.refs_1_ = bf16[24,80,128]{2,1,0:T(8,128)(2,1)S(1)} collective-permute-done((bf16[24,80,128]{2,1,0:T(8,128)(2,1)S(1)}, bf16[24,80,128]{2,1,0:T(8,128)(2,1)S(1)}, u32[]{:S(2)}, u32[]{:S(2)}) %collective-permute-start.14) | collective-permute-done | bytes 491552 | tf_op jit(solution)/shard_map/ppermute | solution.py:36
  130.8 1.5 collective-permute-start.30
  132.3 10.3 %collective-permute-done.15.refs_2_ = bf16[24,80,128]{2,1,0:T(8,128)(2,1)S(1)} collective-permute-done((bf16[24,80,128]{2,1,0:T(8,128)(2,1)S(1)}, bf16[24,80,128]{2,1,0:T(8,128)(2,1)S(1)}, u32[]{:S(2)}, u32[]{:S(2)}) %collective-permute-start.15) | collective-permute-done | bytes 491552 | tf_op jit(solution)/shard_map/ppermute | solution.py:36
  142.5 1.4 add_blocks.2
  144.0 7.9 %collective-permute-done.28.refs_1_.refs_3_ = bf16[24,80,128]{2,1,0:T(8,128)(2,1)S(1)} collective-permute-done((bf16[24,80,128]{2,1,0:T(8,128)(2,1)S(1)}, bf16[24,80,128]{2,1,0:T(8,128)(2,1)S(1)}, u32[]{:S(2)}, u32[]{:S(2)}) %collective-permute-start.28) | collective-permute-done | bytes 491552 | tf_op jit(solution)/shard_map/ppermute | solution.py:36
  151.9 9.7 %collective-permute-done.29.refs_2_.refs_3_ = bf16[24,80,128]{2,1,0:T(8,128)(2,1)S(1)} collective-permute-done((bf16[24,80,128]{2,1,0:T(8,128)(2,1)S(1)}, bf16[24,80,128]{2,1,0:T(8,128)(2,1)S(1)}, u32[]{:S(2)}, u32[]{:S(2)}) %collective-permute-start.29) | collective-permute-done | bytes 491552 | tf_op jit(solution)/shard_map/ppermute | solution.py:36
  161.6 11.1 %residual_and_back.3 = (bf16[24,80,128]{2,1,0:T(8,128)(2,1)S(1)}, bf16[24,80,128]{2,1,0:T(8,128)(2,1)S(1)}, bf16[24,80,128]{2,1,0:T(8,128)(2,1)S(1)}, bf16[24,80...) custom-call(s32[384]{0:T(512)S(1)} %select_reduce_fusion.1.position_ref, s32[384]{0:T(512)S(1)} %select_reduce_fusion.order_ref, ...), custom_call_target="tpu_custom_call" | custom-call | tf_op jit(solution)/shard_map/residual_and_back/pallas_call | solution.py:198
  173.4 1.5 collective-permute-start.32
  174.8 1.5 collective-permute-start.33
  176.3 10.6 %collective-permute-done.31.refs_1_ = bf16[24,80,128]{2,1,0:T(8,128)(2,1)S(1)} collective-permute-done((bf16[24,80,128]{2,1,0:T(8,128)(2,1)S(1)}, bf16[24,80,128]{2,1,0:T(8,128)(2,1)S(1)}, u32[]{:S(2)}, u32[]{:S(2)}) %collective-permute-start.31) | collective-permute-done | bytes 491552 | tf_op jit(solution)/shard_map/ppermute | solution.py:36
  186.9 7.8 %collective-permute-done.32.refs_2_ = bf16[24,80,128]{2,1,0:T(8,128)(2,1)S(1)} collective-permute-done((bf16[24,80,128]{2,1,0:T(8,128)(2,1)S(1)}, bf16[24,80,128]{2,1,0:T(8,128)(2,1)S(1)}, u32[]{:S(2)}, u32[]{:S(2)}) %collective-permute-start.32) | collective-permute-done | bytes 491552 | tf_op jit(solution)/shard_map/ppermute | solution.py:36
  194.7 1.4 add_blocks.3
  196.4 1.9 collective-permute-start.18
  198.3 2.6 collective-permute-start.19
  201.1 1.9 collective-permute-start.35
  203.0 2.4 collective-permute-done.18
  205.4 1.7 collective-permute-start.36
  207.1 4.0 %collective-permute-done.20 = bf16[8,80,128]{2,1,0:T(8,128)(2,1)S(1)} collective-permute-done((bf16[8,80,128]{2,1,0:T(8,128)(2,1)S(1)}, bf16[8,80,128]{2,1,0:T(8,128)(2,1)S(1)}, u32[]{:S(2)}, u32[]{:S(2)}) %collective-permute-start.20) | collective-permute-done | bytes 163872 | tf_op jit(solution)/shard_map/ppermute | solution.py:27
  211.1 5.9 %collective-permute-done.19 = bf16[8,80,128]{2,1,0:T(8,128)(2,1)S(1)} collective-permute-done((bf16[8,80,128]{2,1,0:T(8,128)(2,1)S(1)}, bf16[8,80,128]{2,1,0:T(8,128)(2,1)S(1)}, u32[]{:S(2)}, u32[]{:S(2)}) %collective-permute-start.19) | collective-permute-done | bytes 163872 | tf_op jit(solution)/shard_map/ppermute | solution.py:27
  217.1 1.6 collective-permute-start.23
  218.8 12.9 %collective-permute-start.21 = (bf16[8,80,128]{2,1,0:T(8,128)(2,1)S(1)}, bf16[8,80,128]{2,1,0:T(8,128)(2,1)S(1)}, u32[]{:S(2)}, u32[]{:S(2)}) collective-permute-start(bf16[8,80,128]{2,1,0:T(8,128)(2,1)S(1)} %select_convert_fusion.1), channel_id=1, source_target_pairs={{0,2},{1,3},{2,0},{3,1},{4,6},{5,7},{6,4},{7,5},{8,10},{9,11},{10,... | collective-permute-start | bytes 491528 | tf_op jit(solution)/shard_map/ppermute | solution.py:27
  231.6 3.0 %collective-permute-done.36 = bf16[8,80,128]{2,1,0:T(8,128)(2,1)S(1)} collective-permute-done((bf16[8,80,128]{2,1,0:T(8,128)(2,1)S(1)}, bf16[8,80,128]{2,1,0:T(8,128)(2,1)S(1)}, u32[]{:S(2)}, u32[]{:S(2)}) %collective-permute-start.36) | collective-permute-done | bytes 163872 | tf_op jit(solution)/shard_map/ppermute | solution.py:27
  234.7 6.4 %collective-permute-done.22 = bf16[8,80,128]{2,1,0:T(8,128)(2,1)S(1)} collective-permute-done((bf16[8,80,128]{2,1,0:T(8,128)(2,1)S(1)}, bf16[8,80,128]{2,1,0:T(8,128)(2,1)S(1)}, u32[]{:S(2)}, u32[]{:S(2)}) %collective-permute-start.22) | collective-permute-done | bytes 163872 | tf_op jit(solution)/shard_map/ppermute | solution.py:27
  241.3 1.6 collective-permute-start.40
  242.9 2.8 %collective-permute-start.38 = (bf16[8,80,128]{2,1,0:T(8,128)(2,1)S(1)}, bf16[8,80,128]{2,1,0:T(8,128)(2,1)S(1)}, u32[]{:S(2)}, u32[]{:S(2)}) collective-permute-start(bf16[8,80,128]{2,1,0:T(8,128)(2,1)S(1)} %select_convert_fusion), channel_id=1, source_target_pairs={{0,2},{1,3},{2,0},{3,1},{4,6},{5,7},{6,4},{7,5},{8,10},{9,11},{10,... | collective-permute-start | bytes 491528 | tf_op jit(solution)/shard_map/ppermute | solution.py:27
  245.8 4.6 %collective-permute-done.40 = bf16[8,80,128]{2,1,0:T(8,128)(2,1)S(1)} collective-permute-done((bf16[8,80,128]{2,1,0:T(8,128)(2,1)S(1)}, bf16[8,80,128]{2,1,0:T(8,128)(2,1)S(1)}, u32[]{:S(2)}, u32[]{:S(2)}) %collective-permute-start.40) | collective-permute-done | bytes 163872 | tf_op jit(solution)/shard_map/ppermute | solution.py:27
  250.4 5.6 %collective-permute-done.39 = bf16[8,80,128]{2,1,0:T(8,128)(2,1)S(1)} collective-permute-done((bf16[8,80,128]{2,1,0:T(8,128)(2,1)S(1)}, bf16[8,80,128]{2,1,0:T(8,128)(2,1)S(1)}, u32[]{:S(2)}, u32[]{:S(2)}) %collective-permute-start.39) | collective-permute-done | bytes 163872 | tf_op jit(solution)/shard_map/ppermute | solution.py:27
  256.2 3.4 %block_weight_grad.4.refs_4_ = bf16[384,128,128]{2,1,0:T(8,128)(2,1)} custom-call(s32[96]{0:T(128)S(1)} %get-tuple-element.82.order_ref, bf16[24,80,128]{2,1,0:T(8,128)(2,1)S(1)} %get-tuple-element.70.refs_0_, bf16[24,80,128]{2,1,0:T(8,128)(2,1)S(1)} %get-tuple-element.71.refs_1_, bf16[24,80,128]{2,1,0:T(8,128)(2,1)S(1)} %get-tuple-element.48.refs_0_.refs_2_, ...), custom_call_target="tpu_custom_call" | custom-call | tf_op jit(solution)/shard_map/block_weight_grad/pallas_call | solution.py:250
  259.6 3.4 %block_weight_grad.5.refs_4_ = bf16[384,128,128]{2,1,0:T(8,128)(2,1)} custom-call(s32[96]{0:T(128)S(1)} %get-tuple-element.83.order_ref, bf16[24,80,128]{2,1,0:T(8,128)(2,1)S(1)} %get-tuple-element.70.refs_0_, bf16[24,80,128]{2,1,0:T(8,128)(2,1)S(1)} %get-tuple-element.71.refs_1_, ...), custom_call_target="tpu_custom_call", output_to_operand_aliasing={{}: (5, {})} | custom-call | tf_op jit(solution)/shard_map/block_weight_grad/pallas_call | solution.py:250
  263.0 3.4 %block_weight_grad.6.refs_4_ = bf16[384,128,128]{2,1,0:T(8,128)(2,1)} custom-call(s32[96]{0:T(128)S(1)} %get-tuple-element.84.order_ref, bf16[24,80,128]{2,1,0:T(8,128)(2,1)S(1)} %get-tuple-element.70.refs_0_, bf16[24,80,128]{2,1,0:T(8,128)(2,1)S(1)} %get-tuple-element.71.refs_1_, ...), custom_call_target="tpu_custom_call", output_to_operand_aliasing={{}: (5, {})} | custom-call | tf_op jit(solution)/shard_map/block_weight_grad/pallas_call | solution.py:250
  266.4 3.4 %block_weight_grad.7 = bf16[384,128,128]{2,1,0:T(8,128)(2,1)} custom-call(s32[96]{0:T(128)S(1)} %get-tuple-element.85.order_ref, bf16[24,80,128]{2,1,0:T(8,128)(2,1)S(1)} %get-tuple-element.70.refs_0_, bf16[24,80,128]{2,1,0:T(8,128)(2,1)S(1)} %get-tuple-element.71.refs_1_, ...), custom_call_target="tpu_custom_call", output_to_operand_aliasing={{}: (5, {})} | custom-call | tf_op jit(solution)/shard_map/block_weight_grad/pallas_call | solution.py:250
  269.7 2.6 expand_weight_grad.1
  (89 shorter events, 7.4 us)
Async XLA Ops:
  0.7 1.6 copy-start
  2.2 0.8 copy-start.1
  2.3 10.3 %copy-start.2 = (s32[768,16]{0,1:T(8,128)S(1)}, s32[768,16]{0,1:T(8,128)}, u32[]{:S(2)}) copy-start(s32[768,16]{0,1:T(8,128)} %param.8) | copy-start | bytes 147460
  2.3 11.1 %copy-start.3 = (s32[160,8]{0,1:T(8,128)S(1)}, s32[160,8]{0,1:T(8,128)}, u32[]{:S(2)}) copy-start(s32[160,8]{0,1:T(8,128)} %param.9) | copy-start | bytes 15364
  3.0 23.4 %collective-permute-start.5 = (bf16[160,128]{1,0:T(8,128)(2,1)S(1)}, bf16[160,128]{1,0:T(8,128)(2,1)S(1)}, u32[]{:S(2)}, u32[]{:S(2)}) collective-permute-start(bf16[160,128]{1,0:T(8,128)(2,1)S(1)} %copy-done.1), channel_id=1, source_target_pairs={{0,6},{1,7},{2,4},{3,5},{4,2},{5,3},{6,0},{7,1},{8,14},{9,15},{10,... | collective-permute-start | bytes 122888 | tf_op jit(solution)/shard_map/ppermute | solution.py:27
  8.1 30.8 %collective-permute-start.3 = (bf16[160,128]{1,0:T(8,128)(2,1)S(1)}, bf16[160,128]{1,0:T(8,128)(2,1)S(1)}, u32[]{:S(2)}, u32[]{:S(2)}) collective-permute-start(bf16[160,128]{1,0:T(8,128)(2,1)S(1)} %copy-done.1), channel_id=1, source_target_pairs={{0,4},{1,5},{2,6},{3,7},{4,0},{5,1},{6,2},{7,3},{8,12},{9,13},{10,... | collective-permute-start | bytes 122888 | tf_op jit(solution)/shard_map/ppermute | solution.py:27
  8.1 7.1 %collective-permute-start.1 = (bf16[160,128]{1,0:T(8,128)(2,1)S(1)}, bf16[160,128]{1,0:T(8,128)(2,1)}, u32[]{:S(2)}, u32[]{:S(2)}) collective-permute-start(bf16[160,128]{1,0:T(8,128)(2,1)S(1)} %copy-done.1), channel_id=1, source_target_pairs={{0,2},{1,3},{2,0},{3,1},{4,6},{5,7},{6,4},{7,5},{8,10},{9,11},{10,... | collective-permute-start | bytes 122888 | tf_op jit(solution)/shard_map/ppermute | solution.py:27
  8.7 16.3 %collective-permute-start = (bf16[128,2048]{1,0:T(8,128)(2,1)S(1)}, bf16[128,2048]{1,0:T(8,128)(2,1)}, u32[]{:S(2)}, u32[]{:S(2)}) collective-permute-start(bf16[128,2048]{1,0:T(8,128)(2,1)S(1)} %get-tuple-element.38), channel_id=1, source_target_pairs={{0,2},{1,3},{2,0},{3,1},{4,6},{5,7},{6,4},{7,5},{8,10},{9,11},{10,... | collective-permute-start | bytes 1572872 | tf_op jit(solution)/shard_map/ppermute | solution.py:27
  10.1 27.4 %collective-permute-start.4 = (bf16[128,2048]{1,0:T(8,128)(2,1)S(1)}, bf16[128,2048]{1,0:T(8,128)(2,1)}, u32[]{:S(2)}, u32[]{:S(2)}) collective-permute-start(bf16[128,2048]{1,0:T(8,128)(2,1)S(1)} %get-tuple-element.41), channel_id=1, source_target_pairs={{0,6},{1,7},{2,4},{3,5},{4,2},{5,3},{6,0},{7,1},{8,14},{9,15},{10,... | collective-permute-start | bytes 1572872 | tf_op jit(solution)/shard_map/ppermute | solution.py:27
  15.2 42.7 %collective-permute-start.2 = (bf16[128,2048]{1,0:T(8,128)(2,1)S(1)}, bf16[128,2048]{1,0:T(8,128)(2,1)S(1)}, u32[]{:S(2)}, u32[]{:S(2)}) collective-permute-start(bf16[128,2048]{1,0:T(8,128)(2,1)S(1)} %get-tuple-element.40), channel_id=1, source_target_pairs={{0,4},{1,5},{2,6},{3,7},{4,0},{5,1},{6,2},{7,3},{8,12},{9,13},{10,... | collective-permute-start | bytes 1572872 | tf_op jit(solution)/shard_map/ppermute | solution.py:27
  58.3 2.2 collective-permute-start.6
  60.6 9.1 %collective-permute-start.9 = (bf16[8,80,128]{2,1,0:T(8,128)(2,1)S(1)}, bf16[8,80,128]{2,1,0:T(8,128)(2,1)S(1)}, u32[]{:S(2)}, u32[]{:S(2)}) collective-permute-start(bf16[8,80,128]{2,1,0:T(8,128)(2,1)S(1)} %get-tuple-element.79), channel_id=1, source_target_pairs={{0,6},{1,7},{2,4},{3,5},{4,2},{5,3},{6,0},{7,1},{8,14},{9,15},{10,... | collective-permute-start | bytes 491528 | tf_op jit(solution)/shard_map/ppermute | solution.py:27
  62.9 13.4 %collective-permute-start.8 = (bf16[8,80,128]{2,1,0:T(8,128)(2,1)S(1)}, bf16[8,80,128]{2,1,0:T(8,128)(2,1)S(1)}, u32[]{:S(2)}, u32[]{:S(2)}) collective-permute-start(bf16[8,80,128]{2,1,0:T(8,128)(2,1)S(1)} %get-tuple-element.79), channel_id=1, source_target_pairs={{0,4},{1,5},{2,6},{3,7},{4,0},{5,1},{6,2},{7,3},{8,12},{9,13},{10,... | collective-permute-start | bytes 491528 | tf_op jit(solution)/shard_map/ppermute | solution.py:27
  62.9 13.4 %collective-permute-start.7 = (bf16[8,80,128]{2,1,0:T(8,128)(2,1)S(1)}, bf16[8,80,128]{2,1,0:T(8,128)(2,1)S(1)}, u32[]{:S(2)}, u32[]{:S(2)}) collective-permute-start(bf16[8,80,128]{2,1,0:T(8,128)(2,1)S(1)} %get-tuple-element.79), channel_id=1, source_target_pairs={{0,2},{1,3},{2,0},{3,1},{4,6},{5,7},{6,4},{7,5},{8,10},{9,11},{10,... | collective-permute-start | bytes 491528 | tf_op jit(solution)/shard_map/ppermute | solution.py:27
  76.5 2.2 collective-permute-start.10
  76.6 8.5 %collective-permute-start.26 = (bf16[8,80,128]{2,1,0:T(8,128)(2,1)S(1)}, bf16[8,80,128]{2,1,0:T(8,128)(2,1)S(1)}, u32[]{:S(2)}, u32[]{:S(2)}) collective-permute-start(bf16[8,80,128]{2,1,0:T(8,128)(2,1)S(1)} %get-tuple-element.78), channel_id=1, source_target_pairs={{0,6},{1,7},{2,4},{3,5},{4,2},{5,3},{6,0},{7,1},{8,14},{9,15},{10,... | collective-permute-start | bytes 491528 | tf_op jit(solution)/shard_map/ppermute | solution.py:27
  80.4 18.5 %collective-permute-start.11 = (bf16[24,80,128]{2,1,0:T(8,128)(2,1)S(1)}, bf16[24,80,128]{2,1,0:T(8,128)(2,1)S(1)}, u32[]{:S(2)}, u32[]{:S(2)}) collective-permute-start(bf16[24,80,128]{2,1,0:T(8,128)(2,1)S(1)} %get-tuple-element.49), channel_id=1, source_target_pairs={{0,8},{8,0},{16,24},{24,16},{1,9},{9,1},{17,25},{25,17},{2,10},{10... | collective-permute-start | bytes 1474568 | tf_op jit(solution)/shard_map/ppermute | solution.py:36
  81.9 23.5 %collective-permute-start.12 = (bf16[24,80,128]{2,1,0:T(8,128)(2,1)S(1)}, bf16[24,80,128]{2,1,0:T(8,128)(2,1)S(1)}, u32[]{:S(2)}, u32[]{:S(2)}) collective-permute-start(bf16[24,80,128]{2,1,0:T(8,128)(2,1)S(1)} %get-tuple-element.50), channel_id=1, source_target_pairs={{0,16},{8,24},{16,0},{24,8},{1,17},{9,25},{17,1},{25,9},{2,18},{10... | collective-permute-start | bytes 1474568 | tf_op jit(solution)/shard_map/ppermute | solution.py:36
  83.5 22.0 %collective-permute-start.13 = (bf16[24,80,128]{2,1,0:T(8,128)(2,1)S(1)}, bf16[24,80,128]{2,1,0:T(8,128)(2,1)S(1)}, u32[]{:S(2)}, u32[]{:S(2)}) collective-permute-start(bf16[24,80,128]{2,1,0:T(8,128)(2,1)S(1)} %get-tuple-element.51), channel_id=1, source_target_pairs={{0,24},{8,16},{16,8},{24,0},{1,25},{9,17},{17,9},{25,1},{2,26},{10... | collective-permute-start | bytes 1474568 | tf_op jit(solution)/shard_map/ppermute | solution.py:36
  83.9 9.2 %collective-permute-start.25 = (bf16[8,80,128]{2,1,0:T(8,128)(2,1)S(1)}, bf16[8,80,128]{2,1,0:T(8,128)(2,1)S(1)}, u32[]{:S(2)}, u32[]{:S(2)}) collective-permute-start(bf16[8,80,128]{2,1,0:T(8,128)(2,1)S(1)} %get-tuple-element.78), channel_id=1, source_target_pairs={{0,4},{1,5},{2,6},{3,7},{4,0},{5,1},{6,2},{7,3},{8,12},{9,13},{10,... | collective-permute-start | bytes 491528 | tf_op jit(solution)/shard_map/ppermute | solution.py:27
  85.0 9.1 %collective-permute-start.24 = (bf16[8,80,128]{2,1,0:T(8,128)(2,1)S(1)}, bf16[8,80,128]{2,1,0:T(8,128)(2,1)S(1)}, u32[]{:S(2)}, u32[]{:S(2)}) collective-permute-start(bf16[8,80,128]{2,1,0:T(8,128)(2,1)S(1)} %get-tuple-element.78), channel_id=1, source_target_pairs={{0,2},{1,3},{2,0},{3,1},{4,6},{5,7},{6,4},{7,5},{8,10},{9,11},{10,... | collective-permute-start | bytes 491528 | tf_op jit(solution)/shard_map/ppermute | solution.py:27
  94.2 25.9 %collective-permute-start.27 = (bf16[32,80,128]{2,1,0:T(8,128)(2,1)S(1)}, bf16[32,80,128]{2,1,0:T(8,128)(2,1)S(1)}, u32[]{:S(2)}, u32[]{:S(2)}) collective-permute-start(bf16[32,80,128]{2,1,0:T(8,128)(2,1)S(1)} %pad_maximum_fusion.2.refs_0_), channel_id=1, source_target_pairs={{0,1},{1,0},{2,3},{3,2},{4,5},{5,4},{6,7},{7,6},{8,9},{9,8},{10,11... | collective-permute-start | bytes 1966088 | tf_op jit(solution)/shard_map/ppermute | solution.py:32
  116.6 14.2 %collective-permute-start.14 = (bf16[24,80,128]{2,1,0:T(8,128)(2,1)S(1)}, bf16[24,80,128]{2,1,0:T(8,128)(2,1)S(1)}, u32[]{:S(2)}, u32[]{:S(2)}) collective-permute-start(bf16[24,80,128]{2,1,0:T(8,128)(2,1)S(1)} %get-tuple-element.53), channel_id=1, source_target_pairs={{0,8},{8,0},{16,24},{24,16},{1,9},{9,1},{17,25},{25,17},{2,10},{10... | collective-permute-start | bytes 1474568 | tf_op jit(solution)/shard_map/ppermute | solution.py:36
  117.9 24.6 %collective-permute-start.15 = (bf16[24,80,128]{2,1,0:T(8,128)(2,1)S(1)}, bf16[24,80,128]{2,1,0:T(8,128)(2,1)S(1)}, u32[]{:S(2)}, u32[]{:S(2)}) collective-permute-start(bf16[24,80,128]{2,1,0:T(8,128)(2,1)S(1)} %get-tuple-element.54), channel_id=1, source_target_pairs={{0,16},{8,24},{16,0},{24,8},{1,17},{9,25},{17,1},{25,9},{2,18},{10... | collective-permute-start | bytes 1474568 | tf_op jit(solution)/shard_map/ppermute | solution.py:36
  118.7 23.8 %collective-permute-start.16 = (bf16[24,80,128]{2,1,0:T(8,128)(2,1)S(1)}, bf16[24,80,128]{2,1,0:T(8,128)(2,1)S(1)}, u32[]{:S(2)}, u32[]{:S(2)}) collective-permute-start(bf16[24,80,128]{2,1,0:T(8,128)(2,1)S(1)} %get-tuple-element.55), channel_id=1, source_target_pairs={{0,24},{8,16},{16,8},{24,0},{1,25},{9,17},{17,9},{25,1},{2,26},{10... | collective-permute-start | bytes 1474568 | tf_op jit(solution)/shard_map/ppermute | solution.py:36
  121.7 30.2 %collective-permute-start.28 = (bf16[24,80,128]{2,1,0:T(8,128)(2,1)S(1)}, bf16[24,80,128]{2,1,0:T(8,128)(2,1)S(1)}, u32[]{:S(2)}, u32[]{:S(2)}) collective-permute-start(bf16[24,80,128]{2,1,0:T(8,128)(2,1)S(1)} %get-tuple-element.60), channel_id=1, source_target_pairs={{0,8},{8,0},{16,24},{24,16},{1,9},{9,1},{17,25},{25,17},{2,10},{10... | collective-permute-start | bytes 1474568 | tf_op jit(solution)/shard_map/ppermute | solution.py:36
  123.0 38.6 %collective-permute-start.29 = (bf16[24,80,128]{2,1,0:T(8,128)(2,1)S(1)}, bf16[24,80,128]{2,1,0:T(8,128)(2,1)S(1)}, u32[]{:S(2)}, u32[]{:S(2)}) collective-permute-start(bf16[24,80,128]{2,1,0:T(8,128)(2,1)S(1)} %get-tuple-element.61), channel_id=1, source_target_pairs={{0,16},{8,24},{16,0},{24,8},{1,17},{9,25},{17,1},{25,9},{2,18},{10... | collective-permute-start | bytes 1474568 | tf_op jit(solution)/shard_map/ppermute | solution.py:36
  130.8 30.9 %collective-permute-start.30 = (bf16[24,80,128]{2,1,0:T(8,128)(2,1)S(1)}, bf16[24,80,128]{2,1,0:T(8,128)(2,1)S(1)}, u32[]{:S(2)}, u32[]{:S(2)}) collective-permute-start(bf16[24,80,128]{2,1,0:T(8,128)(2,1)S(1)} %get-tuple-element.62), channel_id=1, source_target_pairs={{0,24},{8,16},{16,8},{24,0},{1,25},{9,17},{17,9},{25,1},{2,26},{10... | collective-permute-start | bytes 1474568 | tf_op jit(solution)/shard_map/ppermute | solution.py:36
  143.9 52.3 %collective-permute-start.17 = (bf16[32,80,128]{2,1,0:T(8,128)(2,1)S(1)}, bf16[32,80,128]{2,1,0:T(8,128)(2,1)S(1)}, u32[]{:S(2)}, u32[]{:S(2)}) collective-permute-start(bf16[32,80,128]{2,1,0:T(8,128)(2,1)S(1)} %get-tuple-element.57), channel_id=1, source_target_pairs={{0,1},{1,0},{2,3},{3,2},{4,5},{5,4},{6,7},{7,6},{8,9},{9,8},{10,11... | collective-permute-start | bytes 1966088 | tf_op jit(solution)/shard_map/ppermute | solution.py:32
  172.8 14.2 %collective-permute-start.31 = (bf16[24,80,128]{2,1,0:T(8,128)(2,1)S(1)}, bf16[24,80,128]{2,1,0:T(8,128)(2,1)S(1)}, u32[]{:S(2)}, u32[]{:S(2)}) collective-permute-start(bf16[24,80,128]{2,1,0:T(8,128)(2,1)S(1)} %get-tuple-element.64), channel_id=1, source_target_pairs={{0,8},{8,0},{16,24},{24,16},{1,9},{9,1},{17,25},{25,17},{2,10},{10... | collective-permute-start | bytes 1474568 | tf_op jit(solution)/shard_map/ppermute | solution.py:36
  173.4 21.3 %collective-permute-start.32 = (bf16[24,80,128]{2,1,0:T(8,128)(2,1)S(1)}, bf16[24,80,128]{2,1,0:T(8,128)(2,1)S(1)}, u32[]{:S(2)}, u32[]{:S(2)}) collective-permute-start(bf16[24,80,128]{2,1,0:T(8,128)(2,1)S(1)} %get-tuple-element.65), channel_id=1, source_target_pairs={{0,16},{8,24},{16,0},{24,8},{1,17},{9,25},{17,1},{25,9},{2,18},{10... | collective-permute-start | bytes 1474568 | tf_op jit(solution)/shard_map/ppermute | solution.py:36
  174.8 19.9 %collective-permute-start.33 = (bf16[24,80,128]{2,1,0:T(8,128)(2,1)S(1)}, bf16[24,80,128]{2,1,0:T(8,128)(2,1)S(1)}, u32[]{:S(2)}, u32[]{:S(2)}) collective-permute-start(bf16[24,80,128]{2,1,0:T(8,128)(2,1)S(1)} %get-tuple-element.66), channel_id=1, source_target_pairs={{0,24},{8,16},{16,8},{24,0},{1,25},{9,17},{17,9},{25,1},{2,26},{10... | collective-permute-start | bytes 1474568 | tf_op jit(solution)/shard_map/ppermute | solution.py:36
  196.1 4.8 %collective-permute-start.34 = (bf16[32,80,128]{2,1,0:T(8,128)(2,1)S(1)}, bf16[32,80,128]{2,1,0:T(8,128)(2,1)S(1)}, u32[]{:S(2)}, u32[]{:S(2)}) collective-permute-start(bf16[32,80,128]{2,1,0:T(8,128)(2,1)S(1)} %get-tuple-element.68), channel_id=1, source_target_pairs={{0,1},{1,0},{2,3},{3,2},{4,5},{5,4},{6,7},{7,6},{8,9},{9,8},{10,11... | collective-permute-start | bytes 1966088 | tf_op jit(solution)/shard_map/ppermute | solution.py:32
  196.4 9.0 %collective-permute-start.18 = (bf16[8,80,128]{2,1,0:T(8,128)(2,1)S(1)}, bf16[8,80,128]{2,1,0:T(8,128)(2,1)S(1)}, u32[]{:S(2)}, u32[]{:S(2)}) collective-permute-start(bf16[8,80,128]{2,1,0:T(8,128)(2,1)S(1)} %get-tuple-element.75), channel_id=1, source_target_pairs={{0,6},{1,7},{2,4},{3,5},{4,2},{5,3},{6,0},{7,1},{8,14},{9,15},{10,... | collective-permute-start | bytes 491528 | tf_op jit(solution)/shard_map/ppermute | solution.py:27
  198.3 12.8 %collective-permute-start.20 = (bf16[8,80,128]{2,1,0:T(8,128)(2,1)S(1)}, bf16[8,80,128]{2,1,0:T(8,128)(2,1)S(1)}, u32[]{:S(2)}, u32[]{:S(2)}) collective-permute-start(bf16[8,80,128]{2,1,0:T(8,128)(2,1)S(1)} %get-tuple-element.76), channel_id=1, source_target_pairs={{0,2},{1,3},{2,0},{3,1},{4,6},{5,7},{6,4},{7,5},{8,10},{9,11},{10,... | collective-permute-start | bytes 491528 | tf_op jit(solution)/shard_map/ppermute | solution.py:27
  198.3 18.7 %collective-permute-start.19 = (bf16[8,80,128]{2,1,0:T(8,128)(2,1)S(1)}, bf16[8,80,128]{2,1,0:T(8,128)(2,1)S(1)}, u32[]{:S(2)}, u32[]{:S(2)}) collective-permute-start(bf16[8,80,128]{2,1,0:T(8,128)(2,1)S(1)} %get-tuple-element.77), channel_id=1, source_target_pairs={{0,4},{1,5},{2,6},{3,7},{4,0},{5,1},{6,2},{7,3},{8,12},{9,13},{10,... | collective-permute-start | bytes 491528 | tf_op jit(solution)/shard_map/ppermute | solution.py:27
  201.1 17.7 %collective-permute-start.35 = (bf16[8,80,128]{2,1,0:T(8,128)(2,1)S(1)}, bf16[8,80,128]{2,1,0:T(8,128)(2,1)S(1)}, u32[]{:S(2)}, u32[]{:S(2)}) collective-permute-start(bf16[8,80,128]{2,1,0:T(8,128)(2,1)S(1)} %get-tuple-element.72), channel_id=1, source_target_pairs={{0,6},{1,7},{2,4},{3,5},{4,2},{5,3},{6,0},{7,1},{8,14},{9,15},{10,... | collective-permute-start | bytes 491528 | tf_op jit(solution)/shard_map/ppermute | solution.py:27
  203.0 28.6 %collective-permute-start.37 = (bf16[8,80,128]{2,1,0:T(8,128)(2,1)S(1)}, bf16[8,80,128]{2,1,0:T(8,128)(2,1)S(1)}, u32[]{:S(2)}, u32[]{:S(2)}) collective-permute-start(bf16[8,80,128]{2,1,0:T(8,128)(2,1)S(1)} %get-tuple-element.73), channel_id=1, source_target_pairs={{0,2},{1,3},{2,0},{3,1},{4,6},{5,7},{6,4},{7,5},{8,10},{9,11},{10,... | collective-permute-start | bytes 491528 | tf_op jit(solution)/shard_map/ppermute | solution.py:27
  205.4 29.2 %collective-permute-start.36 = (bf16[8,80,128]{2,1,0:T(8,128)(2,1)S(1)}, bf16[8,80,128]{2,1,0:T(8,128)(2,1)S(1)}, u32[]{:S(2)}, u32[]{:S(2)}) collective-permute-start(bf16[8,80,128]{2,1,0:T(8,128)(2,1)S(1)} %get-tuple-element.74), channel_id=1, source_target_pairs={{0,4},{1,5},{2,6},{3,7},{4,0},{5,1},{6,2},{7,3},{8,12},{9,13},{10,... | collective-permute-start | bytes 491528 | tf_op jit(solution)/shard_map/ppermute | solution.py:27
  217.1 17.6 %collective-permute-start.23 = (bf16[8,80,128]{2,1,0:T(8,128)(2,1)S(1)}, bf16[8,80,128]{2,1,0:T(8,128)(2,1)S(1)}, u32[]{:S(2)}, u32[]{:S(2)}) collective-permute-start(bf16[8,80,128]{2,1,0:T(8,128)(2,1)S(1)} %select_convert_fusion.1), channel_id=1, source_target_pairs={{0,6},{1,7},{2,4},{3,5},{4,2},{5,3},{6,0},{7,1},{8,14},{9,15},{10,... | collective-permute-start | bytes 491528 | tf_op jit(solution)/shard_map/ppermute | solution.py:27
  218.8 22.4 %collective-permute-start.22 = (bf16[8,80,128]{2,1,0:T(8,128)(2,1)S(1)}, bf16[8,80,128]{2,1,0:T(8,128)(2,1)S(1)}, u32[]{:S(2)}, u32[]{:S(2)}) collective-permute-start(bf16[8,80,128]{2,1,0:T(8,128)(2,1)S(1)} %select_convert_fusion.1), channel_id=1, source_target_pairs={{0,4},{1,5},{2,6},{3,7},{4,0},{5,1},{6,2},{7,3},{8,12},{9,13},{10,... | collective-permute-start | bytes 491528 | tf_op jit(solution)/shard_map/ppermute | solution.py:27
  218.8 22.4 %collective-permute-start.21 = (bf16[8,80,128]{2,1,0:T(8,128)(2,1)S(1)}, bf16[8,80,128]{2,1,0:T(8,128)(2,1)S(1)}, u32[]{:S(2)}, u32[]{:S(2)}) collective-permute-start(bf16[8,80,128]{2,1,0:T(8,128)(2,1)S(1)} %select_convert_fusion.1), channel_id=1, source_target_pairs={{0,2},{1,3},{2,0},{3,1},{4,6},{5,7},{6,4},{7,5},{8,10},{9,11},{10,... | collective-permute-start | bytes 491528 | tf_op jit(solution)/shard_map/ppermute | solution.py:27
  241.3 9.1 %collective-permute-start.40 = (bf16[8,80,128]{2,1,0:T(8,128)(2,1)S(1)}, bf16[8,80,128]{2,1,0:T(8,128)(2,1)S(1)}, u32[]{:S(2)}, u32[]{:S(2)}) collective-permute-start(bf16[8,80,128]{2,1,0:T(8,128)(2,1)S(1)} %select_convert_fusion), channel_id=1, source_target_pairs={{0,6},{1,7},{2,4},{3,5},{4,2},{5,3},{6,0},{7,1},{8,14},{9,15},{10,... | collective-permute-start | bytes 491528 | tf_op jit(solution)/shard_map/ppermute | solution.py:27
  242.9 13.0 %collective-permute-start.39 = (bf16[8,80,128]{2,1,0:T(8,128)(2,1)S(1)}, bf16[8,80,128]{2,1,0:T(8,128)(2,1)S(1)}, u32[]{:S(2)}, u32[]{:S(2)}) collective-permute-start(bf16[8,80,128]{2,1,0:T(8,128)(2,1)S(1)} %select_convert_fusion), channel_id=1, source_target_pairs={{0,4},{1,5},{2,6},{3,7},{4,0},{5,1},{6,2},{7,3},{8,12},{9,13},{10,... | collective-permute-start | bytes 491528 | tf_op jit(solution)/shard_map/ppermute | solution.py:27
  242.9 13.0 %collective-permute-start.38 = (bf16[8,80,128]{2,1,0:T(8,128)(2,1)S(1)}, bf16[8,80,128]{2,1,0:T(8,128)(2,1)S(1)}, u32[]{:S(2)}, u32[]{:S(2)}) collective-permute-start(bf16[8,80,128]{2,1,0:T(8,128)(2,1)S(1)} %select_convert_fusion), channel_id=1, source_target_pairs={{0,2},{1,3},{2,0},{3,1},{4,6},{5,7},{6,4},{7,5},{8,10},{9,11},{10,... | collective-permute-start | bytes 491528 | tf_op jit(solution)/shard_map/ppermute | solution.py:27
  245.8 24.0 %collective-permute-start.41 = (bf16[32,80,128]{2,1,0:T(8,128)(2,1)S(1)}, bf16[32,80,128]{2,1,0:T(8,128)(2,1)S(1)}, u32[]{:S(2)}, u32[]{:S(2)}) collective-permute-start(bf16[32,80,128]{2,1,0:T(8,128)(2,1)S(1)} %pad_maximum_fusion.1.refs_0_), channel_id=1, source_target_pairs={{0,1},{1,0},{2,3},{3,2},{4,5},{5,4},{6,7},{7,6},{8,9},{9,8},{10,11... | collective-permute-start | bytes 1966088 | tf_op jit(solution)/shard_map/ppermute | solution.py:32
  256.1 13.7 %collective-permute-start.42 = (bf16[32,80,128]{2,1,0:T(8,128)(2,1)S(1)}, bf16[32,80,128]{2,1,0:T(8,128)(2,1)S(1)}, u32[]{:S(2)}, u32[]{:S(2)}) collective-permute-start(bf16[32,80,128]{2,1,0:T(8,128)(2,1)S(1)} %pad_maximum_fusion.3.refs_1_), channel_id=1, source_target_pairs={{0,1},{1,0},{2,3},{3,2},{4,5},{5,4},{6,7},{7,6},{8,9},{9,8},{10,11... | collective-permute-start | bytes 1966088 | tf_op jit(solution)/shard_map/ppermute | solution.py:32

commit v5 on v4

--- a/solution.py
+++ b/solution.py
@@ -11,7 +11,7 @@
 BLK = 128
 CAP = 24
 CORES = 2
-CHUNKS = 2
+CHUNK_TENTHS = (3, 4, 3)
 UNROLL = 4
 SPARE_BYTES = 2 << 20
 
@@ -356,8 +356,8 @@
     own_blocks = own_count // label_count
     label_blocks, slots = sparse_weight.shape[:2]
     cap = CAP
-    chunk = docs // CHUNKS
-    cuts = [slice(i * chunk, (i + 1) * chunk) for i in range(CHUNKS)]
+    edges = [docs * sum(CHUNK_TENTHS[:i]) // 10 for i in range(len(CHUNK_TENTHS) + 1)]
+    cuts = [slice(start, end) for start, end in zip(edges[:-1], edges[1:])]
 
     ring_width = width // ring
     starts = (jnp.arange(ring, dtype=jnp.int32) ^ ring_index) * ring_width
@@ -411,8 +411,8 @@
         total = pieces[0].astype(F32)
         for k in range(ring - 1, 0, -1):
             total = total + ring_exchange(pieces[k], k).astype(F32)
-        if gradients:
-            total, _ = lax.optimization_barrier((total, gradients[-1][0]))
+        if i:
+            total, _ = lax.optimization_barrier((total, gradient))
         gradient = jnp.where(hidden[:, cut] > 0, total, 0.0).astype(BF16)
         gathered = jnp.concatenate(ring_gather(gradient), axis=0)
         gradients.append((gathered, swap_cores(gathered)))

time: 273 us -> 271 us (level)
  waiting for transfers between devices: 154 us -> 125 us
  starting transfers between devices: 59.4 us -> 76.7 us
  Pallas kernels: 49.6 us -> 57.9 us
    ppermute x12 -> x18, waiting for transfers between devices: 59.8 us -> 34.9 us  [feat_exchange(): lax.ppermute(x, 'feat', [(i, i ^ flip) for i in range(lax.axis_size('feat...]
    ppermute x12 -> x18, starting transfers between devices: 14.3 us -> 22.2 us  [feat_exchange(): lax.ppermute(x, 'feat', [(i, i ^ flip) for i in range(lax.axis_size('feat...]
    ppermute x24 -> x33, starting transfers between devices: 44.7 us -> 52.4 us  [ring_exchange(): lax.ppermute(x, 'label', [(i, i ^ flip * CORES) for i in range(count)])]
    pallas_call x2 -> x3, Pallas kernels: 22.3 us -> 28.7 us  [residual_and_back(): pl.pallas_call(kernel, out_shape=[jax.ShapeDtypeStruct((label_blocks, doc...]
    ppermute x24 -> x33, waiting for transfers between devices: 91.4 us -> 86.9 us  [ring_exchange(): lax.ppermute(x, 'label', [(i, i ^ flip * CORES) for i in range(count)])]
  transfers between devices with their start and end apart: 43 -> 61, of which waited for: 24 -> 24; matrix products, arithmetic and copies ran while one was open for 2% -> 3% of each run, Pallas kernels for 17% -> 20%
where the time goes in v5:
time: 271 us; the launch traced here: 270 us
  waiting for transfers between devices  125 us (46%)
  starting transfers between devices  76.7 us (28%)
  Pallas kernels  57.9 us (21%)
  matrix products  3.37 us (1%)
  other arithmetic  3.22 us (1%)
  local copies, waits for them, and re-layouts  3.1 us (1%)
    ppermute x33, waiting for transfers between devices, ring_exchange(): lax.ppermute(x, 'label', [(i, i ^ flip * CORES) for i in range(count)])  86.9 us
    ppermute x33, starting transfers between devices, ring_exchange(): lax.ppermute(x, 'label', [(i, i ^ flip * CORES) for i in range(count)])  52.4 us
    ppermute x18, waiting for transfers between devices, feat_exchange(): lax.ppermute(x, 'feat', [(i, i ^ flip) for i in range(lax.axis_size('feat...  34.9 us
    pallas_call x3, Pallas kernels, residual_and_back(): pl.pallas_call(kernel, out_shape=[jax.ShapeDtypeStruct((label_blocks, doc...  28.7 us
    ppermute x18, starting transfers between devices, feat_exchange(): lax.ppermute(x, 'feat', [(i, i ^ flip) for i in range(lax.axis_size('feat...  22.2 us
    pallas_call x4, Pallas kernels, block_weight_grad(): pl.pallas_call(kernel, out_shape=jax.ShapeDtypeStruct((label_blocks * slo...  13.5 us
  transfers between devices with their start and end apart: 61, of which 24 were waited for; matrix products, arithmetic and copies ran while one was open for 3% of the time, Pallas kernels for 20%

profile of v5, /device:TPU:0, one launch (start us, length us, event | category | flops | bytes accessed | tf_op | source)
XLA Modules:
  0.0 270.4 jit_solution(3447657521746479618)
XLA Ops:
  0.7 1.6 copy-done
  3.0 5.1 %collective-permute-start.5 = (bf16[160,128]{1,0:T(8,128)(2,1)S(1)}, bf16[160,128]{1,0:T(8,128)(2,1)S(1)}, u32[]{:S(2)}, u32[]{:S(2)}) collective-permute-start(bf16[160,128]{1,0:T(8,128)(2,1)S(1)} %copy-done.1), channel_id=1, source_target_pairs={{0,6},{1,7},{2,4},{3,5},{4,2},{5,3},{6,0},{7,1},{8,14},{9,15},{10,... | collective-permute-start | bytes 122888 | tf_op jit(solution)/shard_map/ppermute | solution.py:27
  8.7 1.4 collective-permute-start
  10.1 2.4 collective-permute-start.4
  16.8 8.2 %collective-permute-done = bf16[128,2048]{1,0:T(8,128)(2,1)} collective-permute-done((bf16[128,2048]{1,0:T(8,128)(2,1)S(1)}, bf16[128,2048]{1,0:T(8,128)(2,1)}, u32[]{:S(2)}, u32[]{:S(2)}) %collective-permute-start) | collective-permute-done | bytes 524320 | tf_op jit(solution)/shard_map/ppermute | solution.py:27
  25.0 1.4 convolution_add_fusion.1
  26.4 11.2 %collective-permute-done.4 = bf16[128,2048]{1,0:T(8,128)(2,1)} collective-permute-done((bf16[128,2048]{1,0:T(8,128)(2,1)S(1)}, bf16[128,2048]{1,0:T(8,128)(2,1)}, u32[]{:S(2)}, u32[]{:S(2)}) %collective-permute-start.4) | collective-permute-done | bytes 524320 | tf_op jit(solution)/shard_map/ppermute | solution.py:27
  37.6 1.4 fusion.4
  39.0 19.0 %collective-permute-done.2 = bf16[128,2048]{1,0:T(8,128)(2,1)S(1)} collective-permute-done((bf16[128,2048]{1,0:T(8,128)(2,1)S(1)}, bf16[128,2048]{1,0:T(8,128)(2,1)S(1)}, u32[]{:S(2)}, u32[]{:S(2)}) %collective-permute-start.2) | collective-permute-done | bytes 524320 | tf_op jit(solution)/shard_map/ppermute | solution.py:27
  58.4 2.1 collective-permute-done.6
  60.6 2.3 collective-permute-start.43
  62.9 1.6 collective-permute-start.9
  64.5 2.8 %collective-permute-start.7 = (bf16[8,48,128]{2,1,0:T(8,128)(2,1)S(1)}, bf16[8,48,128]{2,1,0:T(8,128)(2,1)S(1)}, u32[]{:S(2)}, u32[]{:S(2)}) collective-permute-start(bf16[8,48,128]{2,1,0:T(8,128)(2,1)S(1)} %get-tuple-element.108), channel_id=1, source_target_pairs={{0,2},{1,3},{2,0},{3,1},{4,6},{5,7},{6,4},{7,5},{8,10},{9,11},{10,... | collective-permute-start | bytes 294920 | tf_op jit(solution)/shard_map/ppermute | solution.py:27
  67.3 1.6 collective-permute-start.26
  69.0 1.5 collective-permute-done.9
  70.5 4.7 %collective-permute-start.24 = (bf16[8,64,128]{2,1,0:T(8,128)(2,1)S(1)}, bf16[8,64,128]{2,1,0:T(8,128)(2,1)S(1)}, u32[]{:S(2)}, u32[]{:S(2)}) collective-permute-start(bf16[8,64,128]{2,1,0:T(8,128)(2,1)S(1)} %slice.96), channel_id=1, source_target_pairs={{0,2},{1,3},{2,0},{3,1},{4,6},{5,7},{6,4},{7,5},{8,10},{9,11},{10,... | collective-permute-start | bytes 393224 | tf_op jit(solution)/shard_map/ppermute | solution.py:27
  75.1 6.2 %collective-permute-done.8 = bf16[8,48,128]{2,1,0:T(8,128)(2,1)S(1)} collective-permute-done((bf16[8,48,128]{2,1,0:T(8,128)(2,1)S(1)}, bf16[8,48,128]{2,1,0:T(8,128)(2,1)S(1)}, u32[]{:S(2)}, u32[]{:S(2)}) %collective-permute-start.8) | collective-permute-done | bytes 98336 | tf_op jit(solution)/shard_map/ppermute | solution.py:27
  81.4 1.9 collective-permute-start.41
  83.3 7.1 %collective-permute-done.42 = bf16[8,48,128]{2,1,0:T(8,128)(2,1)S(1)} collective-permute-done((bf16[8,48,128]{2,1,0:T(8,128)(2,1)S(1)}, bf16[8,48,128]{2,1,0:T(8,128)(2,1)S(1)}, u32[]{:S(2)}, u32[]{:S(2)}) %collective-permute-start.42) | collective-permute-done | bytes 98336 | tf_op jit(solution)/shard_map/ppermute | solution.py:27
  92.1 1.5 select_blocks.3
  93.7 1.5 collective-permute-start.11
  95.2 1.5 collective-permute-start.12
  97.2 1.4 select_blocks.5
  98.6 1.5 collective-permute-start.45
  100.1 1.5 select_blocks.4
  102.2 1.4 collective-permute-done.11.refs_1_.refs_3_
  103.6 1.5 collective-permute-start.29
  105.1 5.3 %collective-permute-done.12.refs_2_.refs_3_ = bf16[24,48,128]{2,1,0:T(8,128)(2,1)S(1)} collective-permute-done((bf16[24,48,128]{2,1,0:T(8,128)(2,1)S(1)}, bf16[24,48,128]{2,1,0:T(8,128)(2,1)S(1)}, u32[]{:S(2)}, u32[]{:S(2)}) %collective-permute-start.12) | collective-permute-done | bytes 294944 | tf_op jit(solution)/shard_map/ppermute | solution.py:36
  110.5 2.5 collective-permute-start.46
  112.9 3.4 %collective-permute-done.45.refs_1_.refs_5_ = bf16[24,48,128]{2,1,0:T(8,128)(2,1)S(1)} collective-permute-done((bf16[24,48,128]{2,1,0:T(8,128)(2,1)S(1)}, bf16[24,48,128]{2,1,0:T(8,128)(2,1)S(1)}, u32[]{:S(2)}, u32[]{:S(2)}) %collective-permute-start.45) | collective-permute-done | bytes 294944 | tf_op jit(solution)/shard_map/ppermute | solution.py:36
  116.3 2.4 collective-permute-start.47
  118.7 4.6 %fetch.1.weight_ref = bf16[24,16,128,128]{3,2,1,0:T(8,128)(2,1)S(1)} custom-call(bf16[24,16,128,128]{3,2,1,0:T(8,128)(2,1)} %source.1), custom_call_target="tpu_custom_call" | custom-call | tf_op jit(solution)/shard_map/fetch/pallas_call | solution.py:78
  123.3 9.3 %residual_and_back.3 = (bf16[24,48,128]{2,1,0:T(8,128)(2,1)S(1)}, bf16[24,48,128]{2,1,0:T(8,128)(2,1)S(1)}, bf16[24,48,128]{2,1,0:T(8,128)(2,1)S(1)}, bf16[24,48...) custom-call(s32[384]{0:T(512)S(1)} %select_reduce_fusion.1.position_ref, s32[384]{0:T(512)S(1)} %select_reduce_fusion.order_ref, ...), custom_call_target="tpu_custom_call" | custom-call | tf_op jit(solution)/shard_map/residual_and_back/pallas_call | solution.py:198
  132.6 6.5 %collective-permute-done.46.refs_2_.refs_5_ = bf16[24,48,128]{2,1,0:T(8,128)(2,1)S(1)} collective-permute-done((bf16[24,48,128]{2,1,0:T(8,128)(2,1)S(1)}, bf16[24,48,128]{2,1,0:T(8,128)(2,1)S(1)}, u32[]{:S(2)}, u32[]{:S(2)}) %collective-permute-start.46) | collective-permute-done | bytes 294944 | tf_op jit(solution)/shard_map/ppermute | solution.py:36
  139.1 1.3 collective-permute-done.47.refs_3_.refs_5_
  141.3 2.0 collective-permute-start.16
  143.4 9.2 %residual_and_back.5 = (bf16[24,48,128]{2,1,0:T(8,128)(2,1)S(1)}, bf16[24,48,128]{2,1,0:T(8,128)(2,1)S(1)}, bf16[24,48,128]{2,1,0:T(8,128)(2,1)S(1)}, bf16[24,48...) custom-call(s32[384]{0:T(512)S(1)} %select_reduce_fusion.1.position_ref, s32[384]{0:T(512)S(1)} %select_reduce_fusion.order_ref, ...), custom_call_target="tpu_custom_call" | custom-call | tf_op jit(solution)/shard_map/residual_and_back/pallas_call | solution.py:198
  154.2 10.2 %residual_and_back.4 = (bf16[24,64,128]{2,1,0:T(8,128)(2,1)S(1)}, bf16[24,64,128]{2,1,0:T(8,128)(2,1)S(1)}, bf16[24,64,128]{2,1,0:T(8,128)(2,1)S(1)}, bf16[24,64...) custom-call(s32[384]{0:T(512)S(1)} %select_reduce_fusion.1.position_ref, s32[384]{0:T(512)S(1)} %select_reduce_fusion.order_ref, ...), custom_call_target="tpu_custom_call" | custom-call | tf_op jit(solution)/shard_map/residual_and_back/pallas_call | solution.py:198
  164.4 2.0 collective-permute-start.31
  169.3 2.0 collective-permute-start.50
  171.3 16.9 %collective-permute-done.50.refs_3_ = bf16[24,48,128]{2,1,0:T(8,128)(2,1)S(1)} collective-permute-done((bf16[24,48,128]{2,1,0:T(8,128)(2,1)S(1)}, bf16[24,48,128]{2,1,0:T(8,128)(2,1)S(1)}, u32[]{:S(2)}, u32[]{:S(2)}) %collective-permute-start.50) | collective-permute-done | bytes 294944 | tf_op jit(solution)/shard_map/ppermute | solution.py:36
  191.5 1.8 collective-permute-start.18
  193.3 2.6 collective-permute-start.19
  196.1 1.8 collective-permute-start.52
  199.0 4.0 %collective-permute-done.20 = bf16[8,48,128]{2,1,0:T(8,128)(2,1)S(1)} collective-permute-done((bf16[8,48,128]{2,1,0:T(8,128)(2,1)S(1)}, bf16[8,48,128]{2,1,0:T(8,128)(2,1)S(1)}, u32[]{:S(2)}, u32[]{:S(2)}) %collective-permute-start.20) | collective-permute-done | bytes 98336 | tf_op jit(solution)/shard_map/ppermute | solution.py:27
  204.1 2.1 collective-permute-start.23
  207.1 2.3 collective-permute-start.35
  209.4 7.3 %collective-permute-start.37 = (bf16[8,64,128]{2,1,0:T(8,128)(2,1)S(1)}, bf16[8,64,128]{2,1,0:T(8,128)(2,1)S(1)}, u32[]{:S(2)}, u32[]{:S(2)}) collective-permute-start(bf16[8,64,128]{2,1,0:T(8,128)(2,1)S(1)} %get-tuple-element.99), channel_id=1, source_target_pairs={{0,2},{1,3},{2,0},{3,1},{4,6},{5,7},{6,4},{7,5},{8,10},{9,11},{10,... | collective-permute-start | bytes 393224 | tf_op jit(solution)/shard_map/ppermute | solution.py:27
  216.7 1.4 collective-permute-done.53
  218.1 2.2 collective-permute-done.37
  220.3 10.1 %collective-permute-done.36 = bf16[8,64,128]{2,1,0:T(8,128)(2,1)S(1)} collective-permute-done((bf16[8,64,128]{2,1,0:T(8,128)(2,1)S(1)}, bf16[8,64,128]{2,1,0:T(8,128)(2,1)S(1)}, u32[]{:S(2)}, u32[]{:S(2)}) %collective-permute-start.36) | collective-permute-done | bytes 131104 | tf_op jit(solution)/shard_map/ppermute | solution.py:27
  230.5 1.8 collective-permute-start.40
  232.3 2.6 collective-permute-start.38
  235.0 3.8 %collective-permute-done.40 = bf16[8,64,128]{2,1,0:T(8,128)(2,1)S(1)} collective-permute-done((bf16[8,64,128]{2,1,0:T(8,128)(2,1)S(1)}, bf16[8,64,128]{2,1,0:T(8,128)(2,1)S(1)}, u32[]{:S(2)}, u32[]{:S(2)}) %collective-permute-start.40) | collective-permute-done | bytes 131104 | tf_op jit(solution)/shard_map/ppermute | solution.py:27
  238.9 4.5 %collective-permute-done.39 = bf16[8,64,128]{2,1,0:T(8,128)(2,1)S(1)} collective-permute-done((bf16[8,64,128]{2,1,0:T(8,128)(2,1)S(1)}, bf16[8,64,128]{2,1,0:T(8,128)(2,1)S(1)}, u32[]{:S(2)}, u32[]{:S(2)}) %collective-permute-start.39) | collective-permute-done | bytes 131104 | tf_op jit(solution)/shard_map/ppermute | solution.py:27
  243.4 1.5 collective-permute-start.57
  245.0 2.9 %collective-permute-start.55 = (bf16[8,48,128]{2,1,0:T(8,128)(2,1)S(1)}, bf16[8,48,128]{2,1,0:T(8,128)(2,1)S(1)}, u32[]{:S(2)}, u32[]{:S(2)}) collective-permute-start(bf16[8,48,128]{2,1,0:T(8,128)(2,1)S(1)} %select_convert_fusion.1), channel_id=1, source_target_pairs={{0,2},{1,3},{2,0},{3,1},{4,6},{5,7},{6,4},{7,5},{8,10},{9,11},{10,... | collective-permute-start | bytes 294920 | tf_op jit(solution)/shard_map/ppermute | solution.py:27
  248.5 2.4 collective-permute-done.57
  250.9 3.1 %collective-permute-done.56 = bf16[8,48,128]{2,1,0:T(8,128)(2,1)S(1)} collective-permute-done((bf16[8,48,128]{2,1,0:T(8,128)(2,1)S(1)}, bf16[8,48,128]{2,1,0:T(8,128)(2,1)S(1)}, u32[]{:S(2)}, u32[]{:S(2)}) %collective-permute-start.56) | collective-permute-done | bytes 98336 | tf_op jit(solution)/shard_map/ppermute | solution.py:27
  254.3 3.4 %block_weight_grad.4.refs_6_ = bf16[384,128,128]{2,1,0:T(8,128)(2,1)} custom-call(s32[96]{0:T(128)S(1)} %get-tuple-element.111.order_ref, bf16[24,48,128]{2,1,0:T(8,128)(2,1)S(1)} %get-tuple-element.95.refs_0_, bf16[24,64,128]{2,1,0:T(8,128)(2,1)S(1)} %get-tuple-element.96.refs_1_, bf16[24,48,128]{2,1,0:T(8,128)(2,1)S(1)} %get-tuple-element.97.refs_2_, ...), custom_call_target="tpu_custom_call" | custom-call | tf_op jit(solution)/shard_map/block_weight_grad/pallas_call | solution.py:250
  257.6 3.4 %block_weight_grad.5.refs_6_ = bf16[384,128,128]{2,1,0:T(8,128)(2,1)} custom-call(s32[96]{0:T(128)S(1)} %get-tuple-element.112.order_ref, bf16[24,48,128]{2,1,0:T(8,128)(2,1)S(1)} %get-tuple-element.95.refs_0_, bf16[24,64,128]{2,1,0:T(8,128)(2,1)S(1)} %get-tuple-element.96.refs_1_, ...), custom_call_target="tpu_custom_call", output_to_operand_aliasing={{}: (7, {})} | custom-call | tf_op jit(solution)/shard_map/block_weight_grad/pallas_call | solution.py:250
  261.0 3.4 %block_weight_grad.6.refs_6_ = bf16[384,128,128]{2,1,0:T(8,128)(2,1)} custom-call(s32[96]{0:T(128)S(1)} %get-tuple-element.113.order_ref, bf16[24,48,128]{2,1,0:T(8,128)(2,1)S(1)} %get-tuple-element.95.refs_0_, bf16[24,64,128]{2,1,0:T(8,128)(2,1)S(1)} %get-tuple-element.96.refs_1_, ...), custom_call_target="tpu_custom_call", output_to_operand_aliasing={{}: (7, {})} | custom-call | tf_op jit(solution)/shard_map/block_weight_grad/pallas_call | solution.py:250
  264.4 3.4 %block_weight_grad.7 = bf16[384,128,128]{2,1,0:T(8,128)(2,1)} custom-call(s32[96]{0:T(128)S(1)} %get-tuple-element.114.order_ref, bf16[24,48,128]{2,1,0:T(8,128)(2,1)S(1)} %get-tuple-element.95.refs_0_, bf16[24,64,128]{2,1,0:T(8,128)(2,1)S(1)} %get-tuple-element.96.refs_1_, ...), custom_call_target="tpu_custom_call", output_to_operand_aliasing={{}: (7, {})} | custom-call | tf_op jit(solution)/shard_map/block_weight_grad/pallas_call | solution.py:250
  267.8 2.6 expand_weight_grad.1
  (139 shorter events, 21.8 us)
Async XLA Ops:
  0.7 1.6 copy-start
  2.3 10.3 %copy-start.2 = (s32[768,16]{0,1:T(8,128)S(1)}, s32[768,16]{0,1:T(8,128)}, u32[]{:S(2)}) copy-start(s32[768,16]{0,1:T(8,128)} %param.8) | copy-start | bytes 147460
  2.3 11.1 %copy-start.3 = (s32[160,8]{0,1:T(8,128)S(1)}, s32[160,8]{0,1:T(8,128)}, u32[]{:S(2)}) copy-start(s32[160,8]{0,1:T(8,128)} %param.9) | copy-start | bytes 15364
  3.0 23.4 %collective-permute-start.5 = (bf16[160,128]{1,0:T(8,128)(2,1)S(1)}, bf16[160,128]{1,0:T(8,128)(2,1)S(1)}, u32[]{:S(2)}, u32[]{:S(2)}) collective-permute-start(bf16[160,128]{1,0:T(8,128)(2,1)S(1)} %copy-done.1), channel_id=1, source_target_pairs={{0,6},{1,7},{2,4},{3,5},{4,2},{5,3},{6,0},{7,1},{8,14},{9,15},{10,... | collective-permute-start | bytes 122888 | tf_op jit(solution)/shard_map/ppermute | solution.py:27
  8.1 30.8 %collective-permute-start.3 = (bf16[160,128]{1,0:T(8,128)(2,1)S(1)}, bf16[160,128]{1,0:T(8,128)(2,1)S(1)}, u32[]{:S(2)}, u32[]{:S(2)}) collective-permute-start(bf16[160,128]{1,0:T(8,128)(2,1)S(1)} %copy-done.1), channel_id=1, source_target_pairs={{0,4},{1,5},{2,6},{3,7},{4,0},{5,1},{6,2},{7,3},{8,12},{9,13},{10,... | collective-permute-start | bytes 122888 | tf_op jit(solution)/shard_map/ppermute | solution.py:27
  8.1 8.1 %collective-permute-start.1 = (bf16[160,128]{1,0:T(8,128)(2,1)S(1)}, bf16[160,128]{1,0:T(8,128)(2,1)}, u32[]{:S(2)}, u32[]{:S(2)}) collective-permute-start(bf16[160,128]{1,0:T(8,128)(2,1)S(1)} %copy-done.1), channel_id=1, source_target_pairs={{0,2},{1,3},{2,0},{3,1},{4,6},{5,7},{6,4},{7,5},{8,10},{9,11},{10,... | collective-permute-start | bytes 122888 | tf_op jit(solution)/shard_map/ppermute | solution.py:27
  8.7 16.3 %collective-permute-start = (bf16[128,2048]{1,0:T(8,128)(2,1)S(1)}, bf16[128,2048]{1,0:T(8,128)(2,1)}, u32[]{:S(2)}, u32[]{:S(2)}) collective-permute-start(bf16[128,2048]{1,0:T(8,128)(2,1)S(1)} %get-tuple-element.51), channel_id=1, source_target_pairs={{0,2},{1,3},{2,0},{3,1},{4,6},{5,7},{6,4},{7,5},{8,10},{9,11},{10,... | collective-permute-start | bytes 1572872 | tf_op jit(solution)/shard_map/ppermute | solution.py:27
  10.1 27.4 %collective-permute-start.4 = (bf16[128,2048]{1,0:T(8,128)(2,1)S(1)}, bf16[128,2048]{1,0:T(8,128)(2,1)}, u32[]{:S(2)}, u32[]{:S(2)}) collective-permute-start(bf16[128,2048]{1,0:T(8,128)(2,1)S(1)} %get-tuple-element.54), channel_id=1, source_target_pairs={{0,6},{1,7},{2,4},{3,5},{4,2},{5,3},{6,0},{7,1},{8,14},{9,15},{10,... | collective-permute-start | bytes 1572872 | tf_op jit(solution)/shard_map/ppermute | solution.py:27
  16.3 41.7 %collective-permute-start.2 = (bf16[128,2048]{1,0:T(8,128)(2,1)S(1)}, bf16[128,2048]{1,0:T(8,128)(2,1)S(1)}, u32[]{:S(2)}, u32[]{:S(2)}) collective-permute-start(bf16[128,2048]{1,0:T(8,128)(2,1)S(1)} %get-tuple-element.53), channel_id=1, source_target_pairs={{0,4},{1,5},{2,6},{3,7},{4,0},{5,1},{6,2},{7,3},{8,12},{9,13},{10,... | collective-permute-start | bytes 1572872 | tf_op jit(solution)/shard_map/ppermute | solution.py:27
  58.3 2.2 collective-permute-start.6
  60.6 8.4 %collective-permute-start.43 = (bf16[8,48,128]{2,1,0:T(8,128)(2,1)S(1)}, bf16[8,48,128]{2,1,0:T(8,128)(2,1)S(1)}, u32[]{:S(2)}, u32[]{:S(2)}) collective-permute-start(bf16[8,48,128]{2,1,0:T(8,128)(2,1)S(1)} %get-tuple-element.107), channel_id=1, source_target_pairs={{0,6},{1,7},{2,4},{3,5},{4,2},{5,3},{6,0},{7,1},{8,14},{9,15},{10,... | collective-permute-start | bytes 294920 | tf_op jit(solution)/shard_map/ppermute | solution.py:27
  62.9 7.5 %collective-permute-start.9 = (bf16[8,48,128]{2,1,0:T(8,128)(2,1)S(1)}, bf16[8,48,128]{2,1,0:T(8,128)(2,1)S(1)}, u32[]{:S(2)}, u32[]{:S(2)}) collective-permute-start(bf16[8,48,128]{2,1,0:T(8,128)(2,1)S(1)} %get-tuple-element.108), channel_id=1, source_target_pairs={{0,6},{1,7},{2,4},{3,5},{4,2},{5,3},{6,0},{7,1},{8,14},{9,15},{10,... | collective-permute-start | bytes 294920 | tf_op jit(solution)/shard_map/ppermute | solution.py:27
  64.5 16.9 %collective-permute-start.8 = (bf16[8,48,128]{2,1,0:T(8,128)(2,1)S(1)}, bf16[8,48,128]{2,1,0:T(8,128)(2,1)S(1)}, u32[]{:S(2)}, u32[]{:S(2)}) collective-permute-start(bf16[8,48,128]{2,1,0:T(8,128)(2,1)S(1)} %get-tuple-element.108), channel_id=1, source_target_pairs={{0,4},{1,5},{2,6},{3,7},{4,0},{5,1},{6,2},{7,3},{8,12},{9,13},{10,... | collective-permute-start | bytes 294920 | tf_op jit(solution)/shard_map/ppermute | solution.py:27
  64.5 16.9 %collective-permute-start.7 = (bf16[8,48,128]{2,1,0:T(8,128)(2,1)S(1)}, bf16[8,48,128]{2,1,0:T(8,128)(2,1)S(1)}, u32[]{:S(2)}, u32[]{:S(2)}) collective-permute-start(bf16[8,48,128]{2,1,0:T(8,128)(2,1)S(1)} %get-tuple-element.108), channel_id=1, source_target_pairs={{0,2},{1,3},{2,0},{3,1},{4,6},{5,7},{6,4},{7,5},{8,10},{9,11},{10,... | collective-permute-start | bytes 294920 | tf_op jit(solution)/shard_map/ppermute | solution.py:27
  67.3 23.7 %collective-permute-start.26 = (bf16[8,64,128]{2,1,0:T(8,128)(2,1)S(1)}, bf16[8,64,128]{2,1,0:T(8,128)(2,1)S(1)}, u32[]{:S(2)}, u32[]{:S(2)}) collective-permute-start(bf16[8,64,128]{2,1,0:T(8,128)(2,1)S(1)} %slice.96), channel_id=1, source_target_pairs={{0,6},{1,7},{2,4},{3,5},{4,2},{5,3},{6,0},{7,1},{8,14},{9,15},{10,... | collective-permute-start | bytes 393224 | tf_op jit(solution)/shard_map/ppermute | solution.py:27
  69.0 22.1 %collective-permute-start.25 = (bf16[8,64,128]{2,1,0:T(8,128)(2,1)S(1)}, bf16[8,64,128]{2,1,0:T(8,128)(2,1)S(1)}, u32[]{:S(2)}, u32[]{:S(2)}) collective-permute-start(bf16[8,64,128]{2,1,0:T(8,128)(2,1)S(1)} %slice.96), channel_id=1, source_target_pairs={{0,4},{1,5},{2,6},{3,7},{4,0},{5,1},{6,2},{7,3},{8,12},{9,13},{10,... | collective-permute-start | bytes 393224 | tf_op jit(solution)/shard_map/ppermute | solution.py:27
  70.5 20.6 %collective-permute-start.24 = (bf16[8,64,128]{2,1,0:T(8,128)(2,1)S(1)}, bf16[8,64,128]{2,1,0:T(8,128)(2,1)S(1)}, u32[]{:S(2)}, u32[]{:S(2)}) collective-permute-start(bf16[8,64,128]{2,1,0:T(8,128)(2,1)S(1)} %slice.96), channel_id=1, source_target_pairs={{0,2},{1,3},{2,0},{3,1},{4,6},{5,7},{6,4},{7,5},{8,10},{9,11},{10,... | collective-permute-start | bytes 393224 | tf_op jit(solution)/shard_map/ppermute | solution.py:27
  81.4 9.0 %collective-permute-start.42 = (bf16[8,48,128]{2,1,0:T(8,128)(2,1)S(1)}, bf16[8,48,128]{2,1,0:T(8,128)(2,1)S(1)}, u32[]{:S(2)}, u32[]{:S(2)}) collective-permute-start(bf16[8,48,128]{2,1,0:T(8,128)(2,1)S(1)} %get-tuple-element.107), channel_id=1, source_target_pairs={{0,4},{1,5},{2,6},{3,7},{4,0},{5,1},{6,2},{7,3},{8,12},{9,13},{10,... | collective-permute-start | bytes 294920 | tf_op jit(solution)/shard_map/ppermute | solution.py:27
  81.4 9.0 %collective-permute-start.41 = (bf16[8,48,128]{2,1,0:T(8,128)(2,1)S(1)}, bf16[8,48,128]{2,1,0:T(8,128)(2,1)S(1)}, u32[]{:S(2)}, u32[]{:S(2)}) collective-permute-start(bf16[8,48,128]{2,1,0:T(8,128)(2,1)S(1)} %get-tuple-element.107), channel_id=1, source_target_pairs={{0,2},{1,3},{2,0},{3,1},{4,6},{5,7},{6,4},{7,5},{8,10},{9,11},{10,... | collective-permute-start | bytes 294920 | tf_op jit(solution)/shard_map/ppermute | solution.py:27
  90.4 1.7 collective-permute-start.10
  90.5 6.8 %collective-permute-start.44 = (bf16[32,48,128]{2,1,0:T(8,128)(2,1)S(1)}, bf16[32,48,128]{2,1,0:T(8,128)(2,1)S(1)}, u32[]{:S(2)}, u32[]{:S(2)}) collective-permute-start(bf16[32,48,128]{2,1,0:T(8,128)(2,1)S(1)} %pad_maximum_fusion.4.refs_0_), channel_id=1, source_target_pairs={{0,1},{1,0},{2,3},{3,2},{4,5},{5,4},{6,7},{7,6},{8,9},{9,8},{10,11... | collective-permute-start | bytes 1179656 | tf_op jit(solution)/shard_map/ppermute | solution.py:32
  91.1 9.0 %collective-permute-start.27 = (bf16[32,64,128]{2,1,0:T(8,128)(2,1)S(1)}, bf16[32,64,128]{2,1,0:T(8,128)(2,1)S(1)}, u32[]{:S(2)}, u32[]{:S(2)}) collective-permute-start(bf16[32,64,128]{2,1,0:T(8,128)(2,1)S(1)} %pad_maximum_fusion.refs_0_), channel_id=1, source_target_pairs={{0,1},{1,0},{2,3},{3,2},{4,5},{5,4},{6,7},{7,6},{8,9},{9,8},{10,11... | collective-permute-start | bytes 1572872 | tf_op jit(solution)/shard_map/ppermute | solution.py:32
  93.7 9.9 %collective-permute-start.11 = (bf16[24,48,128]{2,1,0:T(8,128)(2,1)S(1)}, bf16[24,48,128]{2,1,0:T(8,128)(2,1)S(1)}, u32[]{:S(2)}, u32[]{:S(2)}) collective-permute-start(bf16[24,48,128]{2,1,0:T(8,128)(2,1)S(1)} %get-tuple-element.62), channel_id=1, source_target_pairs={{0,8},{8,0},{16,24},{24,16},{1,9},{9,1},{17,25},{25,17},{2,10},{10... | collective-permute-start | bytes 884744 | tf_op jit(solution)/shard_map/ppermute | solution.py:36
  95.2 15.2 %collective-permute-start.12 = (bf16[24,48,128]{2,1,0:T(8,128)(2,1)S(1)}, bf16[24,48,128]{2,1,0:T(8,128)(2,1)S(1)}, u32[]{:S(2)}, u32[]{:S(2)}) collective-permute-start(bf16[24,48,128]{2,1,0:T(8,128)(2,1)S(1)} %get-tuple-element.63), channel_id=1, source_target_pairs={{0,16},{8,24},{16,0},{24,8},{1,17},{9,25},{17,1},{25,9},{2,18},{10... | collective-permute-start | bytes 884744 | tf_op jit(solution)/shard_map/ppermute | solution.py:36
  96.7 16.2 %collective-permute-start.13 = (bf16[24,48,128]{2,1,0:T(8,128)(2,1)S(1)}, bf16[24,48,128]{2,1,0:T(8,128)(2,1)S(1)}, u32[]{:S(2)}, u32[]{:S(2)}) collective-permute-start(bf16[24,48,128]{2,1,0:T(8,128)(2,1)S(1)} %get-tuple-element.64), channel_id=1, source_target_pairs={{0,24},{8,16},{16,8},{24,0},{1,25},{9,17},{17,9},{25,1},{2,26},{10... | collective-permute-start | bytes 884744 | tf_op jit(solution)/shard_map/ppermute | solution.py:36
  98.6 17.7 %collective-permute-start.45 = (bf16[24,48,128]{2,1,0:T(8,128)(2,1)S(1)}, bf16[24,48,128]{2,1,0:T(8,128)(2,1)S(1)}, u32[]{:S(2)}, u32[]{:S(2)}) collective-permute-start(bf16[24,48,128]{2,1,0:T(8,128)(2,1)S(1)} %get-tuple-element.85), channel_id=1, source_target_pairs={{0,8},{8,0},{16,24},{24,16},{1,9},{9,1},{17,25},{25,17},{2,10},{10... | collective-permute-start | bytes 884744 | tf_op jit(solution)/shard_map/ppermute | solution.py:36
  101.6 39.7 %collective-permute-start.28 = (bf16[24,64,128]{2,1,0:T(8,128)(2,1)S(1)}, bf16[24,64,128]{2,1,0:T(8,128)(2,1)S(1)}, u32[]{:S(2)}, u32[]{:S(2)}) collective-permute-start(bf16[24,64,128]{2,1,0:T(8,128)(2,1)S(1)} %get-tuple-element.73), channel_id=1, source_target_pairs={{0,8},{8,0},{16,24},{24,16},{1,9},{9,1},{17,25},{25,17},{2,10},{10... | collective-permute-start | bytes 1179656 | tf_op jit(solution)/shard_map/ppermute | solution.py:36
  103.6 49.0 %collective-permute-start.29 = (bf16[24,64,128]{2,1,0:T(8,128)(2,1)S(1)}, bf16[24,64,128]{2,1,0:T(8,128)(2,1)S(1)}, u32[]{:S(2)}, u32[]{:S(2)}) collective-permute-start(bf16[24,64,128]{2,1,0:T(8,128)(2,1)S(1)} %get-tuple-element.74), channel_id=1, source_target_pairs={{0,16},{8,24},{16,0},{24,8},{1,17},{9,25},{17,1},{25,9},{2,18},{10... | collective-permute-start | bytes 1179656 | tf_op jit(solution)/shard_map/ppermute | solution.py:36
  110.5 28.7 %collective-permute-start.46 = (bf16[24,48,128]{2,1,0:T(8,128)(2,1)S(1)}, bf16[24,48,128]{2,1,0:T(8,128)(2,1)S(1)}, u32[]{:S(2)}, u32[]{:S(2)}) collective-permute-start(bf16[24,48,128]{2,1,0:T(8,128)(2,1)S(1)} %get-tuple-element.86), channel_id=1, source_target_pairs={{0,16},{8,24},{16,0},{24,8},{1,17},{9,25},{17,1},{25,9},{2,18},{10... | collective-permute-start | bytes 884744 | tf_op jit(solution)/shard_map/ppermute | solution.py:36
  112.9 40.4 %collective-permute-start.30 = (bf16[24,64,128]{2,1,0:T(8,128)(2,1)S(1)}, bf16[24,64,128]{2,1,0:T(8,128)(2,1)S(1)}, u32[]{:S(2)}, u32[]{:S(2)}) collective-permute-start(bf16[24,64,128]{2,1,0:T(8,128)(2,1)S(1)} %get-tuple-element.75), channel_id=1, source_target_pairs={{0,24},{8,16},{16,8},{24,0},{1,25},{9,17},{17,9},{25,1},{2,26},{10... | collective-permute-start | bytes 1179656 | tf_op jit(solution)/shard_map/ppermute | solution.py:36
  116.3 24.2 %collective-permute-start.47 = (bf16[24,48,128]{2,1,0:T(8,128)(2,1)S(1)}, bf16[24,48,128]{2,1,0:T(8,128)(2,1)S(1)}, u32[]{:S(2)}, u32[]{:S(2)}) collective-permute-start(bf16[24,48,128]{2,1,0:T(8,128)(2,1)S(1)} %get-tuple-element.87), channel_id=1, source_target_pairs={{0,24},{8,16},{16,8},{24,0},{1,25},{9,17},{17,9},{25,1},{2,26},{10... | collective-permute-start | bytes 884744 | tf_op jit(solution)/shard_map/ppermute | solution.py:36
  139.1 25.3 %collective-permute-start.14 = (bf16[24,48,128]{2,1,0:T(8,128)(2,1)S(1)}, bf16[24,48,128]{2,1,0:T(8,128)(2,1)S(1)}, u32[]{:S(2)}, u32[]{:S(2)}) collective-permute-start(bf16[24,48,128]{2,1,0:T(8,128)(2,1)S(1)} %get-tuple-element.66), channel_id=1, source_target_pairs={{0,8},{8,0},{16,24},{24,16},{1,9},{9,1},{17,25},{25,17},{2,10},{10... | collective-permute-start | bytes 884744 | tf_op jit(solution)/shard_map/ppermute | solution.py:36
  140.5 26.0 %collective-permute-start.15 = (bf16[24,48,128]{2,1,0:T(8,128)(2,1)S(1)}, bf16[24,48,128]{2,1,0:T(8,128)(2,1)S(1)}, u32[]{:S(2)}, u32[]{:S(2)}) collective-permute-start(bf16[24,48,128]{2,1,0:T(8,128)(2,1)S(1)} %get-tuple-element.67), channel_id=1, source_target_pairs={{0,16},{8,24},{16,0},{24,8},{1,17},{9,25},{17,1},{25,9},{2,18},{10... | collective-permute-start | bytes 884744 | tf_op jit(solution)/shard_map/ppermute | solution.py:36
  141.3 25.7 %collective-permute-start.16 = (bf16[24,48,128]{2,1,0:T(8,128)(2,1)S(1)}, bf16[24,48,128]{2,1,0:T(8,128)(2,1)S(1)}, u32[]{:S(2)}, u32[]{:S(2)}) collective-permute-start(bf16[24,48,128]{2,1,0:T(8,128)(2,1)S(1)} %get-tuple-element.68), channel_id=1, source_target_pairs={{0,24},{8,16},{16,8},{24,0},{1,25},{9,17},{17,9},{25,1},{2,26},{10... | collective-permute-start | bytes 884744 | tf_op jit(solution)/shard_map/ppermute | solution.py:36
  152.6 16.5 %collective-permute-start.48 = (bf16[24,48,128]{2,1,0:T(8,128)(2,1)S(1)}, bf16[24,48,128]{2,1,0:T(8,128)(2,1)S(1)}, u32[]{:S(2)}, u32[]{:S(2)}) collective-permute-start(bf16[24,48,128]{2,1,0:T(8,128)(2,1)S(1)} %get-tuple-element.89), channel_id=1, source_target_pairs={{0,8},{8,0},{16,24},{24,16},{1,9},{9,1},{17,25},{25,17},{2,10},{10... | collective-permute-start | bytes 884744 | tf_op jit(solution)/shard_map/ppermute | solution.py:36
  153.3 16.0 %collective-permute-start.49 = (bf16[24,48,128]{2,1,0:T(8,128)(2,1)S(1)}, bf16[24,48,128]{2,1,0:T(8,128)(2,1)S(1)}, u32[]{:S(2)}, u32[]{:S(2)}) collective-permute-start(bf16[24,48,128]{2,1,0:T(8,128)(2,1)S(1)} %get-tuple-element.90), channel_id=1, source_target_pairs={{0,16},{8,24},{16,0},{24,8},{1,17},{9,25},{17,1},{25,9},{2,18},{10... | collective-permute-start | bytes 884744 | tf_op jit(solution)/shard_map/ppermute | solution.py:36
  164.4 25.0 %collective-permute-start.31 = (bf16[24,64,128]{2,1,0:T(8,128)(2,1)S(1)}, bf16[24,64,128]{2,1,0:T(8,128)(2,1)S(1)}, u32[]{:S(2)}, u32[]{:S(2)}) collective-permute-start(bf16[24,64,128]{2,1,0:T(8,128)(2,1)S(1)} %get-tuple-element.77), channel_id=1, source_target_pairs={{0,8},{8,0},{16,24},{24,16},{1,9},{9,1},{17,25},{25,17},{2,10},{10... | collective-permute-start | bytes 1179656 | tf_op jit(solution)/shard_map/ppermute | solution.py:36
  166.4 23.0 %collective-permute-start.32 = (bf16[24,64,128]{2,1,0:T(8,128)(2,1)S(1)}, bf16[24,64,128]{2,1,0:T(8,128)(2,1)S(1)}, u32[]{:S(2)}, u32[]{:S(2)}) collective-permute-start(bf16[24,64,128]{2,1,0:T(8,128)(2,1)S(1)} %get-tuple-element.78), channel_id=1, source_target_pairs={{0,16},{8,24},{16,0},{24,8},{1,17},{9,25},{17,1},{25,9},{2,18},{10... | collective-permute-start | bytes 1179656 | tf_op jit(solution)/shard_map/ppermute | solution.py:36
  167.0 22.5 %collective-permute-start.33 = (bf16[24,64,128]{2,1,0:T(8,128)(2,1)S(1)}, bf16[24,64,128]{2,1,0:T(8,128)(2,1)S(1)}, u32[]{:S(2)}, u32[]{:S(2)}) collective-permute-start(bf16[24,64,128]{2,1,0:T(8,128)(2,1)S(1)} %get-tuple-element.79), channel_id=1, source_target_pairs={{0,24},{8,16},{16,8},{24,0},{1,25},{9,17},{17,9},{25,1},{2,26},{10... | collective-permute-start | bytes 1179656 | tf_op jit(solution)/shard_map/ppermute | solution.py:36
  169.2 22.1 %collective-permute-start.17 = (bf16[32,48,128]{2,1,0:T(8,128)(2,1)S(1)}, bf16[32,48,128]{2,1,0:T(8,128)(2,1)S(1)}, u32[]{:S(2)}, u32[]{:S(2)}) collective-permute-start(bf16[32,48,128]{2,1,0:T(8,128)(2,1)S(1)} %get-tuple-element.70), channel_id=1, source_target_pairs={{0,1},{1,0},{2,3},{3,2},{4,5},{5,4},{6,7},{7,6},{8,9},{9,8},{10,11... | collective-permute-start | bytes 1179656 | tf_op jit(solution)/shard_map/ppermute | solution.py:32
  169.3 18.9 %collective-permute-start.50 = (bf16[24,48,128]{2,1,0:T(8,128)(2,1)S(1)}, bf16[24,48,128]{2,1,0:T(8,128)(2,1)S(1)}, u32[]{:S(2)}, u32[]{:S(2)}) collective-permute-start(bf16[24,48,128]{2,1,0:T(8,128)(2,1)S(1)} %get-tuple-element.91), channel_id=1, source_target_pairs={{0,24},{8,16},{16,8},{24,0},{1,25},{9,17},{17,9},{25,1},{2,26},{10... | collective-permute-start | bytes 884744 | tf_op jit(solution)/shard_map/ppermute | solution.py:36
  189.4 6.5 %collective-permute-start.51 = (bf16[32,48,128]{2,1,0:T(8,128)(2,1)S(1)}, bf16[32,48,128]{2,1,0:T(8,128)(2,1)S(1)}, u32[]{:S(2)}, u32[]{:S(2)}) collective-permute-start(bf16[32,48,128]{2,1,0:T(8,128)(2,1)S(1)} %get-tuple-element.93), channel_id=1, source_target_pairs={{0,1},{1,0},{2,3},{3,2},{4,5},{5,4},{6,7},{7,6},{8,9},{9,8},{10,11... | collective-permute-start | bytes 1179656 | tf_op jit(solution)/shard_map/ppermute | solution.py:32
  190.8 15.5 %collective-permute-start.34 = (bf16[32,64,128]{2,1,0:T(8,128)(2,1)S(1)}, bf16[32,64,128]{2,1,0:T(8,128)(2,1)S(1)}, u32[]{:S(2)}, u32[]{:S(2)}) collective-permute-start(bf16[32,64,128]{2,1,0:T(8,128)(2,1)S(1)} %get-tuple-element.81), channel_id=1, source_target_pairs={{0,1},{1,0},{2,3},{3,2},{4,5},{5,4},{6,7},{7,6},{8,9},{9,8},{10,11... | collective-permute-start | bytes 1572872 | tf_op jit(solution)/shard_map/ppermute | solution.py:32
  191.5 7.6 %collective-permute-start.18 = (bf16[8,48,128]{2,1,0:T(8,128)(2,1)S(1)}, bf16[8,48,128]{2,1,0:T(8,128)(2,1)S(1)}, u32[]{:S(2)}, u32[]{:S(2)}) collective-permute-start(bf16[8,48,128]{2,1,0:T(8,128)(2,1)S(1)} %get-tuple-element.104), channel_id=1, source_target_pairs={{0,6},{1,7},{2,4},{3,5},{4,2},{5,3},{6,0},{7,1},{8,14},{9,15},{10,... | collective-permute-start | bytes 294920 | tf_op jit(solution)/shard_map/ppermute | solution.py:27
  193.3 9.8 %collective-permute-start.20 = (bf16[8,48,128]{2,1,0:T(8,128)(2,1)S(1)}, bf16[8,48,128]{2,1,0:T(8,128)(2,1)S(1)}, u32[]{:S(2)}, u32[]{:S(2)}) collective-permute-start(bf16[8,48,128]{2,1,0:T(8,128)(2,1)S(1)} %get-tuple-element.105), channel_id=1, source_target_pairs={{0,2},{1,3},{2,0},{3,1},{4,6},{5,7},{6,4},{7,5},{8,10},{9,11},{10,... | collective-permute-start | bytes 294920 | tf_op jit(solution)/shard_map/ppermute | solution.py:27
  193.3 10.8 %collective-permute-start.19 = (bf16[8,48,128]{2,1,0:T(8,128)(2,1)S(1)}, bf16[8,48,128]{2,1,0:T(8,128)(2,1)S(1)}, u32[]{:S(2)}, u32[]{:S(2)}) collective-permute-start(bf16[8,48,128]{2,1,0:T(8,128)(2,1)S(1)} %get-tuple-element.106), channel_id=1, source_target_pairs={{0,4},{1,5},{2,6},{3,7},{4,0},{5,1},{6,2},{7,3},{8,12},{9,13},{10,... | collective-permute-start | bytes 294920 | tf_op jit(solution)/shard_map/ppermute | solution.py:27
  196.1 11.0 %collective-permute-start.52 = (bf16[8,48,128]{2,1,0:T(8,128)(2,1)S(1)}, bf16[8,48,128]{2,1,0:T(8,128)(2,1)S(1)}, u32[]{:S(2)}, u32[]{:S(2)}) collective-permute-start(bf16[8,48,128]{2,1,0:T(8,128)(2,1)S(1)} %get-tuple-element.101), channel_id=1, source_target_pairs={{0,6},{1,7},{2,4},{3,5},{4,2},{5,3},{6,0},{7,1},{8,14},{9,15},{10,... | collective-permute-start | bytes 294920 | tf_op jit(solution)/shard_map/ppermute | solution.py:27
  199.0 10.3 %collective-permute-start.54 = (bf16[8,48,128]{2,1,0:T(8,128)(2,1)S(1)}, bf16[8,48,128]{2,1,0:T(8,128)(2,1)S(1)}, u32[]{:S(2)}, u32[]{:S(2)}) collective-permute-start(bf16[8,48,128]{2,1,0:T(8,128)(2,1)S(1)} %get-tuple-element.102), channel_id=1, source_target_pairs={{0,2},{1,3},{2,0},{3,1},{4,6},{5,7},{6,4},{7,5},{8,10},{9,11},{10,... | collective-permute-start | bytes 294920 | tf_op jit(solution)/shard_map/ppermute | solution.py:27
  203.1 14.9 %collective-permute-start.53 = (bf16[8,48,128]{2,1,0:T(8,128)(2,1)S(1)}, bf16[8,48,128]{2,1,0:T(8,128)(2,1)S(1)}, u32[]{:S(2)}, u32[]{:S(2)}) collective-permute-start(bf16[8,48,128]{2,1,0:T(8,128)(2,1)S(1)} %get-tuple-element.103), channel_id=1, source_target_pairs={{0,4},{1,5},{2,6},{3,7},{4,0},{5,1},{6,2},{7,3},{8,12},{9,13},{10,... | collective-permute-start | bytes 294920 | tf_op jit(solution)/shard_map/ppermute | solution.py:27
  204.1 40.9 %collective-permute-start.23 = (bf16[8,48,128]{2,1,0:T(8,128)(2,1)S(1)}, bf16[8,48,128]{2,1,0:T(8,128)(2,1)S(1)}, u32[]{:S(2)}, u32[]{:S(2)}) collective-permute-start(bf16[8,48,128]{2,1,0:T(8,128)(2,1)S(1)} %select_convert_fusion.2), channel_id=1, source_target_pairs={{0,6},{1,7},{2,4},{3,5},{4,2},{5,3},{6,0},{7,1},{8,14},{9,15},{10,... | collective-permute-start | bytes 294920 | tf_op jit(solution)/shard_map/ppermute | solution.py:27
  206.3 41.6 %collective-permute-start.22 = (bf16[8,48,128]{2,1,0:T(8,128)(2,1)S(1)}, bf16[8,48,128]{2,1,0:T(8,128)(2,1)S(1)}, u32[]{:S(2)}, u32[]{:S(2)}) collective-permute-start(bf16[8,48,128]{2,1,0:T(8,128)(2,1)S(1)} %select_convert_fusion.2), channel_id=1, source_target_pairs={{0,4},{1,5},{2,6},{3,7},{4,0},{5,1},{6,2},{7,3},{8,12},{9,13},{10,... | collective-permute-start | bytes 294920 | tf_op jit(solution)/shard_map/ppermute | solution.py:27
  207.1 11.0 %collective-permute-start.35 = (bf16[8,64,128]{2,1,0:T(8,128)(2,1)S(1)}, bf16[8,64,128]{2,1,0:T(8,128)(2,1)S(1)}, u32[]{:S(2)}, u32[]{:S(2)}) collective-permute-start(bf16[8,64,128]{2,1,0:T(8,128)(2,1)S(1)} %get-tuple-element.98), channel_id=1, source_target_pairs={{0,6},{1,7},{2,4},{3,5},{4,2},{5,3},{6,0},{7,1},{8,14},{9,15},{10,... | collective-permute-start | bytes 393224 | tf_op jit(solution)/shard_map/ppermute | solution.py:27
  209.4 10.9 %collective-permute-start.37 = (bf16[8,64,128]{2,1,0:T(8,128)(2,1)S(1)}, bf16[8,64,128]{2,1,0:T(8,128)(2,1)S(1)}, u32[]{:S(2)}, u32[]{:S(2)}) collective-permute-start(bf16[8,64,128]{2,1,0:T(8,128)(2,1)S(1)} %get-tuple-element.99), channel_id=1, source_target_pairs={{0,2},{1,3},{2,0},{3,1},{4,6},{5,7},{6,4},{7,5},{8,10},{9,11},{10,... | collective-permute-start | bytes 393224 | tf_op jit(solution)/shard_map/ppermute | solution.py:27
  218.0 12.4 %collective-permute-start.36 = (bf16[8,64,128]{2,1,0:T(8,128)(2,1)S(1)}, bf16[8,64,128]{2,1,0:T(8,128)(2,1)S(1)}, u32[]{:S(2)}, u32[]{:S(2)}) collective-permute-start(bf16[8,64,128]{2,1,0:T(8,128)(2,1)S(1)} %get-tuple-element.100), channel_id=1, source_target_pairs={{0,4},{1,5},{2,6},{3,7},{4,0},{5,1},{6,2},{7,3},{8,12},{9,13},{10,... | collective-permute-start | bytes 393224 | tf_op jit(solution)/shard_map/ppermute | solution.py:27
  230.5 8.3 %collective-permute-start.40 = (bf16[8,64,128]{2,1,0:T(8,128)(2,1)S(1)}, bf16[8,64,128]{2,1,0:T(8,128)(2,1)S(1)}, u32[]{:S(2)}, u32[]{:S(2)}) collective-permute-start(bf16[8,64,128]{2,1,0:T(8,128)(2,1)S(1)} %select_convert_fusion), channel_id=1, source_target_pairs={{0,6},{1,7},{2,4},{3,5},{4,2},{5,3},{6,0},{7,1},{8,14},{9,15},{10,... | collective-permute-start | bytes 393224 | tf_op jit(solution)/shard_map/ppermute | solution.py:27
  232.3 11.0 %collective-permute-start.39 = (bf16[8,64,128]{2,1,0:T(8,128)(2,1)S(1)}, bf16[8,64,128]{2,1,0:T(8,128)(2,1)S(1)}, u32[]{:S(2)}, u32[]{:S(2)}) collective-permute-start(bf16[8,64,128]{2,1,0:T(8,128)(2,1)S(1)} %select_convert_fusion), channel_id=1, source_target_pairs={{0,4},{1,5},{2,6},{3,7},{4,0},{5,1},{6,2},{7,3},{8,12},{9,13},{10,... | collective-permute-start | bytes 393224 | tf_op jit(solution)/shard_map/ppermute | solution.py:27
  232.3 12.5 %collective-permute-start.38 = (bf16[8,64,128]{2,1,0:T(8,128)(2,1)S(1)}, bf16[8,64,128]{2,1,0:T(8,128)(2,1)S(1)}, u32[]{:S(2)}, u32[]{:S(2)}) collective-permute-start(bf16[8,64,128]{2,1,0:T(8,128)(2,1)S(1)} %select_convert_fusion), channel_id=1, source_target_pairs={{0,2},{1,3},{2,0},{3,1},{4,6},{5,7},{6,4},{7,5},{8,10},{9,11},{10,... | collective-permute-start | bytes 393224 | tf_op jit(solution)/shard_map/ppermute | solution.py:27
  238.9 9.1 %collective-permute-start.21 = (bf16[8,48,128]{2,1,0:T(8,128)(2,1)S(1)}, bf16[8,48,128]{2,1,0:T(8,128)(2,1)S(1)}, u32[]{:S(2)}, u32[]{:S(2)}) collective-permute-start(bf16[8,48,128]{2,1,0:T(8,128)(2,1)S(1)} %select_convert_fusion.2), channel_id=1, source_target_pairs={{0,2},{1,3},{2,0},{3,1},{4,6},{5,7},{6,4},{7,5},{8,10},{9,11},{10,... | collective-permute-start | bytes 294920 | tf_op jit(solution)/shard_map/ppermute | solution.py:27
  243.4 7.6 %collective-permute-start.57 = (bf16[8,48,128]{2,1,0:T(8,128)(2,1)S(1)}, bf16[8,48,128]{2,1,0:T(8,128)(2,1)S(1)}, u32[]{:S(2)}, u32[]{:S(2)}) collective-permute-start(bf16[8,48,128]{2,1,0:T(8,128)(2,1)S(1)} %select_convert_fusion.1), channel_id=1, source_target_pairs={{0,6},{1,7},{2,4},{3,5},{4,2},{5,3},{6,0},{7,1},{8,14},{9,15},{10,... | collective-permute-start | bytes 294920 | tf_op jit(solution)/shard_map/ppermute | solution.py:27
  244.8 9.2 %collective-permute-start.56 = (bf16[8,48,128]{2,1,0:T(8,128)(2,1)S(1)}, bf16[8,48,128]{2,1,0:T(8,128)(2,1)S(1)}, u32[]{:S(2)}, u32[]{:S(2)}) collective-permute-start(bf16[8,48,128]{2,1,0:T(8,128)(2,1)S(1)} %select_convert_fusion.1), channel_id=1, source_target_pairs={{0,4},{1,5},{2,6},{3,7},{4,0},{5,1},{6,2},{7,3},{8,12},{9,13},{10,... | collective-permute-start | bytes 294920 | tf_op jit(solution)/shard_map/ppermute | solution.py:27
  245.0 9.0 %collective-permute-start.55 = (bf16[8,48,128]{2,1,0:T(8,128)(2,1)S(1)}, bf16[8,48,128]{2,1,0:T(8,128)(2,1)S(1)}, u32[]{:S(2)}, u32[]{:S(2)}) collective-permute-start(bf16[8,48,128]{2,1,0:T(8,128)(2,1)S(1)} %select_convert_fusion.1), channel_id=1, source_target_pairs={{0,2},{1,3},{2,0},{3,1},{4,6},{5,7},{6,4},{7,5},{8,10},{9,11},{10,... | collective-permute-start | bytes 294920 | tf_op jit(solution)/shard_map/ppermute | solution.py:27
  247.9 19.9 %collective-permute-start.59 = (bf16[32,64,128]{2,1,0:T(8,128)(2,1)S(1)}, bf16[32,64,128]{2,1,0:T(8,128)(2,1)S(1)}, u32[]{:S(2)}, u32[]{:S(2)}) collective-permute-start(bf16[32,64,128]{2,1,0:T(8,128)(2,1)S(1)} %pad_maximum_fusion.1.refs_1_), channel_id=1, source_target_pairs={{0,1},{1,0},{2,3},{3,2},{4,5},{5,4},{6,7},{7,6},{8,9},{9,8},{10,11... | collective-permute-start | bytes 1572872 | tf_op jit(solution)/shard_map/ppermute | solution.py:32
  248.0 19.8 %collective-permute-start.58 = (bf16[32,48,128]{2,1,0:T(8,128)(2,1)S(1)}, bf16[32,48,128]{2,1,0:T(8,128)(2,1)S(1)}, u32[]{:S(2)}, u32[]{:S(2)}) collective-permute-start(bf16[32,48,128]{2,1,0:T(8,128)(2,1)S(1)} %pad_maximum_fusion.3.refs_0_), channel_id=1, source_target_pairs={{0,1},{1,0},{2,3},{3,2},{4,5},{5,4},{6,7},{7,6},{8,9},{9,8},{10,11... | collective-permute-start | bytes 1179656 | tf_op jit(solution)/shard_map/ppermute | solution.py:32
  254.1 13.7 %collective-permute-start.60 = (bf16[32,48,128]{2,1,0:T(8,128)(2,1)S(1)}, bf16[32,48,128]{2,1,0:T(8,128)(2,1)S(1)}, u32[]{:S(2)}, u32[]{:S(2)}) collective-permute-start(bf16[32,48,128]{2,1,0:T(8,128)(2,1)S(1)} %pad_maximum_fusion.5.refs_2_), channel_id=1, source_target_pairs={{0,1},{1,0},{2,3},{3,2},{4,5},{5,4},{6,7},{7,6},{8,9},{9,8},{10,11... | collective-permute-start | bytes 1179656 | tf_op jit(solution)/shard_map/ppermute | solution.py:32
  (2 other events, 1.5 us)

commit v6 on v5

--- a/solution.py
+++ b/solution.py
@@ -14,6 +14,7 @@
 CHUNK_TENTHS = (3, 4, 3)
 UNROLL = 4
 SPARE_BYTES = 2 << 20
+LATE_QUARTERS = 3
 
 BF16 = jnp.bfloat16
 F32 = jnp.float32
@@ -52,21 +53,64 @@
     return [(x.shape, x.dtype) for x in arrays]
 
 
-def cut_columns(weight, starts, width):
-    count = starts.shape[0]
+def cut_columns(weight, cuts):
+    starts = jnp.stack([start for cut in cuts for start, _ in cut]).astype(jnp.int32)
+    widths = [[width for _, width in cut] for cut in cuts]
+    shapes = [(weight.shape[0], sum(width)) for width in widths]
 
     def kernel(starts_ref, weight_ref, *outs):
-        for k, out in enumerate(outs):
-            out[...] = weight_ref[:, pl.ds(pl.multiple_of(starts_ref[k], BLK), width)]
-
-    return pl.pallas_call(
-        kernel,
-        out_shape=[jax.ShapeDtypeStruct((weight.shape[0], width), weight.dtype)] * count,
+        at = 0
+        for width, out in zip(widths, outs):
+            done = 0
+            for w in width:
+                start = pl.multiple_of(starts_ref[at], BLK)
+                out[:, done : done + w] = weight_ref[:, pl.ds(start, w)]
+                done += w
+                at += 1
+
+    return pl.pallas_call(
+        kernel,
+        out_shape=[jax.ShapeDtypeStruct(shape, weight.dtype) for shape in shapes],
         in_specs=[SMEM, VMEM],
-        out_specs=[VMEM] * count,
-        compiler_params=grant((weight.shape, BF16), (weight.shape, BF16)),
+        out_specs=[VMEM] * len(cuts),
+        compiler_params=grant((weight.shape, BF16), *[(shape, BF16) for shape in shapes]),
         name="cut_columns",
     )(starts, weight)
+
+
+def expand_blocks(pairs, shorter, core):
+    docs, _ = pairs[0][0].shape
+    size = pairs[0][1].shape[1] // (CORES * BLK)
+    every = pairs + shorter
+
+    def kernel(core_ref, *refs):
+        lefts, rights = refs[: len(every)], refs[len(every) : 2 * len(every)]
+        for side, out in enumerate(refs[2 * len(every) :]):
+            half = core_ref[0] if side == 0 else 1 - core_ref[0]
+            total = None
+            for left, right in zip(lefts, rights):
+                width = right.shape[1] // CORES
+                columns = right[:, pl.ds(pl.multiple_of(half * width, BLK), width)]
+                term = jnp.dot(left[...], columns, preferred_element_type=F32)
+                if total is None:
+                    total = term
+                elif width == size * BLK:
+                    total = total + term
+                else:
+                    total = jnp.concatenate([total[:, :width] + term, total[:, width:]], axis=1)
+            for j in range(size):
+                out[j] = total[:, j * BLK : (j + 1) * BLK]
+
+    shape = jax.ShapeDtypeStruct((size, docs, BLK), F32)
+    lefts, rights = [left for left, _ in every], [right for _, right in every]
+    return pl.pallas_call(
+        kernel,
+        out_shape=[shape] * CORES,
+        in_specs=[SMEM] + [VMEM] * (2 * len(every)),
+        out_specs=[VMEM] * CORES,
+        compiler_params=grant(*blocks_of(lefts + rights), *[((4 * size, docs, BLK), F32)]),
+        name="expand_blocks",
+    )(core.reshape(1), *lefts, *rights)
 
 
 def fetch(array):
@@ -359,24 +403,36 @@
     edges = [docs * sum(CHUNK_TENTHS[:i]) // 10 for i in range(len(CHUNK_TENTHS) + 1)]
     cuts = [slice(start, end) for start, end in zip(edges[:-1], edges[1:])]
 
-    ring_width = width // ring
-    starts = (jnp.arange(ring, dtype=jnp.int32) ^ ring_index) * ring_width
-
-    def product(left, right):
-        right = right.reshape(right.shape[0], ring_width // BLK, BLK)
-        return jnp.einsum("dk,kbc->bdc", left, right, preferred_element_type=F32)
-
-    columns = cut_columns(expand_weight, starts, ring_width)
-    arrived = [columns[0]] + [None] * (ring - 1)
-    for k in range(ring - 1, 0, -1):
-        arrived[k] = ring_exchange(columns[k], k)
-    documents_late, _ = lax.optimization_barrier((documents, columns[0]))
-    expanded = product(documents, columns[0])
-    for k in range(1, ring):
-        other = ring_exchange(documents_late, k)
-        expanded = expanded + product(other, arrived[k])
-    kept = lax.dynamic_slice_in_dim(expanded, core * own_blocks, own_blocks, 0)
-    given = lax.dynamic_slice_in_dim(expanded, (1 - core) * own_blocks, own_blocks, 0)
+    late_blocks = max(own_blocks * LATE_QUARTERS // 4, 1)
+    raw_blocks = own_blocks - late_blocks
+    pairs = range(2, ring, 2)
+
+    def part(place, first, count):
+        return [((place * CORES + c) * own_blocks * BLK + first * BLK, count * BLK) for c in range(CORES)]
+
+    cut_list = [part(ring_index, 0, own_blocks), part(ring_index ^ 1, 0, own_blocks)]
+    cut_list += [part(ring_index ^ k, 0, raw_blocks) for k in range(2, ring)]
+    cut_list += [part(ring_index ^ k ^ 1, raw_blocks, late_blocks) for k in pairs]
+    cut_list += [part(ring_index ^ k, raw_blocks, late_blocks) for k in pairs]
+    pieces = cut_columns(expand_weight, cut_list)
+    own, near, raw = pieces[0], pieces[1], [None] * 2 + list(pieces[2:ring])
+    lent = dict(zip(pairs, pieces[ring:]))
+    late = dict(zip(pairs, pieces[ring + len(pairs) :]))
+    documents_late, _ = lax.optimization_barrier((documents, own))
+    lent = {k: ring_exchange(lent[k], 1) for k in pairs}
+    beside = ring_exchange(documents_late, 1)
+    raw = raw[:2] + [ring_exchange(raw[k], k) for k in range(2, ring)]
+    near = ring_exchange(near, 1)
+    others = [None] * 2 + [ring_exchange(documents_late, k) for k in range(2, ring)]
+    sums = {}
+    for k in pairs:
+        kept, given = expand_blocks([(documents, late[k]), (beside, lent[k])], [], core)
+        sums[k] = kept + swap_cores(given)
+    kept, given = expand_blocks(
+        [(documents, own), (beside, near)],
+        [(others[k], raw[k]) for k in range(2, ring)] if raw_blocks else [],
+        core,
+    )
 
     block_weight = fetch(sparse_weight)
     send, position, order = list_tables(
@@ -387,11 +443,18 @@
     given, send, position, order, known, first_label = lax.optimization_barrier(
         (given, send, position, order, known, first_label)
     )
-    hidden = jnp.maximum(kept + swap_cores(given), 0.0).astype(BF16)
+    expanded = kept + swap_cores(given)
 
     picked, residuals, gradients = [], [], []
     for i, cut in enumerate(cuts):
-        pool = jnp.concatenate(ring_gather(hidden[:, cut]), axis=0)
+        whole = expanded[:, cut]
+        sent = [sums[k][:, cut] for k in pairs]
+        if i:
+            whole, sent, _ = lax.optimization_barrier((whole, sent, hidden))
+        far = sum(ring_exchange(x, k) for x, k in zip(sent, pairs))
+        whole = jnp.concatenate([whole[:raw_blocks], whole[raw_blocks:] + far], axis=0)
+        hidden = jnp.maximum(whole, 0.0).astype(BF16)
+        pool = jnp.concatenate(ring_gather(hidden), axis=0)
         pools = [pool, swap_cores(pool)]
         outgoing = select_blocks(pools, send, cap)
         parts = [outgoing[0]] + [None] * (feat_count - 1)
@@ -413,7 +476,7 @@
             total = total + ring_exchange(pieces[k], k).astype(F32)
         if i:
             total, _ = lax.optimization_barrier((total, gradient))
-        gradient = jnp.where(hidden[:, cut] > 0, total, 0.0).astype(BF16)
+        gradient = jnp.where(hidden > 0, total, 0.0).astype(BF16)
         gathered = jnp.concatenate(ring_gather(gradient), axis=0)
         gradients.append((gathered, swap_cores(gathered)))
 

time: 271 us -> 280 us (1.033)
  local copies, waits for them, and re-layouts: 3.1 us -> 8.31 us
  waiting for transfers between devices: 125 us -> 129 us
  matrix products: 3.37 us -> 0 us
    ppermute x18, waiting for transfers between devices: 34.9 us -> 52 us  [feat_exchange(): lax.ppermute(x, 'feat', [(i, i ^ flip) for i in range(lax.axis_size('feat...]
    ppermute x33 -> x37, waiting for transfers between devices: 86.9 us -> 77.2 us  [ring_exchange(): lax.ppermute(x, 'label', [(i, i ^ flip * CORES) for i in range(count)])]
    ppermute x33 -> x37, starting transfers between devices: 52.4 us -> 56.8 us  [ring_exchange(): lax.ppermute(x, 'label', [(i, i ^ flip * CORES) for i in range(count)])]
    dot_general x4 -> x0, matrix products: 3.37 us -> none  [product(): return jnp.einsum('dk,kbc->bdc', left, right, preferred_element_type=F32)]
    ppermute x18, starting transfers between devices: 22.2 us -> 18.9 us  [feat_exchange(): lax.ppermute(x, 'feat', [(i, i ^ flip) for i in range(lax.axis_size('feat...]
    ppermute x10 -> x11, waiting for transfers between devices: 3 us -> 0.03 us  [swap_cores(): return lax.ppermute(x, 'label', [(i, i ^ 1) for i in range(count)])]
  transfers between devices with their start and end apart: 61 -> 66, of which waited for: 24 -> 27; matrix products, arithmetic and copies ran while one was open for 3% -> 3% of each run, Pallas kernels for 20% -> 20%
where the time goes in v6:
time: 280 us
  waiting for transfers between devices  129 us (46%)
  starting transfers between devices  77.3 us (28%)
  Pallas kernels  59.8 us (21%)
  local copies, waits for them, and re-layouts  8.31 us (3%)
  other arithmetic  3.89 us (1%)
    ppermute x37, waiting for transfers between devices, ring_exchange(): lax.ppermute(x, 'label', [(i, i ^ flip * CORES) for i in range(count)])  77.2 us
    ppermute x37, starting transfers between devices, ring_exchange(): lax.ppermute(x, 'label', [(i, i ^ flip * CORES) for i in range(count)])  56.8 us
    ppermute x18, waiting for transfers between devices, feat_exchange(): lax.ppermute(x, 'feat', [(i, i ^ flip) for i in range(lax.axis_size('feat...  52 us
    pallas_call x3, Pallas kernels, residual_and_back(): pl.pallas_call(kernel, out_shape=[jax.ShapeDtypeStruct((label_blocks, doc...  28.5 us
    ppermute x18, starting transfers between devices, feat_exchange(): lax.ppermute(x, 'feat', [(i, i ^ flip) for i in range(lax.axis_size('feat...  18.9 us
    pallas_call x4, Pallas kernels, block_weight_grad(): pl.pallas_call(kernel, out_shape=jax.ShapeDtypeStruct((label_blocks * slo...  13.4 us
  transfers between devices with their start and end apart: 66, of which 27 were waited for; matrix products, arithmetic and copies ran while one was open for 3% of the time, Pallas kernels for 20%

profile of v6, /device:TPU:0, one launch (start us, length us, event | category | flops | bytes accessed | tf_op | source)
XLA Modules:
  0.0 279.8 jit_solution(2342155139002562060)
XLA Ops:
  0.8 1.6 copy-done
  3.0 5.1 %collective-permute-start.2 = (bf16[160,128]{1,0:T(8,128)(2,1)}, bf16[160,128]{1,0:T(8,128)(2,1)S(1)}, u32[]{:S(2)}, u32[]{:S(2)}) collective-permute-start(bf16[160,128]{1,0:T(8,128)(2,1)} %documents_ref.1), channel_id=1, source_target_pairs={{0,6},{1,7},{2,4},{3,5},{4,2},{5,3},{6,0},{7,1},{8,14},{9,15},{10,... | collective-permute-start | bytes 122888 | tf_op jit(solution)/shard_map/ppermute | solution.py:28
  10.9 1.7 copy.17
  16.2 3.8 %collective-permute-start.5 = (bf16[128,512]{1,0:T(8,128)(2,1)S(1)}, bf16[128,512]{1,0:T(8,128)(2,1)S(1)}, u32[]{:S(2)}, u32[]{:S(2)}) collective-permute-start(bf16[128,512]{1,0:T(8,128)(2,1)S(1)} %get-tuple-element.64), channel_id=1, source_target_pairs={{0,6},{1,7},{2,4},{3,5},{4,2},{5,3},{6,0},{7,1},{8,14},{9,15},{10,... | collective-permute-start | bytes 393224 | tf_op jit(solution)/shard_map/ppermute | solution.py:28
  20.0 3.4 %collective-permute-done.7.refs_3_ = bf16[128,1536]{1,0:T(8,128)(2,1)S(1)} collective-permute-done((bf16[128,1536]{1,0:T(8,128)(2,1)S(1)}, bf16[128,1536]{1,0:T(8,128)(2,1)S(1)}, u32[]{:S(2)}, u32[]{:S(2)}) %collective-permute-start.7) | collective-permute-done | bytes 393248 | tf_op jit(solution)/shard_map/ppermute | solution.py:28
  25.4 2.5 collective-permute-start.1
  29.1 7.3 %collective-permute-done.1.refs_2_ = bf16[160,128]{1,0:T(8,128)(2,1)S(1)} collective-permute-done((bf16[160,128]{1,0:T(8,128)(2,1)}, bf16[160,128]{1,0:T(8,128)(2,1)S(1)}, u32[]{:S(2)}, u32[]{:S(2)}) %collective-permute-start.1) | collective-permute-done | bytes 40992 | tf_op jit(solution)/shard_map/ppermute | solution.py:28
  36.4 1.8 collective-permute-done.5.refs_7_
  40.8 1.5 collective-permute-start.9
  42.4 8.7 %collective-permute-done.9 = f32[6,48,128]{2,1,0:T(8,128)S(1)} collective-permute-done((f32[6,48,128]{2,1,0:T(8,128)S(1)}, f32[6,48,128]{2,1,0:T(8,128)S(1)}, u32[]{:S(2)}, u32[]{:S(2)}) %collective-permute-start.9) | collective-permute-done | bytes 147488 | tf_op jit(solution)/shard_map/ppermute | solution.py:28
  51.3 2.0 collective-permute-start.12
  53.2 1.9 collective-permute-start.11
  55.7 10.7 %collective-permute-done.27 = f32[6,64,128]{2,1,0:T(8,128)S(1)} collective-permute-done((f32[6,64,128]{2,1,0:T(8,128)S(1)}, f32[6,64,128]{2,1,0:T(8,128)S(1)}, u32[]{:S(2)}, u32[]{:S(2)}) %collective-permute-start.27) | collective-permute-done | bytes 196640 | tf_op jit(solution)/shard_map/ppermute | solution.py:28
  66.6 7.2 %collective-permute-done.11 = bf16[8,48,128]{2,1,0:T(8,128)(2,1)S(1)} collective-permute-done((bf16[8,48,128]{2,1,0:T(8,128)(2,1)S(1)}, bf16[8,48,128]{2,1,0:T(8,128)(2,1)S(1)}, u32[]{:S(2)}, u32[]{:S(2)}) %collective-permute-start.11) | collective-permute-done | bytes 98336 | tf_op jit(solution)/shard_map/ppermute | solution.py:28
  73.9 2.0 collective-permute-start.30
  75.9 2.5 collective-permute-start.28
  78.4 2.0 collective-permute-start.48
  80.4 1.5 select_blocks.3
  82.3 3.6 %collective-permute-start.46 = (bf16[8,48,128]{2,1,0:T(8,128)(2,1)S(1)}, bf16[8,48,128]{2,1,0:T(8,128)(2,1)S(1)}, u32[]{:S(2)}, u32[]{:S(2)}) collective-permute-start(bf16[8,48,128]{2,1,0:T(8,128)(2,1)S(1)} %fusion.5), channel_id=1, source_target_pairs={{0,2},{1,3},{2,0},{3,1},{4,6},{5,7},{6,4},{7,5},{8,10},{9,11},{10,... | collective-permute-start | bytes 294920 | tf_op jit(solution)/shard_map/ppermute | solution.py:28
  85.9 6.5 %collective-permute-done.29 = bf16[8,64,128]{2,1,0:T(8,128)(2,1)S(1)} collective-permute-done((bf16[8,64,128]{2,1,0:T(8,128)(2,1)S(1)}, bf16[8,64,128]{2,1,0:T(8,128)(2,1)S(1)}, u32[]{:S(2)}, u32[]{:S(2)}) %collective-permute-start.29) | collective-permute-done | bytes 131104 | tf_op jit(solution)/shard_map/ppermute | solution.py:28
  92.4 1.5 collective-permute-start.14
  93.9 1.5 collective-permute-start.15
  97.2 4.6 %fetch.1.weight_ref = bf16[24,16,128,128]{3,2,1,0:T(8,128)(2,1)S(1)} custom-call(bf16[24,16,128,128]{3,2,1,0:T(8,128)(2,1)} %source.1), custom_call_target="tpu_custom_call" | custom-call | tf_op jit(solution)/shard_map/fetch/pallas_call | solution.py:122
  102.3 6.5 %collective-permute-done.15.refs_2_.refs_3_ = bf16[24,48,128]{2,1,0:T(8,128)(2,1)S(1)} collective-permute-done((bf16[24,48,128]{2,1,0:T(8,128)(2,1)S(1)}, bf16[24,48,128]{2,1,0:T(8,128)(2,1)S(1)}, u32[]{:S(2)}, u32[]{:S(2)}) %collective-permute-start.15) | collective-permute-done | bytes 294944 | tf_op jit(solution)/shard_map/ppermute | solution.py:37
  108.8 9.2 %residual_and_back.3 = (bf16[24,48,128]{2,1,0:T(8,128)(2,1)S(1)}, bf16[24,48,128]{2,1,0:T(8,128)(2,1)S(1)}, bf16[24,48,128]{2,1,0:T(8,128)(2,1)S(1)}, bf16[24,48...) custom-call(s32[384]{0:T(512)S(1)} %select_reduce_fusion.1.position_ref, s32[384]{0:T(512)S(1)} %select_reduce_fusion.order_ref, ...), custom_call_target="tpu_custom_call" | custom-call | tf_op jit(solution)/shard_map/residual_and_back/pallas_call | solution.py:242
  120.2 1.4 collective-permute-start.19
  124.3 1.5 select_blocks.4
  126.6 1.4 collective-permute-done.17.refs_1_
  128.0 1.5 collective-permute-start.33
  129.5 5.9 %collective-permute-done.18.refs_2_ = bf16[24,48,128]{2,1,0:T(8,128)(2,1)S(1)} collective-permute-done((bf16[24,48,128]{2,1,0:T(8,128)(2,1)S(1)}, bf16[24,48,128]{2,1,0:T(8,128)(2,1)S(1)}, u32[]{:S(2)}, u32[]{:S(2)}) %collective-permute-start.18) | collective-permute-done | bytes 294944 | tf_op jit(solution)/shard_map/ppermute | solution.py:37
  136.5 4.2 %collective-permute-done.50.refs_1_.refs_5_ = bf16[24,48,128]{2,1,0:T(8,128)(2,1)S(1)} collective-permute-done((bf16[24,48,128]{2,1,0:T(8,128)(2,1)S(1)}, bf16[24,48,128]{2,1,0:T(8,128)(2,1)S(1)}, u32[]{:S(2)}, u32[]{:S(2)}) %collective-permute-start.50) | collective-permute-done | bytes 294944 | tf_op jit(solution)/shard_map/ppermute | solution.py:37
  140.7 1.5 collective-permute-start.34
  143.3 19.5 %collective-permute-done.51.refs_2_.refs_5_ = bf16[24,48,128]{2,1,0:T(8,128)(2,1)S(1)} collective-permute-done((bf16[24,48,128]{2,1,0:T(8,128)(2,1)S(1)}, bf16[24,48,128]{2,1,0:T(8,128)(2,1)S(1)}, u32[]{:S(2)}, u32[]{:S(2)}) %collective-permute-start.51) | collective-permute-done | bytes 294944 | tf_op jit(solution)/shard_map/ppermute | solution.py:37
  162.9 9.2 %residual_and_back.5 = (bf16[24,48,128]{2,1,0:T(8,128)(2,1)S(1)}, bf16[24,48,128]{2,1,0:T(8,128)(2,1)S(1)}, bf16[24,48,128]{2,1,0:T(8,128)(2,1)S(1)}, bf16[24,48...) custom-call(s32[384]{0:T(512)S(1)} %select_reduce_fusion.1.position_ref, s32[384]{0:T(512)S(1)} %select_reduce_fusion.order_ref, ...), custom_call_target="tpu_custom_call" | custom-call | tf_op jit(solution)/shard_map/residual_and_back/pallas_call | solution.py:242
  172.8 2.9 %collective-permute-start.55 = (bf16[24,48,128]{2,1,0:T(8,128)(2,1)S(1)}, bf16[24,48,128]{2,1,0:T(8,128)(2,1)S(1)}, u32[]{:S(2)}, u32[]{:S(2)}) collective-permute-start(bf16[24,48,128]{2,1,0:T(8,128)(2,1)S(1)} %get-tuple-element.111), channel_id=1, source_target_pairs={{0,24},{8,16},{16,8},{24,0},{1,25},{9,17},{17,9},{25,1},{2,26},{10... | collective-permute-start | bytes 884744 | tf_op jit(solution)/shard_map/ppermute | solution.py:37
  175.6 10.1 %residual_and_back.4 = (bf16[24,64,128]{2,1,0:T(8,128)(2,1)S(1)}, bf16[24,64,128]{2,1,0:T(8,128)(2,1)S(1)}, bf16[24,64,128]{2,1,0:T(8,128)(2,1)S(1)}, bf16[24,64...) custom-call(s32[384]{0:T(512)S(1)} %select_reduce_fusion.1.position_ref, s32[384]{0:T(512)S(1)} %select_reduce_fusion.order_ref, ...), custom_call_target="tpu_custom_call" | custom-call | tf_op jit(solution)/shard_map/residual_and_back/pallas_call | solution.py:242
  186.5 1.7 collective-permute-done.54.refs_2_
  188.2 1.4 collective-permute-start.37
  191.0 2.0 collective-permute-start.21
  193.0 4.8 %collective-permute-done.35.refs_1_ = bf16[24,64,128]{2,1,0:T(8,128)(2,1)S(1)} collective-permute-done((bf16[24,64,128]{2,1,0:T(8,128)(2,1)S(1)}, bf16[24,64,128]{2,1,0:T(8,128)(2,1)S(1)}, u32[]{:S(2)}, u32[]{:S(2)}) %collective-permute-start.35) | collective-permute-done | bytes 393248 | tf_op jit(solution)/shard_map/ppermute | solution.py:37
  197.8 7.4 %collective-permute-done.36.refs_2_ = bf16[24,64,128]{2,1,0:T(8,128)(2,1)S(1)} collective-permute-done((bf16[24,64,128]{2,1,0:T(8,128)(2,1)S(1)}, bf16[24,64,128]{2,1,0:T(8,128)(2,1)S(1)}, u32[]{:S(2)}, u32[]{:S(2)}) %collective-permute-start.36) | collective-permute-done | bytes 393248 | tf_op jit(solution)/shard_map/ppermute | solution.py:37
  205.2 1.5 add_blocks.4
  206.8 4.0 %collective-permute-done.22 = bf16[8,48,128]{2,1,0:T(8,128)(2,1)S(1)} collective-permute-done((bf16[8,48,128]{2,1,0:T(8,128)(2,1)S(1)}, bf16[8,48,128]{2,1,0:T(8,128)(2,1)S(1)}, u32[]{:S(2)}, u32[]{:S(2)}) %collective-permute-start.22) | collective-permute-done | bytes 98336 | tf_op jit(solution)/shard_map/ppermute | solution.py:28
  210.9 2.0 collective-permute-start.26
  213.0 2.0 collective-permute-start.57
  215.0 1.6 collective-permute-start.59
  217.7 4.7 %collective-permute-done.57 = bf16[8,48,128]{2,1,0:T(8,128)(2,1)S(1)} collective-permute-done((bf16[8,48,128]{2,1,0:T(8,128)(2,1)S(1)}, bf16[8,48,128]{2,1,0:T(8,128)(2,1)S(1)}, u32[]{:S(2)}, u32[]{:S(2)}) %collective-permute-start.57) | collective-permute-done | bytes 98336 | tf_op jit(solution)/shard_map/ppermute | solution.py:28
  222.4 1.9 collective-permute-start.39
  224.3 7.2 %collective-permute-start.41 = (bf16[8,64,128]{2,1,0:T(8,128)(2,1)S(1)}, bf16[8,64,128]{2,1,0:T(8,128)(2,1)S(1)}, u32[]{:S(2)}, u32[]{:S(2)}) collective-permute-start(bf16[8,64,128]{2,1,0:T(8,128)(2,1)S(1)} %get-tuple-element.119), channel_id=1, source_target_pairs={{0,2},{1,3},{2,0},{3,1},{4,6},{5,7},{6,4},{7,5},{8,10},{9,11},{10,... | collective-permute-start | bytes 393224 | tf_op jit(solution)/shard_map/ppermute | solution.py:28
  232.2 2.3 collective-permute-done.41
  234.5 6.0 %collective-permute-done.40 = bf16[8,64,128]{2,1,0:T(8,128)(2,1)S(1)} collective-permute-done((bf16[8,64,128]{2,1,0:T(8,128)(2,1)S(1)}, bf16[8,64,128]{2,1,0:T(8,128)(2,1)S(1)}, u32[]{:S(2)}, u32[]{:S(2)}) %collective-permute-start.40) | collective-permute-done | bytes 131104 | tf_op jit(solution)/shard_map/ppermute | solution.py:28
  240.7 2.0 collective-permute-start.44
  242.7 2.5 collective-permute-start.42
  245.2 3.8 %collective-permute-done.44 = bf16[8,64,128]{2,1,0:T(8,128)(2,1)S(1)} collective-permute-done((bf16[8,64,128]{2,1,0:T(8,128)(2,1)S(1)}, bf16[8,64,128]{2,1,0:T(8,128)(2,1)S(1)}, u32[]{:S(2)}, u32[]{:S(2)}) %collective-permute-start.44) | collective-permute-done | bytes 131104 | tf_op jit(solution)/shard_map/ppermute | solution.py:28
  249.0 3.8 %collective-permute-done.43 = bf16[8,64,128]{2,1,0:T(8,128)(2,1)S(1)} collective-permute-done((bf16[8,64,128]{2,1,0:T(8,128)(2,1)S(1)}, bf16[8,64,128]{2,1,0:T(8,128)(2,1)S(1)}, u32[]{:S(2)}, u32[]{:S(2)}) %collective-permute-start.43) | collective-permute-done | bytes 131104 | tf_op jit(solution)/shard_map/ppermute | solution.py:28
  252.7 1.9 collective-permute-start.62
  254.8 2.5 collective-permute-start.60
  257.9 2.4 collective-permute-done.62
  260.3 3.2 %collective-permute-done.61 = bf16[8,48,128]{2,1,0:T(8,128)(2,1)S(1)} collective-permute-done((bf16[8,48,128]{2,1,0:T(8,128)(2,1)S(1)}, bf16[8,48,128]{2,1,0:T(8,128)(2,1)S(1)}, u32[]{:S(2)}, u32[]{:S(2)}) %collective-permute-start.61) | collective-permute-done | bytes 98336 | tf_op jit(solution)/shard_map/ppermute | solution.py:28
  263.7 3.3 %block_weight_grad.4.refs_6_ = bf16[384,128,128]{2,1,0:T(8,128)(2,1)} custom-call(s32[96]{0:T(128)S(1)} %get-tuple-element.131.order_ref, bf16[24,48,128]{2,1,0:T(8,128)(2,1)S(1)} %get-tuple-element.115.refs_0_, bf16[24,64,128]{2,1,0:T(8,128)(2,1)S(1)} %get-tuple-element.116.refs_1_, bf16[24,48,128]{2,1,0:T(8,128)(2,1)S(1)} %get-tuple-element.117.refs_2_, ...), custom_call_target="tpu_custom_call" | custom-call | tf_op jit(solution)/shard_map/block_weight_grad/pallas_call | solution.py:294
  267.0 3.4 %block_weight_grad.5.refs_6_ = bf16[384,128,128]{2,1,0:T(8,128)(2,1)} custom-call(s32[96]{0:T(128)S(1)} %get-tuple-element.132.order_ref, bf16[24,48,128]{2,1,0:T(8,128)(2,1)S(1)} %get-tuple-element.115.refs_0_, bf16[24,64,128]{2,1,0:T(8,128)(2,1)S(1)} %get-tuple-element.116.refs_1_, ...), custom_call_target="tpu_custom_call", output_to_operand_aliasing={{}: (7, {})} | custom-call | tf_op jit(solution)/shard_map/block_weight_grad/pallas_call | solution.py:294
  270.4 3.4 %block_weight_grad.6.refs_6_ = bf16[384,128,128]{2,1,0:T(8,128)(2,1)} custom-call(s32[96]{0:T(128)S(1)} %get-tuple-element.133.order_ref, bf16[24,48,128]{2,1,0:T(8,128)(2,1)S(1)} %get-tuple-element.115.refs_0_, bf16[24,64,128]{2,1,0:T(8,128)(2,1)S(1)} %get-tuple-element.116.refs_1_, ...), custom_call_target="tpu_custom_call", output_to_operand_aliasing={{}: (7, {})} | custom-call | tf_op jit(solution)/shard_map/block_weight_grad/pallas_call | solution.py:294
  273.8 3.4 %block_weight_grad.7 = bf16[384,128,128]{2,1,0:T(8,128)(2,1)} custom-call(s32[96]{0:T(128)S(1)} %get-tuple-element.134.order_ref, bf16[24,48,128]{2,1,0:T(8,128)(2,1)S(1)} %get-tuple-element.115.refs_0_, bf16[24,64,128]{2,1,0:T(8,128)(2,1)S(1)} %get-tuple-element.116.refs_1_, ...), custom_call_target="tpu_custom_call", output_to_operand_aliasing={{}: (7, {})} | custom-call | tf_op jit(solution)/shard_map/block_weight_grad/pallas_call | solution.py:294
  277.2 2.6 expand_weight_grad.1
  (156 shorter events, 30.1 us)
Async XLA Ops:
  3.0 22.4 %collective-permute-start.2 = (bf16[160,128]{1,0:T(8,128)(2,1)}, bf16[160,128]{1,0:T(8,128)(2,1)S(1)}, u32[]{:S(2)}, u32[]{:S(2)}) collective-permute-start(bf16[160,128]{1,0:T(8,128)(2,1)} %documents_ref.1), channel_id=1, source_target_pairs={{0,6},{1,7},{2,4},{3,5},{4,2},{5,3},{6,0},{7,1},{8,14},{9,15},{10,... | collective-permute-start | bytes 122888 | tf_op jit(solution)/shard_map/ppermute | solution.py:28
  8.2 8.0 %collective-permute-start = (bf16[160,128]{1,0:T(8,128)(2,1)}, bf16[160,128]{1,0:T(8,128)(2,1)S(1)}, u32[]{:S(2)}, u32[]{:S(2)}) collective-permute-start(bf16[160,128]{1,0:T(8,128)(2,1)} %documents_ref.1), channel_id=1, source_target_pairs={{0,2},{1,3},{2,0},{3,1},{4,6},{5,7},{6,4},{7,5},{8,10},{9,11},{10,... | collective-permute-start | bytes 122888 | tf_op jit(solution)/shard_map/ppermute | solution.py:28
  8.2 28.2 %collective-permute-start.4 = (bf16[128,512]{1,0:T(8,128)(2,1)S(1)}, bf16[128,512]{1,0:T(8,128)(2,1)S(1)}, u32[]{:S(2)}, u32[]{:S(2)}) collective-permute-start(bf16[128,512]{1,0:T(8,128)(2,1)S(1)} %get-tuple-element.63), channel_id=1, source_target_pairs={{0,4},{1,5},{2,6},{3,7},{4,0},{5,1},{6,2},{7,3},{8,12},{9,13},{10,... | collective-permute-start | bytes 393224 | tf_op jit(solution)/shard_map/ppermute | solution.py:28
  8.8 14.6 %collective-permute-start.7 = (bf16[128,1536]{1,0:T(8,128)(2,1)S(1)}, bf16[128,1536]{1,0:T(8,128)(2,1)S(1)}, u32[]{:S(2)}, u32[]{:S(2)}) collective-permute-start(bf16[128,1536]{1,0:T(8,128)(2,1)S(1)} %get-tuple-element.69), channel_id=1, source_target_pairs={{0,2},{1,3},{2,0},{3,1},{4,6},{5,7},{6,4},{7,5},{8,10},{9,11},{10,... | collective-permute-start | bytes 1179656 | tf_op jit(solution)/shard_map/ppermute | solution.py:28
  10.2 28.0 %collective-permute-start.3 = (bf16[128,2048]{1,0:T(8,128)(2,1)S(1)}, bf16[128,2048]{1,0:T(8,128)(2,1)S(1)}, u32[]{:S(2)}, u32[]{:S(2)}) collective-permute-start(bf16[128,2048]{1,0:T(8,128)(2,1)S(1)} %get-tuple-element.62), channel_id=1, source_target_pairs={{0,2},{1,3},{2,0},{3,1},{4,6},{5,7},{6,4},{7,5},{8,10},{9,11},{10,... | collective-permute-start | bytes 1572872 | tf_op jit(solution)/shard_map/ppermute | solution.py:28
  16.2 22.0 %collective-permute-start.5 = (bf16[128,512]{1,0:T(8,128)(2,1)S(1)}, bf16[128,512]{1,0:T(8,128)(2,1)S(1)}, u32[]{:S(2)}, u32[]{:S(2)}) collective-permute-start(bf16[128,512]{1,0:T(8,128)(2,1)S(1)} %get-tuple-element.64), channel_id=1, source_target_pairs={{0,6},{1,7},{2,4},{3,5},{4,2},{5,3},{6,0},{7,1},{8,14},{9,15},{10,... | collective-permute-start | bytes 393224 | tf_op jit(solution)/shard_map/ppermute | solution.py:28
  25.4 14.2 %collective-permute-start.8 = (f32[6,160,128]{2,1,0:T(8,128)}, f32[6,160,128]{2,1,0:T(8,128)}, u32[]{:S(2)}, u32[]{:S(2)}) collective-permute-start(f32[6,160,128]{2,1,0:T(8,128)} %get-tuple-element.71), channel_id=1, source_target_pairs={{0,1},{1,0},{2,3},{3,2},{4,5},{5,4},{6,7},{7,6},{8,9},{9,8},{10,11... | collective-permute-start | bytes 1474568 | tf_op jit(solution)/shard_map/ppermute | solution.py:33
  25.4 10.9 %collective-permute-start.1 = (bf16[160,128]{1,0:T(8,128)(2,1)}, bf16[160,128]{1,0:T(8,128)(2,1)S(1)}, u32[]{:S(2)}, u32[]{:S(2)}) collective-permute-start(bf16[160,128]{1,0:T(8,128)(2,1)} %documents_ref.1), channel_id=1, source_target_pairs={{0,4},{1,5},{2,6},{3,7},{4,0},{5,1},{6,2},{7,3},{8,12},{9,13},{10,... | collective-permute-start | bytes 122888 | tf_op jit(solution)/shard_map/ppermute | solution.py:28
  40.8 10.4 %collective-permute-start.9 = (f32[6,48,128]{2,1,0:T(8,128)S(1)}, f32[6,48,128]{2,1,0:T(8,128)S(1)}, u32[]{:S(2)}, u32[]{:S(2)}) collective-permute-start(f32[6,48,128]{2,1,0:T(8,128)S(1)} %get-tuple-element.122), channel_id=1, source_target_pairs={{0,4},{1,5},{2,6},{3,7},{4,0},{5,1},{6,2},{7,3},{8,12},{9,13},{10,... | collective-permute-start | bytes 442376 | tf_op jit(solution)/shard_map/ppermute | solution.py:28
  51.2 15.2 %collective-permute-start.27 = (f32[6,64,128]{2,1,0:T(8,128)S(1)}, f32[6,64,128]{2,1,0:T(8,128)S(1)}, u32[]{:S(2)}, u32[]{:S(2)}) collective-permute-start(f32[6,64,128]{2,1,0:T(8,128)S(1)} %slice.131), channel_id=1, source_target_pairs={{0,4},{1,5},{2,6},{3,7},{4,0},{5,1},{6,2},{7,3},{8,12},{9,13},{10,... | collective-permute-start | bytes 589832 | tf_op jit(solution)/shard_map/ppermute | solution.py:28
  51.3 15.3 %collective-permute-start.12 = (bf16[8,48,128]{2,1,0:T(8,128)(2,1)S(1)}, bf16[8,48,128]{2,1,0:T(8,128)(2,1)S(1)}, u32[]{:S(2)}, u32[]{:S(2)}) collective-permute-start(bf16[8,48,128]{2,1,0:T(8,128)(2,1)S(1)} %fusion.4), channel_id=1, source_target_pairs={{0,6},{1,7},{2,4},{3,5},{4,2},{5,3},{6,0},{7,1},{8,14},{9,15},{10,... | collective-permute-start | bytes 294920 | tf_op jit(solution)/shard_map/ppermute | solution.py:28
  53.2 20.5 %collective-permute-start.11 = (bf16[8,48,128]{2,1,0:T(8,128)(2,1)S(1)}, bf16[8,48,128]{2,1,0:T(8,128)(2,1)S(1)}, u32[]{:S(2)}, u32[]{:S(2)}) collective-permute-start(bf16[8,48,128]{2,1,0:T(8,128)(2,1)S(1)} %fusion.4), channel_id=1, source_target_pairs={{0,4},{1,5},{2,6},{3,7},{4,0},{5,1},{6,2},{7,3},{8,12},{9,13},{10,... | collective-permute-start | bytes 294920 | tf_op jit(solution)/shard_map/ppermute | solution.py:28
  55.2 18.6 %collective-permute-start.10 = (bf16[8,48,128]{2,1,0:T(8,128)(2,1)S(1)}, bf16[8,48,128]{2,1,0:T(8,128)(2,1)S(1)}, u32[]{:S(2)}, u32[]{:S(2)}) collective-permute-start(bf16[8,48,128]{2,1,0:T(8,128)(2,1)S(1)} %fusion.4), channel_id=1, source_target_pairs={{0,2},{1,3},{2,0},{3,1},{4,6},{5,7},{6,4},{7,5},{8,10},{9,11},{10,... | collective-permute-start | bytes 294920 | tf_op jit(solution)/shard_map/ppermute | solution.py:28
  66.5 11.9 %collective-permute-start.45 = (f32[6,48,128]{2,1,0:T(8,128)S(1)}, f32[6,48,128]{2,1,0:T(8,128)S(1)}, u32[]{:S(2)}, u32[]{:S(2)}) collective-permute-start(f32[6,48,128]{2,1,0:T(8,128)S(1)} %get-tuple-element.102), channel_id=1, source_target_pairs={{0,4},{1,5},{2,6},{3,7},{4,0},{5,1},{6,2},{7,3},{8,12},{9,13},{10,... | collective-permute-start | bytes 442376 | tf_op jit(solution)/shard_map/ppermute | solution.py:28
  73.8 6.6 %collective-permute-start.13 = (bf16[32,48,128]{2,1,0:T(8,128)(2,1)S(1)}, bf16[32,48,128]{2,1,0:T(8,128)(2,1)S(1)}, u32[]{:S(2)}, u32[]{:S(2)}) collective-permute-start(bf16[32,48,128]{2,1,0:T(8,128)(2,1)S(1)} %pad_maximum_fusion.2.refs_0_), channel_id=1, source_target_pairs={{0,1},{1,0},{2,3},{3,2},{4,5},{5,4},{6,7},{7,6},{8,9},{9,8},{10,11... | collective-permute-start | bytes 1179656 | tf_op jit(solution)/shard_map/ppermute | solution.py:33
  73.9 8.4 %collective-permute-start.30 = (bf16[8,64,128]{2,1,0:T(8,128)(2,1)S(1)}, bf16[8,64,128]{2,1,0:T(8,128)(2,1)S(1)}, u32[]{:S(2)}, u32[]{:S(2)}) collective-permute-start(bf16[8,64,128]{2,1,0:T(8,128)(2,1)S(1)} %fusion.2), channel_id=1, source_target_pairs={{0,6},{1,7},{2,4},{3,5},{4,2},{5,3},{6,0},{7,1},{8,14},{9,15},{10,... | collective-permute-start | bytes 393224 | tf_op jit(solution)/shard_map/ppermute | solution.py:28
  75.9 16.6 %collective-permute-start.29 = (bf16[8,64,128]{2,1,0:T(8,128)(2,1)S(1)}, bf16[8,64,128]{2,1,0:T(8,128)(2,1)S(1)}, u32[]{:S(2)}, u32[]{:S(2)}) collective-permute-start(bf16[8,64,128]{2,1,0:T(8,128)(2,1)S(1)} %fusion.2), channel_id=1, source_target_pairs={{0,4},{1,5},{2,6},{3,7},{4,0},{5,1},{6,2},{7,3},{8,12},{9,13},{10,... | collective-permute-start | bytes 393224 | tf_op jit(solution)/shard_map/ppermute | solution.py:28
  75.9 18.0 %collective-permute-start.28 = (bf16[8,64,128]{2,1,0:T(8,128)(2,1)S(1)}, bf16[8,64,128]{2,1,0:T(8,128)(2,1)S(1)}, u32[]{:S(2)}, u32[]{:S(2)}) collective-permute-start(bf16[8,64,128]{2,1,0:T(8,128)(2,1)S(1)} %fusion.2), channel_id=1, source_target_pairs={{0,2},{1,3},{2,0},{3,1},{4,6},{5,7},{6,4},{7,5},{8,10},{9,11},{10,... | collective-permute-start | bytes 393224 | tf_op jit(solution)/shard_map/ppermute | solution.py:28
  78.4 17.0 %collective-permute-start.48 = (bf16[8,48,128]{2,1,0:T(8,128)(2,1)S(1)}, bf16[8,48,128]{2,1,0:T(8,128)(2,1)S(1)}, u32[]{:S(2)}, u32[]{:S(2)}) collective-permute-start(bf16[8,48,128]{2,1,0:T(8,128)(2,1)S(1)} %fusion.5), channel_id=1, source_target_pairs={{0,6},{1,7},{2,4},{3,5},{4,2},{5,3},{6,0},{7,1},{8,14},{9,15},{10,... | collective-permute-start | bytes 294920 | tf_op jit(solution)/shard_map/ppermute | solution.py:28
  80.4 16.1 %collective-permute-start.47 = (bf16[8,48,128]{2,1,0:T(8,128)(2,1)S(1)}, bf16[8,48,128]{2,1,0:T(8,128)(2,1)S(1)}, u32[]{:S(2)}, u32[]{:S(2)}) collective-permute-start(bf16[8,48,128]{2,1,0:T(8,128)(2,1)S(1)} %fusion.5), channel_id=1, source_target_pairs={{0,4},{1,5},{2,6},{3,7},{4,0},{5,1},{6,2},{7,3},{8,12},{9,13},{10,... | collective-permute-start | bytes 294920 | tf_op jit(solution)/shard_map/ppermute | solution.py:28
  82.3 14.3 %collective-permute-start.46 = (bf16[8,48,128]{2,1,0:T(8,128)(2,1)S(1)}, bf16[8,48,128]{2,1,0:T(8,128)(2,1)S(1)}, u32[]{:S(2)}, u32[]{:S(2)}) collective-permute-start(bf16[8,48,128]{2,1,0:T(8,128)(2,1)S(1)} %fusion.5), channel_id=1, source_target_pairs={{0,2},{1,3},{2,0},{3,1},{4,6},{5,7},{6,4},{7,5},{8,10},{9,11},{10,... | collective-permute-start | bytes 294920 | tf_op jit(solution)/shard_map/ppermute | solution.py:28
  92.4 9.9 %collective-permute-start.14 = (bf16[24,48,128]{2,1,0:T(8,128)(2,1)S(1)}, bf16[24,48,128]{2,1,0:T(8,128)(2,1)S(1)}, u32[]{:S(2)}, u32[]{:S(2)}) collective-permute-start(bf16[24,48,128]{2,1,0:T(8,128)(2,1)S(1)} %get-tuple-element.78), channel_id=1, source_target_pairs={{0,8},{8,0},{16,24},{24,16},{1,9},{9,1},{17,25},{25,17},{2,10},{10... | collective-permute-start | bytes 884744 | tf_op jit(solution)/shard_map/ppermute | solution.py:37
  93.9 14.9 %collective-permute-start.15 = (bf16[24,48,128]{2,1,0:T(8,128)(2,1)S(1)}, bf16[24,48,128]{2,1,0:T(8,128)(2,1)S(1)}, u32[]{:S(2)}, u32[]{:S(2)}) collective-permute-start(bf16[24,48,128]{2,1,0:T(8,128)(2,1)S(1)} %get-tuple-element.79), channel_id=1, source_target_pairs={{0,16},{8,24},{16,0},{24,8},{1,17},{9,25},{17,1},{25,9},{2,18},{10... | collective-permute-start | bytes 884744 | tf_op jit(solution)/shard_map/ppermute | solution.py:37
  95.4 13.4 %collective-permute-start.16 = (bf16[24,48,128]{2,1,0:T(8,128)(2,1)S(1)}, bf16[24,48,128]{2,1,0:T(8,128)(2,1)S(1)}, u32[]{:S(2)}, u32[]{:S(2)}) collective-permute-start(bf16[24,48,128]{2,1,0:T(8,128)(2,1)S(1)} %get-tuple-element.80), channel_id=1, source_target_pairs={{0,24},{8,16},{16,8},{24,0},{1,25},{9,17},{17,9},{25,1},{2,26},{10... | collective-permute-start | bytes 884744 | tf_op jit(solution)/shard_map/ppermute | solution.py:37
  96.5 27.7 %collective-permute-start.31 = (bf16[32,64,128]{2,1,0:T(8,128)(2,1)S(1)}, bf16[32,64,128]{2,1,0:T(8,128)(2,1)S(1)}, u32[]{:S(2)}, u32[]{:S(2)}) collective-permute-start(bf16[32,64,128]{2,1,0:T(8,128)(2,1)S(1)} %pad_maximum_fusion.refs_0_), channel_id=1, source_target_pairs={{0,1},{1,0},{2,3},{3,2},{4,5},{5,4},{6,7},{7,6},{8,9},{9,8},{10,11... | collective-permute-start | bytes 1572872 | tf_op jit(solution)/shard_map/ppermute | solution.py:33
  96.6 25.0 %collective-permute-start.49 = (bf16[32,48,128]{2,1,0:T(8,128)(2,1)S(1)}, bf16[32,48,128]{2,1,0:T(8,128)(2,1)S(1)}, u32[]{:S(2)}, u32[]{:S(2)}) collective-permute-start(bf16[32,48,128]{2,1,0:T(8,128)(2,1)S(1)} %pad_maximum_fusion.4.refs_0_), channel_id=1, source_target_pairs={{0,1},{1,0},{2,3},{3,2},{4,5},{5,4},{6,7},{7,6},{8,9},{9,8},{10,11... | collective-permute-start | bytes 1179656 | tf_op jit(solution)/shard_map/ppermute | solution.py:33
  118.0 9.9 %collective-permute-start.17 = (bf16[24,48,128]{2,1,0:T(8,128)(2,1)S(1)}, bf16[24,48,128]{2,1,0:T(8,128)(2,1)S(1)}, u32[]{:S(2)}, u32[]{:S(2)}) collective-permute-start(bf16[24,48,128]{2,1,0:T(8,128)(2,1)S(1)} %get-tuple-element.82), channel_id=1, source_target_pairs={{0,8},{8,0},{16,24},{24,16},{1,9},{9,1},{17,25},{25,17},{2,10},{10... | collective-permute-start | bytes 884744 | tf_op jit(solution)/shard_map/ppermute | solution.py:37
  119.3 16.1 %collective-permute-start.18 = (bf16[24,48,128]{2,1,0:T(8,128)(2,1)S(1)}, bf16[24,48,128]{2,1,0:T(8,128)(2,1)S(1)}, u32[]{:S(2)}, u32[]{:S(2)}) collective-permute-start(bf16[24,48,128]{2,1,0:T(8,128)(2,1)S(1)} %get-tuple-element.83), channel_id=1, source_target_pairs={{0,16},{8,24},{16,0},{24,8},{1,17},{9,25},{17,1},{25,9},{2,18},{10... | collective-permute-start | bytes 884744 | tf_op jit(solution)/shard_map/ppermute | solution.py:37
  120.2 15.3 %collective-permute-start.19 = (bf16[24,48,128]{2,1,0:T(8,128)(2,1)S(1)}, bf16[24,48,128]{2,1,0:T(8,128)(2,1)S(1)}, u32[]{:S(2)}, u32[]{:S(2)}) collective-permute-start(bf16[24,48,128]{2,1,0:T(8,128)(2,1)S(1)} %get-tuple-element.84), channel_id=1, source_target_pairs={{0,24},{8,16},{16,8},{24,0},{1,25},{9,17},{17,9},{25,1},{2,26},{10... | collective-permute-start | bytes 884744 | tf_op jit(solution)/shard_map/ppermute | solution.py:37
  123.0 17.7 %collective-permute-start.50 = (bf16[24,48,128]{2,1,0:T(8,128)(2,1)S(1)}, bf16[24,48,128]{2,1,0:T(8,128)(2,1)S(1)}, u32[]{:S(2)}, u32[]{:S(2)}) collective-permute-start(bf16[24,48,128]{2,1,0:T(8,128)(2,1)S(1)} %get-tuple-element.105), channel_id=1, source_target_pairs={{0,8},{8,0},{16,24},{24,16},{1,9},{9,1},{17,25},{25,17},{2,10},{10... | collective-permute-start | bytes 884744 | tf_op jit(solution)/shard_map/ppermute | solution.py:37
  125.7 47.0 %collective-permute-start.32 = (bf16[24,64,128]{2,1,0:T(8,128)(2,1)S(1)}, bf16[24,64,128]{2,1,0:T(8,128)(2,1)S(1)}, u32[]{:S(2)}, u32[]{:S(2)}) collective-permute-start(bf16[24,64,128]{2,1,0:T(8,128)(2,1)S(1)} %get-tuple-element.91), channel_id=1, source_target_pairs={{0,8},{8,0},{16,24},{24,16},{1,9},{9,1},{17,25},{25,17},{2,10},{10... | collective-permute-start | bytes 1179656 | tf_op jit(solution)/shard_map/ppermute | solution.py:37
  128.0 44.8 %collective-permute-start.33 = (bf16[24,64,128]{2,1,0:T(8,128)(2,1)S(1)}, bf16[24,64,128]{2,1,0:T(8,128)(2,1)S(1)}, u32[]{:S(2)}, u32[]{:S(2)}) collective-permute-start(bf16[24,64,128]{2,1,0:T(8,128)(2,1)S(1)} %get-tuple-element.92), channel_id=1, source_target_pairs={{0,16},{8,24},{16,0},{24,8},{1,17},{9,25},{17,1},{25,9},{2,18},{10... | collective-permute-start | bytes 1179656 | tf_op jit(solution)/shard_map/ppermute | solution.py:37
  135.4 27.4 %collective-permute-start.51 = (bf16[24,48,128]{2,1,0:T(8,128)(2,1)S(1)}, bf16[24,48,128]{2,1,0:T(8,128)(2,1)S(1)}, u32[]{:S(2)}, u32[]{:S(2)}) collective-permute-start(bf16[24,48,128]{2,1,0:T(8,128)(2,1)S(1)} %get-tuple-element.106), channel_id=1, source_target_pairs={{0,16},{8,24},{16,0},{24,8},{1,17},{9,25},{17,1},{25,9},{2,18},{10... | collective-permute-start | bytes 884744 | tf_op jit(solution)/shard_map/ppermute | solution.py:37
  135.4 27.4 %collective-permute-start.52 = (bf16[24,48,128]{2,1,0:T(8,128)(2,1)S(1)}, bf16[24,48,128]{2,1,0:T(8,128)(2,1)S(1)}, u32[]{:S(2)}, u32[]{:S(2)}) collective-permute-start(bf16[24,48,128]{2,1,0:T(8,128)(2,1)S(1)} %get-tuple-element.107), channel_id=1, source_target_pairs={{0,24},{8,16},{16,8},{24,0},{1,25},{9,17},{17,9},{25,1},{2,26},{10... | collective-permute-start | bytes 884744 | tf_op jit(solution)/shard_map/ppermute | solution.py:37
  140.7 35.0 %collective-permute-start.34 = (bf16[24,64,128]{2,1,0:T(8,128)(2,1)S(1)}, bf16[24,64,128]{2,1,0:T(8,128)(2,1)S(1)}, u32[]{:S(2)}, u32[]{:S(2)}) collective-permute-start(bf16[24,64,128]{2,1,0:T(8,128)(2,1)S(1)} %get-tuple-element.93), channel_id=1, source_target_pairs={{0,24},{8,16},{16,8},{24,0},{1,25},{9,17},{17,9},{25,1},{2,26},{10... | collective-permute-start | bytes 1179656 | tf_op jit(solution)/shard_map/ppermute | solution.py:37
  162.8 28.0 %collective-permute-start.20 = (bf16[32,48,128]{2,1,0:T(8,128)(2,1)S(1)}, bf16[32,48,128]{2,1,0:T(8,128)(2,1)S(1)}, u32[]{:S(2)}, u32[]{:S(2)}) collective-permute-start(bf16[32,48,128]{2,1,0:T(8,128)(2,1)S(1)} %get-tuple-element.86), channel_id=1, source_target_pairs={{0,1},{1,0},{2,3},{3,2},{4,5},{5,4},{6,7},{7,6},{8,9},{9,8},{10,11... | collective-permute-start | bytes 1179656 | tf_op jit(solution)/shard_map/ppermute | solution.py:33
  172.1 14.3 %collective-permute-start.53 = (bf16[24,48,128]{2,1,0:T(8,128)(2,1)S(1)}, bf16[24,48,128]{2,1,0:T(8,128)(2,1)S(1)}, u32[]{:S(2)}, u32[]{:S(2)}) collective-permute-start(bf16[24,48,128]{2,1,0:T(8,128)(2,1)S(1)} %get-tuple-element.109), channel_id=1, source_target_pairs={{0,8},{8,0},{16,24},{24,16},{1,9},{9,1},{17,25},{25,17},{2,10},{10... | collective-permute-start | bytes 884744 | tf_op jit(solution)/shard_map/ppermute | solution.py:37
  172.7 15.5 %collective-permute-start.54 = (bf16[24,48,128]{2,1,0:T(8,128)(2,1)S(1)}, bf16[24,48,128]{2,1,0:T(8,128)(2,1)S(1)}, u32[]{:S(2)}, u32[]{:S(2)}) collective-permute-start(bf16[24,48,128]{2,1,0:T(8,128)(2,1)S(1)} %get-tuple-element.110), channel_id=1, source_target_pairs={{0,16},{8,24},{16,0},{24,8},{1,17},{9,25},{17,1},{25,9},{2,18},{10... | collective-permute-start | bytes 884744 | tf_op jit(solution)/shard_map/ppermute | solution.py:37
  172.8 16.9 %collective-permute-start.55 = (bf16[24,48,128]{2,1,0:T(8,128)(2,1)S(1)}, bf16[24,48,128]{2,1,0:T(8,128)(2,1)S(1)}, u32[]{:S(2)}, u32[]{:S(2)}) collective-permute-start(bf16[24,48,128]{2,1,0:T(8,128)(2,1)S(1)} %get-tuple-element.111), channel_id=1, source_target_pairs={{0,24},{8,16},{16,8},{24,0},{1,25},{9,17},{17,9},{25,1},{2,26},{10... | collective-permute-start | bytes 884744 | tf_op jit(solution)/shard_map/ppermute | solution.py:37
  185.8 12.1 %collective-permute-start.35 = (bf16[24,64,128]{2,1,0:T(8,128)(2,1)S(1)}, bf16[24,64,128]{2,1,0:T(8,128)(2,1)S(1)}, u32[]{:S(2)}, u32[]{:S(2)}) collective-permute-start(bf16[24,64,128]{2,1,0:T(8,128)(2,1)S(1)} %get-tuple-element.95), channel_id=1, source_target_pairs={{0,8},{8,0},{16,24},{24,16},{1,9},{9,1},{17,25},{25,17},{2,10},{10... | collective-permute-start | bytes 1179656 | tf_op jit(solution)/shard_map/ppermute | solution.py:37
  186.4 18.8 %collective-permute-start.36 = (bf16[24,64,128]{2,1,0:T(8,128)(2,1)S(1)}, bf16[24,64,128]{2,1,0:T(8,128)(2,1)S(1)}, u32[]{:S(2)}, u32[]{:S(2)}) collective-permute-start(bf16[24,64,128]{2,1,0:T(8,128)(2,1)S(1)} %get-tuple-element.96), channel_id=1, source_target_pairs={{0,16},{8,24},{16,0},{24,8},{1,17},{9,25},{17,1},{25,9},{2,18},{10... | collective-permute-start | bytes 1179656 | tf_op jit(solution)/shard_map/ppermute | solution.py:37
  188.2 17.1 %collective-permute-start.37 = (bf16[24,64,128]{2,1,0:T(8,128)(2,1)S(1)}, bf16[24,64,128]{2,1,0:T(8,128)(2,1)S(1)}, u32[]{:S(2)}, u32[]{:S(2)}) collective-permute-start(bf16[24,64,128]{2,1,0:T(8,128)(2,1)S(1)} %get-tuple-element.97), channel_id=1, source_target_pairs={{0,24},{8,16},{16,8},{24,0},{1,25},{9,17},{17,9},{25,1},{2,26},{10... | collective-permute-start | bytes 1179656 | tf_op jit(solution)/shard_map/ppermute | solution.py:37
  190.8 22.1 %collective-permute-start.56 = (bf16[32,48,128]{2,1,0:T(8,128)(2,1)S(1)}, bf16[32,48,128]{2,1,0:T(8,128)(2,1)S(1)}, u32[]{:S(2)}, u32[]{:S(2)}) collective-permute-start(bf16[32,48,128]{2,1,0:T(8,128)(2,1)S(1)} %get-tuple-element.113), channel_id=1, source_target_pairs={{0,1},{1,0},{2,3},{3,2},{4,5},{5,4},{6,7},{7,6},{8,9},{9,8},{10,11... | collective-permute-start | bytes 1179656 | tf_op jit(solution)/shard_map/ppermute | solution.py:33
  191.0 15.8 %collective-permute-start.21 = (bf16[8,48,128]{2,1,0:T(8,128)(2,1)S(1)}, bf16[8,48,128]{2,1,0:T(8,128)(2,1)S(1)}, u32[]{:S(2)}, u32[]{:S(2)}) collective-permute-start(bf16[8,48,128]{2,1,0:T(8,128)(2,1)S(1)} %get-tuple-element.126), channel_id=1, source_target_pairs={{0,6},{1,7},{2,4},{3,5},{4,2},{5,3},{6,0},{7,1},{8,14},{9,15},{10,... | collective-permute-start | bytes 294920 | tf_op jit(solution)/shard_map/ppermute | solution.py:28
  197.8 9.0 %collective-permute-start.23 = (bf16[8,48,128]{2,1,0:T(8,128)(2,1)S(1)}, bf16[8,48,128]{2,1,0:T(8,128)(2,1)S(1)}, u32[]{:S(2)}, u32[]{:S(2)}) collective-permute-start(bf16[8,48,128]{2,1,0:T(8,128)(2,1)S(1)} %get-tuple-element.127), channel_id=1, source_target_pairs={{0,2},{1,3},{2,0},{3,1},{4,6},{5,7},{6,4},{7,5},{8,10},{9,11},{10,... | collective-permute-start | bytes 294920 | tf_op jit(solution)/shard_map/ppermute | solution.py:28
  206.7 9.9 %collective-permute-start.38 = (bf16[32,64,128]{2,1,0:T(8,128)(2,1)S(1)}, bf16[32,64,128]{2,1,0:T(8,128)(2,1)S(1)}, u32[]{:S(2)}, u32[]{:S(2)}) collective-permute-start(bf16[32,64,128]{2,1,0:T(8,128)(2,1)S(1)} %get-tuple-element.99), channel_id=1, source_target_pairs={{0,1},{1,0},{2,3},{3,2},{4,5},{5,4},{6,7},{7,6},{8,9},{9,8},{10,11... | collective-permute-start | bytes 1572872 | tf_op jit(solution)/shard_map/ppermute | solution.py:33
  210.9 43.9 %collective-permute-start.26 = (bf16[8,48,128]{2,1,0:T(8,128)(2,1)S(1)}, bf16[8,48,128]{2,1,0:T(8,128)(2,1)S(1)}, u32[]{:S(2)}, u32[]{:S(2)}) collective-permute-start(bf16[8,48,128]{2,1,0:T(8,128)(2,1)S(1)} %select_convert_fusion.2), channel_id=1, source_target_pairs={{0,6},{1,7},{2,4},{3,5},{4,2},{5,3},{6,0},{7,1},{8,14},{9,15},{10,... | collective-permute-start | bytes 294920 | tf_op jit(solution)/shard_map/ppermute | solution.py:28
  212.9 44.4 %collective-permute-start.25 = (bf16[8,48,128]{2,1,0:T(8,128)(2,1)S(1)}, bf16[8,48,128]{2,1,0:T(8,128)(2,1)S(1)}, u32[]{:S(2)}, u32[]{:S(2)}) collective-permute-start(bf16[8,48,128]{2,1,0:T(8,128)(2,1)S(1)} %select_convert_fusion.2), channel_id=1, source_target_pairs={{0,4},{1,5},{2,6},{3,7},{4,0},{5,1},{6,2},{7,3},{8,12},{9,13},{10,... | collective-permute-start | bytes 294920 | tf_op jit(solution)/shard_map/ppermute | solution.py:28
  213.0 9.3 %collective-permute-start.57 = (bf16[8,48,128]{2,1,0:T(8,128)(2,1)S(1)}, bf16[8,48,128]{2,1,0:T(8,128)(2,1)S(1)}, u32[]{:S(2)}, u32[]{:S(2)}) collective-permute-start(bf16[8,48,128]{2,1,0:T(8,128)(2,1)S(1)} %get-tuple-element.123), channel_id=1, source_target_pairs={{0,6},{1,7},{2,4},{3,5},{4,2},{5,3},{6,0},{7,1},{8,14},{9,15},{10,... | collective-permute-start | bytes 294920 | tf_op jit(solution)/shard_map/ppermute | solution.py:28
  215.0 9.3 %collective-permute-start.59 = (bf16[8,48,128]{2,1,0:T(8,128)(2,1)S(1)}, bf16[8,48,128]{2,1,0:T(8,128)(2,1)S(1)}, u32[]{:S(2)}, u32[]{:S(2)}) collective-permute-start(bf16[8,48,128]{2,1,0:T(8,128)(2,1)S(1)} %get-tuple-element.124), channel_id=1, source_target_pairs={{0,2},{1,3},{2,0},{3,1},{4,6},{5,7},{6,4},{7,5},{8,10},{9,11},{10,... | collective-permute-start | bytes 294920 | tf_op jit(solution)/shard_map/ppermute | solution.py:28
  216.6 15.5 %collective-permute-start.58 = (bf16[8,48,128]{2,1,0:T(8,128)(2,1)S(1)}, bf16[8,48,128]{2,1,0:T(8,128)(2,1)S(1)}, u32[]{:S(2)}, u32[]{:S(2)}) collective-permute-start(bf16[8,48,128]{2,1,0:T(8,128)(2,1)S(1)} %get-tuple-element.125), channel_id=1, source_target_pairs={{0,4},{1,5},{2,6},{3,7},{4,0},{5,1},{6,2},{7,3},{8,12},{9,13},{10,... | collective-permute-start | bytes 294920 | tf_op jit(solution)/shard_map/ppermute | solution.py:28
  222.4 9.8 %collective-permute-start.39 = (bf16[8,64,128]{2,1,0:T(8,128)(2,1)S(1)}, bf16[8,64,128]{2,1,0:T(8,128)(2,1)S(1)}, u32[]{:S(2)}, u32[]{:S(2)}) collective-permute-start(bf16[8,64,128]{2,1,0:T(8,128)(2,1)S(1)} %get-tuple-element.118), channel_id=1, source_target_pairs={{0,6},{1,7},{2,4},{3,5},{4,2},{5,3},{6,0},{7,1},{8,14},{9,15},{10,... | collective-permute-start | bytes 393224 | tf_op jit(solution)/shard_map/ppermute | solution.py:28
  224.3 10.2 %collective-permute-start.41 = (bf16[8,64,128]{2,1,0:T(8,128)(2,1)S(1)}, bf16[8,64,128]{2,1,0:T(8,128)(2,1)S(1)}, u32[]{:S(2)}, u32[]{:S(2)}) collective-permute-start(bf16[8,64,128]{2,1,0:T(8,128)(2,1)S(1)} %get-tuple-element.119), channel_id=1, source_target_pairs={{0,2},{1,3},{2,0},{3,1},{4,6},{5,7},{6,4},{7,5},{8,10},{9,11},{10,... | collective-permute-start | bytes 393224 | tf_op jit(solution)/shard_map/ppermute | solution.py:28
  232.1 8.4 %collective-permute-start.40 = (bf16[8,64,128]{2,1,0:T(8,128)(2,1)S(1)}, bf16[8,64,128]{2,1,0:T(8,128)(2,1)S(1)}, u32[]{:S(2)}, u32[]{:S(2)}) collective-permute-start(bf16[8,64,128]{2,1,0:T(8,128)(2,1)S(1)} %get-tuple-element.120), channel_id=1, source_target_pairs={{0,4},{1,5},{2,6},{3,7},{4,0},{5,1},{6,2},{7,3},{8,12},{9,13},{10,... | collective-permute-start | bytes 393224 | tf_op jit(solution)/shard_map/ppermute | solution.py:28
  240.7 8.3 %collective-permute-start.44 = (bf16[8,64,128]{2,1,0:T(8,128)(2,1)S(1)}, bf16[8,64,128]{2,1,0:T(8,128)(2,1)S(1)}, u32[]{:S(2)}, u32[]{:S(2)}) collective-permute-start(bf16[8,64,128]{2,1,0:T(8,128)(2,1)S(1)} %select_convert_fusion), channel_id=1, source_target_pairs={{0,6},{1,7},{2,4},{3,5},{4,2},{5,3},{6,0},{7,1},{8,14},{9,15},{10,... | collective-permute-start | bytes 393224 | tf_op jit(solution)/shard_map/ppermute | solution.py:28
  242.7 10.1 %collective-permute-start.43 = (bf16[8,64,128]{2,1,0:T(8,128)(2,1)S(1)}, bf16[8,64,128]{2,1,0:T(8,128)(2,1)S(1)}, u32[]{:S(2)}, u32[]{:S(2)}) collective-permute-start(bf16[8,64,128]{2,1,0:T(8,128)(2,1)S(1)} %select_convert_fusion), channel_id=1, source_target_pairs={{0,4},{1,5},{2,6},{3,7},{4,0},{5,1},{6,2},{7,3},{8,12},{9,13},{10,... | collective-permute-start | bytes 393224 | tf_op jit(solution)/shard_map/ppermute | solution.py:28
  242.7 12.0 %collective-permute-start.42 = (bf16[8,64,128]{2,1,0:T(8,128)(2,1)S(1)}, bf16[8,64,128]{2,1,0:T(8,128)(2,1)S(1)}, u32[]{:S(2)}, u32[]{:S(2)}) collective-permute-start(bf16[8,64,128]{2,1,0:T(8,128)(2,1)S(1)} %select_convert_fusion), channel_id=1, source_target_pairs={{0,2},{1,3},{2,0},{3,1},{4,6},{5,7},{6,4},{7,5},{8,10},{9,11},{10,... | collective-permute-start | bytes 393224 | tf_op jit(solution)/shard_map/ppermute | solution.py:28
  248.9 8.3 %collective-permute-start.24 = (bf16[8,48,128]{2,1,0:T(8,128)(2,1)S(1)}, bf16[8,48,128]{2,1,0:T(8,128)(2,1)S(1)}, u32[]{:S(2)}, u32[]{:S(2)}) collective-permute-start(bf16[8,48,128]{2,1,0:T(8,128)(2,1)S(1)} %select_convert_fusion.2), channel_id=1, source_target_pairs={{0,2},{1,3},{2,0},{3,1},{4,6},{5,7},{6,4},{7,5},{8,10},{9,11},{10,... | collective-permute-start | bytes 294920 | tf_op jit(solution)/shard_map/ppermute | solution.py:28
  252.7 7.6 %collective-permute-start.62 = (bf16[8,48,128]{2,1,0:T(8,128)(2,1)S(1)}, bf16[8,48,128]{2,1,0:T(8,128)(2,1)S(1)}, u32[]{:S(2)}, u32[]{:S(2)}) collective-permute-start(bf16[8,48,128]{2,1,0:T(8,128)(2,1)S(1)} %select_convert_fusion.1), channel_id=1, source_target_pairs={{0,6},{1,7},{2,4},{3,5},{4,2},{5,3},{6,0},{7,1},{8,14},{9,15},{10,... | collective-permute-start | bytes 294920 | tf_op jit(solution)/shard_map/ppermute | solution.py:28
  254.7 8.8 %collective-permute-start.61 = (bf16[8,48,128]{2,1,0:T(8,128)(2,1)S(1)}, bf16[8,48,128]{2,1,0:T(8,128)(2,1)S(1)}, u32[]{:S(2)}, u32[]{:S(2)}) collective-permute-start(bf16[8,48,128]{2,1,0:T(8,128)(2,1)S(1)} %select_convert_fusion.1), channel_id=1, source_target_pairs={{0,4},{1,5},{2,6},{3,7},{4,0},{5,1},{6,2},{7,3},{8,12},{9,13},{10,... | collective-permute-start | bytes 294920 | tf_op jit(solution)/shard_map/ppermute | solution.py:28
  254.8 8.7 %collective-permute-start.60 = (bf16[8,48,128]{2,1,0:T(8,128)(2,1)S(1)}, bf16[8,48,128]{2,1,0:T(8,128)(2,1)S(1)}, u32[]{:S(2)}, u32[]{:S(2)}) collective-permute-start(bf16[8,48,128]{2,1,0:T(8,128)(2,1)S(1)} %select_convert_fusion.1), channel_id=1, source_target_pairs={{0,2},{1,3},{2,0},{3,1},{4,6},{5,7},{6,4},{7,5},{8,10},{9,11},{10,... | collective-permute-start | bytes 294920 | tf_op jit(solution)/shard_map/ppermute | solution.py:28
  257.3 19.9 %collective-permute-start.64 = (bf16[32,64,128]{2,1,0:T(8,128)(2,1)S(1)}, bf16[32,64,128]{2,1,0:T(8,128)(2,1)S(1)}, u32[]{:S(2)}, u32[]{:S(2)}) collective-permute-start(bf16[32,64,128]{2,1,0:T(8,128)(2,1)S(1)} %pad_maximum_fusion.1.refs_1_), channel_id=1, source_target_pairs={{0,1},{1,0},{2,3},{3,2},{4,5},{5,4},{6,7},{7,6},{8,9},{9,8},{10,11... | collective-permute-start | bytes 1572872 | tf_op jit(solution)/shard_map/ppermute | solution.py:33
  257.3 19.8 %collective-permute-start.63 = (bf16[32,48,128]{2,1,0:T(8,128)(2,1)S(1)}, bf16[32,48,128]{2,1,0:T(8,128)(2,1)S(1)}, u32[]{:S(2)}, u32[]{:S(2)}) collective-permute-start(bf16[32,48,128]{2,1,0:T(8,128)(2,1)S(1)} %pad_maximum_fusion.3.refs_0_), channel_id=1, source_target_pairs={{0,1},{1,0},{2,3},{3,2},{4,5},{5,4},{6,7},{7,6},{8,9},{9,8},{10,11... | collective-permute-start | bytes 1179656 | tf_op jit(solution)/shard_map/ppermute | solution.py:33
  263.5 13.7 %collective-permute-start.65 = (bf16[32,48,128]{2,1,0:T(8,128)(2,1)S(1)}, bf16[32,48,128]{2,1,0:T(8,128)(2,1)S(1)}, u32[]{:S(2)}, u32[]{:S(2)}) collective-permute-start(bf16[32,48,128]{2,1,0:T(8,128)(2,1)S(1)} %pad_maximum_fusion.5.refs_2_), channel_id=1, source_target_pairs={{0,1},{1,0},{2,3},{3,2},{4,5},{5,4},{6,7},{7,6},{8,9},{9,8},{10,11... | collective-permute-start | bytes 1179656 | tf_op jit(solution)/shard_map/ppermute | solution.py:33
  (6 other events, 14.9 us)

commit v7 on v5

--- a/solution.py
+++ b/solution.py
@@ -54,19 +54,48 @@
 
 def cut_columns(weight, starts, width):
     count = starts.shape[0]
+    shape = (weight.shape[0], width)
 
     def kernel(starts_ref, weight_ref, *outs):
-        for k, out in enumerate(outs):
-            out[...] = weight_ref[:, pl.ds(pl.multiple_of(starts_ref[k], BLK), width)]
-
-    return pl.pallas_call(
-        kernel,
-        out_shape=[jax.ShapeDtypeStruct((weight.shape[0], width), weight.dtype)] * count,
+        for i, out in enumerate(outs):
+            out[...] = weight_ref[:, pl.ds(pl.multiple_of(starts_ref[i], BLK), width)]
+
+    return pl.pallas_call(
+        kernel,
+        out_shape=[jax.ShapeDtypeStruct(shape, weight.dtype)] * count,
         in_specs=[SMEM, VMEM],
         out_specs=[VMEM] * count,
-        compiler_params=grant((weight.shape, BF16), (weight.shape, BF16)),
+        compiler_params=grant((weight.shape, BF16), ((count, *shape), BF16)),
         name="cut_columns",
     )(starts, weight)
+
+
+def expand_blocks(pairs, core):
+    docs = pairs[0][0].shape[0]
+    half = pairs[0][1].shape[1] // CORES
+    size = half // BLK
+
+    def kernel(core_ref, *refs):
+        lefts, rights = refs[: len(pairs)], refs[len(pairs) : 2 * len(pairs)]
+        for side, out in enumerate(refs[2 * len(pairs) :]):
+            which = core_ref[0] if side == 0 else 1 - core_ref[0]
+            columns = pl.ds(pl.multiple_of(which * half, BLK), half)
+            total = sum(
+                jnp.dot(left[...], right[:, columns], preferred_element_type=F32)
+                for left, right in zip(lefts, rights)
+            )
+            for j in range(size):
+                out[j] = total[:, j * BLK : (j + 1) * BLK]
+
+    lefts, rights = [left for left, _ in pairs], [right for _, right in pairs]
+    return pl.pallas_call(
+        kernel,
+        out_shape=[jax.ShapeDtypeStruct((size, docs, BLK), F32)] * CORES,
+        in_specs=[SMEM] + [VMEM] * (2 * len(pairs)),
+        out_specs=[VMEM] * CORES,
+        compiler_params=grant(*blocks_of(lefts + rights), ((4 * size, docs, BLK), F32)),
+        name="expand_blocks",
+    )(core.reshape(1), *lefts, *rights)
 
 
 def fetch(array):
@@ -359,24 +388,24 @@
     edges = [docs * sum(CHUNK_TENTHS[:i]) // 10 for i in range(len(CHUNK_TENTHS) + 1)]
     cuts = [slice(start, end) for start, end in zip(edges[:-1], edges[1:])]
 
+    pairs = range(2, ring, 2)
     ring_width = width // ring
-    starts = (jnp.arange(ring, dtype=jnp.int32) ^ ring_index) * ring_width
-
-    def product(left, right):
-        right = right.reshape(right.shape[0], ring_width // BLK, BLK)
-        return jnp.einsum("dk,kbc->bdc", left, right, preferred_element_type=F32)
-
-    columns = cut_columns(expand_weight, starts, ring_width)
-    arrived = [columns[0]] + [None] * (ring - 1)
-    for k in range(ring - 1, 0, -1):
-        arrived[k] = ring_exchange(columns[k], k)
-    documents_late, _ = lax.optimization_barrier((documents, columns[0]))
-    expanded = product(documents, columns[0])
-    for k in range(1, ring):
-        other = ring_exchange(documents_late, k)
-        expanded = expanded + product(other, arrived[k])
-    kept = lax.dynamic_slice_in_dim(expanded, core * own_blocks, own_blocks, 0)
-    given = lax.dynamic_slice_in_dim(expanded, (1 - core) * own_blocks, own_blocks, 0)
+
+    places = [ring_index, ring_index ^ 1]
+    places += [ring_index ^ k ^ 1 for k in pairs] + [ring_index ^ k for k in pairs]
+    pieces = cut_columns(expand_weight, jnp.stack(places) * ring_width, ring_width)
+    own, near = pieces[:2]
+    lent = dict(zip(pairs, pieces[2:]))
+    late = dict(zip(pairs, pieces[2 + len(pairs) :]))
+    documents_late, _ = lax.optimization_barrier((documents, own))
+    lent = {k: ring_exchange(lent[k], 1) for k in pairs}
+    beside = ring_exchange(documents_late, 1)
+    near = ring_exchange(near, 1)
+    sums = {}
+    for k in pairs:
+        kept, given = expand_blocks([(documents, late[k]), (beside, lent[k])], core)
+        sums[k] = kept + swap_cores(given)
+    kept, given = expand_blocks([(documents, own), (beside, near)], core)
 
     block_weight = fetch(sparse_weight)
     send, position, order = list_tables(
@@ -387,11 +416,16 @@
     given, send, position, order, known, first_label = lax.optimization_barrier(
         (given, send, position, order, known, first_label)
     )
-    hidden = jnp.maximum(kept + swap_cores(given), 0.0).astype(BF16)
+    expanded = kept + swap_cores(given)
 
     picked, residuals, gradients = [], [], []
     for i, cut in enumerate(cuts):
-        pool = jnp.concatenate(ring_gather(hidden[:, cut]), axis=0)
+        whole = expanded[:, cut]
+        far = sum(ring_exchange(sums[k][:, cut], k) for k in pairs)
+        if i:
+            whole, far, _ = lax.optimization_barrier((whole, far, hidden))
+        hidden = jnp.maximum(whole + far, 0.0).astype(BF16)
+        pool = jnp.concatenate(ring_gather(hidden), axis=0)
         pools = [pool, swap_cores(pool)]
         outgoing = select_blocks(pools, send, cap)
         parts = [outgoing[0]] + [None] * (feat_count - 1)
@@ -413,7 +447,7 @@
             total = total + ring_exchange(pieces[k], k).astype(F32)
         if i:
             total, _ = lax.optimization_barrier((total, gradient))
-        gradient = jnp.where(hidden[:, cut] > 0, total, 0.0).astype(BF16)
+        gradient = jnp.where(hidden > 0, total, 0.0).astype(BF16)
         gathered = jnp.concatenate(ring_gather(gradient), axis=0)
         gradients.append((gathered, swap_cores(gathered)))
 

time: 271 us -> 281 us (1.037)
  waiting for transfers between devices: 125 us -> 133 us
  local copies, waits for them, and re-layouts: 3.1 us -> 8.2 us
  matrix products: 3.37 us -> 0 us
    ppermute x18, waiting for transfers between devices: 34.9 us -> 41.2 us  [feat_exchange(): lax.ppermute(x, 'feat', [(i, i ^ flip) for i in range(lax.axis_size('feat...]
    ppermute x33, waiting for transfers between devices: 86.9 us -> 91.7 us  [ring_exchange(): lax.ppermute(x, 'label', [(i, i ^ flip * CORES) for i in range(count)])]
    dot_general x4 -> x0, matrix products: 3.37 us -> none  [product(): return jnp.einsum('dk,kbc->bdc', left, right, preferred_element_type=F32)]
    ppermute x33, starting transfers between devices: 52.4 us -> 49.2 us  [ring_exchange(): lax.ppermute(x, 'label', [(i, i ^ flip * CORES) for i in range(count)])]
    ppermute x18, starting transfers between devices: 22.2 us -> 25.3 us  [feat_exchange(): lax.ppermute(x, 'feat', [(i, i ^ flip) for i in range(lax.axis_size('feat...]
    ppermute x10 -> x11, waiting for transfers between devices: 3 us -> 0.03 us  [swap_cores(): return lax.ppermute(x, 'label', [(i, i ^ 1) for i in range(count)])]
  transfers between devices with their start and end apart: 61 -> 62, of which waited for: 24 -> 21; matrix products, arithmetic and copies ran while one was open for 3% -> 3% of each run, Pallas kernels for 20% -> 20%
where the time goes in v7:
time: 281 us; the launch traced here: 280 us
  waiting for transfers between devices  133 us (47%)
  starting transfers between devices  76.2 us (27%)
  Pallas kernels  58.9 us (21%)
  local copies, waits for them, and re-layouts  8.2 us (3%)
  other arithmetic  2.87 us (1%)
    ppermute x33, waiting for transfers between devices, ring_exchange(): lax.ppermute(x, 'label', [(i, i ^ flip * CORES) for i in range(count)])  91.7 us
    ppermute x33, starting transfers between devices, ring_exchange(): lax.ppermute(x, 'label', [(i, i ^ flip * CORES) for i in range(count)])  49.2 us
    ppermute x18, waiting for transfers between devices, feat_exchange(): lax.ppermute(x, 'feat', [(i, i ^ flip) for i in range(lax.axis_size('feat...  41.2 us
    pallas_call x3, Pallas kernels, residual_and_back(): pl.pallas_call(kernel, out_shape=[jax.ShapeDtypeStruct((label_blocks, doc...  28.7 us
    ppermute x18, starting transfers between devices, feat_exchange(): lax.ppermute(x, 'feat', [(i, i ^ flip) for i in range(lax.axis_size('feat...  25.3 us
    pallas_call x4, Pallas kernels, block_weight_grad(): pl.pallas_call(kernel, out_shape=jax.ShapeDtypeStruct((label_blocks * slo...  13.4 us
  transfers between devices with their start and end apart: 62, of which 21 were waited for; matrix products, arithmetic and copies ran while one was open for 3% of the time, Pallas kernels for 20%

profile of v7, /device:TPU:0, one launch (start us, length us, event | category | flops | bytes accessed | tf_op | source)
XLA Modules:
  0.0 280.3 jit_solution(16443685838370653142)
XLA Ops:
  0.7 1.6 copy-done
  3.0 3.1 %collective-permute-start = (bf16[160,128]{1,0:T(8,128)(2,1)}, bf16[160,128]{1,0:T(8,128)(2,1)S(1)}, u32[]{:S(2)}, u32[]{:S(2)}) collective-permute-start(bf16[160,128]{1,0:T(8,128)(2,1)} %documents_ref.1), channel_id=1, source_target_pairs={{0,2},{1,3},{2,0},{3,1},{4,6},{5,7},{6,4},{7,5},{8,10},{9,11},{10,... | collective-permute-start | bytes 122888 | tf_op jit(solution)/shard_map/ppermute | solution.py:27
  6.2 1.9 collective-permute-start.3
  8.2 1.7 copy.17
  14.2 16.6 %collective-permute-done.3.refs_3_ = bf16[128,2048]{1,0:T(8,128)(2,1)S(1)} collective-permute-done((bf16[128,2048]{1,0:T(8,128)(2,1)S(1)}, bf16[128,2048]{1,0:T(8,128)(2,1)S(1)}, u32[]{:S(2)}, u32[]{:S(2)}) %collective-permute-start.3) | collective-permute-done | bytes 524320 | tf_op jit(solution)/shard_map/ppermute | solution.py:27
  34.5 3.0 %collective-permute-start.5 = (f32[8,48,128]{2,1,0:T(8,128)S(1)}, f32[8,48,128]{2,1,0:T(8,128)S(1)}, u32[]{:S(2)}, u32[]{:S(2)}) collective-permute-start(f32[8,48,128]{2,1,0:T(8,128)S(1)} %get-tuple-element.115), channel_id=1, source_target_pairs={{0,4},{1,5},{2,6},{3,7},{4,0},{5,1},{6,2},{7,3},{8,12},{9,13},{10,... | collective-permute-start | bytes 589832 | tf_op jit(solution)/shard_map/ppermute | solution.py:27
  37.6 2.9 %collective-permute-start.41 = (f32[8,48,128]{2,1,0:T(8,128)S(1)}, f32[8,48,128]{2,1,0:T(8,128)S(1)}, u32[]{:S(2)}, u32[]{:S(2)}) collective-permute-start(f32[8,48,128]{2,1,0:T(8,128)S(1)} %get-tuple-element.114), channel_id=1, source_target_pairs={{0,4},{1,5},{2,6},{3,7},{4,0},{5,1},{6,2},{7,3},{8,12},{9,13},{10,... | collective-permute-start | bytes 589832 | tf_op jit(solution)/shard_map/ppermute | solution.py:27
  40.6 16.5 %collective-permute-done.5 = f32[8,48,128]{2,1,0:T(8,128)S(1)} collective-permute-done((f32[8,48,128]{2,1,0:T(8,128)S(1)}, f32[8,48,128]{2,1,0:T(8,128)S(1)}, u32[]{:S(2)}, u32[]{:S(2)}) %collective-permute-start.5) | collective-permute-done | bytes 196640 | tf_op jit(solution)/shard_map/ppermute | solution.py:27
  57.2 3.2 %collective-permute-start.8 = (bf16[8,48,128]{2,1,0:T(8,128)(2,1)S(1)}, bf16[8,48,128]{2,1,0:T(8,128)(2,1)S(1)}, u32[]{:S(2)}, u32[]{:S(2)}) collective-permute-start(bf16[8,48,128]{2,1,0:T(8,128)(2,1)S(1)} %get-tuple-element.117), channel_id=1, source_target_pairs={{0,6},{1,7},{2,4},{3,5},{4,2},{5,3},{6,0},{7,1},{8,14},{9,15},{10,... | collective-permute-start | bytes 294920 | tf_op jit(solution)/shard_map/ppermute | solution.py:27
  60.4 1.3 collective-permute-start.6
  61.7 5.3 %collective-permute-done.23 = f32[8,64,128]{2,1,0:T(8,128)S(1)} collective-permute-done((f32[8,64,128]{2,1,0:T(8,128)S(1)}, f32[8,64,128]{2,1,0:T(8,128)S(1)}, u32[]{:S(2)}, u32[]{:S(2)}) %collective-permute-start.23) | collective-permute-done | bytes 262176 | tf_op jit(solution)/shard_map/ppermute | solution.py:27
  67.0 4.2 %collective-permute-done.41 = f32[8,48,128]{2,1,0:T(8,128)S(1)} collective-permute-done((f32[8,48,128]{2,1,0:T(8,128)S(1)}, f32[8,48,128]{2,1,0:T(8,128)S(1)}, u32[]{:S(2)}, u32[]{:S(2)}) %collective-permute-start.41) | collective-permute-done | bytes 196640 | tf_op jit(solution)/shard_map/ppermute | solution.py:27
  71.2 3.7 %collective-permute-done.7 = bf16[8,48,128]{2,1,0:T(8,128)(2,1)S(1)} collective-permute-done((bf16[8,48,128]{2,1,0:T(8,128)(2,1)S(1)}, bf16[8,48,128]{2,1,0:T(8,128)(2,1)S(1)}, u32[]{:S(2)}, u32[]{:S(2)}) %collective-permute-start.7) | collective-permute-done | bytes 98336 | tf_op jit(solution)/shard_map/ppermute | solution.py:27
  75.1 3.1 %collective-permute-start.44 = (bf16[8,48,128]{2,1,0:T(8,128)(2,1)S(1)}, bf16[8,48,128]{2,1,0:T(8,128)(2,1)S(1)}, u32[]{:S(2)}, u32[]{:S(2)}) collective-permute-start(bf16[8,48,128]{2,1,0:T(8,128)(2,1)S(1)} %maximum_convert_fusion.1), channel_id=1, source_target_pairs={{0,6},{1,7},{2,4},{3,5},{4,2},{5,3},{6,0},{7,1},{8,14},{9,15},{10,... | collective-permute-start | bytes 294920 | tf_op jit(solution)/shard_map/ppermute | solution.py:27
  78.2 1.4 collective-permute-start.42
  79.5 3.0 %collective-permute-start.26 = (bf16[8,64,128]{2,1,0:T(8,128)(2,1)S(1)}, bf16[8,64,128]{2,1,0:T(8,128)(2,1)S(1)}, u32[]{:S(2)}, u32[]{:S(2)}) collective-permute-start(bf16[8,64,128]{2,1,0:T(8,128)(2,1)S(1)} %maximum_convert_fusion), channel_id=1, source_target_pairs={{0,6},{1,7},{2,4},{3,5},{4,2},{5,3},{6,0},{7,1},{8,14},{9,15},{10,... | collective-permute-start | bytes 393224 | tf_op jit(solution)/shard_map/ppermute | solution.py:27
  82.7 4.2 %collective-permute-done.43 = bf16[8,48,128]{2,1,0:T(8,128)(2,1)S(1)} collective-permute-done((bf16[8,48,128]{2,1,0:T(8,128)(2,1)S(1)}, bf16[8,48,128]{2,1,0:T(8,128)(2,1)S(1)}, u32[]{:S(2)}, u32[]{:S(2)}) %collective-permute-start.43) | collective-permute-done | bytes 98336 | tf_op jit(solution)/shard_map/ppermute | solution.py:27
  87.1 1.5 select_blocks.3
  88.6 1.6 collective-permute-start.10
  90.2 1.5 collective-permute-start.11
  91.7 5.9 %collective-permute-done.25 = bf16[8,64,128]{2,1,0:T(8,128)(2,1)S(1)} collective-permute-done((bf16[8,64,128]{2,1,0:T(8,128)(2,1)S(1)}, bf16[8,64,128]{2,1,0:T(8,128)(2,1)S(1)}, u32[]{:S(2)}, u32[]{:S(2)}) %collective-permute-start.25) | collective-permute-done | bytes 131104 | tf_op jit(solution)/shard_map/ppermute | solution.py:27
  97.6 2.5 collective-permute-start.12
  100.2 4.6 %fetch.1.weight_ref = bf16[24,16,128,128]{3,2,1,0:T(8,128)(2,1)S(1)} custom-call(bf16[24,16,128,128]{3,2,1,0:T(8,128)(2,1)} %source.1), custom_call_target="tpu_custom_call" | custom-call | tf_op jit(solution)/shard_map/fetch/pallas_call | solution.py:107
  104.9 1.4 select_blocks.5
  107.5 9.2 %residual_and_back.3 = (bf16[24,48,128]{2,1,0:T(8,128)(2,1)S(1)}, bf16[24,48,128]{2,1,0:T(8,128)(2,1)S(1)}, bf16[24,48,128]{2,1,0:T(8,128)(2,1)S(1)}, bf16[24,48...) custom-call(s32[384]{0:T(512)S(1)} %select_reduce_fusion.1.position_ref, s32[384]{0:T(512)S(1)} %select_reduce_fusion.order_ref, ...), custom_call_target="tpu_custom_call" | custom-call | tf_op jit(solution)/shard_map/residual_and_back/pallas_call | solution.py:227
  116.7 1.6 collective-permute-start.13
  118.3 1.5 collective-permute-start.14
  120.3 1.5 select_blocks.4
  121.7 1.6 collective-permute-start.28
  123.3 1.5 collective-permute-start.29
  124.9 1.8 collective-permute-done.13.refs_1_
  126.7 1.6 collective-permute-start.47
  128.2 6.3 %collective-permute-done.14.refs_2_ = bf16[24,48,128]{2,1,0:T(8,128)(2,1)S(1)} collective-permute-done((bf16[24,48,128]{2,1,0:T(8,128)(2,1)S(1)}, bf16[24,48,128]{2,1,0:T(8,128)(2,1)S(1)}, u32[]{:S(2)}, u32[]{:S(2)}) %collective-permute-start.14) | collective-permute-done | bytes 294944 | tf_op jit(solution)/shard_map/ppermute | solution.py:36
  134.5 1.5 collective-permute-start.48
  136.0 1.4 collective-permute-start.30
  138.6 23.7 %collective-permute-done.47.refs_2_.refs_5_ = bf16[24,48,128]{2,1,0:T(8,128)(2,1)S(1)} collective-permute-done((bf16[24,48,128]{2,1,0:T(8,128)(2,1)S(1)}, bf16[24,48,128]{2,1,0:T(8,128)(2,1)S(1)}, u32[]{:S(2)}, u32[]{:S(2)}) %collective-permute-start.47) | collective-permute-done | bytes 294944 | tf_op jit(solution)/shard_map/ppermute | solution.py:36
  162.3 9.3 %residual_and_back.5 = (bf16[24,48,128]{2,1,0:T(8,128)(2,1)S(1)}, bf16[24,48,128]{2,1,0:T(8,128)(2,1)S(1)}, bf16[24,48,128]{2,1,0:T(8,128)(2,1)S(1)}, bf16[24,48...) custom-call(s32[384]{0:T(512)S(1)} %select_reduce_fusion.1.position_ref, s32[384]{0:T(512)S(1)} %select_reduce_fusion.order_ref, ...), custom_call_target="tpu_custom_call" | custom-call | tf_op jit(solution)/shard_map/residual_and_back/pallas_call | solution.py:227
  173.4 1.8 collective-permute-start.51
  175.1 10.2 %residual_and_back.4 = (bf16[24,64,128]{2,1,0:T(8,128)(2,1)S(1)}, bf16[24,64,128]{2,1,0:T(8,128)(2,1)S(1)}, bf16[24,64,128]{2,1,0:T(8,128)(2,1)S(1)}, bf16[24,64...) custom-call(s32[384]{0:T(512)S(1)} %select_reduce_fusion.1.position_ref, s32[384]{0:T(512)S(1)} %select_reduce_fusion.order_ref, ...), custom_call_target="tpu_custom_call" | custom-call | tf_op jit(solution)/shard_map/residual_and_back/pallas_call | solution.py:227
  186.0 1.2 collective-permute-start.32
  187.2 2.6 collective-permute-start.33
  191.2 2.1 collective-permute-start.17
  193.2 4.2 %collective-permute-done.31.refs_1_ = bf16[24,64,128]{2,1,0:T(8,128)(2,1)S(1)} collective-permute-done((bf16[24,64,128]{2,1,0:T(8,128)(2,1)S(1)}, bf16[24,64,128]{2,1,0:T(8,128)(2,1)S(1)}, u32[]{:S(2)}, u32[]{:S(2)}) %collective-permute-start.31) | collective-permute-done | bytes 393248 | tf_op jit(solution)/shard_map/ppermute | solution.py:36
  197.4 2.8 collective-permute-start.19
  200.7 4.5 %collective-permute-done.33.refs_3_ = bf16[24,64,128]{2,1,0:T(8,128)(2,1)S(1)} collective-permute-done((bf16[24,64,128]{2,1,0:T(8,128)(2,1)S(1)}, bf16[24,64,128]{2,1,0:T(8,128)(2,1)S(1)}, u32[]{:S(2)}, u32[]{:S(2)}) %collective-permute-start.33) | collective-permute-done | bytes 393248 | tf_op jit(solution)/shard_map/ppermute | solution.py:36
  205.2 1.3 add_blocks.4
  206.7 3.9 %collective-permute-start.53 = (bf16[8,48,128]{2,1,0:T(8,128)(2,1)S(1)}, bf16[8,48,128]{2,1,0:T(8,128)(2,1)S(1)}, u32[]{:S(2)}, u32[]{:S(2)}) collective-permute-start(bf16[8,48,128]{2,1,0:T(8,128)(2,1)S(1)} %get-tuple-element.121), channel_id=1, source_target_pairs={{0,6},{1,7},{2,4},{3,5},{4,2},{5,3},{6,0},{7,1},{8,14},{9,15},{10,... | collective-permute-start | bytes 294920 | tf_op jit(solution)/shard_map/ppermute | solution.py:27
  211.5 3.7 %collective-permute-start.22 = (bf16[8,48,128]{2,1,0:T(8,128)(2,1)S(1)}, bf16[8,48,128]{2,1,0:T(8,128)(2,1)S(1)}, u32[]{:S(2)}, u32[]{:S(2)}) collective-permute-start(bf16[8,48,128]{2,1,0:T(8,128)(2,1)S(1)} %select_convert_fusion.2), channel_id=1, source_target_pairs={{0,6},{1,7},{2,4},{3,5},{4,2},{5,3},{6,0},{7,1},{8,14},{9,15},{10,... | collective-permute-start | bytes 294920 | tf_op jit(solution)/shard_map/ppermute | solution.py:27
  215.4 2.7 collective-permute-start.35
  218.9 8.5 %collective-permute-done.54 = bf16[8,48,128]{2,1,0:T(8,128)(2,1)S(1)} collective-permute-done((bf16[8,48,128]{2,1,0:T(8,128)(2,1)S(1)}, bf16[8,48,128]{2,1,0:T(8,128)(2,1)S(1)}, u32[]{:S(2)}, u32[]{:S(2)}) %collective-permute-start.54) | collective-permute-done | bytes 98336 | tf_op jit(solution)/shard_map/ppermute | solution.py:27
  228.1 12.0 %collective-permute-done.36 = bf16[8,64,128]{2,1,0:T(8,128)(2,1)S(1)} collective-permute-done((bf16[8,64,128]{2,1,0:T(8,128)(2,1)S(1)}, bf16[8,64,128]{2,1,0:T(8,128)(2,1)S(1)}, u32[]{:S(2)}, u32[]{:S(2)}) %collective-permute-start.36) | collective-permute-done | bytes 131104 | tf_op jit(solution)/shard_map/ppermute | solution.py:27
  240.2 2.1 collective-permute-start.40
  242.3 2.3 collective-permute-start.38
  244.7 3.9 %collective-permute-done.40 = bf16[8,64,128]{2,1,0:T(8,128)(2,1)S(1)} collective-permute-done((bf16[8,64,128]{2,1,0:T(8,128)(2,1)S(1)}, bf16[8,64,128]{2,1,0:T(8,128)(2,1)S(1)}, u32[]{:S(2)}, u32[]{:S(2)}) %collective-permute-start.40) | collective-permute-done | bytes 131104 | tf_op jit(solution)/shard_map/ppermute | solution.py:27
  248.6 4.7 %collective-permute-done.39 = bf16[8,64,128]{2,1,0:T(8,128)(2,1)S(1)} collective-permute-done((bf16[8,64,128]{2,1,0:T(8,128)(2,1)S(1)}, bf16[8,64,128]{2,1,0:T(8,128)(2,1)S(1)}, u32[]{:S(2)}, u32[]{:S(2)}) %collective-permute-start.39) | collective-permute-done | bytes 131104 | tf_op jit(solution)/shard_map/ppermute | solution.py:27
  253.3 1.5 collective-permute-start.58
  254.9 3.0 %collective-permute-start.56 = (bf16[8,48,128]{2,1,0:T(8,128)(2,1)S(1)}, bf16[8,48,128]{2,1,0:T(8,128)(2,1)S(1)}, u32[]{:S(2)}, u32[]{:S(2)}) collective-permute-start(bf16[8,48,128]{2,1,0:T(8,128)(2,1)S(1)} %select_convert_fusion.1), channel_id=1, source_target_pairs={{0,2},{1,3},{2,0},{3,1},{4,6},{5,7},{6,4},{7,5},{8,10},{9,11},{10,... | collective-permute-start | bytes 294920 | tf_op jit(solution)/shard_map/ppermute | solution.py:27
  258.4 2.4 collective-permute-done.58
  260.8 3.1 %collective-permute-done.57 = bf16[8,48,128]{2,1,0:T(8,128)(2,1)S(1)} collective-permute-done((bf16[8,48,128]{2,1,0:T(8,128)(2,1)S(1)}, bf16[8,48,128]{2,1,0:T(8,128)(2,1)S(1)}, u32[]{:S(2)}, u32[]{:S(2)}) %collective-permute-start.57) | collective-permute-done | bytes 98336 | tf_op jit(solution)/shard_map/ppermute | solution.py:27
  264.2 3.3 %block_weight_grad.4.refs_6_ = bf16[384,128,128]{2,1,0:T(8,128)(2,1)} custom-call(s32[96]{0:T(128)S(1)} %get-tuple-element.129.order_ref, bf16[24,48,128]{2,1,0:T(8,128)(2,1)S(1)} %get-tuple-element.111.refs_0_, bf16[24,64,128]{2,1,0:T(8,128)(2,1)S(1)} %get-tuple-element.112.refs_1_, bf16[24,48,128]{2,1,0:T(8,128)(2,1)S(1)} %get-tuple-element.113.refs_2_, ...), custom_call_target="tpu_custom_call" | custom-call | tf_op jit(solution)/shard_map/block_weight_grad/pallas_call | solution.py:279
  267.5 3.4 %block_weight_grad.5.refs_6_ = bf16[384,128,128]{2,1,0:T(8,128)(2,1)} custom-call(s32[96]{0:T(128)S(1)} %get-tuple-element.130.order_ref, bf16[24,48,128]{2,1,0:T(8,128)(2,1)S(1)} %get-tuple-element.111.refs_0_, bf16[24,64,128]{2,1,0:T(8,128)(2,1)S(1)} %get-tuple-element.112.refs_1_, ...), custom_call_target="tpu_custom_call", output_to_operand_aliasing={{}: (7, {})} | custom-call | tf_op jit(solution)/shard_map/block_weight_grad/pallas_call | solution.py:279
  270.9 3.4 %block_weight_grad.6.refs_6_ = bf16[384,128,128]{2,1,0:T(8,128)(2,1)} custom-call(s32[96]{0:T(128)S(1)} %get-tuple-element.131.order_ref, bf16[24,48,128]{2,1,0:T(8,128)(2,1)S(1)} %get-tuple-element.111.refs_0_, bf16[24,64,128]{2,1,0:T(8,128)(2,1)S(1)} %get-tuple-element.112.refs_1_, ...), custom_call_target="tpu_custom_call", output_to_operand_aliasing={{}: (7, {})} | custom-call | tf_op jit(solution)/shard_map/block_weight_grad/pallas_call | solution.py:279
  274.3 3.4 %block_weight_grad.7 = bf16[384,128,128]{2,1,0:T(8,128)(2,1)} custom-call(s32[96]{0:T(128)S(1)} %get-tuple-element.132.order_ref, bf16[24,48,128]{2,1,0:T(8,128)(2,1)S(1)} %get-tuple-element.111.refs_0_, bf16[24,64,128]{2,1,0:T(8,128)(2,1)S(1)} %get-tuple-element.112.refs_1_, ...), custom_call_target="tpu_custom_call", output_to_operand_aliasing={{}: (7, {})} | custom-call | tf_op jit(solution)/shard_map/block_weight_grad/pallas_call | solution.py:279
  277.7 2.6 expand_weight_grad.1
  (141 shorter events, 20.5 us)
Async XLA Ops:
  0.7 1.6 copy-start
  3.0 11.2 %collective-permute-start = (bf16[160,128]{1,0:T(8,128)(2,1)}, bf16[160,128]{1,0:T(8,128)(2,1)S(1)}, u32[]{:S(2)}, u32[]{:S(2)}) collective-permute-start(bf16[160,128]{1,0:T(8,128)(2,1)} %documents_ref.1), channel_id=1, source_target_pairs={{0,2},{1,3},{2,0},{3,1},{4,6},{5,7},{6,4},{7,5},{8,10},{9,11},{10,... | collective-permute-start | bytes 122888 | tf_op jit(solution)/shard_map/ppermute | solution.py:27
  6.1 26.4 %collective-permute-start.1 = (bf16[128,2048]{1,0:T(8,128)(2,1)S(1)}, bf16[128,2048]{1,0:T(8,128)(2,1)S(1)}, u32[]{:S(2)}, u32[]{:S(2)}) collective-permute-start(bf16[128,2048]{1,0:T(8,128)(2,1)S(1)} %get-tuple-element.60), channel_id=1, source_target_pairs={{0,2},{1,3},{2,0},{3,1},{4,6},{5,7},{6,4},{7,5},{8,10},{9,11},{10,... | collective-permute-start | bytes 1572872 | tf_op jit(solution)/shard_map/ppermute | solution.py:27
  6.2 24.6 %collective-permute-start.3 = (bf16[128,2048]{1,0:T(8,128)(2,1)S(1)}, bf16[128,2048]{1,0:T(8,128)(2,1)S(1)}, u32[]{:S(2)}, u32[]{:S(2)}) collective-permute-start(bf16[128,2048]{1,0:T(8,128)(2,1)S(1)} %get-tuple-element.65), channel_id=1, source_target_pairs={{0,2},{1,3},{2,0},{3,1},{4,6},{5,7},{6,4},{7,5},{8,10},{9,11},{10,... | collective-permute-start | bytes 1572872 | tf_op jit(solution)/shard_map/ppermute | solution.py:27
  32.1 2.3 collective-permute-start.4
  33.8 6.7 %collective-permute-start.2 = (f32[8,160,128]{2,1,0:T(8,128)S(1)}, f32[8,160,128]{2,1,0:T(8,128)S(1)}, u32[]{:S(2)}, u32[]{:S(2)}) collective-permute-start(f32[8,160,128]{2,1,0:T(8,128)S(1)} %get-tuple-element.63), channel_id=1, source_target_pairs={{0,1},{1,0},{2,3},{3,2},{4,5},{5,4},{6,7},{7,6},{8,9},{9,8},{10,11... | collective-permute-start | bytes 1966088 | tf_op jit(solution)/shard_map/ppermute | solution.py:32
  34.5 22.7 %collective-permute-start.5 = (f32[8,48,128]{2,1,0:T(8,128)S(1)}, f32[8,48,128]{2,1,0:T(8,128)S(1)}, u32[]{:S(2)}, u32[]{:S(2)}) collective-permute-start(f32[8,48,128]{2,1,0:T(8,128)S(1)} %get-tuple-element.115), channel_id=1, source_target_pairs={{0,4},{1,5},{2,6},{3,7},{4,0},{5,1},{6,2},{7,3},{8,12},{9,13},{10,... | collective-permute-start | bytes 589832 | tf_op jit(solution)/shard_map/ppermute | solution.py:27
  37.5 29.5 %collective-permute-start.23 = (f32[8,64,128]{2,1,0:T(8,128)S(1)}, f32[8,64,128]{2,1,0:T(8,128)S(1)}, u32[]{:S(2)}, u32[]{:S(2)}) collective-permute-start(f32[8,64,128]{2,1,0:T(8,128)S(1)} %slice.107), channel_id=1, source_target_pairs={{0,4},{1,5},{2,6},{3,7},{4,0},{5,1},{6,2},{7,3},{8,12},{9,13},{10,... | collective-permute-start | bytes 786440 | tf_op jit(solution)/shard_map/ppermute | solution.py:27
  37.6 33.6 %collective-permute-start.41 = (f32[8,48,128]{2,1,0:T(8,128)S(1)}, f32[8,48,128]{2,1,0:T(8,128)S(1)}, u32[]{:S(2)}, u32[]{:S(2)}) collective-permute-start(f32[8,48,128]{2,1,0:T(8,128)S(1)} %get-tuple-element.114), channel_id=1, source_target_pairs={{0,4},{1,5},{2,6},{3,7},{4,0},{5,1},{6,2},{7,3},{8,12},{9,13},{10,... | collective-permute-start | bytes 589832 | tf_op jit(solution)/shard_map/ppermute | solution.py:27
  57.2 14.0 %collective-permute-start.8 = (bf16[8,48,128]{2,1,0:T(8,128)(2,1)S(1)}, bf16[8,48,128]{2,1,0:T(8,128)(2,1)S(1)}, u32[]{:S(2)}, u32[]{:S(2)}) collective-permute-start(bf16[8,48,128]{2,1,0:T(8,128)(2,1)S(1)} %get-tuple-element.117), channel_id=1, source_target_pairs={{0,6},{1,7},{2,4},{3,5},{4,2},{5,3},{6,0},{7,1},{8,14},{9,15},{10,... | collective-permute-start | bytes 294920 | tf_op jit(solution)/shard_map/ppermute | solution.py:27
  60.4 14.5 %collective-permute-start.7 = (bf16[8,48,128]{2,1,0:T(8,128)(2,1)S(1)}, bf16[8,48,128]{2,1,0:T(8,128)(2,1)S(1)}, u32[]{:S(2)}, u32[]{:S(2)}) collective-permute-start(bf16[8,48,128]{2,1,0:T(8,128)(2,1)S(1)} %get-tuple-element.117), channel_id=1, source_target_pairs={{0,4},{1,5},{2,6},{3,7},{4,0},{5,1},{6,2},{7,3},{8,12},{9,13},{10,... | collective-permute-start | bytes 294920 | tf_op jit(solution)/shard_map/ppermute | solution.py:27
  60.4 14.5 %collective-permute-start.6 = (bf16[8,48,128]{2,1,0:T(8,128)(2,1)S(1)}, bf16[8,48,128]{2,1,0:T(8,128)(2,1)S(1)}, u32[]{:S(2)}, u32[]{:S(2)}) collective-permute-start(bf16[8,48,128]{2,1,0:T(8,128)(2,1)S(1)} %get-tuple-element.117), channel_id=1, source_target_pairs={{0,2},{1,3},{2,0},{3,1},{4,6},{5,7},{6,4},{7,5},{8,10},{9,11},{10,... | collective-permute-start | bytes 294920 | tf_op jit(solution)/shard_map/ppermute | solution.py:27
  75.0 12.1 %collective-permute-start.9 = (bf16[32,48,128]{2,1,0:T(8,128)(2,1)S(1)}, bf16[32,48,128]{2,1,0:T(8,128)(2,1)S(1)}, u32[]{:S(2)}, u32[]{:S(2)}) collective-permute-start(bf16[32,48,128]{2,1,0:T(8,128)(2,1)S(1)} %pad_maximum_fusion.2.refs_0_), channel_id=1, source_target_pairs={{0,1},{1,0},{2,3},{3,2},{4,5},{5,4},{6,7},{7,6},{8,9},{9,8},{10,11... | collective-permute-start | bytes 1179656 | tf_op jit(solution)/shard_map/ppermute | solution.py:32
  75.1 7.6 %collective-permute-start.44 = (bf16[8,48,128]{2,1,0:T(8,128)(2,1)S(1)}, bf16[8,48,128]{2,1,0:T(8,128)(2,1)S(1)}, u32[]{:S(2)}, u32[]{:S(2)}) collective-permute-start(bf16[8,48,128]{2,1,0:T(8,128)(2,1)S(1)} %maximum_convert_fusion.1), channel_id=1, source_target_pairs={{0,6},{1,7},{2,4},{3,5},{4,2},{5,3},{6,0},{7,1},{8,14},{9,15},{10,... | collective-permute-start | bytes 294920 | tf_op jit(solution)/shard_map/ppermute | solution.py:27
  78.2 8.7 %collective-permute-start.43 = (bf16[8,48,128]{2,1,0:T(8,128)(2,1)S(1)}, bf16[8,48,128]{2,1,0:T(8,128)(2,1)S(1)}, u32[]{:S(2)}, u32[]{:S(2)}) collective-permute-start(bf16[8,48,128]{2,1,0:T(8,128)(2,1)S(1)} %maximum_convert_fusion.1), channel_id=1, source_target_pairs={{0,4},{1,5},{2,6},{3,7},{4,0},{5,1},{6,2},{7,3},{8,12},{9,13},{10,... | collective-permute-start | bytes 294920 | tf_op jit(solution)/shard_map/ppermute | solution.py:27
  78.2 8.8 %collective-permute-start.42 = (bf16[8,48,128]{2,1,0:T(8,128)(2,1)S(1)}, bf16[8,48,128]{2,1,0:T(8,128)(2,1)S(1)}, u32[]{:S(2)}, u32[]{:S(2)}) collective-permute-start(bf16[8,48,128]{2,1,0:T(8,128)(2,1)S(1)} %maximum_convert_fusion.1), channel_id=1, source_target_pairs={{0,2},{1,3},{2,0},{3,1},{4,6},{5,7},{6,4},{7,5},{8,10},{9,11},{10,... | collective-permute-start | bytes 294920 | tf_op jit(solution)/shard_map/ppermute | solution.py:27
  79.5 10.7 %collective-permute-start.26 = (bf16[8,64,128]{2,1,0:T(8,128)(2,1)S(1)}, bf16[8,64,128]{2,1,0:T(8,128)(2,1)S(1)}, u32[]{:S(2)}, u32[]{:S(2)}) collective-permute-start(bf16[8,64,128]{2,1,0:T(8,128)(2,1)S(1)} %maximum_convert_fusion), channel_id=1, source_target_pairs={{0,6},{1,7},{2,4},{3,5},{4,2},{5,3},{6,0},{7,1},{8,14},{9,15},{10,... | collective-permute-start | bytes 393224 | tf_op jit(solution)/shard_map/ppermute | solution.py:27
  82.7 14.9 %collective-permute-start.25 = (bf16[8,64,128]{2,1,0:T(8,128)(2,1)S(1)}, bf16[8,64,128]{2,1,0:T(8,128)(2,1)S(1)}, u32[]{:S(2)}, u32[]{:S(2)}) collective-permute-start(bf16[8,64,128]{2,1,0:T(8,128)(2,1)S(1)} %maximum_convert_fusion), channel_id=1, source_target_pairs={{0,4},{1,5},{2,6},{3,7},{4,0},{5,1},{6,2},{7,3},{8,12},{9,13},{10,... | collective-permute-start | bytes 393224 | tf_op jit(solution)/shard_map/ppermute | solution.py:27
  86.9 13.2 %collective-permute-start.24 = (bf16[8,64,128]{2,1,0:T(8,128)(2,1)S(1)}, bf16[8,64,128]{2,1,0:T(8,128)(2,1)S(1)}, u32[]{:S(2)}, u32[]{:S(2)}) collective-permute-start(bf16[8,64,128]{2,1,0:T(8,128)(2,1)S(1)} %maximum_convert_fusion), channel_id=1, source_target_pairs={{0,2},{1,3},{2,0},{3,1},{4,6},{5,7},{6,4},{7,5},{8,10},{9,11},{10,... | collective-permute-start | bytes 393224 | tf_op jit(solution)/shard_map/ppermute | solution.py:27
  87.0 17.9 %collective-permute-start.45 = (bf16[32,48,128]{2,1,0:T(8,128)(2,1)S(1)}, bf16[32,48,128]{2,1,0:T(8,128)(2,1)S(1)}, u32[]{:S(2)}, u32[]{:S(2)}) collective-permute-start(bf16[32,48,128]{2,1,0:T(8,128)(2,1)S(1)} %pad_maximum_fusion.4.refs_0_), channel_id=1, source_target_pairs={{0,1},{1,0},{2,3},{3,2},{4,5},{5,4},{6,7},{7,6},{8,9},{9,8},{10,11... | collective-permute-start | bytes 1179656 | tf_op jit(solution)/shard_map/ppermute | solution.py:32
  88.6 18.2 %collective-permute-start.10 = (bf16[24,48,128]{2,1,0:T(8,128)(2,1)S(1)}, bf16[24,48,128]{2,1,0:T(8,128)(2,1)S(1)}, u32[]{:S(2)}, u32[]{:S(2)}) collective-permute-start(bf16[24,48,128]{2,1,0:T(8,128)(2,1)S(1)} %get-tuple-element.74), channel_id=1, source_target_pairs={{0,8},{8,0},{16,24},{24,16},{1,9},{9,1},{17,25},{25,17},{2,10},{10... | collective-permute-start | bytes 884744 | tf_op jit(solution)/shard_map/ppermute | solution.py:36
  90.2 16.6 %collective-permute-start.11 = (bf16[24,48,128]{2,1,0:T(8,128)(2,1)S(1)}, bf16[24,48,128]{2,1,0:T(8,128)(2,1)S(1)}, u32[]{:S(2)}, u32[]{:S(2)}) collective-permute-start(bf16[24,48,128]{2,1,0:T(8,128)(2,1)S(1)} %get-tuple-element.75), channel_id=1, source_target_pairs={{0,16},{8,24},{16,0},{24,8},{1,17},{9,25},{17,1},{25,9},{2,18},{10... | collective-permute-start | bytes 884744 | tf_op jit(solution)/shard_map/ppermute | solution.py:36
  97.6 9.9 %collective-permute-start.12 = (bf16[24,48,128]{2,1,0:T(8,128)(2,1)S(1)}, bf16[24,48,128]{2,1,0:T(8,128)(2,1)S(1)}, u32[]{:S(2)}, u32[]{:S(2)}) collective-permute-start(bf16[24,48,128]{2,1,0:T(8,128)(2,1)S(1)} %get-tuple-element.76), channel_id=1, source_target_pairs={{0,24},{8,16},{16,8},{24,0},{1,25},{9,17},{17,9},{25,1},{2,26},{10... | collective-permute-start | bytes 884744 | tf_op jit(solution)/shard_map/ppermute | solution.py:36
  100.2 20.1 %collective-permute-start.27 = (bf16[32,64,128]{2,1,0:T(8,128)(2,1)S(1)}, bf16[32,64,128]{2,1,0:T(8,128)(2,1)S(1)}, u32[]{:S(2)}, u32[]{:S(2)}) collective-permute-start(bf16[32,64,128]{2,1,0:T(8,128)(2,1)S(1)} %pad_maximum_fusion.refs_0_), channel_id=1, source_target_pairs={{0,1},{1,0},{2,3},{3,2},{4,5},{5,4},{6,7},{7,6},{8,9},{9,8},{10,11... | collective-permute-start | bytes 1572872 | tf_op jit(solution)/shard_map/ppermute | solution.py:32
  106.2 17.1 %collective-permute-start.46 = (bf16[24,48,128]{2,1,0:T(8,128)(2,1)S(1)}, bf16[24,48,128]{2,1,0:T(8,128)(2,1)S(1)}, u32[]{:S(2)}, u32[]{:S(2)}) collective-permute-start(bf16[24,48,128]{2,1,0:T(8,128)(2,1)S(1)} %get-tuple-element.101), channel_id=1, source_target_pairs={{0,8},{8,0},{16,24},{24,16},{1,9},{9,1},{17,25},{25,17},{2,10},{10... | collective-permute-start | bytes 884744 | tf_op jit(solution)/shard_map/ppermute | solution.py:36
  116.7 9.9 %collective-permute-start.13 = (bf16[24,48,128]{2,1,0:T(8,128)(2,1)S(1)}, bf16[24,48,128]{2,1,0:T(8,128)(2,1)S(1)}, u32[]{:S(2)}, u32[]{:S(2)}) collective-permute-start(bf16[24,48,128]{2,1,0:T(8,128)(2,1)S(1)} %get-tuple-element.78), channel_id=1, source_target_pairs={{0,8},{8,0},{16,24},{24,16},{1,9},{9,1},{17,25},{25,17},{2,10},{10... | collective-permute-start | bytes 884744 | tf_op jit(solution)/shard_map/ppermute | solution.py:36
  118.3 16.2 %collective-permute-start.14 = (bf16[24,48,128]{2,1,0:T(8,128)(2,1)S(1)}, bf16[24,48,128]{2,1,0:T(8,128)(2,1)S(1)}, u32[]{:S(2)}, u32[]{:S(2)}) collective-permute-start(bf16[24,48,128]{2,1,0:T(8,128)(2,1)S(1)} %get-tuple-element.79), channel_id=1, source_target_pairs={{0,16},{8,24},{16,0},{24,8},{1,17},{9,25},{17,1},{25,9},{2,18},{10... | collective-permute-start | bytes 884744 | tf_op jit(solution)/shard_map/ppermute | solution.py:36
  119.9 16.2 %collective-permute-start.15 = (bf16[24,48,128]{2,1,0:T(8,128)(2,1)S(1)}, bf16[24,48,128]{2,1,0:T(8,128)(2,1)S(1)}, u32[]{:S(2)}, u32[]{:S(2)}) collective-permute-start(bf16[24,48,128]{2,1,0:T(8,128)(2,1)S(1)} %get-tuple-element.80), channel_id=1, source_target_pairs={{0,24},{8,16},{16,8},{24,0},{1,25},{9,17},{17,9},{25,1},{2,26},{10... | collective-permute-start | bytes 884744 | tf_op jit(solution)/shard_map/ppermute | solution.py:36
  121.7 50.5 %collective-permute-start.28 = (bf16[24,64,128]{2,1,0:T(8,128)(2,1)S(1)}, bf16[24,64,128]{2,1,0:T(8,128)(2,1)S(1)}, u32[]{:S(2)}, u32[]{:S(2)}) collective-permute-start(bf16[24,64,128]{2,1,0:T(8,128)(2,1)S(1)} %get-tuple-element.87), channel_id=1, source_target_pairs={{0,8},{8,0},{16,24},{24,16},{1,9},{9,1},{17,25},{25,17},{2,10},{10... | collective-permute-start | bytes 1179656 | tf_op jit(solution)/shard_map/ppermute | solution.py:36
  123.3 50.0 %collective-permute-start.29 = (bf16[24,64,128]{2,1,0:T(8,128)(2,1)S(1)}, bf16[24,64,128]{2,1,0:T(8,128)(2,1)S(1)}, u32[]{:S(2)}, u32[]{:S(2)}) collective-permute-start(bf16[24,64,128]{2,1,0:T(8,128)(2,1)S(1)} %get-tuple-element.88), channel_id=1, source_target_pairs={{0,16},{8,24},{16,0},{24,8},{1,17},{9,25},{17,1},{25,9},{2,18},{10... | collective-permute-start | bytes 1179656 | tf_op jit(solution)/shard_map/ppermute | solution.py:36
  126.7 35.7 %collective-permute-start.47 = (bf16[24,48,128]{2,1,0:T(8,128)(2,1)S(1)}, bf16[24,48,128]{2,1,0:T(8,128)(2,1)S(1)}, u32[]{:S(2)}, u32[]{:S(2)}) collective-permute-start(bf16[24,48,128]{2,1,0:T(8,128)(2,1)S(1)} %get-tuple-element.102), channel_id=1, source_target_pairs={{0,16},{8,24},{16,0},{24,8},{1,17},{9,25},{17,1},{25,9},{2,18},{10... | collective-permute-start | bytes 884744 | tf_op jit(solution)/shard_map/ppermute | solution.py:36
  134.5 27.8 %collective-permute-start.48 = (bf16[24,48,128]{2,1,0:T(8,128)(2,1)S(1)}, bf16[24,48,128]{2,1,0:T(8,128)(2,1)S(1)}, u32[]{:S(2)}, u32[]{:S(2)}) collective-permute-start(bf16[24,48,128]{2,1,0:T(8,128)(2,1)S(1)} %get-tuple-element.103), channel_id=1, source_target_pairs={{0,24},{8,16},{16,8},{24,0},{1,25},{9,17},{17,9},{25,1},{2,26},{10... | collective-permute-start | bytes 884744 | tf_op jit(solution)/shard_map/ppermute | solution.py:36
  136.0 39.1 %collective-permute-start.30 = (bf16[24,64,128]{2,1,0:T(8,128)(2,1)S(1)}, bf16[24,64,128]{2,1,0:T(8,128)(2,1)S(1)}, u32[]{:S(2)}, u32[]{:S(2)}) collective-permute-start(bf16[24,64,128]{2,1,0:T(8,128)(2,1)S(1)} %get-tuple-element.89), channel_id=1, source_target_pairs={{0,24},{8,16},{16,8},{24,0},{1,25},{9,17},{17,9},{25,1},{2,26},{10... | collective-permute-start | bytes 1179656 | tf_op jit(solution)/shard_map/ppermute | solution.py:36
  162.3 28.7 %collective-permute-start.16 = (bf16[32,48,128]{2,1,0:T(8,128)(2,1)S(1)}, bf16[32,48,128]{2,1,0:T(8,128)(2,1)S(1)}, u32[]{:S(2)}, u32[]{:S(2)}) collective-permute-start(bf16[32,48,128]{2,1,0:T(8,128)(2,1)S(1)} %get-tuple-element.82), channel_id=1, source_target_pairs={{0,1},{1,0},{2,3},{3,2},{4,5},{5,4},{6,7},{7,6},{8,9},{9,8},{10,11... | collective-permute-start | bytes 1179656 | tf_op jit(solution)/shard_map/ppermute | solution.py:32
  171.6 14.4 %collective-permute-start.49 = (bf16[24,48,128]{2,1,0:T(8,128)(2,1)S(1)}, bf16[24,48,128]{2,1,0:T(8,128)(2,1)S(1)}, u32[]{:S(2)}, u32[]{:S(2)}) collective-permute-start(bf16[24,48,128]{2,1,0:T(8,128)(2,1)S(1)} %get-tuple-element.105), channel_id=1, source_target_pairs={{0,8},{8,0},{16,24},{24,16},{1,9},{9,1},{17,25},{25,17},{2,10},{10... | collective-permute-start | bytes 884744 | tf_op jit(solution)/shard_map/ppermute | solution.py:36
  172.2 15.0 %collective-permute-start.50 = (bf16[24,48,128]{2,1,0:T(8,128)(2,1)S(1)}, bf16[24,48,128]{2,1,0:T(8,128)(2,1)S(1)}, u32[]{:S(2)}, u32[]{:S(2)}) collective-permute-start(bf16[24,48,128]{2,1,0:T(8,128)(2,1)S(1)} %get-tuple-element.106), channel_id=1, source_target_pairs={{0,16},{8,24},{16,0},{24,8},{1,17},{9,25},{17,1},{25,9},{2,18},{10... | collective-permute-start | bytes 884744 | tf_op jit(solution)/shard_map/ppermute | solution.py:36
  173.4 16.4 %collective-permute-start.51 = (bf16[24,48,128]{2,1,0:T(8,128)(2,1)S(1)}, bf16[24,48,128]{2,1,0:T(8,128)(2,1)S(1)}, u32[]{:S(2)}, u32[]{:S(2)}) collective-permute-start(bf16[24,48,128]{2,1,0:T(8,128)(2,1)S(1)} %get-tuple-element.107), channel_id=1, source_target_pairs={{0,24},{8,16},{16,8},{24,0},{1,25},{9,17},{17,9},{25,1},{2,26},{10... | collective-permute-start | bytes 884744 | tf_op jit(solution)/shard_map/ppermute | solution.py:36
  185.4 12.1 %collective-permute-start.31 = (bf16[24,64,128]{2,1,0:T(8,128)(2,1)S(1)}, bf16[24,64,128]{2,1,0:T(8,128)(2,1)S(1)}, u32[]{:S(2)}, u32[]{:S(2)}) collective-permute-start(bf16[24,64,128]{2,1,0:T(8,128)(2,1)S(1)} %get-tuple-element.91), channel_id=1, source_target_pairs={{0,8},{8,0},{16,24},{24,16},{1,9},{9,1},{17,25},{25,17},{2,10},{10... | collective-permute-start | bytes 1179656 | tf_op jit(solution)/shard_map/ppermute | solution.py:36
  186.0 14.2 %collective-permute-start.32 = (bf16[24,64,128]{2,1,0:T(8,128)(2,1)S(1)}, bf16[24,64,128]{2,1,0:T(8,128)(2,1)S(1)}, u32[]{:S(2)}, u32[]{:S(2)}) collective-permute-start(bf16[24,64,128]{2,1,0:T(8,128)(2,1)S(1)} %get-tuple-element.92), channel_id=1, source_target_pairs={{0,16},{8,24},{16,0},{24,8},{1,17},{9,25},{17,1},{25,9},{2,18},{10... | collective-permute-start | bytes 1179656 | tf_op jit(solution)/shard_map/ppermute | solution.py:36
  187.2 18.0 %collective-permute-start.33 = (bf16[24,64,128]{2,1,0:T(8,128)(2,1)S(1)}, bf16[24,64,128]{2,1,0:T(8,128)(2,1)S(1)}, u32[]{:S(2)}, u32[]{:S(2)}) collective-permute-start(bf16[24,64,128]{2,1,0:T(8,128)(2,1)S(1)} %get-tuple-element.93), channel_id=1, source_target_pairs={{0,24},{8,16},{16,8},{24,0},{1,25},{9,17},{17,9},{25,1},{2,26},{10... | collective-permute-start | bytes 1179656 | tf_op jit(solution)/shard_map/ppermute | solution.py:36
  190.9 15.6 %collective-permute-start.52 = (bf16[32,48,128]{2,1,0:T(8,128)(2,1)S(1)}, bf16[32,48,128]{2,1,0:T(8,128)(2,1)S(1)}, u32[]{:S(2)}, u32[]{:S(2)}) collective-permute-start(bf16[32,48,128]{2,1,0:T(8,128)(2,1)S(1)} %get-tuple-element.109), channel_id=1, source_target_pairs={{0,1},{1,0},{2,3},{3,2},{4,5},{5,4},{6,7},{7,6},{8,9},{9,8},{10,11... | collective-permute-start | bytes 1179656 | tf_op jit(solution)/shard_map/ppermute | solution.py:32
  191.2 19.4 %collective-permute-start.17 = (bf16[8,48,128]{2,1,0:T(8,128)(2,1)S(1)}, bf16[8,48,128]{2,1,0:T(8,128)(2,1)S(1)}, u32[]{:S(2)}, u32[]{:S(2)}) collective-permute-start(bf16[8,48,128]{2,1,0:T(8,128)(2,1)S(1)} %get-tuple-element.124), channel_id=1, source_target_pairs={{0,6},{1,7},{2,4},{3,5},{4,2},{5,3},{6,0},{7,1},{8,14},{9,15},{10,... | collective-permute-start | bytes 294920 | tf_op jit(solution)/shard_map/ppermute | solution.py:27
  197.4 13.2 %collective-permute-start.19 = (bf16[8,48,128]{2,1,0:T(8,128)(2,1)S(1)}, bf16[8,48,128]{2,1,0:T(8,128)(2,1)S(1)}, u32[]{:S(2)}, u32[]{:S(2)}) collective-permute-start(bf16[8,48,128]{2,1,0:T(8,128)(2,1)S(1)} %get-tuple-element.125), channel_id=1, source_target_pairs={{0,2},{1,3},{2,0},{3,1},{4,6},{5,7},{6,4},{7,5},{8,10},{9,11},{10,... | collective-permute-start | bytes 294920 | tf_op jit(solution)/shard_map/ppermute | solution.py:27
  200.2 11.2 %collective-permute-start.18 = (bf16[8,48,128]{2,1,0:T(8,128)(2,1)S(1)}, bf16[8,48,128]{2,1,0:T(8,128)(2,1)S(1)}, u32[]{:S(2)}, u32[]{:S(2)}) collective-permute-start(bf16[8,48,128]{2,1,0:T(8,128)(2,1)S(1)} %get-tuple-element.126), channel_id=1, source_target_pairs={{0,4},{1,5},{2,6},{3,7},{4,0},{5,1},{6,2},{7,3},{8,12},{9,13},{10,... | collective-permute-start | bytes 294920 | tf_op jit(solution)/shard_map/ppermute | solution.py:27
  206.4 8.7 %collective-permute-start.34 = (bf16[32,64,128]{2,1,0:T(8,128)(2,1)S(1)}, bf16[32,64,128]{2,1,0:T(8,128)(2,1)S(1)}, u32[]{:S(2)}, u32[]{:S(2)}) collective-permute-start(bf16[32,64,128]{2,1,0:T(8,128)(2,1)S(1)} %get-tuple-element.95), channel_id=1, source_target_pairs={{0,1},{1,0},{2,3},{3,2},{4,5},{5,4},{6,7},{7,6},{8,9},{9,8},{10,11... | collective-permute-start | bytes 1572872 | tf_op jit(solution)/shard_map/ppermute | solution.py:32
  206.7 8.7 %collective-permute-start.53 = (bf16[8,48,128]{2,1,0:T(8,128)(2,1)S(1)}, bf16[8,48,128]{2,1,0:T(8,128)(2,1)S(1)}, u32[]{:S(2)}, u32[]{:S(2)}) collective-permute-start(bf16[8,48,128]{2,1,0:T(8,128)(2,1)S(1)} %get-tuple-element.121), channel_id=1, source_target_pairs={{0,6},{1,7},{2,4},{3,5},{4,2},{5,3},{6,0},{7,1},{8,14},{9,15},{10,... | collective-permute-start | bytes 294920 | tf_op jit(solution)/shard_map/ppermute | solution.py:27
  210.6 7.5 %collective-permute-start.55 = (bf16[8,48,128]{2,1,0:T(8,128)(2,1)S(1)}, bf16[8,48,128]{2,1,0:T(8,128)(2,1)S(1)}, u32[]{:S(2)}, u32[]{:S(2)}) collective-permute-start(bf16[8,48,128]{2,1,0:T(8,128)(2,1)S(1)} %get-tuple-element.122), channel_id=1, source_target_pairs={{0,2},{1,3},{2,0},{3,1},{4,6},{5,7},{6,4},{7,5},{8,10},{9,11},{10,... | collective-permute-start | bytes 294920 | tf_op jit(solution)/shard_map/ppermute | solution.py:27
  210.6 16.9 %collective-permute-start.54 = (bf16[8,48,128]{2,1,0:T(8,128)(2,1)S(1)}, bf16[8,48,128]{2,1,0:T(8,128)(2,1)S(1)}, u32[]{:S(2)}, u32[]{:S(2)}) collective-permute-start(bf16[8,48,128]{2,1,0:T(8,128)(2,1)S(1)} %get-tuple-element.123), channel_id=1, source_target_pairs={{0,4},{1,5},{2,6},{3,7},{4,0},{5,1},{6,2},{7,3},{8,12},{9,13},{10,... | collective-permute-start | bytes 294920 | tf_op jit(solution)/shard_map/ppermute | solution.py:27
  211.5 43.4 %collective-permute-start.22 = (bf16[8,48,128]{2,1,0:T(8,128)(2,1)S(1)}, bf16[8,48,128]{2,1,0:T(8,128)(2,1)S(1)}, u32[]{:S(2)}, u32[]{:S(2)}) collective-permute-start(bf16[8,48,128]{2,1,0:T(8,128)(2,1)S(1)} %select_convert_fusion.2), channel_id=1, source_target_pairs={{0,6},{1,7},{2,4},{3,5},{4,2},{5,3},{6,0},{7,1},{8,14},{9,15},{10,... | collective-permute-start | bytes 294920 | tf_op jit(solution)/shard_map/ppermute | solution.py:27
  215.1 42.7 %collective-permute-start.21 = (bf16[8,48,128]{2,1,0:T(8,128)(2,1)S(1)}, bf16[8,48,128]{2,1,0:T(8,128)(2,1)S(1)}, u32[]{:S(2)}, u32[]{:S(2)}) collective-permute-start(bf16[8,48,128]{2,1,0:T(8,128)(2,1)S(1)} %select_convert_fusion.2), channel_id=1, source_target_pairs={{0,4},{1,5},{2,6},{3,7},{4,0},{5,1},{6,2},{7,3},{8,12},{9,13},{10,... | collective-permute-start | bytes 294920 | tf_op jit(solution)/shard_map/ppermute | solution.py:27
  215.4 12.2 %collective-permute-start.35 = (bf16[8,64,128]{2,1,0:T(8,128)(2,1)S(1)}, bf16[8,64,128]{2,1,0:T(8,128)(2,1)S(1)}, u32[]{:S(2)}, u32[]{:S(2)}) collective-permute-start(bf16[8,64,128]{2,1,0:T(8,128)(2,1)S(1)} %get-tuple-element.118), channel_id=1, source_target_pairs={{0,6},{1,7},{2,4},{3,5},{4,2},{5,3},{6,0},{7,1},{8,14},{9,15},{10,... | collective-permute-start | bytes 393224 | tf_op jit(solution)/shard_map/ppermute | solution.py:27
  218.1 10.0 %collective-permute-start.37 = (bf16[8,64,128]{2,1,0:T(8,128)(2,1)S(1)}, bf16[8,64,128]{2,1,0:T(8,128)(2,1)S(1)}, u32[]{:S(2)}, u32[]{:S(2)}) collective-permute-start(bf16[8,64,128]{2,1,0:T(8,128)(2,1)S(1)} %get-tuple-element.119), channel_id=1, source_target_pairs={{0,2},{1,3},{2,0},{3,1},{4,6},{5,7},{6,4},{7,5},{8,10},{9,11},{10,... | collective-permute-start | bytes 393224 | tf_op jit(solution)/shard_map/ppermute | solution.py:27
  227.5 12.6 %collective-permute-start.36 = (bf16[8,64,128]{2,1,0:T(8,128)(2,1)S(1)}, bf16[8,64,128]{2,1,0:T(8,128)(2,1)S(1)}, u32[]{:S(2)}, u32[]{:S(2)}) collective-permute-start(bf16[8,64,128]{2,1,0:T(8,128)(2,1)S(1)} %get-tuple-element.120), channel_id=1, source_target_pairs={{0,4},{1,5},{2,6},{3,7},{4,0},{5,1},{6,2},{7,3},{8,12},{9,13},{10,... | collective-permute-start | bytes 393224 | tf_op jit(solution)/shard_map/ppermute | solution.py:27
  240.2 8.4 %collective-permute-start.40 = (bf16[8,64,128]{2,1,0:T(8,128)(2,1)S(1)}, bf16[8,64,128]{2,1,0:T(8,128)(2,1)S(1)}, u32[]{:S(2)}, u32[]{:S(2)}) collective-permute-start(bf16[8,64,128]{2,1,0:T(8,128)(2,1)S(1)} %select_convert_fusion), channel_id=1, source_target_pairs={{0,6},{1,7},{2,4},{3,5},{4,2},{5,3},{6,0},{7,1},{8,14},{9,15},{10,... | collective-permute-start | bytes 393224 | tf_op jit(solution)/shard_map/ppermute | solution.py:27
  242.3 10.9 %collective-permute-start.39 = (bf16[8,64,128]{2,1,0:T(8,128)(2,1)S(1)}, bf16[8,64,128]{2,1,0:T(8,128)(2,1)S(1)}, u32[]{:S(2)}, u32[]{:S(2)}) collective-permute-start(bf16[8,64,128]{2,1,0:T(8,128)(2,1)S(1)} %select_convert_fusion), channel_id=1, source_target_pairs={{0,4},{1,5},{2,6},{3,7},{4,0},{5,1},{6,2},{7,3},{8,12},{9,13},{10,... | collective-permute-start | bytes 393224 | tf_op jit(solution)/shard_map/ppermute | solution.py:27
  242.3 12.4 %collective-permute-start.38 = (bf16[8,64,128]{2,1,0:T(8,128)(2,1)S(1)}, bf16[8,64,128]{2,1,0:T(8,128)(2,1)S(1)}, u32[]{:S(2)}, u32[]{:S(2)}) collective-permute-start(bf16[8,64,128]{2,1,0:T(8,128)(2,1)S(1)} %select_convert_fusion), channel_id=1, source_target_pairs={{0,2},{1,3},{2,0},{3,1},{4,6},{5,7},{6,4},{7,5},{8,10},{9,11},{10,... | collective-permute-start | bytes 393224 | tf_op jit(solution)/shard_map/ppermute | solution.py:27
  248.5 9.3 %collective-permute-start.20 = (bf16[8,48,128]{2,1,0:T(8,128)(2,1)S(1)}, bf16[8,48,128]{2,1,0:T(8,128)(2,1)S(1)}, u32[]{:S(2)}, u32[]{:S(2)}) collective-permute-start(bf16[8,48,128]{2,1,0:T(8,128)(2,1)S(1)} %select_convert_fusion.2), channel_id=1, source_target_pairs={{0,2},{1,3},{2,0},{3,1},{4,6},{5,7},{6,4},{7,5},{8,10},{9,11},{10,... | collective-permute-start | bytes 294920 | tf_op jit(solution)/shard_map/ppermute | solution.py:27
  253.3 7.6 %collective-permute-start.58 = (bf16[8,48,128]{2,1,0:T(8,128)(2,1)S(1)}, bf16[8,48,128]{2,1,0:T(8,128)(2,1)S(1)}, u32[]{:S(2)}, u32[]{:S(2)}) collective-permute-start(bf16[8,48,128]{2,1,0:T(8,128)(2,1)S(1)} %select_convert_fusion.1), channel_id=1, source_target_pairs={{0,6},{1,7},{2,4},{3,5},{4,2},{5,3},{6,0},{7,1},{8,14},{9,15},{10,... | collective-permute-start | bytes 294920 | tf_op jit(solution)/shard_map/ppermute | solution.py:27
  254.8 9.2 %collective-permute-start.57 = (bf16[8,48,128]{2,1,0:T(8,128)(2,1)S(1)}, bf16[8,48,128]{2,1,0:T(8,128)(2,1)S(1)}, u32[]{:S(2)}, u32[]{:S(2)}) collective-permute-start(bf16[8,48,128]{2,1,0:T(8,128)(2,1)S(1)} %select_convert_fusion.1), channel_id=1, source_target_pairs={{0,4},{1,5},{2,6},{3,7},{4,0},{5,1},{6,2},{7,3},{8,12},{9,13},{10,... | collective-permute-start | bytes 294920 | tf_op jit(solution)/shard_map/ppermute | solution.py:27
  254.9 9.1 %collective-permute-start.56 = (bf16[8,48,128]{2,1,0:T(8,128)(2,1)S(1)}, bf16[8,48,128]{2,1,0:T(8,128)(2,1)S(1)}, u32[]{:S(2)}, u32[]{:S(2)}) collective-permute-start(bf16[8,48,128]{2,1,0:T(8,128)(2,1)S(1)} %select_convert_fusion.1), channel_id=1, source_target_pairs={{0,2},{1,3},{2,0},{3,1},{4,6},{5,7},{6,4},{7,5},{8,10},{9,11},{10,... | collective-permute-start | bytes 294920 | tf_op jit(solution)/shard_map/ppermute | solution.py:27
  257.8 19.9 %collective-permute-start.60 = (bf16[32,64,128]{2,1,0:T(8,128)(2,1)S(1)}, bf16[32,64,128]{2,1,0:T(8,128)(2,1)S(1)}, u32[]{:S(2)}, u32[]{:S(2)}) collective-permute-start(bf16[32,64,128]{2,1,0:T(8,128)(2,1)S(1)} %pad_maximum_fusion.1.refs_1_), channel_id=1, source_target_pairs={{0,1},{1,0},{2,3},{3,2},{4,5},{5,4},{6,7},{7,6},{8,9},{9,8},{10,11... | collective-permute-start | bytes 1572872 | tf_op jit(solution)/shard_map/ppermute | solution.py:32
  257.9 19.8 %collective-permute-start.59 = (bf16[32,48,128]{2,1,0:T(8,128)(2,1)S(1)}, bf16[32,48,128]{2,1,0:T(8,128)(2,1)S(1)}, u32[]{:S(2)}, u32[]{:S(2)}) collective-permute-start(bf16[32,48,128]{2,1,0:T(8,128)(2,1)S(1)} %pad_maximum_fusion.3.refs_0_), channel_id=1, source_target_pairs={{0,1},{1,0},{2,3},{3,2},{4,5},{5,4},{6,7},{7,6},{8,9},{9,8},{10,11... | collective-permute-start | bytes 1179656 | tf_op jit(solution)/shard_map/ppermute | solution.py:32
  264.0 13.7 %collective-permute-start.61 = (bf16[32,48,128]{2,1,0:T(8,128)(2,1)S(1)}, bf16[32,48,128]{2,1,0:T(8,128)(2,1)S(1)}, u32[]{:S(2)}, u32[]{:S(2)}) collective-permute-start(bf16[32,48,128]{2,1,0:T(8,128)(2,1)S(1)} %pad_maximum_fusion.5.refs_2_), channel_id=1, source_target_pairs={{0,1},{1,0},{2,3},{3,2},{4,5},{5,4},{6,7},{7,6},{8,9},{9,8},{10,11... | collective-permute-start | bytes 1179656 | tf_op jit(solution)/shard_map/ppermute | solution.py:32
  274.2 3.4 %copy-start.3 = (bf16[160,128]{1,0:T(8,128)(2,1)S(1)}, bf16[160,128]{1,0:T(8,128)(2,1)}, u32[]{:S(2)}) copy-start(bf16[160,128]{1,0:T(8,128)(2,1)} %documents_ref.1) | copy-start | bytes 122884
  (2 other events, 1.6 us)
